TPU v7x, 128 devices: a whole 4x4x4 slice. The times are simulated.
128 devices in a mesh: lat: 8 (over y_lo, x), lon: 16 (over z, y_hi, core).
Axes of the slice: x: 4, y: 4 (y_hi: 2, y_lo: 2; y = y_hi * 2 + y_lo), z: 4, core: 2. Of those that a mesh axis runs over, the one named last changes fastest.
Arguments:
- block_input: float32 [192, 384, 384], P('lat', 'lon'), may hold values from -90 to 90, as said below
- cotangent: float32 [192, 384, 384], P('lat', 'lon'), may hold values from -6 to 6
- weights: float32 [1769472], replicated, may hold values from -4 to 4, as said below
- first_moment: float32 [1769472], P(('lat', 'lon')), may hold values from -3 to 3
- second_moment: float32 [1769472], P(('lat', 'lon')), may hold values from 0.05 to 2
- bias_table: float32 [12, 529], replicated, may hold values from -5 to 5
- bias_index: int32 [144, 144], replicated, may hold values from 0 to 528
- region_ids: int32 [192, 384], P('lat', 'lon'), may hold values from 0 to 2
Outputs:
- grad_input: float32 [192, 384, 384], P('lat', 'lon')
- weights_new: float32 [1769472], replicated
- first_new: float32 [1769472], P(('lat', 'lon'))
- second_new: float32 [1769472], P(('lat', 'lon'))
- table_grad: float32 [12, 529], replicated
Inputs may be any that keep to these rules, and one draw needn't show every extreme that they name: `block_input`: Tokens' features; real values. `weights`: real values. `region_ids`: entry (r, c) is the region of the token at ((r + 6) mod 192, (c + 6) mod 384) of the input grid.
All inputs are finite; a program needn't handle non-finite values.
Results may differ from a plain program's by a relative error of at most 0.0003.
Values sent between devices are 32-bit elements; how exact they have to be, the bound alone decides.
No kernel may reach another device: no remote copies, remote signals or barrier semaphores. Data moves between devices by JAX's collectives and lax.ppermute only.
A program may use at most 128 MiB of HBM per device.

v0:
```python
import math

import jax
import jax.numpy as jnp
from jax import lax
from jax.sharding import PartitionSpec as P

D = 384
HEADS = 12
FF = 1536
WIN = 12
HEAD_DIM = 32
SHIFT = 6


precise = lax.Precision.HIGHEST


def passed_along(value, axis, by):
    size = lax.axis_size(axis)
    return lax.ppermute(value, axis, [(i, (i + by) % size) for i in range(size)])


def split_up(value, dim, size):
    before, after = (value.shape[:dim], value.shape[dim + 1 :])
    return jnp.moveaxis(value.reshape(*before, size, -1, *after), dim, 0)


def sent_and_summed(value, axis, dim):
    blocks = split_up(value, dim, lax.axis_size(axis))
    arrived = lax.all_to_all(blocks, axis, split_axis=0, concat_axis=0, tiled=True)
    return arrived.sum(axis=0)


def laid_out(blocks, dim):
    blocks = jnp.moveaxis(blocks, 0, dim)
    dims = blocks.shape
    return blocks.reshape(*dims[:dim], dims[dim] * dims[dim + 1], *dims[dim + 2 :])


def copy_for_each(value, axis):
    copies = jnp.broadcast_to(value, (lax.axis_size(axis), *value.shape))
    return lax.all_to_all(copies, axis, split_axis=0, concat_axis=0, tiled=True)


def collect(value, axis, dim):
    return laid_out(copy_for_each(value, axis), dim)


def normalize(values):
    center = values - jnp.mean(values, axis=-1, keepdims=True)
    spread = jnp.mean(center * center, axis=-1, keepdims=True)
    return center / jnp.sqrt(spread + 1e-05)


def windows(tensor):
    height, breadth, features = tensor.shape
    blocks = tensor.reshape(height // WIN, WIN, breadth // WIN, WIN, features)
    return blocks.transpose(0, 2, 1, 3, 4).reshape(-1, WIN * WIN, features)


def unwindow(blocks, height, breadth):
    features = blocks.shape[-1]
    tensor = blocks.reshape(height // WIN, breadth // WIN, WIN, WIN, features)
    return tensor.transpose(0, 2, 1, 3, 4).reshape(height, breadth, features)


def unpack(packed):
    first_cut = D * 3 * D
    second_cut = first_cut + D * D
    third_cut = second_cut + D * FF
    return (
        packed[:first_cut].reshape(D, 3 * D),
        packed[first_cut:second_cut].reshape(D, D),
        packed[second_cut:third_cut].reshape(D, FF),
        packed[third_cut:].reshape(FF, D),
    )


def attend(tensor, w_all, bias_table, bias_index, region_ids, wrapped):
    w_qkv, w_proj, _, _ = unpack(w_all)
    height, breadth, _ = tensor.shape
    flat_rows = normalize(tensor).reshape(-1, D)
    mixed = jnp.dot(flat_rows, w_qkv, precision=precise, preferred_element_type=jnp.float32)
    mixed = windows(mixed.reshape(height, breadth, 3 * D))
    window_count = mixed.shape[0]
    query = mixed[:, :, :D].reshape(window_count, WIN * WIN, HEADS, HEAD_DIM)
    keyed = mixed[:, :, D : 2 * D].reshape(window_count, WIN * WIN, HEADS, HEAD_DIM)
    valued = mixed[:, :, 2 * D :].reshape(window_count, WIN * WIN, HEADS, HEAD_DIM)
    scores = jnp.einsum("wihd,wjhd->whij", query, keyed, precision=precise) / math.sqrt(HEAD_DIM)
    scores = scores + jnp.take(bias_table, bias_index, axis=1)[None]
    labels = windows(region_ids[:, :, None])[:, :, 0]
    halves = windows(
        jnp.broadcast_to(wrapped[:, None, None], (height, breadth, 1)).astype(jnp.int32)
    )[:, :, 0]
    allowed = (labels[:, :, None] == labels[:, None, :]) & (
        halves[:, :, None] == halves[:, None, :]
    )
    allowed = allowed[:, None]
    masked = jnp.where(allowed, scores, -jnp.inf)
    summit = lax.stop_gradient(jnp.max(masked, axis=-1, keepdims=True))
    raised = jnp.exp(masked - summit)
    probability = raised / jnp.sum(raised, axis=-1, keepdims=True)
    context = jnp.einsum("whij,wjhd->wihd", probability, valued, precision=precise)
    context = unwindow(context.reshape(window_count, WIN * WIN, D), height, breadth).reshape(-1, D)
    return jnp.dot(context, w_proj, precision=precise, preferred_element_type=jnp.float32).reshape(
        height, breadth, D
    )


def feed(tensor, w_all):
    _, _, w_up, w_down = unpack(w_all)
    flat_rows = normalize(tensor).reshape(-1, D)
    hidden = jax.nn.gelu(
        jnp.dot(flat_rows, w_up, precision=precise, preferred_element_type=jnp.float32),
        approximate=True,
    )
    return jnp.dot(hidden, w_down, precision=precise, preferred_element_type=jnp.float32).reshape(
        tensor.shape
    )


def shift_ahead(stacked):
    from_east = passed_along(stacked[:, :, :SHIFT], "lon", -1)
    widened = jnp.concatenate([stacked[:, :, SHIFT:], from_east], axis=2)
    from_south = passed_along(widened[:, :SHIFT], "lat", -1)
    return jnp.concatenate([widened[:, SHIFT:], from_south], axis=1)


def shift_back(stacked):
    from_north = passed_along(stacked[:, -SHIFT:], "lat", 1)
    lengthened = jnp.concatenate([from_north, stacked[:, :-SHIFT]], axis=1)
    from_west = passed_along(lengthened[:, :, -SHIFT:], "lon", 1)
    return jnp.concatenate([from_west, lengthened[:, :, :-SHIFT]], axis=2)


def per_device(
    block_input, cotangent, weights, first_moment, second_moment, bias_table, bias_index, region_ids
):
    tile_rows, tile_cols, _ = block_input.shape
    lat_count = lax.axis_size("lat")
    lon_count = lax.axis_size("lon")
    global_rows = lax.axis_index("lat") * tile_rows + jnp.arange(tile_rows)
    wrapped = global_rows >= tile_rows * lat_count - SHIFT

    def attention_part(tensor, w_all, table):
        return attend(tensor, w_all, table, bias_index, region_ids, wrapped)

    shifted = shift_ahead(block_input[None])[0]
    attn_shifted, pull_attn = jax.vjp(attention_part, shifted, weights, bias_table)
    mixed = block_input + shift_back(attn_shifted[None])[0]
    _, pull_feed = jax.vjp(feed, mixed, weights)
    grad_feed, weights_feed = pull_feed(cotangent)
    grad_mixed = cotangent + grad_feed
    grad_moved = shift_ahead(grad_mixed[None])[0]
    grad_shifted, weights_attn, grad_table = pull_attn(grad_moved)
    grad_input = grad_mixed + shift_back(grad_shifted[None])[0]
    grad_weights = weights_feed + weights_attn
    factor = 1.0 / math.sqrt(tile_rows * tile_cols * lat_count * lon_count)
    shard_len = first_moment.shape[0]
    partial_sum = sent_and_summed(grad_weights, "lat", 0)
    summed = sent_and_summed(partial_sum, "lon", 0) * factor
    owner_rank = lax.axis_index("lat") * lon_count + lax.axis_index("lon")
    own_weights = lax.dynamic_slice_in_dim(weights, owner_rank * shard_len, shard_len)
    first_new = 0.9 * first_moment + 0.1 * summed
    second_new = 0.95 * second_moment + 0.05 * summed * summed
    own_new = own_weights - 0.01 * first_new / (jnp.sqrt(second_new) + 1e-08)
    along_lon = collect(own_new, "lon", 0)
    gathered = lax.all_gather(along_lon, "lat", axis=0, tiled=True)
    table_grad = lax.psum(grad_table, ("lat", "lon")) * factor
    return (grad_input, gathered, first_new, second_new, table_grad)


def solution(mesh):
    placed = (
        P("lat", "lon", None),
        P("lat", "lon", None),
        P(),
        P(("lat", "lon")),
        P(("lat", "lon")),
        P(),
        P(),
        P("lat", "lon"),
    )
    return jax.shard_map(
        per_device,
        mesh=mesh,
        in_specs=placed,
        out_specs=(P("lat", "lon", None), P(), P(("lat", "lon")), P(("lat", "lon")), P()),
        check_vma=False,
    )
```

profile of v0, /device:TPU:1, one launch (start us, length us, event | category | flops | bytes accessed | tf_op | source)
XLA Modules:
  0.0 691.3 jit_solution(7623276320993546166)
XLA Ops:
  15.0 38.8 %gather_fusion = f32[20736,12]{1,0:T(8,128)} fusion(f32[12,529]{0,1:T(8,128)S(1)} %copy.129, s32[21504]{0:T(1024)S(1)} %pad_clamp_fusion), kind=kCustom, calls=%fused_computation | custom fusion | bytes 2073600 | tf_op jit(solution)/shard_map/jvp(jit(_take))/gather | solution.py:91
  53.8 12.1 %copy.130 = f32[144,144,12]{0,1,2:T(8,128)} copy(f32[144,144,12]{2,1,0:T(8,128)} %bitcast.115) | data formatting | bytes 1990656 | tf_op jit(solution)/shard_map/jvp(jit(_take))/gather | solution.py:91
  88.4 8.2 %convolution_bitcast_fusion = f32[2,2,12,12,1152]{4,3,1,2,0:T(8,128)S(1)} fusion(f32[384,1152,1,1,1]{1,0,2,3,4:T(8,128)} %reshape.392, f32[2,12,2,12,384]{4,3,2,1,0:T(8,128)} %squeeze.11, f32[2,12,2,12]{3,2,1,0:T(2,128)S(1)} %sqrt.38, f32[2,12,2,12]{3,2,1,0:T(2,128)S(1)} %div.137), kind=kOutput, calls=%fused_computation.14 | convolution fusion | flops 3058089984 | bytes 5313024 | tf_op jit(solution)/shard_map/jvp()/dot_general | solution.py:84
  115.0 9.5 %fusion.4 = (f32[4,12,144]{2,1,0:T(8,128)S(1)}, f32[4,12,144,144]{2,3,1,0:T(8,128)S(1)}) fusion(f32[12,144,144]{1,2,0:T(8,128)S(1)} %select_bitcast_fusion, pred[4,144,144]{1,2,0:T(8,128)(4,1)S(1)} %copy-done.23, f32[4,144,12,32]{1,3,2,0:T(8,128)} %bitcast.118, f32[4,144,12,32]{1,3,2,0:T(8,128)} %bitcast.116), kind=kOutput, calls=%fused_computation.11 | convolution fusion | flops 386180352 | bytes 6856704 | tf_op jit(solution)/shard_map/jvp(wihd,wjhd->whij)/dot_general | solution.py:90
  127.4 7.0 %fusion.25 = f32[4,144,12,32]{1,3,2,0:T(8,128)} fusion(f32[4,144,12,32]{1,3,2,0:T(8,128)S(1)} %bitcast.129, f32[4,12,144]{2,1,0:T(8,128)S(1)} %fusion.52, f32[4,12,144,144]{2,3,1,0:T(8,128)S(1)} %get-tuple-element.56, f32[4,12,144]{2,1,0:T(8,128)S(1)} %get-tuple-element.55, f32[12,144,144]{1,2,0:T(8,128)S(1)} %select_bitcast_fusion, ...), kind=kOutput, calls=%fused_computation.37 | convolution fusion | flops 387182592 | bytes 6884352 | tf_op jit(solution)/shard_map/jvp(whij,wjhd->wihd)/dot_general | solution.py:104
  134.4 6.2 copy.132
  173.5 5.9 fusion.59
  179.4 7.9 %fusion.10 = f32[576,1536]{1,0:T(8,128)S(1)} fusion(f32[576,1536]{1,0:T(8,128)S(1)} %fusion.59, f32[576,384]{1,0:T(8,128)S(1)} %bitcast.134, f32[1536,384]{1,0:T(8,128)S(1)} %copy-done.28), kind=kOutput, calls=%fused_computation.20 | convolution fusion | flops 4093673472 | bytes 10321920 | tf_op jit(solution)/shard_map/transpose(jvp())/dot_general | solution.py:118
  194.2 8.4 %collective-permute-start.4 = (f32[1,24,6,384]{3,2,1,0:T(8,128)S(1)}, f32[1,24,6,384]{3,2,1,0:T(8,128)S(1)}, u32[]{:S(2)}, u32[]{:S(2)}) collective-permute-start(f32[1,24,6,384]{3,2,1,0:T(8,128)S(1)} %slice.148), channel_id=1, source_target_pairs={{0,15},{1,0},{2,1},{3,2},{4,3},{5,4},{6,5},{7,6},{8,7},{9,8},{10,9... | collective-permute-start | bytes 663560 | tf_op jit(solution)/shard_map/ppermute | solution.py:21
  202.6 9.7 %fusion.11 = f32[1536,384]{1,0:T(8,128)} fusion(f32[576,384]{1,0:T(8,128)S(1)} %bitcast.135, f32[576,1536]{1,0:T(8,128)S(1)} %fusion.59), kind=kOutput, calls=%fused_computation.21 | convolution fusion | flops 4083941376 | bytes 6782976 | tf_op jit(solution)/shard_map/transpose(jvp())/dot_general | solution.py:118
  217.6 5.9 fusion.60
  246.2 13.7 %fusion.17 = f32[4,12,32,144]{3,2,1,0:T(8,128)} fusion(f32[4,12,32,144]{3,2,1,0:T(8,128)} %copy.135, f32[4,12,144]{2,1,0:T(8,128)} %copy-done.37, f32[4,12,144,144]{2,3,1,0:T(8,128)} %copy-done, f32[4,12,144]{2,1,0:T(8,128)} %copy-done.33, f32[12,144,144]{1,2,0:T(8,128)} %copy-done.1, pred[4,144,144]{1,2,0:T(8,128)(4,1)} %compare_and_fusion), kind=kOutput, calls=%fused_computation.28 | convolution fusion | flops 387182592 | bytes 6884352 | tf_op jit(solution)/shard_map/transpose(jvp(whij,wjhd->wihd))/dot_general | solution.py:104
  260.0 9.2 %multiply_reduce_fusion = (f32[4,12,144]{2,1,0:T(8,128)S(1)}, f32[4,12,144,144]{2,3,1,0:T(8,128)S(1)}) fusion(f32[4,12,144]{2,1,0:T(8,128)S(1)} %copy-done.42, f32[4,12,144]{2,1,0:T(8,128)S(1)} %copy-done.34, f32[12,144,144]{1,2,0:T(8,128)S(1)} %copy-done.2, f32[4,12,144,144]{2,3,1,0:T(8,128)S(1)} %bitcast.112, pred[4,144,144]{1,2,0:T(8,128)(4,1)S(1)} %copy-done.24, ...), kind=kOutput, calls=%fused_computation.4 | convolution fusion | flops 389166336 | bytes 10893312 | tf_op jit(solution)/shard_map/transpose(jvp(whij,wjhd->wihd))/dot_general | solution.py:104
  278.4 8.6 %fusion.2 = f32[4,12,144,32]{2,3,1,0:T(8,128)} fusion(f32[4,144,12,32]{1,3,2,0:T(8,128)S(1)} %bitcast.119, f32[4,12,144,144]{2,3,1,0:T(8,128)S(1)} %get-tuple-element.36), kind=kOutput, calls=%fused_computation.9 | convolution fusion | flops 383201280 | bytes 5750784 | tf_op jit(solution)/shard_map/transpose(jvp(wihd,wjhd->whij))/dot_general | solution.py:90
  310.7 7.0 %fusion.62 = f32[384,1152]{1,0:T(8,128)} fusion(f32[576,384]{1,0:T(8,128)} %bitcast.138, f32[576,1152]{1,0:T(8,128)S(1)} %reshape.369), kind=kOutput, calls=%fused_computation.119 | convolution fusion | flops 3057647616 | bytes 5308416 | tf_op jit(solution)/shard_map/transpose(jvp())/dot_general | solution.py:84
  320.4 9.8 %add_add_fusion = f32[1769472]{0:T(1024)S(1)} fusion(f32[442368]{0:T(1024)} %reshape.370, f32[147456]{0:T(1024)} %reshape.368, f32[589824]{0:T(1024)} %reshape.366, f32[589824]{0:T(1024)S(1)} %copy-done.9), kind=kLoop, calls=%fused_computation.2 | loop fusion | flops 5308416 | bytes 14155776 | tf_op jit(solution)/shard_map/add | solution.py:158
  330.2 84.0 %all_to_all.24 = f32[8,1,221184]{2,1,0:T(1,128)} all-to-all(f32[8,1,221184]{2,1,0:T(1,128)S(1)} %bitcast.113), channel_id=1, replica_groups=mesh['lat'=8,'lon'=16] {'lat'}, dimensions={0} | all-to-all | bytes 14155776 | tf_op jit(solution)/shard_map/all_to_all | solution.py:31
  414.2 10.5 %reduce_sum.132 = f32[221184]{0:T(1024)} reduce(f32[8,1,221184]{2,1,0:T(1,128)} %all_to_all.24, f32[]{:T(128)} %constant.31.clone.1), dimensions={0,1}, to_apply=%region_11.12 | reduce | flops 1548288 | bytes 7962628 | tf_op jit(solution)/shard_map/reduce_sum | solution.py:32
  429.1 15.5 %all-to-all-done.1 = f32[16,1,13824]{2,1,0:T(1,128)S(1)} async-done(((f32[16,1,13824]{2,1,0:T(1,128)}), f32[16,1,13824]{2,1,0:T(1,128)S(1)}, u32[]{:S(2)}, u32[]{:S(2)}) %all-to-all-start.1) | async-done | bytes 884768 | tf_op jit(solution)/shard_map/all_to_all | solution.py:31
  447.2 19.2 %all_to_all.25 = f32[16,1,13824]{2,1,0:T(1,128)} all-to-all(f32[16,1,13824]{2,1,0:T(1,128)S(1)} %broadcast_in_dim.93), channel_id=1, replica_groups=mesh['lat'=8,'lon'=16] {'lon'}, dimensions={0} | all-to-all | bytes 1769472 | tf_op jit(solution)/shard_map/all_to_all | solution.py:43
  470.8 6.4 multiply_reduce_fusion.1
  481.7 10.4 %copy.157 = f32[144,144,12]{2,1,0:T(8,128)} copy(f32[144,144,12]{0,1,2:T(8,128)S(1)} %bitcast.126) | data formatting | bytes 1990656 | tf_op jit(solution)/shard_map/transpose(jvp())/reduce_sum | solution.py:91
  492.1 112.5 %scatter_custom_fusion = f32[12,529]{0,1:T(8,128)S(1)} fusion(s32[20736]{0:T(1024)} %copy-done.39, f32[20736,12]{1,0:T(8,128)} %bitcast.121, f32[]{:T(128)} %constant.31.clone.1), kind=kCustom, calls=%fused_computation.81 | custom fusion | flops 248832 | bytes 25904 | tf_op jit(solution)/shard_map/transpose(jvp(jit(_take)))/scatter-add | solution.py:91
  604.5 65.9 %psum.7 = f32[12,529]{0,1:T(8,128)S(1)} all-reduce(f32[12,529]{0,1:T(8,128)S(1)} %scatter_custom_fusion), channel_id=1, replica_groups=mesh['lat'=8,'lon'=16] {'lat','lon'}, use_global_device_ids=true, to_apply=%region_15.16 | all-reduce | flops 6348 | bytes 50784 | tf_op jit(solution)/shard_map/psum | solution.py:170
  (228 shorter events, 183.9 us)
Async XLA Ops:
  8.2 59.4 %collective-permute-start = (f32[1,24,6,384]{3,2,1,0:T(8,128)S(1)}, f32[1,24,6,384]{3,2,1,0:T(8,128)S(1)}, u32[]{:S(2)}, u32[]{:S(2)}) collective-permute-start(f32[1,24,6,384]{3,2,1,0:T(8,128)S(1)} %slice.139), channel_id=1, source_target_pairs={{0,15},{1,0},{2,1},{3,2},{4,3},{5,4},{6,5},{7,6},{8,7},{9,8},{10,9... | collective-permute-start | bytes 663560 | tf_op jit(solution)/shard_map/ppermute | solution.py:21
  12.8 54.8 %copy-start.12 = (f32[1,24,18,384]{3,2,1,0:T(8,128)}, f32[1,24,18,384]{3,2,1,0:T(8,128)S(1)}, u32[]{:S(2)}) copy-start(f32[1,24,18,384]{3,2,1,0:T(8,128)S(1)} %slice.138) | copy-start | bytes 1990660
  67.5 59.1 %copy-start.1 = (f32[12,144,144]{1,2,0:T(8,128)}, f32[12,144,144]{1,2,0:T(8,128)S(1)}, u32[]{:S(2)}) copy-start(f32[12,144,144]{1,2,0:T(8,128)S(1)} %select_bitcast_fusion) | copy-start | bytes 2985988
  68.4 13.7 %collective-permute-start.1 = (f32[1,6,24,384]{3,2,1,0:T(8,128)}, f32[1,6,24,384]{3,2,1,0:T(8,128)}, u32[]{:S(2)}, u32[]{:S(2)}) collective-permute-start(f32[1,6,24,384]{3,2,1,0:T(8,128)} %pad_maximum_fusion.7), channel_id=1, source_target_pairs={{0,112},{16,0},{32,16},{48,32},{64,48},{80,64},{96,80},{112,96},{1... | collective-permute-start | bytes 663560 | tf_op jit(solution)/shard_map/ppermute | solution.py:21
  126.6 42.4 %copy-start.37 = (f32[4,12,144]{2,1,0:T(8,128)}, f32[4,12,144]{2,1,0:T(8,128)S(1)}, u32[]{:S(2)}) copy-start(f32[4,12,144]{2,1,0:T(8,128)S(1)} %fusion.52) | copy-start | bytes 82948
  149.9 15.1 %collective-permute-start.2 = (f32[1,6,24,384]{3,2,1,0:T(8,128)}, f32[1,6,24,384]{3,2,1,0:T(8,128)S(1)}, u32[]{:S(2)}, u32[]{:S(2)}) collective-permute-start(f32[1,6,24,384]{3,2,1,0:T(8,128)} %slice.145), channel_id=1, source_target_pairs={{0,16},{16,32},{32,48},{48,64},{64,80},{80,96},{96,112},{112,0},{1... | collective-permute-start | bytes 663560 | tf_op jit(solution)/shard_map/ppermute | solution.py:21
  165.1 7.6 %collective-permute-start.3 = (f32[1,24,6,384]{3,2,1,0:T(8,128)S(1)}, f32[1,24,6,384]{3,2,1,0:T(8,128)S(1)}, u32[]{:S(2)}, u32[]{:S(2)}) collective-permute-start(f32[1,24,6,384]{3,2,1,0:T(8,128)S(1)} %pad_maximum_fusion.5), channel_id=1, source_target_pairs={{0,1},{1,2},{2,3},{3,4},{4,5},{5,6},{6,7},{7,8},{8,9},{9,10},{10,1... | collective-permute-start | bytes 663560 | tf_op jit(solution)/shard_map/ppermute | solution.py:21
  194.2 18.2 %collective-permute-start.4 = (f32[1,24,6,384]{3,2,1,0:T(8,128)S(1)}, f32[1,24,6,384]{3,2,1,0:T(8,128)S(1)}, u32[]{:S(2)}, u32[]{:S(2)}) collective-permute-start(f32[1,24,6,384]{3,2,1,0:T(8,128)S(1)} %slice.148), channel_id=1, source_target_pairs={{0,15},{1,0},{2,1},{3,2},{4,3},{5,4},{6,5},{7,6},{8,7},{9,8},{10,9... | collective-permute-start | bytes 663560 | tf_op jit(solution)/shard_map/ppermute | solution.py:21
  213.4 16.3 %collective-permute-start.5 = (f32[1,6,24,384]{3,2,1,0:T(8,128)}, f32[1,6,24,384]{3,2,1,0:T(8,128)S(1)}, u32[]{:S(2)}, u32[]{:S(2)}) collective-permute-start(f32[1,6,24,384]{3,2,1,0:T(8,128)} %pad_maximum_fusion.6), channel_id=1, source_target_pairs={{0,112},{16,0},{32,16},{48,32},{64,48},{80,64},{96,80},{112,96},{1... | collective-permute-start | bytes 663560 | tf_op jit(solution)/shard_map/ppermute | solution.py:21
  240.4 19.5 %slice-start = ((s8[7077888]{0:T(1024)(128)(4,1)}), s8[2883584]{0:T(1024)(128)(4,1)S(1)}, s32[]{:S(2)}) async-start(s8[7077888]{0:T(1024)(128)(4,1)} %bitcast.111), calls=%async_computation.4 | async-start | bytes 5767168
  246.1 13.8 %slice-start.1 = ((s8[7077888]{0:T(1024)(128)(4,1)}), s8[4194304]{0:T(1024)(128)(4,1)S(1)}, s32[]{:S(2)}) async-start(s8[7077888]{0:T(1024)(128)(4,1)} %bitcast.111), calls=%async_computation.5 | async-start | bytes 8388608
  246.1 13.8 %copy-start.2 = (f32[12,144,144]{1,2,0:T(8,128)S(1)}, f32[12,144,144]{1,2,0:T(8,128)}, u32[]{:S(2)}) copy-start(f32[12,144,144]{1,2,0:T(8,128)} %copy-done.1) | copy-start | bytes 2985988
  246.1 13.8 %copy-start.20 = (f32[4,144,384]{1,2,0:T(8,128)S(1)}, f32[4,144,384]{1,2,0:T(8,128)}, u32[]{:S(2)}) copy-start(f32[4,144,384]{1,2,0:T(8,128)} %copy.124) | copy-start | bytes 2654212
  246.1 13.8 %copy-start.21 = (f32[4,12,32,144]{3,2,1,0:T(8,128)S(1)}, f32[4,12,32,144]{3,2,1,0:T(8,128)}, u32[]{:S(2)}) copy-start(f32[4,12,32,144]{3,2,1,0:T(8,128)} %copy.135) | copy-start | bytes 2654212
  246.1 13.8 %copy-start.24 = (pred[4,144,144]{1,2,0:T(8,128)(4,1)S(1)}, pred[4,144,144]{1,2,0:T(8,128)(4,1)}, u32[]{:S(2)}) copy-start(pred[4,144,144]{1,2,0:T(8,128)(4,1)} %compare_and_fusion) | copy-start | bytes 248836
  414.2 31.0 %copy-start.47 = (f32[13824]{0:T(1024)S(1)}, f32[13824]{0:T(1024)}, u32[]{:S(2)}) copy-start(f32[13824]{0:T(1024)} %param.11) | copy-start | bytes 165892
  414.2 31.0 %copy-start.48 = (f32[13824]{0:T(1024)S(1)}, f32[13824]{0:T(1024)}, u32[]{:S(2)}) copy-start(f32[13824]{0:T(1024)} %param.12) | copy-start | bytes 165892
  424.7 41.7 %copy-start.4 = (f32[442368]{0:T(1024)S(1)}, f32[442368]{0:T(1024)}, u32[]{:S(2)}) copy-start(f32[442368]{0:T(1024)} %copy-done.3) | copy-start | bytes 5308420
  424.7 19.9 %all-to-all-start.1 = ((f32[16,1,13824]{2,1,0:T(1,128)}), f32[16,1,13824]{2,1,0:T(1,128)S(1)}, u32[]{:S(2)}, u32[]{:S(2)}) async-start(f32[16,1,13824]{2,1,0:T(1,128)} %bitcast.136), calls=%async_computation.1 | async-start | bytes 1769472 | tf_op jit(solution)/shard_map/all_to_all | solution.py:31
  429.1 249.9 %all-gather.2.cloned.1.call-start = ((), (), s32[]{:S(2)}) async-start(), calls=%async_computation.3 | async-start | bytes 7962624 | tf_op jit(solution)/shard_map/all_gather | solution.py:169
  480.8 189.7 %collective-permute-start.6 = (f32[1,6,24,384]{3,2,1,0:T(8,128)}, f32[1,6,24,384]{3,2,1,0:T(8,128)S(1)}, u32[]{:S(2)}, u32[]{:S(2)}) collective-permute-start(f32[1,6,24,384]{3,2,1,0:T(8,128)} %slice.151), channel_id=1, source_target_pairs={{0,16},{16,32},{32,48},{48,64},{64,80},{80,96},{96,112},{112,0},{1... | collective-permute-start | bytes 663560 | tf_op jit(solution)/shard_map/ppermute | solution.py:21
  481.7 195.0 %copy-start.17 = (f32[24,24,384]{2,1,0:T(8,128)S(1)}, f32[24,24,384]{2,1,0:T(8,128)}, u32[]{:S(2)}) copy-start(f32[24,24,384]{2,1,0:T(8,128)} %copy-done.16) | copy-start | bytes 2654212
  481.7 195.0 %copy-start.44 = (f32[24,24]{1,0:T(8,128)S(1)}, f32[24,24]{1,0:T(8,128)}, u32[]{:S(2)}) copy-start(f32[24,24]{1,0:T(8,128)} %copy-done.43) | copy-start | bytes 6916
  670.5 6.2 collective-permute-start.7
  (39 other events, 244.2 us)
Sparse Core Ops, SparseCore 0:
  466.5 79.8 all-gather.1
where the time goes:
time: 700 us; the launch traced here: 691 us
  local copies, waits for them, and re-layouts  172 us (25%)
  blocking collectives  169 us (24%)
  other arithmetic  165 us (24%)
  matrix products  118 us (17%)
  starting transfers between devices  29.9 us (4%)
  waiting for transfers between devices  21.4 us (3%)
  between operations  15.3 us (2%)
    scatter-add x1, other arithmetic, attend(): scores = scores + jnp.take(bias_table, bias_index, axis=1)[None]  112 us
    all_to_all x1, blocking collectives, sent_and_summed(): lax.all_to_all(blocks, axis, split_axis=0, concat_axis=0, tiled=True)  84 us
    psum x1, blocking collectives, per_device(): table_grad = lax.psum(grad_table, ('lat', 'lon')) * factor  65.9 us
    gather x2, local copies, waits for them, and re-layouts, attend(): scores = scores + jnp.take(bias_table, bias_index, axis=1)[None]  50.9 us
    dot_general x3, matrix products, attend(): jnp.einsum('whij,wjhd->wihd', probability, valued, precision=precise)  30 us
    ppermute x8, starting transfers between devices, passed_along(): lax.ppermute(value, axis, [(i, (i + by) % size) for i in range(size)])  25.5 us
    dot_general x3, matrix products, attend(): jnp.einsum('wihd,wjhd->whij', query, keyed, precision=precise)  22.1 us
    dot_general x3, matrix products, attend(): jnp.dot(flat_rows, w_qkv, precision=precise, preferred_element_type=jnp.f...  21.6 us
  transfers between devices with their start and end apart: 10, of which 3 were waited for; matrix products, arithmetic and copies ran while one was open for 35% of the time, Pallas kernels for 0%

commit v1 on v0

v1 whole, which is shorter than its diff:
```python
import functools
import math

import jax
import jax.numpy as jnp
from jax import lax
from jax.experimental import pallas as pl
from jax.experimental.pallas import tpu as pltpu
from jax.sharding import PartitionSpec as P

D = 384
HEADS = 12
FF = 1536
WIN = 12
SHIFT = 6
WT = WIN * WIN
TILE = 24
TOK = TILE * TILE
WINS = TOK // WT
GROUPS = 3
PER = 4
QKV_ROWS = D * 3 * D // 128
PROJ_ROWS = D * D // 128
MLP_ROWS = D * FF // 128
PROJ_AT = QKV_ROWS
UP_AT = QKV_ROWS + PROJ_ROWS
DOWN_AT = UP_AT + MLP_ROWS
ROWS = DOWN_AT + MLP_ROWS
CHUNK = 256
CHUNKS = FF // CHUNK
HALF = ROWS // 2
OWN = ROWS // 128
BLOCK = OWN + 1
HALF_X = HALF + 64
TABLE_ROWS = 50
BIAS = 529
BOTH = ("lat", "lon")
F32 = jnp.float32
BF16 = jnp.bfloat16
VMEM = pl.BlockSpec(memory_space=pltpu.VMEM)
PARAMS = pltpu.CompilerParams(vmem_limit_bytes=58 * 1024 * 1024)

NN = (((1,), (0,)), ((), ()))
NT = (((1,), (1,)), ((), ()))
TN = (((0,), (0,)), ((), ()))


def split(value):
    high = value.astype(BF16)
    return high, (value - high.astype(F32)).astype(BF16)


def dot(a, b, dims):
    return lax.dot_general(a, b, dims, preferred_element_type=F32)


def dot3(a, b, dims):
    return dot(a[0], b[0], dims) + dot(a[0], b[1], dims) + dot(a[1], b[0], dims)


def unit(value):
    center = value - jnp.mean(value, axis=-1, keepdims=True)
    scale = lax.rsqrt(jnp.mean(center * center, axis=-1, keepdims=True) + 1e-05)
    return center * scale, scale


def unit_back(grad, normed, scale):
    mean = jnp.mean(grad, axis=-1, keepdims=True)
    along = jnp.mean(grad * normed, axis=-1, keepdims=True)
    return scale * (grad - mean - normed * along)


def prepare(flat, table, index, wq_h, wq_l, wp_h, wp_l, wu_h, wu_l, wd_h, wd_l, bias):
    for at, rows, blocks, high, low in (
        (0, D, 9, wq_h, wq_l),
        (PROJ_AT, D, 3, wp_h, wp_l),
    ):
        for b in range(blocks):
            h, l = split(flat[pl.ds(at + b, rows, stride=blocks), :])
            high[:, 128 * b : 128 * b + 128] = h
            low[:, 128 * b : 128 * b + 128] = l
    for f in range(CHUNKS):
        for b in range(2):
            h, l = split(flat[pl.ds(UP_AT + 2 * f + b, D, stride=12), :])
            wu_h[f, :, 128 * b : 128 * b + 128] = h
            wu_l[f, :, 128 * b : 128 * b + 128] = l
        for b in range(3):
            h, l = split(flat[pl.ds(DOWN_AT + 3 * CHUNK * f + b, CHUNK, stride=3), :])
            wd_h[f, :, 128 * b : 128 * b + 128] = h
            wd_l[f, :, 128 * b : 128 * b + 128] = l

    def rows_of(step, carry):
        at = pl.multiple_of(step * 8, 8)
        columns = index[pl.ds(at, 8), :]
        low = columns & 127
        part = columns >> 7
        for h in range(HEADS):
            found = jnp.zeros((8, 256), F32)
            for p in range(5):
                line = jnp.broadcast_to(table[h : h + 1, 128 * p : 128 * p + 128], (8, 128))
                taken = jnp.concatenate(
                    [
                        jnp.take_along_axis(line, low[:, :128], axis=1),
                        jnp.take_along_axis(line, low[:, 128:], axis=1),
                    ],
                    axis=1,
                )
                found = jnp.where(part == p, taken, found)
            bias[h // PER, pl.ds(pl.multiple_of((h % PER) * WT + at, 8), 8), :] = found[:, :WT]
        return carry

    lax.fori_loop(0, WT // 8, rows_of, 0)


def prepared(flat, table, index):
    table = jnp.pad(table, ((0, 4), (0, 640 - BIAS)))
    index = jnp.pad(index, ((0, 0), (0, 256 - WT)))
    shapes = [(D, 3 * D)] * 2 + [(D, D)] * 2 + [(CHUNKS, D, CHUNK)] * 2 + [(CHUNKS, CHUNK, D)] * 2
    return pl.pallas_call(
        prepare,
        out_shape=[jax.ShapeDtypeStruct(s, BF16) for s in shapes]
        + [jax.ShapeDtypeStruct((GROUPS, PER * WT, WT), F32)],
        in_specs=[VMEM] * 3,
        out_specs=[VMEM] * 9,
        compiler_params=PARAMS,
        name="prepare",
    )(flat, table, index)


def gather_windows(target, local, east, south, corner):
    for wr in range(2):
        for wc in range(2):
            for r in range(WIN):
                row = wr * WIN + r
                at = (wr * 2 + wc) * WT + r * WIN
                if row < TILE - SHIFT:
                    near, far, k = local, east, row + SHIFT
                else:
                    near, far, k = south, corner, row - (TILE - SHIFT)
                if wc == 0:
                    target[at : at + WIN, :] = near[k, SHIFT : SHIFT + WIN, :]
                else:
                    target[at : at + SHIFT, :] = near[k, SHIFT + WIN : TILE, :]
                    target[at + SHIFT : at + WIN, :] = far[k, 0:SHIFT, :]


def scatter_windows(source, local, east, south, corner):
    for wr in range(2):
        for wc in range(2):
            for r in range(WIN):
                row = wr * WIN + r
                at = (wr * 2 + wc) * WT + r * WIN
                if row < TILE - SHIFT:
                    near, far, k = local, east, row + SHIFT
                else:
                    near, far, k = south, corner, row - (TILE - SHIFT)
                if wc == 0:
                    near[k, SHIFT : SHIFT + WIN, :] = source[at : at + WIN, :]
                else:
                    near[k, SHIFT + WIN : TILE, :] = source[at : at + SHIFT, :]
                    far[k, 0:SHIFT, :] = source[at + SHIFT : at + WIN, :]


def head_lane():
    return lax.broadcasted_iota(jnp.int32, (WT, 128), 1) >> 5


def stacked(value):
    lane = head_lane()
    return jnp.concatenate([jnp.where(lane == h, value, 0.0) for h in range(PER)], axis=0)


def unstacked(value):
    lane = head_lane()
    total = jnp.where(lane == 0, value[:WT], 0.0)
    for h in range(1, PER):
        total = jnp.where(lane == h, value[h * WT : h * WT + WT], total)
    return total


SCALE = 1.0 / math.sqrt(32.0)


def block_pass(
    x_l, x_e, x_s, x_c, c_l, c_e, c_s, c_c, wq_h, wq_l, wp_h, wp_l, wu_h, wu_l, wd_h, wd_l,
    bias, label_col, label_row,
    grads, dscore, o_l, o_e, o_s, o_c,
    x, cot, qkv, ctx, prob, n2h, n2l, ch, cl, grad, dqkv, dctx,
):
    gather_windows(x, x_l, x_e, x_s, x_c)
    gather_windows(cot, c_l, c_e, c_s, c_c)
    n1 = split(unit(x[...])[0])
    qkv[...] = dot3(n1, (wq_h[...], wq_l[...]), NN)

    def attend(step, carry):
        w, g = step // GROUPS, step % GROUPS
        rows = pl.ds(pl.multiple_of(w * WT, 16), WT)
        lanes = pl.ds(pl.multiple_of(g * 128, 128), 128)
        q = split(stacked(qkv[rows, pl.ds(pl.multiple_of(g * 128, 128), 128)] * SCALE))
        k = split(qkv[rows, pl.ds(pl.multiple_of(D + g * 128, 128), 128)])
        v = split(qkv[rows, pl.ds(pl.multiple_of(2 * D + g * 128, 128), 128)])
        allowed = label_col[w] == label_row[w]
        score = dot3(q, k, NT) + bias[g]
        score = jnp.where(jnp.concatenate([allowed] * PER, axis=0), score, -jnp.inf)
        raised = jnp.exp(score - jnp.max(score, axis=-1, keepdims=True))
        p = raised * (1.0 / jnp.sum(raised, axis=-1, keepdims=True))
        prob[step] = p
        ctx[rows, lanes] = unstacked(dot3(split(p), v, NN))
        return carry

    lax.fori_loop(0, WINS * GROUPS, attend, 0)

    mixed = x[...] + dot3(split(ctx[...]), (wp_h[...], wp_l[...]), NN)
    n2, scale2 = unit(mixed)
    n2h[...], n2l[...] = split(n2)
    ch[...], cl[...] = split(cot[...])
    grad[...] = jnp.zeros_like(grad)

    def feed(f, carry):
        n = (n2h[...], n2l[...])
        c = (ch[...], cl[...])
        up = (wu_h[f], wu_l[f])
        u = dot3(n, up, NN)
        back = dot3(c, (wd_h[f], wd_l[f]), NT)
        inner = 0.7978845608028654 * (u + 0.044715 * u * u * u)
        t = jnp.tanh(inner)
        hidden = split(0.5 * u * (1.0 + t))
        slope = 0.5 * (1.0 + t) + 0.5 * u * (1.0 - t * t) * (
            0.7978845608028654 * (1.0 + 3.0 * 0.044715 * u * u)
        )
        du = split(back * slope)
        gdown = dot3(hidden, c, TN)
        for b in range(3):
            grads[pl.ds(DOWN_AT + 3 * CHUNK * f + b, CHUNK, stride=3), :] = gdown[:, 128 * b : 128 * b + 128]
        gup = dot3(n, du, TN)
        for b in range(2):
            grads[pl.ds(UP_AT + 2 * f + b, D, stride=12), :] = gup[:, 128 * b : 128 * b + 128]
        grad[...] += dot3(du, up, NT)
        return carry

    lax.fori_loop(0, CHUNKS, feed, 0)

    mixed = x[...] + dot3(split(ctx[...]), (wp_h[...], wp_l[...]), NN)
    n2, scale2 = unit(mixed)
    grad[...] = cot[...] + unit_back(grad[...], n2, scale2)
    gm = split(grad[...])
    dctx[...] = dot3(gm, (wp_h[...], wp_l[...]), NT)
    gproj = dot3(split(ctx[...]), gm, TN)
    for b in range(3):
        grads[pl.ds(PROJ_AT + b, D, stride=3), :] = gproj[:, 128 * b : 128 * b + 128]
    dscore[...] = jnp.zeros_like(dscore)

    def attend_back(step, carry):
        w, g = step // GROUPS, step % GROUPS
        rows = pl.ds(pl.multiple_of(w * WT, 16), WT)
        q_at = pl.ds(pl.multiple_of(g * 128, 128), 128)
        k_at = pl.ds(pl.multiple_of(D + g * 128, 128), 128)
        v_at = pl.ds(pl.multiple_of(2 * D + g * 128, 128), 128)
        q = split(stacked(qkv[rows, q_at] * SCALE))
        k = split(qkv[rows, k_at])
        v = split(qkv[rows, v_at])
        d = split(stacked(dctx[rows, q_at]))
        p = prob[step]
        dp = dot3(d, v, NT)
        ds = p * (dp - jnp.sum(dp * p, axis=-1, keepdims=True))
        dscore[g] += ds
        ps, dss = split(p), split(ds)
        dqkv[rows, v_at] = dot3(ps, d, TN)
        dqkv[rows, q_at] = unstacked(dot3(dss, k, NN)) * SCALE
        dqkv[rows, k_at] = dot3(dss, q, TN)
        return carry

    lax.fori_loop(0, WINS * GROUPS, attend_back, 0)

    n1, scale1 = unit(x[...])
    dq = split(dqkv[...])
    gqkv = dot3(split(n1), dq, TN)
    for b in range(9):
        grads[pl.ds(b, D, stride=9), :] = gqkv[:, 128 * b : 128 * b + 128]
    back = dot3(dq, (wq_h[...], wq_l[...]), NT)
    grad[...] += unit_back(back, n1, scale1)
    scatter_windows(grad, o_l, o_e, o_s, o_c)


def run_block(x_parts, c_parts, weights, bias, label_col, label_row):
    halo = [(TILE, TILE, D), (TILE, 8, D), (SHIFT, TILE, D), (SHIFT, 8, D)]
    outs = [(ROWS, 128), (GROUPS, PER * WT, WT)] + halo
    scratch = [
        pltpu.VMEM((TOK, D), F32),
        pltpu.VMEM((TOK, D), F32),
        pltpu.VMEM((TOK, 3 * D), F32),
        pltpu.VMEM((TOK, D), F32),
        pltpu.VMEM((WINS * GROUPS, PER * WT, WT), F32),
        pltpu.VMEM((TOK, D), BF16),
        pltpu.VMEM((TOK, D), BF16),
        pltpu.VMEM((TOK, D), BF16),
        pltpu.VMEM((TOK, D), BF16),
        pltpu.VMEM((TOK, D), F32),
        pltpu.VMEM((TOK, 3 * D), F32),
        pltpu.VMEM((TOK, D), F32),
    ]
    args = (*x_parts, *c_parts, *weights, bias, label_col, label_row)
    return pl.pallas_call(
        block_pass,
        out_shape=[jax.ShapeDtypeStruct(s, F32) for s in outs],
        in_specs=[VMEM] * len(args),
        out_specs=[VMEM] * len(outs),
        scratch_shapes=scratch,
        compiler_params=PARAMS,
        name="block_pass",
    )(*args)


def table_sum(scores, index, out):
    out[...] = jnp.zeros_like(out)
    column = lax.broadcasted_iota(jnp.int32, (128, WT), 0)

    def step(i, carry):
        line = index[i]
        part = line >> 7
        hot = (column == jnp.broadcast_to(line & 127, (128, WT))).astype(F32).astype(BF16)
        high, low = split(scores[i])
        pair = jnp.concatenate([high.astype(F32), low.astype(F32)], axis=0)
        rows = jnp.concatenate([jnp.where(part == p, pair, 0.0) for p in range(5)], axis=0).astype(BF16)
        out[...] += dot(rows, hot, NT)
        return carry

    lax.fori_loop(0, WT, step, 0)


def table_gradient(dscore, index):
    scores = dscore.reshape(HEADS, WT, WT).transpose(1, 0, 2)
    scores = jnp.pad(scores, ((0, 0), (0, 4), (0, 0)))
    sums = pl.pallas_call(
        table_sum,
        out_shape=jax.ShapeDtypeStruct((160, 128), F32),
        in_specs=[VMEM] * 2,
        out_specs=VMEM,
        compiler_params=PARAMS,
        name="table_sum",
    )(scores, index.reshape(WT, 1, WT))
    sums = sums.reshape(5, 2, 16, 128).sum(axis=1)[:, :HEADS]
    return sums.transpose(1, 0, 2).reshape(HEADS, 640)[:, :BIAS]


def chip_order():
    return [(y_lo * 4 + x) * 16 + zy * 2 for y_lo in range(2) for x in range(4) for zy in range(8)]


def chip_groups():
    return [[d + core for d in chip_order()] for core in range(2)]


def core_groups():
    return [[d, d + 1] for d in chip_order()]


def worker_pairs():
    return [(core * 64 + q, d + core) for core in range(2) for q, d in enumerate(chip_order())]


def exchanged(value, groups):
    return lax.all_to_all(value, BOTH, 0, 0, axis_index_groups=groups, tiled=True)


def around(value, axis, by):
    size = lax.axis_size(axis)
    return lax.ppermute(value, axis, [(i, (i + by) % size) for i in range(size)])


def diagonal(value, by):
    lat, lon = lax.axis_size("lat"), lax.axis_size("lon")
    return lax.ppermute(
        value,
        BOTH,
        [
            (a * lon + o, ((a + by) % lat) * lon + (o + by) % lon)
            for a in range(lat)
            for o in range(lon)
        ],
    )


def halo(tile):
    return (
        tile,
        around(tile[:, :8], "lon", -1),
        around(tile[:SHIFT], "lat", -1),
        diagonal(tile[:SHIFT, :8], -1),
    )


def adam(parts, weights, first, second, new, first_new, second_new, factor):
    total = parts[0:BLOCK, :]
    for q in range(1, 64):
        total = total + parts[q * BLOCK : (q + 1) * BLOCK, :]
    total = total * factor
    grad = total[:OWN]
    m = 0.9 * first[...] + 0.1 * grad
    s = 0.95 * second[...] + 0.05 * grad * grad
    first_new[...] = m
    second_new[...] = s
    new[0:OWN, :] = weights[...] - 0.01 * m / (jnp.sqrt(s) + 1e-08)
    new[OWN:BLOCK, :] = total[OWN:BLOCK]


def per_device(
    block_input, cotangent, weights, first_moment, second_moment, bias_table, bias_index, region_ids
):
    lat_at, lon_at = lax.axis_index("lat"), lax.axis_index("lon")
    factor = 1.0 / math.sqrt(TOK * 128)
    flat = weights.reshape(ROWS, 128)
    *pairs, bias = prepared(flat, bias_table, bias_index)
    x_parts = halo(block_input)
    c_parts = halo(cotangent)

    wrapped = (lat_at * TILE + jnp.arange(TILE)) >= TILE * 8 - SHIFT
    labels = region_ids * 2 + wrapped[:, None].astype(jnp.int32)
    labels = labels.reshape(2, WIN, 2, WIN).transpose(0, 2, 1, 3).reshape(WINS, WT)
    grads, dscore, o_l, o_e, o_s, o_c = run_block(
        x_parts, c_parts, pairs, bias, labels[:, :, None], labels[:, None, :]
    )

    from_west = around(o_e, "lon", 1)
    from_north = around(o_s, "lat", 1)
    from_corner = diagonal(o_c, 1)
    top = jnp.concatenate([from_corner[:, :SHIFT], from_north[:, SHIFT:]], axis=1)
    rest = jnp.concatenate([from_west[SHIFT:, :SHIFT], o_l[SHIFT:, SHIFT:]], axis=1)
    grad_input = jnp.concatenate([top, rest], axis=0)

    table = table_gradient(dscore, bias_index).reshape(-1)
    table = jnp.pad(table, (0, 128 * 128 - table.shape[0])).reshape(2, 64, 1, 128)
    sent = jnp.concatenate([grads.reshape(2, 64, OWN, 128), table], axis=2)
    halves = exchanged(sent.reshape(2, 64 * BLOCK, 128), core_groups())
    summed = halves[0] + halves[1]
    parts = exchanged(summed.reshape(64, 1, BLOCK * 128), chip_groups())

    pairs_of = worker_pairs()
    back = [(b, a) for a, b in pairs_of]
    moments = jnp.stack([first_moment.reshape(OWN, 128), second_moment.reshape(OWN, 128)])
    moments = lax.ppermute(moments, BOTH, pairs_of)
    core = lon_at % 2
    shard = core * 64 + lat_at * 8 + lon_at // 2
    own = lax.dynamic_slice_in_dim(flat, shard * OWN, OWN, 0)
    new, first_new, second_new = pl.pallas_call(
        functools.partial(adam, factor=factor),
        out_shape=[jax.ShapeDtypeStruct((n, 128), F32) for n in (BLOCK, OWN, OWN)],
        in_specs=[VMEM] * 4,
        out_specs=[VMEM] * 3,
        compiler_params=PARAMS,
        name="adam",
    )(parts.reshape(64 * BLOCK, 128), own, moments[0], moments[1])
    moments = lax.ppermute(jnp.stack([first_new, second_new]), BOTH, back)
    copies = jnp.broadcast_to(new.reshape(1, 1, BLOCK * 128), (64, 1, BLOCK * 128))
    mine = exchanged(copies, chip_groups()).reshape(1, 64 * BLOCK, 128)
    everything = exchanged(jnp.concatenate([mine, mine]), core_groups())
    everything = everything.reshape(128, BLOCK, 128)
    weights_new = everything[:, :OWN].reshape(-1)
    table_new = everything[:, OWN].reshape(-1)[: HEADS * BIAS].reshape(HEADS, BIAS)
    return (
        grad_input,
        weights_new,
        moments[0].reshape(-1),
        moments[1].reshape(-1),
        table_new,
    )


def solution(mesh):
    placed = (
        P("lat", "lon", None),
        P("lat", "lon", None),
        P(),
        P(BOTH),
        P(BOTH),
        P(),
        P(),
        P("lat", "lon"),
    )
    return jax.shard_map(
        per_device,
        mesh=mesh,
        in_specs=placed,
        out_specs=(P("lat", "lon", None), P(), P(BOTH), P(BOTH), P()),
        check_vma=False,
    )
```

time: 700 us -> 352 us (0.50)
  other arithmetic: 165 us -> 15 us
  blocking collectives: 169 us -> 25.3 us
  matrix products: 118 us -> 0 us
  local copies, waits for them, and re-layouts: 172 us -> 56.3 us
  Pallas kernels: 0 us -> 110 us
  waiting for transfers between devices: 21.4 us -> 86.2 us
  starting transfers between devices: 29.9 us -> 55.8 us
  between operations: 15.3 us -> 0.96 us
    dot_general x17 -> x0, matrix products: 118 us -> none  [the longest x3 30 us: attend(): jnp.einsum('whij,wjhd->wihd', probability, valued, precision=precise)]
    scatter-add x1 -> x0, other arithmetic: 112 us -> none  [attend(): scores = scores + jnp.take(bias_table, bias_index, axis=1)[None]]
    pallas_call x0 -> x4, Pallas kernels: none -> 110 us  [the longest x1 66.5 us: run_block(): pl.pallas_call(block_pass, out_shape=[jax.ShapeDtypeStruct(s, F32) for s...]
    ppermute x8 -> x11, waiting for transfers between devices: 5.91 us -> 86.1 us  [the longest x6 41.1 us: around(): lax.ppermute(value, axis, [(i, (i + by) % size) for i in range(size)])]
    all_to_all x2, blocking collectives: 103 us -> 25.3 us  [exchanged(): lax.all_to_all(value, BOTH, 0, 0, axis_index_groups=groups, tiled=True)]
    psum x1 -> x0, blocking collectives: 65.9 us -> none  [per_device(): table_grad = lax.psum(grad_table, ('lat', 'lon')) * factor]
    gather x2 -> x0, local copies, waits for them, and re-layouts: 50.9 us -> none  [attend(): scores = scores + jnp.take(bias_table, bias_index, axis=1)[None]]
    slice x22 -> x11, local copies, waits for them, and re-layouts: 37.4 us -> 6.83 us  [the longest x2 1.96 us: halo(): tile[:, :8]]
  transfers between devices with their start and end apart: 10 -> 13, of which waited for: 3 -> 6; matrix products, arithmetic and copies ran while one was open for 35% -> 4% of each run, Pallas kernels for 0% -> 3%
where the time goes in v1:
time: 352 us; the launch traced here: 349 us
  Pallas kernels  110 us (31%)
  waiting for transfers between devices  86.2 us (24%)
  local copies, waits for them, and re-layouts  56.3 us (16%)
  starting transfers between devices  55.8 us (16%)
  blocking collectives  25.3 us (7%)
  other arithmetic  15 us (4%)
    pallas_call x1, Pallas kernels, run_block(): pl.pallas_call(block_pass, out_shape=[jax.ShapeDtypeStruct(s, F32) for s...  66.5 us
    ppermute x6, waiting for transfers between devices, around(): lax.ppermute(value, axis, [(i, (i + by) % size) for i in range(size)])  41.1 us
    ppermute x1, waiting for transfers between devices, per_device(): moments = lax.ppermute(moments, BOTH, pairs_of)  37.3 us
    pallas_call x1, Pallas kernels, table_gradient(): pl.pallas_call(table_sum, out_shape=jax.ShapeDtypeStruct((160, 128), F32)...  28.6 us
    all_to_all x2, blocking collectives, exchanged(): lax.all_to_all(value, BOTH, 0, 0, axis_index_groups=groups, tiled=True)  25.3 us
    all_to_all x2, starting transfers between devices, exchanged(): lax.all_to_all(value, BOTH, 0, 0, axis_index_groups=groups, tiled=True)  18.3 us
    ppermute x6, starting transfers between devices, around(): lax.ppermute(value, axis, [(i, (i + by) % size) for i in range(size)])  16 us
    pallas_call x1, Pallas kernels, prepared(): pl.pallas_call(prepare, out_shape=[jax.ShapeDtypeStruct(s, BF16) for s in...  11.5 us
  transfers between devices with their start and end apart: 13, of which 6 were waited for; matrix products, arithmetic and copies ran while one was open for 4% of the time, Pallas kernels for 3%

profile of v1, /device:TPU:1, one launch (start us, length us, event | category | flops | bytes accessed | tf_op | source)
XLA Modules:
  0.0 349.4 jit_solution(9715577424322774257)
XLA Ops:
  4.1 6.3 %collective-permute-start.3 = (f32[24,8,384]{2,1,0:T(8,128)S(1)}, f32[24,8,384]{2,1,0:T(8,128)S(1)}, u32[]{:S(2)}, u32[]{:S(2)}) collective-permute-start(f32[24,8,384]{2,1,0:T(8,128)S(1)} %slice.66), channel_id=1, source_target_pairs={{0,15},{1,0},{2,1},{3,2},{4,3},{5,4},{6,5},{7,6},{8,7},{9,8},{10,9... | collective-permute-start | bytes 884744 | tf_op jit(solution)/shard_map/ppermute | solution.py:368
  11.3 2.7 collective-permute-start.1
  18.7 5.7 %collective-permute-done.2.x_c = f32[6,8,384]{2,1,0:T(8,128)S(1)} collective-permute-done((f32[6,8,384]{2,1,0:T(8,128)S(1)}, f32[6,8,384]{2,1,0:T(8,128)S(1)}, u32[]{:S(2)}, u32[]{:S(2)}) %collective-permute-start.2) | collective-permute-done | bytes 73760 | tf_op jit(solution)/shard_map/ppermute | solution.py:373
  24.4 4.6 %collective-permute-start.5 = (f32[6,8,384]{2,1,0:T(8,128)S(1)}, f32[6,8,384]{2,1,0:T(8,128)S(1)}, u32[]{:S(2)}, u32[]{:S(2)}) collective-permute-start(f32[6,8,384]{2,1,0:T(8,128)S(1)} %slice.68), channel_id=1, source_target_pairs={{0,127},{1,112},{2,113},{3,114},{4,115},{5,116},{6,117},{7,118},{8... | collective-permute-start | bytes 221192 | tf_op jit(solution)/shard_map/ppermute | solution.py:373
  36.2 11.5 %prepare.1 = (bf16[384,1152]{1,0:T(8,128)(2,1)}, bf16[384,1152]{1,0:T(8,128)(2,1)}, bf16[384,384]{1,0:T(8,128)(2,1)}, bf16[384,384]{1,0:T(8,128)(2,1)}, bf16[6,3...) custom-call(f32[13824,128]{1,0:T(8,128)} %bitcast.38, ...), custom_call_target="tpu_custom_call" | custom-call | tf_op jit(solution)/shard_map/prepare/pallas_call | solution.py:119
  48.7 66.5 %block_pass.1 = (f32[13824,128]{1,0:T(8,128)}, f32[3,576,144]{2,1,0:T(8,128)}, f32[24,24,384]{2,1,0:T(8,128)}, f32[24,8,384]{2,1,0:T(8,128)}, f32[6,24,384]{2,1,0:T(8,128)}, /*index=5*/f32[6,8,384]{2,1,0:T(8,128)}) custom-call(f32[24,24,384]{2,1,0:T(8,128)} %x_l.1, f32[24,8,384]{2,1,0:T(8,128)} %copy-done.2, f32[6,24,384]{2,1,0:T(8,128)} %copy-done.4, ...), custom_call_target="tpu_custom_call" | custom-call | tf_op jit(solution)/shard_map/block_pass/pallas_call | solution.py:303
  115.3 8.1 %reshape.87 = f32[2,64,108,128]{3,2,1,0:T(8,128)} reshape(f32[13824,128]{1,0:T(8,128)} %get-tuple-element.36) | data formatting | bytes 14155776 | tf_op jit(solution)/shard_map/reshape | solution.py:433
  126.1 28.6 %table_sum.1 = f32[160,128]{1,0:T(8,128)} custom-call(f32[144,16,144]{2,1,0:T(8,128)} %pad.18.scores, s32[144,1,144]{2,1,0:T(1,128)} %reshape.89.index), custom_call_target="tpu_custom_call" | custom-call | tf_op jit(solution)/shard_map/table_sum/pallas_call | solution.py:334
  155.7 6.6 %pad_maximum_fusion = f32[2,64,109,128]{3,2,1,0:T(8,128)} fusion(f32[2,64,1,128]{3,2,1,0:T(1,128)S(1)} %bitcast.44, f32[2,64,108,128]{3,2,1,0:T(8,128)} %reshape.87), kind=kLoop, calls=%fused_computation | loop fusion | flops 1785856 | bytes 14286848 | tf_op jit(solution)/shard_map/concatenate | solution.py:433
  162.4 7.6 %reshape.94 = f32[2,6976,128]{2,1,0:T(8,128)} reshape(f32[2,64,109,128]{3,2,1,0:T(8,128)} %pad_maximum_fusion) | data formatting | bytes 14286848 | tf_op jit(solution)/shard_map/reshape | solution.py:434
  170.0 14.9 %all_to_all.20 = f32[2,6976,128]{2,1,0:T(8,128)S(1)} all-to-all(f32[2,6976,128]{2,1,0:T(8,128)} %reshape.94), channel_id=1, replica_groups={{0,1},{2,3},{4,5},{6,7},{8,9},{10,11},{12,13},{14,15},{16,17},{18,19},{..., dimensions={0} | all-to-all | bytes 14286848 | tf_op jit(solution)/shard_map/all_to_all | solution.py:363
  187.0 5.6 %all-to-all-start.1 = ((f32[64,1,13952]{2,1,0:T(1,128)}), f32[64,1,13952]{2,1,0:T(1,128)}, u32[]{:S(2)}, u32[]{:S(2)}) async-start(f32[64,1,13952]{2,1,0:T(1,128)} %bitcast.36), calls=%async_computation.1 | async-start | bytes 7143424 | tf_op jit(solution)/shard_map/all_to_all | solution.py:363
  192.7 4.8 %collective-permute-start.9 = (f32[2,108,128]{2,1,0:T(8,128)S(1)}, f32[2,108,128]{2,1,0:T(8,128)S(1)}, u32[]{:S(2)}, u32[]{:S(2)}) collective-permute-start(f32[2,108,128]{2,1,0:T(8,128)S(1)} %pad_maximum_fusion.2), channel_id=1, source_target_pairs={{0,0},{1,2},{2,4},{3,6},{4,8},{5,10},{6,12},{7,14},{8,16},{9,18},{... | collective-permute-start | bytes 331784 | tf_op jit(solution)/shard_map/ppermute | solution.py:441
  199.0 37.3 %collective-permute-done.9 = f32[2,108,128]{2,1,0:T(8,128)S(1)} collective-permute-done((f32[2,108,128]{2,1,0:T(8,128)S(1)}, f32[2,108,128]{2,1,0:T(8,128)S(1)}, u32[]{:S(2)}, u32[]{:S(2)}) %collective-permute-start.9) | collective-permute-done | bytes 110624 | tf_op jit(solution)/shard_map/ppermute | solution.py:441
  237.2 3.1 adam.1
  240.2 4.5 %broadcast_in_dim.9 = f32[64,1,13952]{2,1,0:T(1,128)} broadcast(f32[13952]{0:T(1024)} %bitcast.49), dimensions={2} | broadcast | bytes 3627520 | tf_op jit(solution)/shard_map/broadcast_in_dim | solution.py:454
  244.7 12.7 %all-to-all-start.2 = ((f32[64,1,13952]{2,1,0:T(1,128)}), f32[64,1,13952]{2,1,0:T(1,128)}, u32[]{:S(2)}, u32[]{:S(2)}) async-start(f32[64,1,13952]{2,1,0:T(1,128)} %broadcast_in_dim.9), calls=%async_computation.2 | async-start | bytes 7143424 | tf_op jit(solution)/shard_map/all_to_all | solution.py:363
  257.4 3.8 %collective-permute-start.8 = (f32[24,8,384]{2,1,0:T(8,128)S(1)}, f32[24,8,384]{2,1,0:T(8,128)S(1)}, u32[]{:S(2)}, u32[]{:S(2)}) collective-permute-start(f32[24,8,384]{2,1,0:T(8,128)S(1)} %copy-done.12), channel_id=1, source_target_pairs={{0,1},{1,2},{2,3},{3,4},{4,5},{5,6},{6,7},{7,8},{8,9},{9,10},{10,1... | collective-permute-start | bytes 884744 | tf_op jit(solution)/shard_map/ppermute | solution.py:368
  263.8 39.9 %collective-permute-done.7 = f32[6,24,384]{2,1,0:T(8,128)S(1)} collective-permute-done((f32[6,24,384]{2,1,0:T(8,128)S(1)}, f32[6,24,384]{2,1,0:T(8,128)S(1)}, u32[]{:S(2)}, u32[]{:S(2)}) %collective-permute-start.7) | collective-permute-done | bytes 221216 | tf_op jit(solution)/shard_map/ppermute | solution.py:368
  305.0 9.4 %collective-permute-start.10 = (f32[2,108,128]{2,1,0:T(8,128)S(1)}, f32[2,108,128]{2,1,0:T(8,128)S(1)}, u32[]{:S(2)}, u32[]{:S(2)}) collective-permute-start(f32[2,108,128]{2,1,0:T(8,128)S(1)} %pad_maximum_fusion.3), channel_id=1, source_target_pairs={{0,0},{2,1},{4,2},{6,3},{8,4},{10,5},{12,6},{14,7},{16,8},{18,9},{... | collective-permute-start | bytes 331784 | tf_op jit(solution)/shard_map/ppermute | solution.py:453
  317.9 3.6 %pad_maximum_fusion.1 = f32[2,6976,128]{2,1,0:T(8,128)S(1)} fusion(f32[1,6976,128]{2,1,0:T(8,128)} %bitcast.14), kind=kLoop, calls=%fused_computation.1 | loop fusion | flops 1785856 | bytes 10715136 | tf_op jit(solution)/shard_map/concatenate | solution.py:456
  321.5 10.5 %all_to_all.21 = f32[2,6976,128]{2,1,0:T(8,128)} all-to-all(f32[2,6976,128]{2,1,0:T(8,128)S(1)} %pad_maximum_fusion.1), channel_id=1, replica_groups={{0,1},{2,3},{4,5},{6,7},{8,9},{10,11},{12,13},{14,15},{16,17},{18,19},{..., dimensions={0} | all-to-all | bytes 14286848 | tf_op jit(solution)/shard_map/all_to_all | solution.py:363
  331.9 7.7 %reshape.97 = f32[128,109,128]{2,1,0:T(8,128)} reshape(f32[2,6976,128]{2,1,0:T(8,128)} %all_to_all.21) | data formatting | bytes 14286848 | tf_op jit(solution)/shard_map/reshape | solution.py:457
  340.7 8.0 %reshape.98 = f32[1769472]{0:T(1024)} reshape(f32[128,108,128]{2,1,0:T(8,128)} %bitcast.35) | data formatting | bytes 14155776 | tf_op jit(solution)/shard_map/reshape | solution.py:458
  (82 shorter events, 34.6 us)
Async XLA Ops:
  1.6 46.1 %collective-permute-start = (f32[24,8,384]{2,1,0:T(8,128)S(1)}, f32[24,8,384]{2,1,0:T(8,128)S(1)}, u32[]{:S(2)}, u32[]{:S(2)}) collective-permute-start(f32[24,8,384]{2,1,0:T(8,128)S(1)} %slice.63), channel_id=1, source_target_pairs={{0,15},{1,0},{2,1},{3,2},{4,3},{5,4},{6,5},{7,6},{8,7},{9,8},{10,9... | collective-permute-start | bytes 884744 | tf_op jit(solution)/shard_map/ppermute | solution.py:368
  4.1 43.6 %collective-permute-start.3 = (f32[24,8,384]{2,1,0:T(8,128)S(1)}, f32[24,8,384]{2,1,0:T(8,128)S(1)}, u32[]{:S(2)}, u32[]{:S(2)}) collective-permute-start(f32[24,8,384]{2,1,0:T(8,128)S(1)} %slice.66), channel_id=1, source_target_pairs={{0,15},{1,0},{2,1},{3,2},{4,3},{5,4},{6,5},{7,6},{8,7},{9,8},{10,9... | collective-permute-start | bytes 884744 | tf_op jit(solution)/shard_map/ppermute | solution.py:368
  11.3 36.4 %collective-permute-start.1 = (f32[6,24,384]{2,1,0:T(8,128)S(1)}, f32[6,24,384]{2,1,0:T(8,128)S(1)}, u32[]{:S(2)}, u32[]{:S(2)}) collective-permute-start(f32[6,24,384]{2,1,0:T(8,128)S(1)} %slice.64), channel_id=1, source_target_pairs={{0,112},{16,0},{32,16},{48,32},{64,48},{80,64},{96,80},{112,96},{1... | collective-permute-start | bytes 663560 | tf_op jit(solution)/shard_map/ppermute | solution.py:368
  14.9 32.8 %collective-permute-start.4 = (f32[6,24,384]{2,1,0:T(8,128)S(1)}, f32[6,24,384]{2,1,0:T(8,128)S(1)}, u32[]{:S(2)}, u32[]{:S(2)}) collective-permute-start(f32[6,24,384]{2,1,0:T(8,128)S(1)} %slice.67), channel_id=1, source_target_pairs={{0,112},{16,0},{32,16},{48,32},{64,48},{80,64},{96,80},{112,96},{1... | collective-permute-start | bytes 663560 | tf_op jit(solution)/shard_map/ppermute | solution.py:368
  16.4 8.0 %collective-permute-start.2 = (f32[6,8,384]{2,1,0:T(8,128)S(1)}, f32[6,8,384]{2,1,0:T(8,128)S(1)}, u32[]{:S(2)}, u32[]{:S(2)}) collective-permute-start(f32[6,8,384]{2,1,0:T(8,128)S(1)} %slice.65), channel_id=1, source_target_pairs={{0,127},{1,112},{2,113},{3,114},{4,115},{5,116},{6,117},{7,118},{8... | collective-permute-start | bytes 221192 | tf_op jit(solution)/shard_map/ppermute | solution.py:373
  24.4 23.3 %copy-start.6 = (f32[6,8,384]{2,1,0:T(8,128)}, f32[6,8,384]{2,1,0:T(8,128)S(1)}, u32[]{:S(2)}) copy-start(f32[6,8,384]{2,1,0:T(8,128)S(1)} %collective-permute-done.2.x_c) | copy-start | bytes 221188
  24.4 23.2 %collective-permute-start.5 = (f32[6,8,384]{2,1,0:T(8,128)S(1)}, f32[6,8,384]{2,1,0:T(8,128)S(1)}, u32[]{:S(2)}, u32[]{:S(2)}) collective-permute-start(f32[6,8,384]{2,1,0:T(8,128)S(1)} %slice.68), channel_id=1, source_target_pairs={{0,127},{1,112},{2,113},{3,114},{4,115},{5,116},{6,117},{7,118},{8... | collective-permute-start | bytes 221192 | tf_op jit(solution)/shard_map/ppermute | solution.py:373
  47.7 1.0 copy-start.3
  115.2 8.1 %copy-start = (f32[3,576,144]{2,1,0:T(8,128)S(1)}, f32[3,576,144]{2,1,0:T(8,128)}, u32[]{:S(2)}) copy-start(f32[3,576,144]{2,1,0:T(8,128)} %get-tuple-element.37) | copy-start | bytes 2985988
  184.9 7.8 %copy-start.8 = (f32[13824]{0:T(1024)S(1)}, f32[13824]{0:T(1024)}, u32[]{:S(2)}) copy-start(f32[13824]{0:T(1024)} %param.12) | copy-start | bytes 165892
  184.9 7.8 %copy-start.9 = (f32[13824]{0:T(1024)S(1)}, f32[13824]{0:T(1024)}, u32[]{:S(2)}) copy-start(f32[13824]{0:T(1024)} %param.11) | copy-start | bytes 165892
  187.0 50.1 %all-to-all-start.1 = ((f32[64,1,13952]{2,1,0:T(1,128)}), f32[64,1,13952]{2,1,0:T(1,128)}, u32[]{:S(2)}, u32[]{:S(2)}) async-start(f32[64,1,13952]{2,1,0:T(1,128)} %bitcast.36), calls=%async_computation.1 | async-start | bytes 7143424 | tf_op jit(solution)/shard_map/all_to_all | solution.py:363
  192.7 43.6 %collective-permute-start.9 = (f32[2,108,128]{2,1,0:T(8,128)S(1)}, f32[2,108,128]{2,1,0:T(8,128)S(1)}, u32[]{:S(2)}, u32[]{:S(2)}) collective-permute-start(f32[2,108,128]{2,1,0:T(8,128)S(1)} %pad_maximum_fusion.2), channel_id=1, source_target_pairs={{0,0},{1,2},{2,4},{3,6},{4,8},{5,10},{6,12},{7,14},{8,16},{9,18},{... | collective-permute-start | bytes 331784 | tf_op jit(solution)/shard_map/ppermute | solution.py:441
  237.2 20.2 %copy-start.12 = (f32[24,8,384]{2,1,0:T(8,128)S(1)}, f32[24,8,384]{2,1,0:T(8,128)}, u32[]{:S(2)}) copy-start(f32[24,8,384]{2,1,0:T(8,128)} %get-tuple-element.34) | copy-start | bytes 884740
  237.2 24.0 %copy-start.13 = (f32[6,24,384]{2,1,0:T(8,128)S(1)}, f32[6,24,384]{2,1,0:T(8,128)}, u32[]{:S(2)}) copy-start(f32[6,24,384]{2,1,0:T(8,128)} %get-tuple-element.33) | copy-start | bytes 663556
  237.2 25.2 %copy-start.1 = (f32[24,24,384]{2,1,0:T(8,128)S(1)}, f32[24,24,384]{2,1,0:T(8,128)}, u32[]{:S(2)}) copy-start(f32[24,24,384]{2,1,0:T(8,128)} %get-tuple-element.35) | copy-start | bytes 2654212
  237.2 25.3 %copy-start.14 = (f32[6,8,384]{2,1,0:T(8,128)S(1)}, f32[6,8,384]{2,1,0:T(8,128)}, u32[]{:S(2)}) copy-start(f32[6,8,384]{2,1,0:T(8,128)} %get-tuple-element.32) | copy-start | bytes 221188
  240.2 64.7 %copy-start.10 = (f32[108,128]{1,0:T(8,128)S(1)}, f32[108,128]{1,0:T(8,128)}, u32[]{:S(2)}) copy-start(f32[108,128]{1,0:T(8,128)} %get-tuple-element.39) | copy-start | bytes 165892
  240.2 64.7 %copy-start.11 = (f32[108,128]{1,0:T(8,128)S(1)}, f32[108,128]{1,0:T(8,128)}, u32[]{:S(2)}) copy-start(f32[108,128]{1,0:T(8,128)} %get-tuple-element.40) | copy-start | bytes 165892
  244.7 73.2 %all-to-all-start.2 = ((f32[64,1,13952]{2,1,0:T(1,128)}), f32[64,1,13952]{2,1,0:T(1,128)}, u32[]{:S(2)}, u32[]{:S(2)}) async-start(f32[64,1,13952]{2,1,0:T(1,128)} %broadcast_in_dim.9), calls=%async_computation.2 | async-start | bytes 7143424 | tf_op jit(solution)/shard_map/all_to_all | solution.py:363
  257.4 47.5 %collective-permute-start.8 = (f32[24,8,384]{2,1,0:T(8,128)S(1)}, f32[24,8,384]{2,1,0:T(8,128)S(1)}, u32[]{:S(2)}, u32[]{:S(2)}) collective-permute-start(f32[24,8,384]{2,1,0:T(8,128)S(1)} %copy-done.12), channel_id=1, source_target_pairs={{0,1},{1,2},{2,3},{3,4},{4,5},{5,6},{6,7},{7,8},{8,9},{9,10},{10,1... | collective-permute-start | bytes 884744 | tf_op jit(solution)/shard_map/ppermute | solution.py:368
  261.2 42.5 %collective-permute-start.7 = (f32[6,24,384]{2,1,0:T(8,128)S(1)}, f32[6,24,384]{2,1,0:T(8,128)S(1)}, u32[]{:S(2)}, u32[]{:S(2)}) collective-permute-start(f32[6,24,384]{2,1,0:T(8,128)S(1)} %copy-done.13), channel_id=1, source_target_pairs={{0,16},{16,32},{32,48},{48,64},{64,80},{80,96},{96,112},{112,0},{1... | collective-permute-start | bytes 663560 | tf_op jit(solution)/shard_map/ppermute | solution.py:368
  262.5 51.9 %collective-permute-start.6 = (f32[6,8,384]{2,1,0:T(8,128)S(1)}, f32[6,8,384]{2,1,0:T(8,128)S(1)}, u32[]{:S(2)}, u32[]{:S(2)}) collective-permute-start(f32[6,8,384]{2,1,0:T(8,128)S(1)} %copy-done.14), channel_id=1, source_target_pairs={{0,17},{1,18},{2,19},{3,20},{4,21},{5,22},{6,23},{7,24},{8,25},{9,... | collective-permute-start | bytes 221192 | tf_op jit(solution)/shard_map/ppermute | solution.py:373
  305.0 12.3 %collective-permute-start.10 = (f32[2,108,128]{2,1,0:T(8,128)S(1)}, f32[2,108,128]{2,1,0:T(8,128)S(1)}, u32[]{:S(2)}, u32[]{:S(2)}) collective-permute-start(f32[2,108,128]{2,1,0:T(8,128)S(1)} %pad_maximum_fusion.3), channel_id=1, source_target_pairs={{0,0},{2,1},{4,2},{6,3},{8,4},{10,5},{12,6},{14,7},{16,8},{18,9},{... | collective-permute-start | bytes 331784 | tf_op jit(solution)/shard_map/ppermute | solution.py:453
  (4 other events, 3.0 us)

commit v2 on v1

--- a/solution.py
+++ b/solution.py
@@ -31,8 +31,6 @@
 HALF = ROWS // 2
 OWN = ROWS // 128
 BLOCK = OWN + 1
-HALF_X = HALF + 64
-TABLE_ROWS = 50
 BIAS = 529
 BOTH = ("lat", "lon")
 F32 = jnp.float32
@@ -89,15 +87,18 @@
             wd_h[f, :, 128 * b : 128 * b + 128] = h
             wd_l[f, :, 128 * b : 128 * b + 128] = l
 
+    lines = jnp.concatenate([table[...], jnp.zeros((HEADS, 640 - BIAS), F32)], axis=1)
+
     def rows_of(step, carry):
         at = pl.multiple_of(step * 8, 8)
         columns = index[pl.ds(at, 8), :]
+        columns = jnp.concatenate([columns, jnp.zeros((8, 256 - WT), jnp.int32)], axis=1)
         low = columns & 127
         part = columns >> 7
         for h in range(HEADS):
             found = jnp.zeros((8, 256), F32)
             for p in range(5):
-                line = jnp.broadcast_to(table[h : h + 1, 128 * p : 128 * p + 128], (8, 128))
+                line = jnp.broadcast_to(lines[h : h + 1, 128 * p : 128 * p + 128], (8, 128))
                 taken = jnp.concatenate(
                     [
                         jnp.take_along_axis(line, low[:, :128], axis=1),
@@ -113,8 +114,6 @@
 
 
 def prepared(flat, table, index):
-    table = jnp.pad(table, ((0, 4), (0, 640 - BIAS)))
-    index = jnp.pad(index, ((0, 0), (0, 256 - WT)))
     shapes = [(D, 3 * D)] * 2 + [(D, D)] * 2 + [(CHUNKS, D, CHUNK)] * 2 + [(CHUNKS, CHUNK, D)] * 2
     return pl.pallas_call(
         prepare,
@@ -178,15 +177,32 @@
     return total
 
 
+def find_labels(region, last, label_row, label_col):
+    eye = lax.broadcasted_iota(jnp.int32, (WT, WT), 0) == lax.broadcasted_iota(jnp.int32, (WT, WT), 1)
+    for wr in range(2):
+        for wc in range(2):
+            w = wr * 2 + wc
+            pieces = []
+            for r in range(WIN):
+                row = wr * WIN + r
+                ids = region[row : row + 1, wc * WIN : wc * WIN + WIN]
+                pieces.append(ids + (4 * last if row >= TILE - SHIFT else 0))
+            line = jnp.concatenate(pieces, axis=1).astype(F32)
+            label_row[w] = line
+            wide = jnp.where(eye, jnp.broadcast_to(line, (WT, WT)), 0.0)
+            label_col[w] = jnp.sum(wide, axis=1, keepdims=True)
+
+
 SCALE = 1.0 / math.sqrt(32.0)
 
 
 def block_pass(
     x_l, x_e, x_s, x_c, c_l, c_e, c_s, c_c, wq_h, wq_l, wp_h, wp_l, wu_h, wu_l, wd_h, wd_l,
-    bias, label_col, label_row,
-    grads, dscore, o_l, o_e, o_s, o_c,
-    x, cot, qkv, ctx, prob, n2h, n2l, ch, cl, grad, dqkv, dctx,
+    bias, region, place,
+    keep, send, dscore, o_l, o_e, o_s, o_c,
+    x, cot, qkv, ctx, prob, n2h, n2l, ch, cl, grad, dqkv, dctx, grads, label_row, label_col, sems,
 ):
+    find_labels(region, place[1], label_row, label_col)
     gather_windows(x, x_l, x_e, x_s, x_c)
     gather_windows(cot, c_l, c_e, c_s, c_c)
     n1 = split(unit(x[...])[0])
@@ -279,12 +295,24 @@
         grads[pl.ds(b, D, stride=9), :] = gqkv[:, 128 * b : 128 * b + 128]
     back = dot3(dq, (wq_h[...], wq_l[...]), NT)
     grad[...] += unit_back(back, n1, scale1)
+    core = place[0]
+    out = pltpu.make_async_copy(
+        grads.at[pl.ds(pl.multiple_of((1 - core) * HALF, 8), HALF)], send, sems.at[0]
+    )
+    stay = pltpu.make_async_copy(
+        grads.at[pl.ds(pl.multiple_of(core * HALF, 8), HALF)], keep, sems.at[1]
+    )
+    out.start()
+    stay.start()
     scatter_windows(grad, o_l, o_e, o_s, o_c)
-
-
-def run_block(x_parts, c_parts, weights, bias, label_col, label_row):
+    out.wait()
+    stay.wait()
+
+
+def run_block(x_parts, c_parts, weights, bias, region, place):
     halo = [(TILE, TILE, D), (TILE, 8, D), (SHIFT, TILE, D), (SHIFT, 8, D)]
-    outs = [(ROWS, 128), (GROUPS, PER * WT, WT)] + halo
+    outs = [(HALF, 128), (HALF, 128), (GROUPS, PER * WT, WT)] + halo
+    whole = pl.BlockSpec(memory_space=pl.ANY)
     scratch = [
         pltpu.VMEM((TOK, D), F32),
         pltpu.VMEM((TOK, D), F32),
@@ -298,49 +326,62 @@
         pltpu.VMEM((TOK, D), F32),
         pltpu.VMEM((TOK, 3 * D), F32),
         pltpu.VMEM((TOK, D), F32),
+        pltpu.VMEM((ROWS, 128), F32),
+        pltpu.VMEM((WINS, 1, WT), F32),
+        pltpu.VMEM((WINS, WT, 1), F32),
+        pltpu.SemaphoreType.DMA((2,)),
     ]
-    args = (*x_parts, *c_parts, *weights, bias, label_col, label_row)
+    args = (*x_parts, *c_parts, *weights, bias, region, place)
     return pl.pallas_call(
         block_pass,
         out_shape=[jax.ShapeDtypeStruct(s, F32) for s in outs],
-        in_specs=[VMEM] * len(args),
-        out_specs=[VMEM] * len(outs),
+        in_specs=[VMEM] * (len(args) - 1) + [pl.BlockSpec(memory_space=pltpu.SMEM)],
+        out_specs=[whole] * 2 + [VMEM] * (len(outs) - 2),
         scratch_shapes=scratch,
         compiler_params=PARAMS,
         name="block_pass",
     )(*args)
 
 
-def table_sum(scores, index, out):
-    out[...] = jnp.zeros_like(out)
+def table_sum(scores, index, out, sums):
+    sums[...] = jnp.zeros_like(sums)
     column = lax.broadcasted_iota(jnp.int32, (128, WT), 0)
 
-    def step(i, carry):
-        line = index[i]
-        part = line >> 7
+    def one(i):
+        line = index[pl.ds(i, 1), :]
+        part = jnp.broadcast_to(line >> 7, (16, WT))
         hot = (column == jnp.broadcast_to(line & 127, (128, WT))).astype(F32).astype(BF16)
         high, low = split(scores[i])
-        pair = jnp.concatenate([high.astype(F32), low.astype(F32)], axis=0)
-        rows = jnp.concatenate([jnp.where(part == p, pair, 0.0) for p in range(5)], axis=0).astype(BF16)
-        out[...] += dot(rows, hot, NT)
+        pieces = []
+        for p in range(5):
+            here = part == p
+            pieces.append(jnp.where(here, high, jnp.zeros_like(high)))
+            pieces.append(jnp.where(here, low, jnp.zeros_like(low)))
+        return dot(jnp.concatenate(pieces, axis=0), hot, NT)
+
+    def step(k, carry):
+        sums[...] += (one(4 * k) + one(4 * k + 1)) + (one(4 * k + 2) + one(4 * k + 3))
         return carry
 
-    lax.fori_loop(0, WT, step, 0)
+    lax.fori_loop(0, WT // 4, step, 0)
+    out[...] = jnp.zeros_like(out)
+    for p in range(5):
+        both = sums[32 * p : 32 * p + 16, :] + sums[32 * p + 16 : 32 * p + 32, :]
+        out[HEADS * p : HEADS * p + HEADS, :] = both[:HEADS]
 
 
 def table_gradient(dscore, index):
     scores = dscore.reshape(HEADS, WT, WT).transpose(1, 0, 2)
     scores = jnp.pad(scores, ((0, 0), (0, 4), (0, 0)))
-    sums = pl.pallas_call(
+    return pl.pallas_call(
         table_sum,
-        out_shape=jax.ShapeDtypeStruct((160, 128), F32),
+        out_shape=jax.ShapeDtypeStruct((64, 128), F32),
         in_specs=[VMEM] * 2,
         out_specs=VMEM,
+        scratch_shapes=[pltpu.VMEM((160, 128), F32)],
         compiler_params=PARAMS,
         name="table_sum",
-    )(scores, index.reshape(WT, 1, WT))
-    sums = sums.reshape(5, 2, 16, 128).sum(axis=1)[:, :HEADS]
-    return sums.transpose(1, 0, 2).reshape(HEADS, 640)[:, :BIAS]
+    )(scores, index)
 
 
 def chip_order():
@@ -351,8 +392,8 @@
     return [[d + core for d in chip_order()] for core in range(2)]
 
 
-def core_groups():
-    return [[d, d + 1] for d in chip_order()]
+def core_swap():
+    return [(d, d ^ 1) for d in range(128)]
 
 
 def worker_pairs():
@@ -390,18 +431,55 @@
     )
 
 
+def merge(keep, came, line, line_came, out):
+    for q in range(64):
+        rows = slice(q * OWN, q * OWN + OWN)
+        out[q, 0:OWN, :] = keep[rows, :] + came[rows, :]
+        out[q, OWN:BLOCK, :] = line[q : q + 1, :] + line_came[q : q + 1, :]
+
+
 def adam(parts, weights, first, second, new, first_new, second_new, factor):
-    total = parts[0:BLOCK, :]
+    total = parts[0]
     for q in range(1, 64):
-        total = total + parts[q * BLOCK : (q + 1) * BLOCK, :]
+        total = total + parts[q]
     total = total * factor
-    grad = total[:OWN]
+    grad, line = total[:OWN], total[OWN:]
     m = 0.9 * first[...] + 0.1 * grad
     s = 0.95 * second[...] + 0.05 * grad * grad
     first_new[...] = m
     second_new[...] = s
-    new[0:OWN, :] = weights[...] - 0.01 * m / (jnp.sqrt(s) + 1e-08)
-    new[OWN:BLOCK, :] = total[OWN:BLOCK]
+    fresh = weights[...] - 0.01 * m / (jnp.sqrt(s) + 1e-08)
+    for q in range(64):
+        new[q, 0:OWN, :] = fresh
+        new[q, OWN:BLOCK, :] = line
+
+
+def lay_out(place, blocks, *refs):
+    out = refs[-1]
+    for q in range(8):
+        out[q * OWN : q * OWN + OWN, :] = blocks[q, 0:OWN, :]
+
+
+def half_weights(place, blocks, so_far, other):
+    def out_at(step, spot):
+        half = (1 - spot[0]) if other else spot[0]
+        return half * 8 + step, 0
+
+    spec = pl.BlockSpec((8, BLOCK, 128), lambda step, spot: (step, 0, 0))
+    more = [] if so_far is None else [so_far]
+    return pl.pallas_call(
+        lay_out,
+        out_shape=jax.ShapeDtypeStruct((ROWS, 128), F32),
+        grid_spec=pltpu.PrefetchScalarGridSpec(
+            num_scalar_prefetch=1,
+            grid=(8,),
+            in_specs=[spec] + [pl.BlockSpec(memory_space=pl.ANY)] * len(more),
+            out_specs=pl.BlockSpec((8 * OWN, 128), out_at),
+        ),
+        input_output_aliases={2: 0} if more else {},
+        compiler_params=PARAMS,
+        name="lay_out_other" if other else "lay_out_own",
+    )(place, blocks, *more)
 
 
 def per_device(
@@ -414,52 +492,63 @@
     x_parts = halo(block_input)
     c_parts = halo(cotangent)
 
-    wrapped = (lat_at * TILE + jnp.arange(TILE)) >= TILE * 8 - SHIFT
-    labels = region_ids * 2 + wrapped[:, None].astype(jnp.int32)
-    labels = labels.reshape(2, WIN, 2, WIN).transpose(0, 2, 1, 3).reshape(WINS, WT)
-    grads, dscore, o_l, o_e, o_s, o_c = run_block(
-        x_parts, c_parts, pairs, bias, labels[:, :, None], labels[:, None, :]
-    )
-
+    core = lon_at % 2
+    place = jnp.stack([core, (lat_at == 7).astype(jnp.int32)]).astype(jnp.int32)
+    keep, send, dscore, o_l, o_e, o_s, o_c = run_block(
+        x_parts, c_parts, pairs, bias, region_ids, place
+    )
+    came = lax.ppermute(send, BOTH, core_swap())
+    line = table_gradient(dscore, bias_index)
+    line_came = lax.ppermute(line, BOTH, core_swap())
+    summed = pl.pallas_call(
+        merge,
+        out_shape=jax.ShapeDtypeStruct((64, BLOCK, 128), F32),
+        in_specs=[VMEM] * 4,
+        out_specs=VMEM,
+        compiler_params=PARAMS,
+        name="merge",
+    )(keep, came, line, line_came)
+    parts = exchanged(summed, chip_groups())
+
+    _, o_e, o_s, o_c, first_moment, second_moment = lax.optimization_barrier(
+        (summed, o_e, o_s, o_c, first_moment, second_moment)
+    )
     from_west = around(o_e, "lon", 1)
     from_north = around(o_s, "lat", 1)
     from_corner = diagonal(o_c, 1)
-    top = jnp.concatenate([from_corner[:, :SHIFT], from_north[:, SHIFT:]], axis=1)
-    rest = jnp.concatenate([from_west[SHIFT:, :SHIFT], o_l[SHIFT:, SHIFT:]], axis=1)
-    grad_input = jnp.concatenate([top, rest], axis=0)
-
-    table = table_gradient(dscore, bias_index).reshape(-1)
-    table = jnp.pad(table, (0, 128 * 128 - table.shape[0])).reshape(2, 64, 1, 128)
-    sent = jnp.concatenate([grads.reshape(2, 64, OWN, 128), table], axis=2)
-    halves = exchanged(sent.reshape(2, 64 * BLOCK, 128), core_groups())
-    summed = halves[0] + halves[1]
-    parts = exchanged(summed.reshape(64, 1, BLOCK * 128), chip_groups())
-
     pairs_of = worker_pairs()
-    back = [(b, a) for a, b in pairs_of]
     moments = jnp.stack([first_moment.reshape(OWN, 128), second_moment.reshape(OWN, 128)])
     moments = lax.ppermute(moments, BOTH, pairs_of)
-    core = lon_at % 2
+    parts, from_west, from_north, from_corner, moments = lax.optimization_barrier(
+        (parts, from_west, from_north, from_corner, moments)
+    )
+
     shard = core * 64 + lat_at * 8 + lon_at // 2
     own = lax.dynamic_slice_in_dim(flat, shard * OWN, OWN, 0)
     new, first_new, second_new = pl.pallas_call(
         functools.partial(adam, factor=factor),
-        out_shape=[jax.ShapeDtypeStruct((n, 128), F32) for n in (BLOCK, OWN, OWN)],
+        out_shape=[jax.ShapeDtypeStruct(n, F32) for n in ((64, BLOCK, 128), (OWN, 128), (OWN, 128))],
         in_specs=[VMEM] * 4,
         out_specs=[VMEM] * 3,
         compiler_params=PARAMS,
         name="adam",
-    )(parts.reshape(64 * BLOCK, 128), own, moments[0], moments[1])
+    )(parts, own, moments[0], moments[1])
+    mine = exchanged(new, chip_groups())
+    back = [(b, a) for a, b in pairs_of]
     moments = lax.ppermute(jnp.stack([first_new, second_new]), BOTH, back)
-    copies = jnp.broadcast_to(new.reshape(1, 1, BLOCK * 128), (64, 1, BLOCK * 128))
-    mine = exchanged(copies, chip_groups()).reshape(1, 64 * BLOCK, 128)
-    everything = exchanged(jnp.concatenate([mine, mine]), core_groups())
-    everything = everything.reshape(128, BLOCK, 128)
-    weights_new = everything[:, :OWN].reshape(-1)
-    table_new = everything[:, OWN].reshape(-1)[: HEADS * BIAS].reshape(HEADS, BIAS)
+    top = jnp.concatenate([from_corner[:, :SHIFT], from_north[:, SHIFT:]], axis=1)
+    rest = jnp.concatenate([from_west[SHIFT:, :SHIFT], o_l[SHIFT:, SHIFT:]], axis=1)
+    grad_input = jnp.concatenate([top, rest], axis=0)
+    mine, moments = lax.optimization_barrier((mine, moments))
+
+    theirs = lax.ppermute(mine, BOTH, core_swap())
+    weights_new = half_weights(place, mine, None, False)
+    table_new = mine[: HEADS * 5, OWN].reshape(5, HEADS, 128).transpose(1, 0, 2)
+    table_new = table_new.reshape(HEADS, 640)[:, :BIAS]
+    weights_new = half_weights(place, theirs, weights_new, True)
     return (
         grad_input,
-        weights_new,
+        weights_new.reshape(-1),
         moments[0].reshape(-1),
         moments[1].reshape(-1),
         table_new,

time: 352 us -> 283 us (0.80)
  local copies, waits for them, and re-layouts: 56.3 us -> 28.1 us
  blocking collectives: 25.3 us -> 0 us
  other arithmetic: 15 us -> 1.68 us
  starting transfers between devices: 55.8 us -> 47.1 us
  Pallas kernels: 110 us -> 114 us
  waiting for transfers between devices: 86.2 us -> 90.2 us
    ppermute x6, waiting for transfers between devices: 41.1 us -> 0.02 us  [around(): lax.ppermute(value, axis, [(i, (i + by) % size) for i in range(size)])]
    ppermute x1, waiting for transfers between devices: 1.91 us -> 41.8 us  [per_device(): moments = lax.ppermute(jnp.stack([first_new, second_new]), BOTH, back)]
    ppermute x3, waiting for transfers between devices: 5.73 us -> 40.8 us  [diagonal(): lax.ppermute(value, BOTH, [(a * lon + o, (a + by) % lat * lon + (o + by)...]
    reshape x9 -> x0, local copies, waits for them, and re-layouts: 34 us -> none  [the longest x1 8.11 us: per_device(): sent = jnp.concatenate([grads.reshape(2, 64, OWN, 128), table], axis=2)]
    ppermute x1, waiting for transfers between devices: 37.3 us -> 6.51 us  [per_device(): moments = lax.ppermute(moments, BOTH, pairs_of)]
    all_to_all x2 -> x0, blocking collectives: 25.3 us -> none  [exchanged(): lax.all_to_all(value, BOTH, 0, 0, axis_index_groups=groups, tiled=True)]
    concatenate x2 -> x0, other arithmetic: 10.2 us -> none  [the longest x1 6.61 us: per_device(): sent = jnp.concatenate([grads.reshape(2, 64, OWN, 128), table], axis=2)]
    ppermute x0 -> x1, local copies, waits for them, and re-layouts: none -> 5.86 us  [per_device(): theirs = lax.ppermute(mine, BOTH, core_swap())]
  transfers between devices with their start and end apart: 13 -> 16, of which waited for: 6 -> 5; matrix products, arithmetic and copies ran while one was open for 4% -> 5% of each run, Pallas kernels for 3% -> 11%
where the time goes in v2:
time: 283 us; the launch traced here: 282 us
  Pallas kernels  114 us (40%)
  waiting for transfers between devices  90.2 us (32%)
  starting transfers between devices  47.1 us (17%)
  local copies, waits for them, and re-layouts  28.1 us (10%)
    pallas_call x1, Pallas kernels, run_block(): pl.pallas_call(block_pass, out_shape=[jax.ShapeDtypeStruct(s, F32) for s...  67.5 us
    ppermute x1, waiting for transfers between devices, per_device(): moments = lax.ppermute(jnp.stack([first_new, second_new]), BOTH, back)  41.8 us
    ppermute x3, waiting for transfers between devices, diagonal(): lax.ppermute(value, BOTH, [(a * lon + o, (a + by) % lat * lon + (o + by)...  40.8 us
    all_to_all x2, starting transfers between devices, exchanged(): lax.all_to_all(value, BOTH, 0, 0, axis_index_groups=groups, tiled=True)  17.1 us
    ppermute x6, starting transfers between devices, around(): lax.ppermute(value, axis, [(i, (i + by) % size) for i in range(size)])  15.5 us
    pallas_call x2, Pallas kernels, half_weights(): pl.pallas_call(lay_out, out_shape=jax.ShapeDtypeStruct((ROWS, 128), F32),...  14 us
    pallas_call x1, Pallas kernels, table_gradient(): pl.pallas_call(table_sum, out_shape=jax.ShapeDtypeStruct((64, 128), F32),...  12 us
    pallas_call x1, Pallas kernels, prepared(): pl.pallas_call(prepare, out_shape=[jax.ShapeDtypeStruct(s, BF16) for s in...  11.3 us
  transfers between devices with their start and end apart: 16, of which 5 were waited for; matrix products, arithmetic and copies ran while one was open for 5% of the time, Pallas kernels for 11%

profile of v2, /device:TPU:1, one launch (start us, length us, event | category | flops | bytes accessed | tf_op | source)
XLA Modules:
  0.0 282.3 jit_solution(12938567733656268083)
XLA Ops:
  1.6 1.5 collective-permute-start.3
  4.1 6.3 %collective-permute-start = (f32[24,8,384]{2,1,0:T(8,128)S(1)}, f32[24,8,384]{2,1,0:T(8,128)S(1)}, u32[]{:S(2)}, u32[]{:S(2)}) collective-permute-start(f32[24,8,384]{2,1,0:T(8,128)S(1)} %slice.48), channel_id=1, source_target_pairs={{0,15},{1,0},{2,1},{3,2},{4,3},{5,4},{6,5},{7,6},{8,7},{9,8},{10,9... | collective-permute-start | bytes 884744 | tf_op jit(solution)/shard_map/ppermute | solution.py:409
  11.3 2.7 collective-permute-start.4
  18.7 11.3 %prepare.1 = (bf16[384,1152]{1,0:T(8,128)(2,1)}, bf16[384,1152]{1,0:T(8,128)(2,1)}, bf16[384,384]{1,0:T(8,128)(2,1)}, bf16[384,384]{1,0:T(8,128)(2,1)}, bf16[6,3...) custom-call(f32[13824,128]{1,0:T(8,128)} %bitcast.30, ...), custom_call_target="tpu_custom_call" | custom-call | tf_op jit(solution)/shard_map/prepare/pallas_call | solution.py:118
  31.0 5.4 %collective-permute-done.2.x_c = f32[6,8,384]{2,1,0:T(8,128)S(1)} collective-permute-done((f32[6,8,384]{2,1,0:T(8,128)S(1)}, f32[6,8,384]{2,1,0:T(8,128)S(1)}, u32[]{:S(2)}, u32[]{:S(2)}) %collective-permute-start.2) | collective-permute-done | bytes 73760 | tf_op jit(solution)/shard_map/ppermute | solution.py:414
  37.4 67.5 %block_pass.1 = (f32[6912,128]{1,0:T(8,128)}, f32[6912,128]{1,0:T(8,128)}, f32[3,576,144]{2,1,0:T(8,128)}, f32[24,24,384]{2,1,0:T(8,128)}, f32[24,8,384]{2,1,0:T...) custom-call(f32[24,24,384]{2,1,0:T(8,128)} %x_l.1, f32[24,8,384]{2,1,0:T(8,128)} %copy-done.3, ...), custom_call_target="tpu_custom_call" | custom-call | tf_op jit(solution)/shard_map/block_pass/pallas_call | solution.py:335
  105.0 2.5 copy.25
  107.6 1.7 pad.4.scores
  109.2 12.0 %table_sum.1.line = f32[64,128]{1,0:T(8,128)} custom-call(f32[144,16,144]{2,1,0:T(8,128)} %pad.4.scores, s32[144,144]{1,0:T(8,128)} %index.3), custom_call_target="tpu_custom_call" | custom-call | tf_op jit(solution)/shard_map/table_sum/pallas_call | solution.py:376
  124.6 5.3 %merge.1 = f32[64,109,128]{2,1,0:T(8,128)} custom-call(f32[6912,128]{1,0:T(8,128)} %get-tuple-element.45.keep, f32[6912,128]{1,0:T(8,128)} %copy-done, f32[64,128]{1,0:T(8,128)} %table_sum.1.line, f32[64,128]{1,0:T(8,128)} %copy-done.12), custom_call_target="tpu_custom_call" | custom-call | tf_op jit(solution)/shard_map/merge/pallas_call | solution.py:503
  129.9 8.5 %all-to-all-start = ((f32[64,109,128]{2,1,0:T(8,128)}), f32[64,109,128]{2,1,0:T(8,128)}, u32[]{:S(2)}, u32[]{:S(2)}) async-start(f32[64,109,128]{2,1,0:T(8,128)} %merge.1), calls=%async_computation | async-start | bytes 7340032 | tf_op jit(solution)/shard_map/all_to_all | solution.py:404
  138.4 3.3 %collective-permute-start.8 = (f32[24,8,384]{2,1,0:T(8,128)S(1)}, f32[24,8,384]{2,1,0:T(8,128)S(1)}, u32[]{:S(2)}, u32[]{:S(2)}) collective-permute-start(f32[24,8,384]{2,1,0:T(8,128)S(1)} %copy-done.13), channel_id=1, source_target_pairs={{0,1},{1,2},{2,3},{3,4},{4,5},{5,6},{6,7},{7,8},{8,9},{9,10},{10,1... | collective-permute-start | bytes 884744 | tf_op jit(solution)/shard_map/ppermute | solution.py:409
  144.0 3.8 %collective-permute-start.11 = (f32[2,108,128]{2,1,0:T(8,128)S(1)}, f32[2,108,128]{2,1,0:T(8,128)S(1)}, u32[]{:S(2)}, u32[]{:S(2)}) collective-permute-start(f32[2,108,128]{2,1,0:T(8,128)S(1)} %pad_maximum_fusion), channel_id=1, source_target_pairs={{0,0},{1,2},{2,4},{3,6},{4,8},{5,10},{6,12},{7,14},{8,16},{9,18},{... | collective-permute-start | bytes 331784 | tf_op jit(solution)/shard_map/ppermute | solution.py:521
  149.3 35.4 %collective-permute-done.10 = f32[6,8,384]{2,1,0:T(8,128)S(1)} collective-permute-done((f32[6,8,384]{2,1,0:T(8,128)S(1)}, f32[6,8,384]{2,1,0:T(8,128)S(1)}, u32[]{:S(2)}, u32[]{:S(2)}) %collective-permute-start.10) | collective-permute-done | bytes 73760 | tf_op jit(solution)/shard_map/ppermute | solution.py:414
  184.6 6.5 %collective-permute-done.11 = f32[2,108,128]{2,1,0:T(8,128)S(1)} collective-permute-done((f32[2,108,128]{2,1,0:T(8,128)S(1)}, f32[2,108,128]{2,1,0:T(8,128)S(1)}, u32[]{:S(2)}, u32[]{:S(2)}) %collective-permute-start.11) | collective-permute-done | bytes 110624 | tf_op jit(solution)/shard_map/ppermute | solution.py:521
  191.8 4.3 %adam.1 = (f32[64,109,128]{2,1,0:T(8,128)}, f32[108,128]{1,0:T(8,128)}, f32[108,128]{1,0:T(8,128)}) custom-call(f32[64,109,128]{2,1,0:T(8,128)} %all-to-all-done.parts, f32[108,128]{1,0:T(8,128)} %constant_dynamic-slice_fusion.weights, f32[108,128]{1,0:T(8,128)} %get-tuple-element.70.first, f32[108,128]{1,0:T(8,128)} %get-tuple-element.69.second), custom_call_target="tpu_custom_call" | custom-call | tf_op jit(solution)/shard_map/adam/pallas_call | solution.py:528
  196.1 8.7 %all-to-all-start.1 = ((f32[64,109,128]{2,1,0:T(8,128)}), f32[64,109,128]{2,1,0:T(8,128)}, u32[]{:S(2)}, u32[]{:S(2)}) async-start(f32[64,109,128]{2,1,0:T(8,128)} %get-tuple-element.62), calls=%async_computation.1 | async-start | bytes 7340032 | tf_op jit(solution)/shard_map/all_to_all | solution.py:404
  204.8 4.6 %collective-permute-start.12 = (f32[2,108,128]{2,1,0:T(8,128)S(1)}, f32[2,108,128]{2,1,0:T(8,128)S(1)}, u32[]{:S(2)}, u32[]{:S(2)}) collective-permute-start(f32[2,108,128]{2,1,0:T(8,128)S(1)} %pad_maximum_fusion.1), channel_id=1, source_target_pairs={{0,0},{2,1},{4,2},{6,3},{8,4},{10,5},{12,6},{14,7},{16,8},{18,9},{... | collective-permute-start | bytes 331784 | tf_op jit(solution)/shard_map/ppermute | solution.py:538
  209.4 41.8 %collective-permute-done.12 = f32[2,108,128]{2,1,0:T(8,128)S(1)} collective-permute-done((f32[2,108,128]{2,1,0:T(8,128)S(1)}, f32[2,108,128]{2,1,0:T(8,128)S(1)}, u32[]{:S(2)}, u32[]{:S(2)}) %collective-permute-start.12) | collective-permute-done | bytes 110624 | tf_op jit(solution)/shard_map/ppermute | solution.py:538
  251.2 5.1 %copy.18 = f32[64,109,128]{2,0,1:T(8,128)} copy(f32[64,109,128]{2,1,0:T(8,128)} %all-to-all-done.1.blocks) | data formatting | bytes 7143424 | tf_op jit(solution)/shard_map/optimization_barrier | solution.py:542
  256.3 2.7 collective-permute-start.13
  260.1 7.0 %lay_out_own.1.refs_0_ = f32[13824,128]{1,0:T(8,128)} custom-call(s32[2]{0:T(128)} %pad_add_fusion.place, f32[64,109,128]{2,1,0:T(8,128)} %all-to-all-done.1.blocks), custom_call_target="tpu_custom_call" | custom-call | tf_op jit(solution)/shard_map/lay_out_own/pallas_call | solution.py:470
  269.5 5.9 %copy.19.blocks = f32[64,109,128]{2,1,0:T(8,128)} copy(f32[64,109,128]{2,0,1:T(8,128)} %collective-permute-done.13) | data formatting | bytes 7143424 | tf_op jit(solution)/shard_map/ppermute | solution.py:544
  275.3 7.0 %lay_out_other.1 = f32[13824,128]{1,0:T(8,128)} custom-call(s32[2]{0:T(128)} %pad_add_fusion.place, f32[64,109,128]{2,1,0:T(8,128)} %copy.19.blocks, f32[13824,128]{1,0:T(8,128)} %lay_out_own.1.refs_0_), custom_call_target="tpu_custom_call", output_to_operand_aliasing={{}: (2, {})} | custom-call | tf_op jit(solution)/shard_map/lay_out_other/pallas_call | solution.py:470
  (72 shorter events, 20.8 us)
Async XLA Ops:
  1.6 34.9 %collective-permute-start.3 = (f32[24,8,384]{2,1,0:T(8,128)S(1)}, f32[24,8,384]{2,1,0:T(8,128)S(1)}, u32[]{:S(2)}, u32[]{:S(2)}) collective-permute-start(f32[24,8,384]{2,1,0:T(8,128)S(1)} %slice.51), channel_id=1, source_target_pairs={{0,15},{1,0},{2,1},{3,2},{4,3},{5,4},{6,5},{7,6},{8,7},{9,8},{10,9... | collective-permute-start | bytes 884744 | tf_op jit(solution)/shard_map/ppermute | solution.py:409
  4.1 32.4 %collective-permute-start = (f32[24,8,384]{2,1,0:T(8,128)S(1)}, f32[24,8,384]{2,1,0:T(8,128)S(1)}, u32[]{:S(2)}, u32[]{:S(2)}) collective-permute-start(f32[24,8,384]{2,1,0:T(8,128)S(1)} %slice.48), channel_id=1, source_target_pairs={{0,15},{1,0},{2,1},{3,2},{4,3},{5,4},{6,5},{7,6},{8,7},{9,8},{10,9... | collective-permute-start | bytes 884744 | tf_op jit(solution)/shard_map/ppermute | solution.py:409
  11.3 25.1 %collective-permute-start.4 = (f32[6,24,384]{2,1,0:T(8,128)S(1)}, f32[6,24,384]{2,1,0:T(8,128)S(1)}, u32[]{:S(2)}, u32[]{:S(2)}) collective-permute-start(f32[6,24,384]{2,1,0:T(8,128)S(1)} %slice.52), channel_id=1, source_target_pairs={{0,112},{16,0},{32,16},{48,32},{64,48},{80,64},{96,80},{112,96},{1... | collective-permute-start | bytes 663560 | tf_op jit(solution)/shard_map/ppermute | solution.py:409
  14.9 21.5 %collective-permute-start.1 = (f32[6,24,384]{2,1,0:T(8,128)S(1)}, f32[6,24,384]{2,1,0:T(8,128)S(1)}, u32[]{:S(2)}, u32[]{:S(2)}) collective-permute-start(f32[6,24,384]{2,1,0:T(8,128)S(1)} %slice.49), channel_id=1, source_target_pairs={{0,112},{16,0},{32,16},{48,32},{64,48},{80,64},{96,80},{112,96},{1... | collective-permute-start | bytes 663560 | tf_op jit(solution)/shard_map/ppermute | solution.py:409
  16.4 13.6 %collective-permute-start.5 = (f32[6,8,384]{2,1,0:T(8,128)S(1)}, f32[6,8,384]{2,1,0:T(8,128)S(1)}, u32[]{:S(2)}, u32[]{:S(2)}) collective-permute-start(f32[6,8,384]{2,1,0:T(8,128)S(1)} %slice.53), channel_id=1, source_target_pairs={{0,127},{1,112},{2,113},{3,114},{4,115},{5,116},{6,117},{7,118},{8... | collective-permute-start | bytes 221192 | tf_op jit(solution)/shard_map/ppermute | solution.py:414
  30.0 6.4 %collective-permute-start.2 = (f32[6,8,384]{2,1,0:T(8,128)S(1)}, f32[6,8,384]{2,1,0:T(8,128)S(1)}, u32[]{:S(2)}, u32[]{:S(2)}) collective-permute-start(f32[6,8,384]{2,1,0:T(8,128)S(1)} %slice.50), channel_id=1, source_target_pairs={{0,127},{1,112},{2,113},{3,114},{4,115},{5,116},{6,117},{7,118},{8... | collective-permute-start | bytes 221192 | tf_op jit(solution)/shard_map/ppermute | solution.py:414
  104.9 17.9 %collective-permute-start.6 = (f32[6912,128]{1,0:T(8,128)}, f32[6912,128]{1,0:T(8,128)S(1)}, u32[]{:S(2)}, u32[]{:S(2)}) collective-permute-start(f32[6912,128]{1,0:T(8,128)} %get-tuple-element.46), channel_id=1, source_target_pairs={{0,1},{1,0},{2,3},{3,2},{4,5},{5,4},{6,7},{7,6},{8,9},{9,8},{10,11... | collective-permute-start | bytes 10616840 | tf_op jit(solution)/shard_map/ppermute | solution.py:500
  121.2 1.6 collective-permute-start.7
  129.9 8.5 %copy-start.13 = (f32[24,8,384]{2,1,0:T(8,128)S(1)}, f32[24,8,384]{2,1,0:T(8,128)}, u32[]{:S(2)}) copy-start(f32[24,8,384]{2,1,0:T(8,128)} %get-tuple-element.51) | copy-start | bytes 884740
  129.9 11.8 %copy-start.15 = (f32[6,8,384]{2,1,0:T(8,128)S(1)}, f32[6,8,384]{2,1,0:T(8,128)}, u32[]{:S(2)}) copy-start(f32[6,8,384]{2,1,0:T(8,128)} %get-tuple-element.53) | copy-start | bytes 221188
  129.9 12.9 %copy-start.14 = (f32[6,24,384]{2,1,0:T(8,128)S(1)}, f32[6,24,384]{2,1,0:T(8,128)}, u32[]{:S(2)}) copy-start(f32[6,24,384]{2,1,0:T(8,128)} %get-tuple-element.52) | copy-start | bytes 663556
  129.9 14.0 %copy-start.8 = (f32[13824]{0:T(1024)S(1)}, f32[13824]{0:T(1024)}, u32[]{:S(2)}) copy-start(f32[13824]{0:T(1024)} %param.12) | copy-start | bytes 165892
  129.9 14.0 %copy-start.9 = (f32[13824]{0:T(1024)S(1)}, f32[13824]{0:T(1024)}, u32[]{:S(2)}) copy-start(f32[13824]{0:T(1024)} %param.11) | copy-start | bytes 165892
  129.9 61.2 %all-to-all-start = ((f32[64,109,128]{2,1,0:T(8,128)}), f32[64,109,128]{2,1,0:T(8,128)}, u32[]{:S(2)}, u32[]{:S(2)}) async-start(f32[64,109,128]{2,1,0:T(8,128)} %merge.1), calls=%async_computation | async-start | bytes 7340032 | tf_op jit(solution)/shard_map/all_to_all | solution.py:404
  138.4 52.7 %collective-permute-start.8 = (f32[24,8,384]{2,1,0:T(8,128)S(1)}, f32[24,8,384]{2,1,0:T(8,128)S(1)}, u32[]{:S(2)}, u32[]{:S(2)}) collective-permute-start(f32[24,8,384]{2,1,0:T(8,128)S(1)} %copy-done.13), channel_id=1, source_target_pairs={{0,1},{1,2},{2,3},{3,4},{4,5},{5,6},{6,7},{7,8},{8,9},{9,10},{10,1... | collective-permute-start | bytes 884744 | tf_op jit(solution)/shard_map/ppermute | solution.py:409
  141.8 42.9 %collective-permute-start.10 = (f32[6,8,384]{2,1,0:T(8,128)S(1)}, f32[6,8,384]{2,1,0:T(8,128)S(1)}, u32[]{:S(2)}, u32[]{:S(2)}) collective-permute-start(f32[6,8,384]{2,1,0:T(8,128)S(1)} %copy-done.15), channel_id=1, source_target_pairs={{0,17},{1,18},{2,19},{3,20},{4,21},{5,22},{6,23},{7,24},{8,25},{9,... | collective-permute-start | bytes 221192 | tf_op jit(solution)/shard_map/ppermute | solution.py:414
  142.8 48.4 %collective-permute-start.9 = (f32[6,24,384]{2,1,0:T(8,128)S(1)}, f32[6,24,384]{2,1,0:T(8,128)S(1)}, u32[]{:S(2)}, u32[]{:S(2)}) collective-permute-start(f32[6,24,384]{2,1,0:T(8,128)S(1)} %copy-done.14), channel_id=1, source_target_pairs={{0,16},{16,32},{32,48},{48,64},{64,80},{80,96},{96,112},{112,0},{1... | collective-permute-start | bytes 663560 | tf_op jit(solution)/shard_map/ppermute | solution.py:409
  144.0 47.2 %collective-permute-start.11 = (f32[2,108,128]{2,1,0:T(8,128)S(1)}, f32[2,108,128]{2,1,0:T(8,128)S(1)}, u32[]{:S(2)}, u32[]{:S(2)}) collective-permute-start(f32[2,108,128]{2,1,0:T(8,128)S(1)} %pad_maximum_fusion), channel_id=1, source_target_pairs={{0,0},{1,2},{2,4},{3,6},{4,8},{5,10},{6,12},{7,14},{8,16},{9,18},{... | collective-permute-start | bytes 331784 | tf_op jit(solution)/shard_map/ppermute | solution.py:521
  196.1 8.7 %copy-start.10 = (f32[108,128]{1,0:T(8,128)S(1)}, f32[108,128]{1,0:T(8,128)}, u32[]{:S(2)}) copy-start(f32[108,128]{1,0:T(8,128)} %get-tuple-element.63) | copy-start | bytes 165892
  196.1 8.7 %copy-start.11 = (f32[108,128]{1,0:T(8,128)S(1)}, f32[108,128]{1,0:T(8,128)}, u32[]{:S(2)}) copy-start(f32[108,128]{1,0:T(8,128)} %get-tuple-element.64) | copy-start | bytes 165892
  196.1 55.1 %all-to-all-start.1 = ((f32[64,109,128]{2,1,0:T(8,128)}), f32[64,109,128]{2,1,0:T(8,128)}, u32[]{:S(2)}, u32[]{:S(2)}) async-start(f32[64,109,128]{2,1,0:T(8,128)} %get-tuple-element.62), calls=%async_computation.1 | async-start | bytes 7340032 | tf_op jit(solution)/shard_map/all_to_all | solution.py:404
  204.8 54.2 %copy-start.1 = (f32[24,24,384]{2,1,0:T(8,128)S(1)}, f32[24,24,384]{2,1,0:T(8,128)}, u32[]{:S(2)}) copy-start(f32[24,24,384]{2,1,0:T(8,128)} %get-tuple-element.59) | copy-start | bytes 2654212
  204.8 46.4 %collective-permute-start.12 = (f32[2,108,128]{2,1,0:T(8,128)S(1)}, f32[2,108,128]{2,1,0:T(8,128)S(1)}, u32[]{:S(2)}, u32[]{:S(2)}) collective-permute-start(f32[2,108,128]{2,1,0:T(8,128)S(1)} %pad_maximum_fusion.1), channel_id=1, source_target_pairs={{0,0},{2,1},{4,2},{6,3},{8,4},{10,5},{12,6},{14,7},{16,8},{18,9},{... | collective-permute-start | bytes 331784 | tf_op jit(solution)/shard_map/ppermute | solution.py:538
  256.3 13.2 %collective-permute-start.13 = (f32[64,109,128]{2,0,1:T(8,128)}, f32[64,109,128]{2,0,1:T(8,128)}, u32[]{:S(2)}, u32[]{:S(2)}) collective-permute-start(f32[64,109,128]{2,0,1:T(8,128)} %copy.18), channel_id=1, source_target_pairs={{0,1},{1,0},{2,3},{3,2},{4,5},{5,4},{6,7},{7,6},{8,9},{9,8},{10,11... | collective-permute-start | bytes 10715144 | tf_op jit(solution)/shard_map/ppermute | solution.py:544
  (8 other events, 12.8 us)

commit v3 on v2

--- a/solution.py
+++ b/solution.py
@@ -30,7 +30,6 @@
 CHUNKS = FF // CHUNK
 HALF = ROWS // 2
 OWN = ROWS // 128
-BLOCK = OWN + 1
 BIAS = 529
 BOTH = ("lat", "lon")
 F32 = jnp.float32
@@ -68,29 +67,27 @@
     return scale * (grad - mean - normed * along)
 
 
-def prepare(flat, table, index, wq_h, wq_l, wp_h, wp_l, wu_h, wu_l, wd_h, wd_l, bias):
-    for at, rows, blocks, high, low in (
-        (0, D, 9, wq_h, wq_l),
-        (PROJ_AT, D, 3, wp_h, wp_l),
+STEPS = 6
+
+
+def prepare(qkv, proj, up, down, table, index, wq_h, wq_l, wp_h, wp_l, wu_h, wu_l, wd_h, wd_l, bias):
+    for flat, rows, blocks, high, low in (
+        (qkv, D // STEPS, 9, wq_h, wq_l),
+        (proj, D // STEPS, 3, wp_h, wp_l),
+        (down, FF // STEPS, 3, wd_h.at[0], wd_l.at[0]),
     ):
         for b in range(blocks):
-            h, l = split(flat[pl.ds(at + b, rows, stride=blocks), :])
+            h, l = split(flat[pl.ds(b, rows, stride=blocks), :])
             high[:, 128 * b : 128 * b + 128] = h
             low[:, 128 * b : 128 * b + 128] = l
     for f in range(CHUNKS):
         for b in range(2):
-            h, l = split(flat[pl.ds(UP_AT + 2 * f + b, D, stride=12), :])
+            h, l = split(up[pl.ds(2 * f + b, D // STEPS, stride=12), :])
             wu_h[f, :, 128 * b : 128 * b + 128] = h
             wu_l[f, :, 128 * b : 128 * b + 128] = l
-        for b in range(3):
-            h, l = split(flat[pl.ds(DOWN_AT + 3 * CHUNK * f + b, CHUNK, stride=3), :])
-            wd_h[f, :, 128 * b : 128 * b + 128] = h
-            wd_l[f, :, 128 * b : 128 * b + 128] = l
-
     lines = jnp.concatenate([table[...], jnp.zeros((HEADS, 640 - BIAS), F32)], axis=1)
-
-    def rows_of(step, carry):
-        at = pl.multiple_of(step * 8, 8)
+    for k in range(WT // 8 // STEPS):
+        at = pl.multiple_of((pl.program_id(0) * (WT // 8 // STEPS) + k) * 8, 8)
         columns = index[pl.ds(at, 8), :]
         columns = jnp.concatenate([columns, jnp.zeros((8, 256 - WT), jnp.int32)], axis=1)
         low = columns & 127
@@ -108,22 +105,39 @@
                 )
                 found = jnp.where(part == p, taken, found)
             bias[h // PER, pl.ds(pl.multiple_of((h % PER) * WT + at, 8), 8), :] = found[:, :WT]
-        return carry
-
-    lax.fori_loop(0, WT // 8, rows_of, 0)
 
 
 def prepared(flat, table, index):
     shapes = [(D, 3 * D)] * 2 + [(D, D)] * 2 + [(CHUNKS, D, CHUNK)] * 2 + [(CHUNKS, CHUNK, D)] * 2
+    piece = D // STEPS
+    outs = [
+        *[pl.BlockSpec((piece, 3 * D), lambda i: (i, 0))] * 2,
+        *[pl.BlockSpec((piece, D), lambda i: (i, 0))] * 2,
+        *[pl.BlockSpec((CHUNKS, piece, CHUNK), lambda i: (0, i, 0))] * 2,
+        *[pl.BlockSpec((1, CHUNK, D), lambda i: (i, 0, 0))] * 2,
+        pl.BlockSpec((GROUPS, PER * WT, WT), lambda i: (0, 0, 0)),
+    ]
+
+    def part(at, rows):
+        return pl.BlockSpec((rows // STEPS, 128), lambda i: (at * STEPS // rows + i, 0))
+
     return pl.pallas_call(
         prepare,
         out_shape=[jax.ShapeDtypeStruct(s, BF16) for s in shapes]
         + [jax.ShapeDtypeStruct((GROUPS, PER * WT, WT), F32)],
-        in_specs=[VMEM] * 3,
-        out_specs=[VMEM] * 9,
+        grid=(STEPS,),
+        in_specs=[
+            part(0, QKV_ROWS),
+            part(PROJ_AT, PROJ_ROWS),
+            part(UP_AT, MLP_ROWS),
+            part(DOWN_AT, MLP_ROWS),
+            pl.BlockSpec((HEADS, BIAS), lambda i: (0, 0)),
+            pl.BlockSpec((WT, WT), lambda i: (0, 0)),
+        ],
+        out_specs=outs,
         compiler_params=PARAMS,
         name="prepare",
-    )(flat, table, index)
+    )(flat, flat, flat, flat, table, index)
 
 
 def gather_windows(target, local, east, south, corner):
@@ -197,14 +211,14 @@
 
 
 def block_pass(
-    x_l, x_e, x_s, x_c, c_l, c_e, c_s, c_c, wq_h, wq_l, wp_h, wp_l, wu_h, wu_l, wd_h, wd_l,
+    x_l, c_l, east, south, corner, wq_h, wq_l, wp_h, wp_l, wu_h, wu_l, wd_h, wd_l,
     bias, region, place,
     keep, send, dscore, o_l, o_e, o_s, o_c,
     x, cot, qkv, ctx, prob, n2h, n2l, ch, cl, grad, dqkv, dctx, grads, label_row, label_col, sems,
 ):
     find_labels(region, place[1], label_row, label_col)
-    gather_windows(x, x_l, x_e, x_s, x_c)
-    gather_windows(cot, c_l, c_e, c_s, c_c)
+    gather_windows(x, x_l, east.at[0], south.at[0], corner.at[0])
+    gather_windows(cot, c_l, east.at[1], south.at[1], corner.at[1])
     n1 = split(unit(x[...])[0])
     qkv[...] = dot3(n1, (wq_h[...], wq_l[...]), NN)
 
@@ -309,7 +323,7 @@
     stay.wait()
 
 
-def run_block(x_parts, c_parts, weights, bias, region, place):
+def run_block(tiles, edges, weights, bias, region, place):
     halo = [(TILE, TILE, D), (TILE, 8, D), (SHIFT, TILE, D), (SHIFT, 8, D)]
     outs = [(HALF, 128), (HALF, 128), (GROUPS, PER * WT, WT)] + halo
     whole = pl.BlockSpec(memory_space=pl.ANY)
@@ -331,7 +345,7 @@
         pltpu.VMEM((WINS, WT, 1), F32),
         pltpu.SemaphoreType.DMA((2,)),
     ]
-    args = (*x_parts, *c_parts, *weights, bias, region, place)
+    args = (*tiles, *edges, *weights, bias, region, place)
     return pl.pallas_call(
         block_pass,
         out_shape=[jax.ShapeDtypeStruct(s, F32) for s in outs],
@@ -422,64 +436,78 @@
     )
 
 
-def halo(tile):
-    return (
-        tile,
-        around(tile[:, :8], "lon", -1),
-        around(tile[:SHIFT], "lat", -1),
-        diagonal(tile[:SHIFT, :8], -1),
-    )
-
-
-def merge(keep, came, line, line_came, out):
-    for q in range(64):
-        rows = slice(q * OWN, q * OWN + OWN)
-        out[q, 0:OWN, :] = keep[rows, :] + came[rows, :]
-        out[q, OWN:BLOCK, :] = line[q : q + 1, :] + line_came[q : q + 1, :]
+def pack(x, c, east, south, corner, sems):
+    copies = []
+    for i, tile in enumerate((x, c)):
+        for j, (rows, cols, out) in enumerate(
+            ((TILE, 8, east), (SHIFT, TILE, south), (SHIFT, 8, corner))
+        ):
+            source = tile.at[pl.ds(0, rows), pl.ds(0, cols)]
+            copies.append(pltpu.make_async_copy(source, out.at[i], sems.at[3 * i + j]))
+    for copy in copies:
+        copy.start()
+    for copy in copies:
+        copy.wait()
+
+
+def edges_of(x, c):
+    whole = pl.BlockSpec(memory_space=pl.ANY)
+    shapes = [(2, TILE, 8, D), (2, SHIFT, TILE, D), (2, SHIFT, 8, D)]
+    east, south, corner = pl.pallas_call(
+        pack,
+        out_shape=[jax.ShapeDtypeStruct(s, F32) for s in shapes],
+        in_specs=[whole] * 2,
+        out_specs=[whole] * 3,
+        scratch_shapes=[pltpu.SemaphoreType.DMA((6,))],
+        compiler_params=PARAMS,
+        name="pack",
+    )(x, c)
+    return around(east, "lon", -1), around(south, "lat", -1), diagonal(corner, -1)
+
+
+def butterfly(value, bit):
+    return value + lax.ppermute(value, BOTH, [(d, d ^ bit) for d in range(128)])
+
+
+def merge(keep, came, out):
+    out[...] = keep[...] + came[...]
 
 
 def adam(parts, weights, first, second, new, first_new, second_new, factor):
-    total = parts[0]
+    grad = parts[0:OWN, :]
     for q in range(1, 64):
-        total = total + parts[q]
-    total = total * factor
-    grad, line = total[:OWN], total[OWN:]
+        grad = grad + parts[q * OWN : q * OWN + OWN, :]
+    grad = grad * factor
     m = 0.9 * first[...] + 0.1 * grad
     s = 0.95 * second[...] + 0.05 * grad * grad
     first_new[...] = m
     second_new[...] = s
     fresh = weights[...] - 0.01 * m / (jnp.sqrt(s) + 1e-08)
     for q in range(64):
-        new[q, 0:OWN, :] = fresh
-        new[q, OWN:BLOCK, :] = line
-
-
-def lay_out(place, blocks, *refs):
-    out = refs[-1]
-    for q in range(8):
-        out[q * OWN : q * OWN + OWN, :] = blocks[q, 0:OWN, :]
-
-
-def half_weights(place, blocks, so_far, other):
-    def out_at(step, spot):
-        half = (1 - spot[0]) if other else spot[0]
-        return half * 8 + step, 0
-
-    spec = pl.BlockSpec((8, BLOCK, 128), lambda step, spot: (step, 0, 0))
+        new[q * OWN : q * OWN + OWN, :] = fresh
+
+
+def put(other, place, half, *refs):
+    out, sem = refs[-2:]
+    at = (1 - place[0]) if other else place[0]
+    copy = pltpu.make_async_copy(half, out.at[pl.ds(pl.multiple_of(at * HALF, 8), HALF)], sem)
+    copy.start()
+    copy.wait()
+
+
+def half_weights(place, half, so_far, other):
     more = [] if so_far is None else [so_far]
+    whole = pl.BlockSpec(memory_space=pl.ANY)
     return pl.pallas_call(
-        lay_out,
+        functools.partial(put, other),
         out_shape=jax.ShapeDtypeStruct((ROWS, 128), F32),
-        grid_spec=pltpu.PrefetchScalarGridSpec(
-            num_scalar_prefetch=1,
-            grid=(8,),
-            in_specs=[spec] + [pl.BlockSpec(memory_space=pl.ANY)] * len(more),
-            out_specs=pl.BlockSpec((8 * OWN, 128), out_at),
-        ),
+        in_specs=[pl.BlockSpec(memory_space=pltpu.SMEM)] + [whole] * (1 + len(more)),
+        out_specs=whole,
+        scratch_shapes=[pltpu.SemaphoreType.DMA(())],
         input_output_aliases={2: 0} if more else {},
         compiler_params=PARAMS,
-        name="lay_out_other" if other else "lay_out_own",
-    )(place, blocks, *more)
+        name="put_other" if other else "put_own",
+    )(place, half, *more)
 
 
 def per_device(
@@ -489,29 +517,27 @@
     factor = 1.0 / math.sqrt(TOK * 128)
     flat = weights.reshape(ROWS, 128)
     *pairs, bias = prepared(flat, bias_table, bias_index)
-    x_parts = halo(block_input)
-    c_parts = halo(cotangent)
-
+    edges = edges_of(block_input, cotangent)
     core = lon_at % 2
     place = jnp.stack([core, (lat_at == 7).astype(jnp.int32)]).astype(jnp.int32)
     keep, send, dscore, o_l, o_e, o_s, o_c = run_block(
-        x_parts, c_parts, pairs, bias, region_ids, place
+        (block_input, cotangent), edges, pairs, bias, region_ids, place
     )
     came = lax.ppermute(send, BOTH, core_swap())
-    line = table_gradient(dscore, bias_index)
-    line_came = lax.ppermute(line, BOTH, core_swap())
+    piece = pl.BlockSpec((HALF // 4, 128), lambda i: (i, 0))
     summed = pl.pallas_call(
         merge,
-        out_shape=jax.ShapeDtypeStruct((64, BLOCK, 128), F32),
-        in_specs=[VMEM] * 4,
-        out_specs=VMEM,
+        out_shape=jax.ShapeDtypeStruct((HALF, 128), F32),
+        grid=(4,),
+        in_specs=[piece] * 2,
+        out_specs=piece,
         compiler_params=PARAMS,
         name="merge",
-    )(keep, came, line, line_came)
-    parts = exchanged(summed, chip_groups())
-
-    _, o_e, o_s, o_c, first_moment, second_moment = lax.optimization_barrier(
-        (summed, o_e, o_s, o_c, first_moment, second_moment)
+    )(keep, came)
+    parts = exchanged(summed.reshape(64, 1, OWN * 128), chip_groups())
+
+    _, o_e, o_s, o_c, dscore, first_moment, second_moment = lax.optimization_barrier(
+        (summed, o_e, o_s, o_c, dscore, first_moment, second_moment)
     )
     from_west = around(o_e, "lon", 1)
     from_north = around(o_s, "lat", 1)
@@ -519,32 +545,37 @@
     pairs_of = worker_pairs()
     moments = jnp.stack([first_moment.reshape(OWN, 128), second_moment.reshape(OWN, 128)])
     moments = lax.ppermute(moments, BOTH, pairs_of)
-    parts, from_west, from_north, from_corner, moments = lax.optimization_barrier(
-        (parts, from_west, from_north, from_corner, moments)
+    table = butterfly(table_gradient(dscore, bias_index), 1)
+    parts, from_west, from_north, from_corner, moments, table = lax.optimization_barrier(
+        (parts, from_west, from_north, from_corner, moments, table)
     )
 
     shard = core * 64 + lat_at * 8 + lon_at // 2
     own = lax.dynamic_slice_in_dim(flat, shard * OWN, OWN, 0)
     new, first_new, second_new = pl.pallas_call(
         functools.partial(adam, factor=factor),
-        out_shape=[jax.ShapeDtypeStruct(n, F32) for n in ((64, BLOCK, 128), (OWN, 128), (OWN, 128))],
+        out_shape=[jax.ShapeDtypeStruct((n, 128), F32) for n in (HALF, OWN, OWN)],
         in_specs=[VMEM] * 4,
         out_specs=[VMEM] * 3,
         compiler_params=PARAMS,
         name="adam",
-    )(parts, own, moments[0], moments[1])
-    mine = exchanged(new, chip_groups())
+    )(parts.reshape(HALF, 128), own, moments[0], moments[1])
+    mine = exchanged(new.reshape(64, 1, OWN * 128), chip_groups())
     back = [(b, a) for a, b in pairs_of]
+    _, table, first_new, second_new = lax.optimization_barrier((new, table, first_new, second_new))
     moments = lax.ppermute(jnp.stack([first_new, second_new]), BOTH, back)
+    for bit in (2, 4, 8, 16, 32, 64):
+        table = butterfly(table, bit)
     top = jnp.concatenate([from_corner[:, :SHIFT], from_north[:, SHIFT:]], axis=1)
     rest = jnp.concatenate([from_west[SHIFT:, :SHIFT], o_l[SHIFT:, SHIFT:]], axis=1)
     grad_input = jnp.concatenate([top, rest], axis=0)
-    mine, moments = lax.optimization_barrier((mine, moments))
-
+    table_new = (table[: HEADS * 5] * factor).reshape(5, HEADS, 128).transpose(1, 0, 2)
+    table_new = table_new.reshape(HEADS, 640)[:, :BIAS]
+    mine, moments, table_new = lax.optimization_barrier((mine, moments, table_new))
+
+    mine = mine.reshape(HALF, 128)
     theirs = lax.ppermute(mine, BOTH, core_swap())
     weights_new = half_weights(place, mine, None, False)
-    table_new = mine[: HEADS * 5, OWN].reshape(5, HEADS, 128).transpose(1, 0, 2)
-    table_new = table_new.reshape(HEADS, 640)[:, :BIAS]
     weights_new = half_weights(place, theirs, weights_new, True)
     return (
         grad_input,

time: 283 us -> 526 us (1.86)
  Pallas kernels: 114 us -> 353 us
  starting transfers between devices: 47.1 us -> 69.3 us
  waiting for transfers between devices: 90.2 us -> 71.8 us
  local copies, waits for them, and re-layouts: 28.1 us -> 19.5 us
    pallas_call x3 -> x4, Pallas kernels: 19.3 us -> 260 us  [the longest x2 218 us: half_weights(): pl.pallas_call(functools.partial(put, other), out_shape=jax.ShapeDtypeStr...]
    ppermute x1 -> x7, waiting for transfers between devices: 1.07 us -> 43.1 us  [butterfly(): return value + lax.ppermute(value, BOTH, [(d, d ^ bit) for d in range(128)])]
    ppermute x1, waiting for transfers between devices: 41.8 us -> 1.86 us  [per_device(): moments = lax.ppermute(jnp.stack([first_new, second_new]), BOTH, back)]
    ppermute x3 -> x2, waiting for transfers between devices: 40.8 us -> 19.4 us  [diagonal(): lax.ppermute(value, BOTH, [(a * lon + o, (a + by) % lat * lon + (o + by)...]
    ppermute x1 -> x7, starting transfers between devices: 0.5 us -> 15.8 us  [butterfly(): return value + lax.ppermute(value, BOTH, [(d, d ^ bit) for d in range(128)])]
    ppermute x3 -> x2, starting transfers between devices: 2.73 us -> 10.5 us  [diagonal(): lax.ppermute(value, BOTH, [(a * lon + o, (a + by) % lat * lon + (o + by)...]
    slice x7 -> x0, local copies, waits for them, and re-layouts: 6.67 us -> none  [the longest x2 1.96 us: halo(): tile[:, :8]]
    ppermute x1, waiting for transfers between devices: 0.01 us -> 6.42 us  [per_device(): came = lax.ppermute(send, BOTH, core_swap())]
  transfers between devices with their start and end apart: 16 -> 19, of which waited for: 5 -> 9; matrix products, arithmetic and copies ran while one was open for 5% -> 4% of each run, Pallas kernels for 11% -> 25%
where the time goes in v3:
time: 526 us; the launch traced here: 522 us
  Pallas kernels  353 us (67%)
  waiting for transfers between devices  71.8 us (14%)
  starting transfers between devices  69.3 us (13%)
  local copies, waits for them, and re-layouts  19.5 us (4%)
  other arithmetic  6.8 us (1%)
    pallas_call x2, Pallas kernels, half_weights(): pl.pallas_call(functools.partial(put, other), out_shape=jax.ShapeDtypeStr...  218 us
    pallas_call x1, Pallas kernels, run_block(): pl.pallas_call(block_pass, out_shape=[jax.ShapeDtypeStruct(s, F32) for s...  67.4 us
    ppermute x7, waiting for transfers between devices, butterfly(): return value + lax.ppermute(value, BOTH, [(d, d ^ bit) for d in range(128)])  43.1 us
    pallas_call x1, Pallas kernels, edges_of(): pl.pallas_call(pack, out_shape=[jax.ShapeDtypeStruct(s, F32) for s in sha...  36.9 us
    all_to_all x2, starting transfers between devices, exchanged(): lax.all_to_all(value, BOTH, 0, 0, axis_index_groups=groups, tiled=True)  21.9 us
    ppermute x2, waiting for transfers between devices, diagonal(): lax.ppermute(value, BOTH, [(a * lon + o, (a + by) % lat * lon + (o + by)...  19.4 us
    ppermute x7, starting transfers between devices, butterfly(): return value + lax.ppermute(value, BOTH, [(d, d ^ bit) for d in range(128)])  15.8 us
    pallas_call x1, Pallas kernels, table_gradient(): pl.pallas_call(table_sum, out_shape=jax.ShapeDtypeStruct((64, 128), F32),...  12 us
  transfers between devices with their start and end apart: 19, of which 9 were waited for; matrix products, arithmetic and copies ran while one was open for 4% of the time, Pallas kernels for 25%

profile of v3, /device:TPU:1, one launch (start us, length us, event | category | flops | bytes accessed | tf_op | source)
XLA Modules:
  0.0 521.8 jit_solution(9357072106779372347)
XLA Ops:
  0.6 36.9 %pack.1 = (f32[2,24,8,384]{3,2,1,0:T(8,128)}, f32[2,6,24,384]{3,2,1,0:T(8,128)}, f32[2,6,8,384]{3,2,1,0:T(8,128)}) custom-call(f32[24,24,384]{2,1,0:T(8,128)} %x_l.1, f32[24,24,384]{2,1,0:T(8,128)} %c_l.1), custom_call_target="tpu_custom_call" | custom-call | tf_op jit(solution)/shard_map/pack/pallas_call | solution.py:456
  39.0 3.6 collective-permute-start.1
  42.6 5.9 %collective-permute-start.2 = (f32[2,6,8,384]{3,2,1,0:T(8,128)}, f32[2,6,8,384]{3,2,1,0:T(8,128)S(1)}, u32[]{:S(2)}, u32[]{:S(2)}) collective-permute-start(f32[2,6,8,384]{3,2,1,0:T(8,128)} %get-tuple-element.47), channel_id=1, source_target_pairs={{0,127},{1,112},{2,113},{3,114},{4,115},{5,116},{6,117},{7,118},{8... | collective-permute-start | bytes 442376 | tf_op jit(solution)/shard_map/ppermute | solution.py:428
  48.5 9.9 %prepare.1 = (bf16[384,1152]{1,0:T(8,128)(2,1)}, bf16[384,1152]{1,0:T(8,128)(2,1)}, bf16[384,384]{1,0:T(8,128)(2,1)}, bf16[384,384]{1,0:T(8,128)(2,1)}, bf16[6,3...) custom-call(f32[13824,128]{1,0:T(8,128)} %bitcast.32, ...), custom_call_target="tpu_custom_call" | custom-call | tf_op jit(solution)/shard_map/prepare/pallas_call | solution.py:124
  60.1 67.4 %block_pass.1 = (f32[6912,128]{1,0:T(8,128)}, f32[6912,128]{1,0:T(8,128)}, f32[3,576,144]{2,1,0:T(8,128)}, f32[24,24,384]{2,1,0:T(8,128)}, f32[24,8,384]{2,1,0:T...) custom-call(f32[24,24,384]{2,1,0:T(8,128)} %x_l.1, f32[24,24,384]{2,1,0:T(8,128)} %c_l.1, ...), custom_call_target="tpu_custom_call" | custom-call | tf_op jit(solution)/shard_map/block_pass/pallas_call | solution.py:349
  127.6 6.4 %collective-permute-done.3.came = f32[6912,128]{1,0:T(8,128)S(1)} collective-permute-done((f32[6912,128]{1,0:T(8,128)}, f32[6912,128]{1,0:T(8,128)S(1)}, u32[]{:S(2)}, u32[]{:S(2)}) %collective-permute-start.3) | collective-permute-done | bytes 3538976 | tf_op jit(solution)/shard_map/ppermute | solution.py:526
  135.8 5.2 %merge.1 = f32[6912,128]{1,0:T(8,128)} custom-call(f32[6912,128]{1,0:T(8,128)} %get-tuple-element.57.keep, f32[6912,128]{1,0:T(8,128)} %copy-done.2), custom_call_target="tpu_custom_call" | custom-call | tf_op jit(solution)/shard_map/merge/pallas_call | solution.py:528
  141.0 14.3 %all-to-all-start = ((f32[64,1,13824]{2,1,0:T(1,128)}), f32[64,1,13824]{2,1,0:T(1,128)S(1)}, u32[]{:S(2)}, u32[]{:S(2)}) async-start(f32[64,1,13824]{2,1,0:T(1,128)} %bitcast.41), calls=%async_computation | async-start | bytes 7077888 | tf_op jit(solution)/shard_map/all_to_all | solution.py:418
  155.3 3.2 collective-permute-start.4
  162.7 12.0 %table_sum.1 = f32[64,128]{1,0:T(8,128)} custom-call(f32[144,16,144]{2,1,0:T(8,128)} %pad.4.scores, s32[144,144]{1,0:T(8,128)} %index.3), custom_call_target="tpu_custom_call" | custom-call | tf_op jit(solution)/shard_map/table_sum/pallas_call | solution.py:390
  175.9 3.8 collective-permute-start.7
  179.7 4.6 collective-permute-start.6
  187.1 19.4 %collective-permute-done.6 = f32[6,8,384]{2,1,0:T(8,128)S(1)} collective-permute-done((f32[6,8,384]{2,1,0:T(8,128)S(1)}, f32[6,8,384]{2,1,0:T(8,128)S(1)}, u32[]{:S(2)}, u32[]{:S(2)}) %collective-permute-start.6) | collective-permute-done | bytes 73760 | tf_op jit(solution)/shard_map/ppermute | solution.py:428
  210.7 4.1 adam.1
  214.8 7.6 %all-to-all-start.1 = ((f32[64,1,13824]{2,1,0:T(1,128)}), f32[64,1,13824]{2,1,0:T(1,128)S(1)}, u32[]{:S(2)}, u32[]{:S(2)}) async-start(f32[64,1,13824]{2,1,0:T(1,128)} %bitcast.43), calls=%async_computation.1 | async-start | bytes 7077888 | tf_op jit(solution)/shard_map/all_to_all | solution.py:418
  222.4 2.6 collective-permute-start.10
  225.0 34.7 %collective-permute-done.10 = f32[64,128]{1,0:T(8,128)S(1)} collective-permute-done((f32[64,128]{1,0:T(8,128)}, f32[64,128]{1,0:T(8,128)S(1)}, u32[]{:S(2)}, u32[]{:S(2)}) %collective-permute-start.10) | collective-permute-done | bytes 32800 | tf_op jit(solution)/shard_map/ppermute | solution.py:469
  260.5 4.3 collective-permute-done.11
  264.8 6.1 %collective-permute-start.12 = (f32[64,128]{1,0:T(8,128)S(1)}, f32[64,128]{1,0:T(8,128)S(1)}, u32[]{:S(2)}, u32[]{:S(2)}) collective-permute-start(f32[64,128]{1,0:T(8,128)S(1)} %add.43), channel_id=1, source_target_pairs={{0,8},{1,9},{2,10},{3,11},{4,12},{5,13},{6,14},{7,15},{8,0},{9,1},... | collective-permute-start | bytes 98312 | tf_op jit(solution)/shard_map/ppermute | solution.py:469
  272.3 3.2 collective-permute-start.13
  276.8 2.9 collective-permute-start.14
  283.7 7.8 %collective-permute-start.9 = (f32[2,108,128]{2,1,0:T(8,128)}, f32[2,108,128]{2,1,0:T(8,128)}, u32[]{:S(2)}, u32[]{:S(2)}) collective-permute-start(f32[2,108,128]{2,1,0:T(8,128)} %pad_maximum_fusion.1), channel_id=1, source_target_pairs={{0,0},{2,1},{4,2},{6,3},{8,4},{10,5},{12,6},{14,7},{16,8},{18,9},{... | collective-permute-start | bytes 331784 | tf_op jit(solution)/shard_map/ppermute | solution.py:566
  302.2 109.0 %put_own.1.refs_0_ = f32[13824,128]{1,0:T(8,128)} custom-call(s32[2]{0:T(128)} %pad_add_fusion.place, f32[6912,128]{1,0:T(8,128)} %bitcast.40), custom_call_target="tpu_custom_call" | custom-call | tf_op jit(solution)/shard_map/put_own/pallas_call | solution.py:501
  412.7 109.0 %put_other.1 = f32[13824,128]{1,0:T(8,128)} custom-call(s32[2]{0:T(128)} %pad_add_fusion.place, f32[6912,128]{1,0:T(8,128)} %collective-permute-done.16.half, f32[13824,128]{1,0:T(8,128)} %put_own.1.refs_0_), custom_call_target="tpu_custom_call", output_to_operand_aliasing={{}: (2, {})} | custom-call | tf_op jit(solution)/shard_map/put_other/pallas_call | solution.py:501
  (71 shorter events, 37.0 us)
Async XLA Ops:
  37.5 21.5 %collective-permute-start = (f32[2,24,8,384]{3,2,1,0:T(8,128)}, f32[2,24,8,384]{3,2,1,0:T(8,128)S(1)}, u32[]{:S(2)}, u32[]{:S(2)}) collective-permute-start(f32[2,24,8,384]{3,2,1,0:T(8,128)} %get-tuple-element.45), channel_id=1, source_target_pairs={{0,15},{1,0},{2,1},{3,2},{4,3},{5,4},{6,5},{7,6},{8,7},{9,8},{10,9... | collective-permute-start | bytes 1769480 | tf_op jit(solution)/shard_map/ppermute | solution.py:423
  39.0 20.0 %collective-permute-start.1 = (f32[2,6,24,384]{3,2,1,0:T(8,128)}, f32[2,6,24,384]{3,2,1,0:T(8,128)S(1)}, u32[]{:S(2)}, u32[]{:S(2)}) collective-permute-start(f32[2,6,24,384]{3,2,1,0:T(8,128)} %get-tuple-element.46), channel_id=1, source_target_pairs={{0,112},{16,0},{32,16},{48,32},{64,48},{80,64},{96,80},{112,96},{1... | collective-permute-start | bytes 1327112 | tf_op jit(solution)/shard_map/ppermute | solution.py:423
  42.6 16.4 %collective-permute-start.2 = (f32[2,6,8,384]{3,2,1,0:T(8,128)}, f32[2,6,8,384]{3,2,1,0:T(8,128)S(1)}, u32[]{:S(2)}, u32[]{:S(2)}) collective-permute-start(f32[2,6,8,384]{3,2,1,0:T(8,128)} %get-tuple-element.47), channel_id=1, source_target_pairs={{0,127},{1,112},{2,113},{3,114},{4,115},{5,116},{6,117},{7,118},{8... | collective-permute-start | bytes 442376 | tf_op jit(solution)/shard_map/ppermute | solution.py:428
  127.5 6.5 %collective-permute-start.3 = (f32[6912,128]{1,0:T(8,128)}, f32[6912,128]{1,0:T(8,128)S(1)}, u32[]{:S(2)}, u32[]{:S(2)}) collective-permute-start(f32[6912,128]{1,0:T(8,128)} %get-tuple-element.58), channel_id=1, source_target_pairs={{0,1},{1,0},{2,3},{3,2},{4,5},{5,4},{6,7},{7,6},{8,9},{9,8},{10,11... | collective-permute-start | bytes 10616840 | tf_op jit(solution)/shard_map/ppermute | solution.py:526
  141.0 67.8 %all-to-all-start = ((f32[64,1,13824]{2,1,0:T(1,128)}), f32[64,1,13824]{2,1,0:T(1,128)S(1)}, u32[]{:S(2)}, u32[]{:S(2)}) async-start(f32[64,1,13824]{2,1,0:T(1,128)} %bitcast.41), calls=%async_computation | async-start | bytes 7077888 | tf_op jit(solution)/shard_map/all_to_all | solution.py:418
  155.3 53.6 %collective-permute-start.4 = (f32[24,8,384]{2,1,0:T(8,128)}, f32[24,8,384]{2,1,0:T(8,128)}, u32[]{:S(2)}, u32[]{:S(2)}) collective-permute-start(f32[24,8,384]{2,1,0:T(8,128)} %get-tuple-element.63), channel_id=1, source_target_pairs={{0,1},{1,2},{2,3},{3,4},{4,5},{5,6},{6,7},{7,8},{8,9},{9,10},{10,1... | collective-permute-start | bytes 884744 | tf_op jit(solution)/shard_map/ppermute | solution.py:423
  161.0 13.7 %copy-start.11 = (f32[6,24,384]{2,1,0:T(8,128)S(1)}, f32[6,24,384]{2,1,0:T(8,128)}, u32[]{:S(2)}) copy-start(f32[6,24,384]{2,1,0:T(8,128)} %get-tuple-element.64) | copy-start | bytes 663556
  161.0 14.9 %copy-start.9 = (f32[13824]{0:T(1024)S(1)}, f32[13824]{0:T(1024)}, u32[]{:S(2)}) copy-start(f32[13824]{0:T(1024)} %param.12) | copy-start | bytes 165892
  161.0 14.9 %copy-start.10 = (f32[13824]{0:T(1024)S(1)}, f32[13824]{0:T(1024)}, u32[]{:S(2)}) copy-start(f32[13824]{0:T(1024)} %param.11) | copy-start | bytes 165892
  161.0 18.7 %copy-start.12 = (f32[6,8,384]{2,1,0:T(8,128)S(1)}, f32[6,8,384]{2,1,0:T(8,128)}, u32[]{:S(2)}) copy-start(f32[6,8,384]{2,1,0:T(8,128)} %get-tuple-element.65) | copy-start | bytes 221188
  174.7 11.1 %collective-permute-start.8 = (f32[64,128]{1,0:T(8,128)}, f32[64,128]{1,0:T(8,128)S(1)}, u32[]{:S(2)}, u32[]{:S(2)}) collective-permute-start(f32[64,128]{1,0:T(8,128)} %table_sum.1), channel_id=1, source_target_pairs={{0,1},{1,0},{2,3},{3,2},{4,5},{5,4},{6,7},{7,6},{8,9},{9,8},{10,11... | collective-permute-start | bytes 98312 | tf_op jit(solution)/shard_map/ppermute | solution.py:469
  174.7 32.8 %collective-permute-start.5 = (f32[6,24,384]{2,1,0:T(8,128)S(1)}, f32[6,24,384]{2,1,0:T(8,128)S(1)}, u32[]{:S(2)}, u32[]{:S(2)}) collective-permute-start(f32[6,24,384]{2,1,0:T(8,128)S(1)} %copy-done.11), channel_id=1, source_target_pairs={{0,16},{16,32},{32,48},{48,64},{64,80},{80,96},{96,112},{112,0},{1... | collective-permute-start | bytes 663560 | tf_op jit(solution)/shard_map/ppermute | solution.py:423
  175.9 31.6 %collective-permute-start.7 = (f32[2,108,128]{2,1,0:T(8,128)S(1)}, f32[2,108,128]{2,1,0:T(8,128)S(1)}, u32[]{:S(2)}, u32[]{:S(2)}) collective-permute-start(f32[2,108,128]{2,1,0:T(8,128)S(1)} %pad_maximum_fusion), channel_id=1, source_target_pairs={{0,0},{1,2},{2,4},{3,6},{4,8},{5,10},{6,12},{7,14},{8,16},{9,18},{... | collective-permute-start | bytes 331784 | tf_op jit(solution)/shard_map/ppermute | solution.py:547
  179.7 26.9 %collective-permute-start.6 = (f32[6,8,384]{2,1,0:T(8,128)S(1)}, f32[6,8,384]{2,1,0:T(8,128)S(1)}, u32[]{:S(2)}, u32[]{:S(2)}) collective-permute-start(f32[6,8,384]{2,1,0:T(8,128)S(1)} %copy-done.12), channel_id=1, source_target_pairs={{0,17},{1,18},{2,19},{3,20},{4,21},{5,22},{6,23},{7,24},{8,25},{9,... | collective-permute-start | bytes 221192 | tf_op jit(solution)/shard_map/ppermute | solution.py:428
  214.8 82.0 %all-to-all-start.1 = ((f32[64,1,13824]{2,1,0:T(1,128)}), f32[64,1,13824]{2,1,0:T(1,128)S(1)}, u32[]{:S(2)}, u32[]{:S(2)}) async-start(f32[64,1,13824]{2,1,0:T(1,128)} %bitcast.43), calls=%async_computation.1 | async-start | bytes 7077888 | tf_op jit(solution)/shard_map/all_to_all | solution.py:418
  222.4 37.3 %collective-permute-start.10 = (f32[64,128]{1,0:T(8,128)}, f32[64,128]{1,0:T(8,128)S(1)}, u32[]{:S(2)}, u32[]{:S(2)}) collective-permute-start(f32[64,128]{1,0:T(8,128)} %add.38), channel_id=1, source_target_pairs={{0,2},{1,3},{2,0},{3,1},{4,6},{5,7},{6,4},{7,5},{8,10},{9,11},{10,... | collective-permute-start | bytes 98312 | tf_op jit(solution)/shard_map/ppermute | solution.py:469
  260.5 4.3 collective-permute-start.11
  264.8 7.5 %collective-permute-start.12 = (f32[64,128]{1,0:T(8,128)S(1)}, f32[64,128]{1,0:T(8,128)S(1)}, u32[]{:S(2)}, u32[]{:S(2)}) collective-permute-start(f32[64,128]{1,0:T(8,128)S(1)} %add.43), channel_id=1, source_target_pairs={{0,8},{1,9},{2,10},{3,11},{4,12},{5,13},{6,14},{7,15},{8,0},{9,1},... | collective-permute-start | bytes 98312 | tf_op jit(solution)/shard_map/ppermute | solution.py:469
  272.3 4.5 collective-permute-start.13
  276.8 4.3 collective-permute-start.14
  281.1 10.3 %collective-permute-start.15 = (f32[64,128]{1,0:T(8,128)S(1)}, f32[64,128]{1,0:T(8,128)S(1)}, u32[]{:S(2)}, u32[]{:S(2)}) collective-permute-start(f32[64,128]{1,0:T(8,128)S(1)} %add.46), channel_id=1, source_target_pairs={{0,64},{1,65},{2,66},{3,67},{4,68},{5,69},{6,70},{7,71},{8,72},{9,... | collective-permute-start | bytes 98312 | tf_op jit(solution)/shard_map/ppermute | solution.py:469
  283.7 13.1 %collective-permute-start.9 = (f32[2,108,128]{2,1,0:T(8,128)}, f32[2,108,128]{2,1,0:T(8,128)}, u32[]{:S(2)}, u32[]{:S(2)}) collective-permute-start(f32[2,108,128]{2,1,0:T(8,128)} %pad_maximum_fusion.1), channel_id=1, source_target_pairs={{0,0},{2,1},{4,2},{6,3},{8,4},{10,5},{12,6},{14,7},{16,8},{18,9},{... | collective-permute-start | bytes 331784 | tf_op jit(solution)/shard_map/ppermute | solution.py:566
  296.8 5.4 %copy-start.1 = (f32[64,1,13824]{2,1,0:T(1,128)}, f32[64,1,13824]{2,1,0:T(1,128)S(1)}, u32[]{:S(2)}) copy-start(f32[64,1,13824]{2,1,0:T(1,128)S(1)} %all-to-all-done.1) | copy-start | bytes 10616836
  296.8 115.9 %collective-permute-start.16 = (f32[6912,128]{1,0:T(8,128)S(1)}, f32[6912,128]{1,0:T(8,128)}, u32[]{:S(2)}, u32[]{:S(2)}) collective-permute-start(f32[6912,128]{1,0:T(8,128)S(1)} %bitcast.39), channel_id=1, source_target_pairs={{0,1},{1,0},{2,3},{3,2},{4,5},{5,4},{6,7},{7,6},{8,9},{9,8},{10,11... | collective-permute-start | bytes 10616840 | tf_op jit(solution)/shard_map/ppermute | solution.py:577
  (8 other events, 8.4 us)

commit v4 on v3

--- a/solution.py
+++ b/solution.py
@@ -30,6 +30,8 @@
 CHUNKS = FF // CHUNK
 HALF = ROWS // 2
 OWN = ROWS // 128
+BLOCK = OWN + 1
+BATCH = 16
 BIAS = 529
 BOTH = ("lat", "lon")
 F32 = jnp.float32
@@ -436,78 +438,115 @@
     )
 
 
-def pack(x, c, east, south, corner, sems):
-    copies = []
-    for i, tile in enumerate((x, c)):
-        for j, (rows, cols, out) in enumerate(
-            ((TILE, 8, east), (SHIFT, TILE, south), (SHIFT, 8, corner))
-        ):
-            source = tile.at[pl.ds(0, rows), pl.ds(0, cols)]
-            copies.append(pltpu.make_async_copy(source, out.at[i], sems.at[3 * i + j]))
-    for copy in copies:
-        copy.start()
-    for copy in copies:
-        copy.wait()
+def pack(x_east, x_south, c_east, c_south, east, south, corner):
+    for i, (e, t) in enumerate(((x_east, x_south), (c_east, c_south))):
+        east[i] = e[...]
+        south[i] = t[...]
+        corner[i] = t[:, 0:8, :]
 
 
 def edges_of(x, c):
-    whole = pl.BlockSpec(memory_space=pl.ANY)
+    east_in = pl.BlockSpec((TILE, 8, D), lambda i: (0, 0, 0))
+    south_in = pl.BlockSpec((SHIFT, TILE, D), lambda i: (0, 0, 0))
     shapes = [(2, TILE, 8, D), (2, SHIFT, TILE, D), (2, SHIFT, 8, D)]
     east, south, corner = pl.pallas_call(
         pack,
         out_shape=[jax.ShapeDtypeStruct(s, F32) for s in shapes],
-        in_specs=[whole] * 2,
-        out_specs=[whole] * 3,
-        scratch_shapes=[pltpu.SemaphoreType.DMA((6,))],
+        grid=(1,),
+        in_specs=[east_in, south_in] * 2,
+        out_specs=[pl.BlockSpec(s, lambda i: (0, 0, 0, 0)) for s in shapes],
         compiler_params=PARAMS,
         name="pack",
-    )(x, c)
+    )(x, x, c, c)
     return around(east, "lon", -1), around(south, "lat", -1), diagonal(corner, -1)
 
 
-def butterfly(value, bit):
-    return value + lax.ppermute(value, BOTH, [(d, d ^ bit) for d in range(128)])
-
-
-def merge(keep, came, out):
-    out[...] = keep[...] + came[...]
+def merge(keep, came, line, line_came, out):
+    for q in range(BATCH):
+        rows = slice(q * OWN, q * OWN + OWN)
+        out[q * BLOCK : q * BLOCK + OWN, :] = keep[rows, :] + came[rows, :]
+        out[q * BLOCK + OWN : (q + 1) * BLOCK, :] = line[q : q + 1, :] + line_came[q : q + 1, :]
+
+
+def merged(keep, came, line, line_came):
+    halves = pl.BlockSpec((BATCH * OWN, 128), lambda i: (i, 0))
+    lines = pl.BlockSpec((BATCH, 128), lambda i: (i, 0))
+    return pl.pallas_call(
+        merge,
+        out_shape=jax.ShapeDtypeStruct((64 * BLOCK, 128), F32),
+        grid=(64 // BATCH,),
+        in_specs=[halves, halves, lines, lines],
+        out_specs=pl.BlockSpec((BATCH * BLOCK, 128), lambda i: (i, 0)),
+        compiler_params=PARAMS,
+        name="merge",
+    )(keep, came, line, line_came)
 
 
 def adam(parts, weights, first, second, new, first_new, second_new, factor):
-    grad = parts[0:OWN, :]
+    total = parts[0:BLOCK, :]
     for q in range(1, 64):
-        grad = grad + parts[q * OWN : q * OWN + OWN, :]
-    grad = grad * factor
+        total = total + parts[q * BLOCK : q * BLOCK + BLOCK, :]
+    total = total * factor
+    grad, line = total[:OWN], total[OWN:]
     m = 0.9 * first[...] + 0.1 * grad
     s = 0.95 * second[...] + 0.05 * grad * grad
     first_new[...] = m
     second_new[...] = s
     fresh = weights[...] - 0.01 * m / (jnp.sqrt(s) + 1e-08)
+    fresh = jnp.concatenate([fresh, line], axis=0)
     for q in range(64):
-        new[q * OWN : q * OWN + OWN, :] = fresh
-
-
-def put(other, place, half, *refs):
-    out, sem = refs[-2:]
-    at = (1 - place[0]) if other else place[0]
-    copy = pltpu.make_async_copy(half, out.at[pl.ds(pl.multiple_of(at * HALF, 8), HALF)], sem)
-    copy.start()
-    copy.wait()
-
-
-def half_weights(place, half, so_far, other):
-    more = [] if so_far is None else [so_far]
-    whole = pl.BlockSpec(memory_space=pl.ANY)
+        new[q * BLOCK : q * BLOCK + BLOCK, :] = fresh
+
+
+def lay_out(place, blocks, *refs):
+    out = refs[-1]
+    for q in range(BATCH):
+        out[q * OWN : q * OWN + OWN, :] = blocks[q * BLOCK : q * BLOCK + OWN, :]
+
+
+def lay_out_own(place, blocks, out, lines):
+    lay_out(place, blocks, out)
+    for q in range(BATCH):
+        lines[q : q + 1, :] = blocks[q * BLOCK + OWN : q * BLOCK + BLOCK, :]
+
+
+def own_half(place, blocks):
+    steps = 64 // BATCH
     return pl.pallas_call(
-        functools.partial(put, other),
+        lay_out_own,
+        out_shape=[jax.ShapeDtypeStruct((ROWS, 128), F32), jax.ShapeDtypeStruct((64, 128), F32)],
+        grid_spec=pltpu.PrefetchScalarGridSpec(
+            num_scalar_prefetch=1,
+            grid=(steps,),
+            in_specs=[pl.BlockSpec((BATCH * BLOCK, 128), lambda i, spot: (i, 0))],
+            out_specs=[
+                pl.BlockSpec((BATCH * OWN, 128), lambda i, spot: (spot[0] * steps + i, 0)),
+                pl.BlockSpec((BATCH, 128), lambda i, spot: (i, 0)),
+            ],
+        ),
+        compiler_params=PARAMS,
+        name="lay_out_own",
+    )(place, blocks)
+
+
+def other_half(place, blocks, so_far):
+    steps = 64 // BATCH
+    return pl.pallas_call(
+        lay_out,
         out_shape=jax.ShapeDtypeStruct((ROWS, 128), F32),
-        in_specs=[pl.BlockSpec(memory_space=pltpu.SMEM)] + [whole] * (1 + len(more)),
-        out_specs=whole,
-        scratch_shapes=[pltpu.SemaphoreType.DMA(())],
-        input_output_aliases={2: 0} if more else {},
-        compiler_params=PARAMS,
-        name="put_other" if other else "put_own",
-    )(place, half, *more)
+        grid_spec=pltpu.PrefetchScalarGridSpec(
+            num_scalar_prefetch=1,
+            grid=(steps,),
+            in_specs=[
+                pl.BlockSpec((BATCH * BLOCK, 128), lambda i, spot: (i, 0)),
+                pl.BlockSpec(memory_space=pl.ANY),
+            ],
+            out_specs=pl.BlockSpec((BATCH * OWN, 128), lambda i, spot: ((1 - spot[0]) * steps + i, 0)),
+        ),
+        input_output_aliases={2: 0},
+        compiler_params=PARAMS,
+        name="lay_out_other",
+    )(place, blocks, so_far)
 
 
 def per_device(
@@ -524,20 +563,13 @@
         (block_input, cotangent), edges, pairs, bias, region_ids, place
     )
     came = lax.ppermute(send, BOTH, core_swap())
-    piece = pl.BlockSpec((HALF // 4, 128), lambda i: (i, 0))
-    summed = pl.pallas_call(
-        merge,
-        out_shape=jax.ShapeDtypeStruct((HALF, 128), F32),
-        grid=(4,),
-        in_specs=[piece] * 2,
-        out_specs=piece,
-        compiler_params=PARAMS,
-        name="merge",
-    )(keep, came)
-    parts = exchanged(summed.reshape(64, 1, OWN * 128), chip_groups())
-
-    _, o_e, o_s, o_c, dscore, first_moment, second_moment = lax.optimization_barrier(
-        (summed, o_e, o_s, o_c, dscore, first_moment, second_moment)
+    line = table_gradient(dscore, bias_index)
+    line_came = lax.ppermute(line, BOTH, core_swap())
+    summed = merged(keep, came, line, line_came)
+    parts = exchanged(summed.reshape(64, 1, BLOCK * 128), chip_groups())
+
+    _, o_e, o_s, o_c, first_moment, second_moment = lax.optimization_barrier(
+        (summed, o_e, o_s, o_c, first_moment, second_moment)
     )
     from_west = around(o_e, "lon", 1)
     from_north = around(o_s, "lat", 1)
@@ -545,38 +577,34 @@
     pairs_of = worker_pairs()
     moments = jnp.stack([first_moment.reshape(OWN, 128), second_moment.reshape(OWN, 128)])
     moments = lax.ppermute(moments, BOTH, pairs_of)
-    table = butterfly(table_gradient(dscore, bias_index), 1)
-    parts, from_west, from_north, from_corner, moments, table = lax.optimization_barrier(
-        (parts, from_west, from_north, from_corner, moments, table)
+    parts, from_west, from_north, from_corner, moments = lax.optimization_barrier(
+        (parts, from_west, from_north, from_corner, moments)
     )
 
     shard = core * 64 + lat_at * 8 + lon_at // 2
     own = lax.dynamic_slice_in_dim(flat, shard * OWN, OWN, 0)
     new, first_new, second_new = pl.pallas_call(
         functools.partial(adam, factor=factor),
-        out_shape=[jax.ShapeDtypeStruct((n, 128), F32) for n in (HALF, OWN, OWN)],
+        out_shape=[jax.ShapeDtypeStruct((n, 128), F32) for n in (64 * BLOCK, OWN, OWN)],
         in_specs=[VMEM] * 4,
         out_specs=[VMEM] * 3,
         compiler_params=PARAMS,
         name="adam",
-    )(parts.reshape(HALF, 128), own, moments[0], moments[1])
-    mine = exchanged(new.reshape(64, 1, OWN * 128), chip_groups())
+    )(parts.reshape(64 * BLOCK, 128), own, moments[0], moments[1])
+    mine = exchanged(new.reshape(64, 1, BLOCK * 128), chip_groups())
     back = [(b, a) for a, b in pairs_of]
-    _, table, first_new, second_new = lax.optimization_barrier((new, table, first_new, second_new))
     moments = lax.ppermute(jnp.stack([first_new, second_new]), BOTH, back)
-    for bit in (2, 4, 8, 16, 32, 64):
-        table = butterfly(table, bit)
     top = jnp.concatenate([from_corner[:, :SHIFT], from_north[:, SHIFT:]], axis=1)
     rest = jnp.concatenate([from_west[SHIFT:, :SHIFT], o_l[SHIFT:, SHIFT:]], axis=1)
     grad_input = jnp.concatenate([top, rest], axis=0)
-    table_new = (table[: HEADS * 5] * factor).reshape(5, HEADS, 128).transpose(1, 0, 2)
+    mine, moments, grad_input = lax.optimization_barrier((mine, moments, grad_input))
+
+    mine = mine.reshape(64 * BLOCK, 128)
+    theirs = lax.ppermute(mine, BOTH, core_swap())
+    weights_new, table = own_half(place, mine)
+    table_new = table[: HEADS * 5].reshape(5, HEADS, 128).transpose(1, 0, 2)
     table_new = table_new.reshape(HEADS, 640)[:, :BIAS]
-    mine, moments, table_new = lax.optimization_barrier((mine, moments, table_new))
-
-    mine = mine.reshape(HALF, 128)
-    theirs = lax.ppermute(mine, BOTH, core_swap())
-    weights_new = half_weights(place, mine, None, False)
-    weights_new = half_weights(place, theirs, weights_new, True)
+    weights_new = other_half(place, theirs, weights_new)
     return (
         grad_input,
         weights_new.reshape(-1),

time: 526 us -> 259 us (0.49)
  Pallas kernels: 353 us -> 111 us
  starting transfers between devices: 69.3 us -> 51.4 us
  waiting for transfers between devices: 71.8 us -> 82.2 us
  local copies, waits for them, and re-layouts: 19.5 us -> 11.3 us
    pallas_call x3, Pallas kernels: 223 us -> 15.4 us  [the longest x1 5.28 us: merged(): pl.pallas_call(merge, out_shape=jax.ShapeDtypeStruct((64 * BLOCK, 128), F...]
    ppermute x7 -> x1, waiting for transfers between devices: 43.1 us -> 1.07 us  [per_device(): line_came = lax.ppermute(line, BOTH, core_swap())]
    ppermute x1, waiting for transfers between devices: 1.86 us -> 41.2 us  [per_device(): moments = lax.ppermute(jnp.stack([first_new, second_new]), BOTH, back)]
    pallas_call x1, Pallas kernels: 36.9 us -> 2.29 us  [edges_of(): pl.pallas_call(pack, out_shape=[jax.ShapeDtypeStruct(s, F32) for s in sha...]
    ppermute x2, waiting for transfers between devices: 19.4 us -> 39.9 us  [diagonal(): lax.ppermute(value, BOTH, [(a * lon + o, (a + by) % lat * lon + (o + by)...]
    ppermute x7 -> x1, starting transfers between devices: 15.8 us -> 0.5 us  [per_device(): line_came = lax.ppermute(line, BOTH, core_swap())]
    ppermute x1, waiting for transfers between devices: 6.42 us -> 0.01 us  [per_device(): came = lax.ppermute(send, BOTH, core_swap())]
  transfers between devices with their start and end apart: 19 -> 13, of which waited for: 9 -> 3; matrix products, arithmetic and copies ran while one was open for 4% -> 4% of each run, Pallas kernels for 25% -> 10%
where the time goes in v4:
time: 259 us; the launch traced here: 258 us
  Pallas kernels  111 us (43%)
  waiting for transfers between devices  82.2 us (32%)
  starting transfers between devices  51.4 us (20%)
  local copies, waits for them, and re-layouts  11.3 us (4%)
    pallas_call x1, Pallas kernels, run_block(): pl.pallas_call(block_pass, out_shape=[jax.ShapeDtypeStruct(s, F32) for s...  67.3 us
    ppermute x1, waiting for transfers between devices, per_device(): moments = lax.ppermute(jnp.stack([first_new, second_new]), BOTH, back)  41.2 us
    ppermute x2, waiting for transfers between devices, diagonal(): lax.ppermute(value, BOTH, [(a * lon + o, (a + by) % lat * lon + (o + by)...  39.9 us
    all_to_all x2, starting transfers between devices, exchanged(): lax.all_to_all(value, BOTH, 0, 0, axis_index_groups=groups, tiled=True)  22.7 us
    pallas_call x1, Pallas kernels, table_gradient(): pl.pallas_call(table_sum, out_shape=jax.ShapeDtypeStruct((64, 128), F32),...  12 us
    pallas_call x1, Pallas kernels, prepared(): pl.pallas_call(prepare, out_shape=[jax.ShapeDtypeStruct(s, BF16) for s in...  9.89 us
    ppermute x4, starting transfers between devices, around(): lax.ppermute(value, axis, [(i, (i + by) % size) for i in range(size)])  9.49 us
    ppermute x2, starting transfers between devices, diagonal(): lax.ppermute(value, BOTH, [(a * lon + o, (a + by) % lat * lon + (o + by)...  9.01 us
  transfers between devices with their start and end apart: 13, of which 3 were waited for; matrix products, arithmetic and copies ran while one was open for 4% of the time, Pallas kernels for 10%

profile of v4, /device:TPU:1, one launch (start us, length us, event | category | flops | bytes accessed | tf_op | source)
XLA Modules:
  0.0 258.5 jit_solution(910590244096910952)
XLA Ops:
  0.6 2.3 pack.1
  2.9 1.4 collective-permute-start
  4.3 3.6 %collective-permute-start.1 = (f32[2,6,24,384]{3,2,1,0:T(8,128)}, f32[2,6,24,384]{3,2,1,0:T(8,128)S(1)}, u32[]{:S(2)}, u32[]{:S(2)}) collective-permute-start(f32[2,6,24,384]{3,2,1,0:T(8,128)} %get-tuple-element.43), channel_id=1, source_target_pairs={{0,112},{16,0},{32,16},{48,32},{64,48},{80,64},{96,80},{112,96},{1... | collective-permute-start | bytes 1327112 | tf_op jit(solution)/shard_map/ppermute | solution.py:425
  7.9 5.9 %collective-permute-start.2 = (f32[2,6,8,384]{3,2,1,0:T(8,128)}, f32[2,6,8,384]{3,2,1,0:T(8,128)S(1)}, u32[]{:S(2)}, u32[]{:S(2)}) collective-permute-start(f32[2,6,8,384]{3,2,1,0:T(8,128)} %get-tuple-element.44), channel_id=1, source_target_pairs={{0,127},{1,112},{2,113},{3,114},{4,115},{5,116},{6,117},{7,118},{8... | collective-permute-start | bytes 442376 | tf_op jit(solution)/shard_map/ppermute | solution.py:430
  13.8 9.9 %prepare.1 = (bf16[384,1152]{1,0:T(8,128)(2,1)}, bf16[384,1152]{1,0:T(8,128)(2,1)}, bf16[384,384]{1,0:T(8,128)(2,1)}, bf16[384,384]{1,0:T(8,128)(2,1)}, bf16[6,3...) custom-call(f32[13824,128]{1,0:T(8,128)} %bitcast.33, ...), custom_call_target="tpu_custom_call" | custom-call | tf_op jit(solution)/shard_map/prepare/pallas_call | solution.py:126
  25.3 67.3 %block_pass.1 = (f32[6912,128]{1,0:T(8,128)}, f32[6912,128]{1,0:T(8,128)}, f32[3,576,144]{2,1,0:T(8,128)}, f32[24,24,384]{2,1,0:T(8,128)}, f32[24,8,384]{2,1,0:T...) custom-call(f32[24,24,384]{2,1,0:T(8,128)} %x_l.1, f32[24,24,384]{2,1,0:T(8,128)} %c_l.1, ...), custom_call_target="tpu_custom_call" | custom-call | tf_op jit(solution)/shard_map/block_pass/pallas_call | solution.py:351
  92.8 2.5 copy.24
  95.3 1.7 pad.4.scores
  97.0 12.0 %table_sum.1.line = f32[64,128]{1,0:T(8,128)} custom-call(f32[144,16,144]{2,1,0:T(8,128)} %pad.4.scores, s32[144,144]{1,0:T(8,128)} %index.3), custom_call_target="tpu_custom_call" | custom-call | tf_op jit(solution)/shard_map/table_sum/pallas_call | solution.py:392
  111.2 1.2 copy-done
  112.4 5.3 %merge.1 = f32[6976,128]{1,0:T(8,128)} custom-call(f32[6912,128]{1,0:T(8,128)} %get-tuple-element.54.keep, f32[6912,128]{1,0:T(8,128)} %copy-done, f32[64,128]{1,0:T(8,128)} %table_sum.1.line, f32[64,128]{1,0:T(8,128)} %copy-done.9), custom_call_target="tpu_custom_call" | custom-call | tf_op jit(solution)/shard_map/merge/pallas_call | solution.py:474
  117.7 14.7 %all-to-all-start = ((f32[64,1,13952]{2,1,0:T(1,128)}), f32[64,1,13952]{2,1,0:T(1,128)}, u32[]{:S(2)}, u32[]{:S(2)}) async-start(f32[64,1,13952]{2,1,0:T(1,128)} %bitcast.38), calls=%async_computation | async-start | bytes 7143424 | tf_op jit(solution)/shard_map/all_to_all | solution.py:420
  132.4 3.3 %collective-permute-start.5 = (f32[24,8,384]{2,1,0:T(8,128)S(1)}, f32[24,8,384]{2,1,0:T(8,128)S(1)}, u32[]{:S(2)}, u32[]{:S(2)}) collective-permute-start(f32[24,8,384]{2,1,0:T(8,128)S(1)} %copy-done.10), channel_id=1, source_target_pairs={{0,1},{1,2},{2,3},{3,4},{4,5},{5,6},{6,7},{7,8},{8,9},{9,10},{10,1... | collective-permute-start | bytes 884744 | tf_op jit(solution)/shard_map/ppermute | solution.py:425
  136.9 2.3 collective-permute-start.8
  139.2 3.1 %collective-permute-start.7 = (f32[6,8,384]{2,1,0:T(8,128)S(1)}, f32[6,8,384]{2,1,0:T(8,128)S(1)}, u32[]{:S(2)}, u32[]{:S(2)}) collective-permute-start(f32[6,8,384]{2,1,0:T(8,128)S(1)} %copy-done.12), channel_id=1, source_target_pairs={{0,17},{1,18},{2,19},{3,20},{4,21},{5,22},{6,23},{7,24},{8,25},{9,... | collective-permute-start | bytes 221192 | tf_op jit(solution)/shard_map/ppermute | solution.py:430
  142.3 1.5 constant_dynamic-slice_fusion.weights
  143.8 39.9 %collective-permute-done.7 = f32[6,8,384]{2,1,0:T(8,128)S(1)} collective-permute-done((f32[6,8,384]{2,1,0:T(8,128)S(1)}, f32[6,8,384]{2,1,0:T(8,128)S(1)}, u32[]{:S(2)}, u32[]{:S(2)}) %collective-permute-start.7) | collective-permute-done | bytes 73760 | tf_op jit(solution)/shard_map/ppermute | solution.py:430
  184.3 4.2 %adam.1 = (f32[6976,128]{1,0:T(8,128)}, f32[108,128]{1,0:T(8,128)}, f32[108,128]{1,0:T(8,128)}) custom-call(f32[6976,128]{1,0:T(8,128)} %bitcast.8.parts, f32[108,128]{1,0:T(8,128)} %constant_dynamic-slice_fusion.weights, f32[108,128]{1,0:T(8,128)} %get-tuple-element.82.first, f32[108,128]{1,0:T(8,128)} %get-tuple-element.81.second), custom_call_target="tpu_custom_call" | custom-call | tf_op jit(solution)/shard_map/adam/pallas_call | solution.py:586
  188.5 8.0 %all-to-all-start.1 = ((f32[64,1,13952]{2,1,0:T(1,128)}), f32[64,1,13952]{2,1,0:T(1,128)}, u32[]{:S(2)}, u32[]{:S(2)}) async-start(f32[64,1,13952]{2,1,0:T(1,128)} %bitcast.41), calls=%async_computation.1 | async-start | bytes 7143424 | tf_op jit(solution)/shard_map/all_to_all | solution.py:420
  196.7 5.4 %collective-permute-start.9 = (f32[2,108,128]{2,1,0:T(8,128)S(1)}, f32[2,108,128]{2,1,0:T(8,128)S(1)}, u32[]{:S(2)}, u32[]{:S(2)}) collective-permute-start(f32[2,108,128]{2,1,0:T(8,128)S(1)} %pad_maximum_fusion.1), channel_id=1, source_target_pairs={{0,0},{2,1},{4,2},{6,3},{8,4},{10,5},{12,6},{14,7},{16,8},{18,9},{... | collective-permute-start | bytes 331784 | tf_op jit(solution)/shard_map/ppermute | solution.py:596
  203.1 41.2 %collective-permute-done.9 = f32[2,108,128]{2,1,0:T(8,128)S(1)} collective-permute-done((f32[2,108,128]{2,1,0:T(8,128)S(1)}, f32[2,108,128]{2,1,0:T(8,128)S(1)}, u32[]{:S(2)}, u32[]{:S(2)}) %collective-permute-start.9) | collective-permute-done | bytes 110624 | tf_op jit(solution)/shard_map/ppermute | solution.py:596
  244.3 2.0 collective-permute-start.10
  246.3 5.1 %lay_out_own.1 = (f32[13824,128]{1,0:T(8,128)}, f32[64,128]{1,0:T(8,128)}) custom-call(s32[2]{0:T(128)} %pad_add_fusion.place, f32[6976,128]{1,0:T(8,128)} %bitcast.14.blocks), custom_call_target="tpu_custom_call" | custom-call | tf_op jit(solution)/shard_map/lay_out_own/pallas_call | solution.py:515
  253.5 5.0 %lay_out_other.1 = f32[13824,128]{1,0:T(8,128)} custom-call(s32[2]{0:T(128)} %pad_add_fusion.place, f32[6976,128]{1,0:T(8,128)} %collective-permute-done.10.blocks, f32[13824,128]{1,0:T(8,128)} %get-tuple-element.76.refs_0_), custom_call_target="tpu_custom_call", output_to_operand_aliasing={{}: (2, {})} | custom-call | tf_op jit(solution)/shard_map/lay_out_other/pallas_call | solution.py:534
  (52 shorter events, 8.9 us)
Async XLA Ops:
  2.9 21.4 %collective-permute-start = (f32[2,24,8,384]{3,2,1,0:T(8,128)}, f32[2,24,8,384]{3,2,1,0:T(8,128)S(1)}, u32[]{:S(2)}, u32[]{:S(2)}) collective-permute-start(f32[2,24,8,384]{3,2,1,0:T(8,128)} %get-tuple-element.42), channel_id=1, source_target_pairs={{0,15},{1,0},{2,1},{3,2},{4,3},{5,4},{6,5},{7,6},{8,7},{9,8},{10,9... | collective-permute-start | bytes 1769480 | tf_op jit(solution)/shard_map/ppermute | solution.py:425
  4.3 20.0 %collective-permute-start.1 = (f32[2,6,24,384]{3,2,1,0:T(8,128)}, f32[2,6,24,384]{3,2,1,0:T(8,128)S(1)}, u32[]{:S(2)}, u32[]{:S(2)}) collective-permute-start(f32[2,6,24,384]{3,2,1,0:T(8,128)} %get-tuple-element.43), channel_id=1, source_target_pairs={{0,112},{16,0},{32,16},{48,32},{64,48},{80,64},{96,80},{112,96},{1... | collective-permute-start | bytes 1327112 | tf_op jit(solution)/shard_map/ppermute | solution.py:425
  7.9 16.4 %collective-permute-start.2 = (f32[2,6,8,384]{3,2,1,0:T(8,128)}, f32[2,6,8,384]{3,2,1,0:T(8,128)S(1)}, u32[]{:S(2)}, u32[]{:S(2)}) collective-permute-start(f32[2,6,8,384]{3,2,1,0:T(8,128)} %get-tuple-element.44), channel_id=1, source_target_pairs={{0,127},{1,112},{2,113},{3,114},{4,115},{5,116},{6,117},{7,118},{8... | collective-permute-start | bytes 442376 | tf_op jit(solution)/shard_map/ppermute | solution.py:430
  24.3 0.8 copy-start.3
  24.3 1.0 copy-start.1
  92.7 17.9 %collective-permute-start.3 = (f32[6912,128]{1,0:T(8,128)}, f32[6912,128]{1,0:T(8,128)S(1)}, u32[]{:S(2)}, u32[]{:S(2)}) collective-permute-start(f32[6912,128]{1,0:T(8,128)} %get-tuple-element.55), channel_id=1, source_target_pairs={{0,1},{1,0},{2,3},{3,2},{4,5},{5,4},{6,7},{7,6},{8,9},{9,8},{10,11... | collective-permute-start | bytes 10616840 | tf_op jit(solution)/shard_map/ppermute | solution.py:565
  109.0 1.6 collective-permute-start.4
  110.6 1.8 copy-start
  117.6 14.7 %copy-start.10 = (f32[24,8,384]{2,1,0:T(8,128)S(1)}, f32[24,8,384]{2,1,0:T(8,128)}, u32[]{:S(2)}) copy-start(f32[24,8,384]{2,1,0:T(8,128)} %get-tuple-element.60) | copy-start | bytes 884740
  117.7 18.1 %copy-start.11 = (f32[6,24,384]{2,1,0:T(8,128)S(1)}, f32[6,24,384]{2,1,0:T(8,128)}, u32[]{:S(2)}) copy-start(f32[6,24,384]{2,1,0:T(8,128)} %get-tuple-element.61) | copy-start | bytes 663556
  117.7 19.2 %copy-start.5 = (f32[13824]{0:T(1024)S(1)}, f32[13824]{0:T(1024)}, u32[]{:S(2)}) copy-start(f32[13824]{0:T(1024)} %param.12) | copy-start | bytes 165892
  117.7 19.2 %copy-start.6 = (f32[13824]{0:T(1024)S(1)}, f32[13824]{0:T(1024)}, u32[]{:S(2)}) copy-start(f32[13824]{0:T(1024)} %param.11) | copy-start | bytes 165892
  117.7 21.6 %copy-start.12 = (f32[6,8,384]{2,1,0:T(8,128)S(1)}, f32[6,8,384]{2,1,0:T(8,128)}, u32[]{:S(2)}) copy-start(f32[6,8,384]{2,1,0:T(8,128)} %get-tuple-element.62) | copy-start | bytes 221188
  117.7 66.0 %all-to-all-start = ((f32[64,1,13952]{2,1,0:T(1,128)}), f32[64,1,13952]{2,1,0:T(1,128)}, u32[]{:S(2)}, u32[]{:S(2)}) async-start(f32[64,1,13952]{2,1,0:T(1,128)} %bitcast.38), calls=%async_computation | async-start | bytes 7143424 | tf_op jit(solution)/shard_map/all_to_all | solution.py:420
  132.4 51.3 %collective-permute-start.5 = (f32[24,8,384]{2,1,0:T(8,128)S(1)}, f32[24,8,384]{2,1,0:T(8,128)S(1)}, u32[]{:S(2)}, u32[]{:S(2)}) collective-permute-start(f32[24,8,384]{2,1,0:T(8,128)S(1)} %copy-done.10), channel_id=1, source_target_pairs={{0,1},{1,2},{2,3},{3,4},{4,5},{5,6},{6,7},{7,8},{8,9},{9,10},{10,1... | collective-permute-start | bytes 884744 | tf_op jit(solution)/shard_map/ppermute | solution.py:425
  135.7 48.0 %collective-permute-start.6 = (f32[6,24,384]{2,1,0:T(8,128)S(1)}, f32[6,24,384]{2,1,0:T(8,128)S(1)}, u32[]{:S(2)}, u32[]{:S(2)}) collective-permute-start(f32[6,24,384]{2,1,0:T(8,128)S(1)} %copy-done.11), channel_id=1, source_target_pairs={{0,16},{16,32},{32,48},{48,64},{64,80},{80,96},{96,112},{112,0},{1... | collective-permute-start | bytes 663560 | tf_op jit(solution)/shard_map/ppermute | solution.py:425
  136.9 46.8 %collective-permute-start.8 = (f32[2,108,128]{2,1,0:T(8,128)S(1)}, f32[2,108,128]{2,1,0:T(8,128)S(1)}, u32[]{:S(2)}, u32[]{:S(2)}) collective-permute-start(f32[2,108,128]{2,1,0:T(8,128)S(1)} %pad_maximum_fusion), channel_id=1, source_target_pairs={{0,0},{1,2},{2,4},{3,6},{4,8},{5,10},{6,12},{7,14},{8,16},{9,18},{... | collective-permute-start | bytes 331784 | tf_op jit(solution)/shard_map/ppermute | solution.py:579
  139.2 44.4 %collective-permute-start.7 = (f32[6,8,384]{2,1,0:T(8,128)S(1)}, f32[6,8,384]{2,1,0:T(8,128)S(1)}, u32[]{:S(2)}, u32[]{:S(2)}) collective-permute-start(f32[6,8,384]{2,1,0:T(8,128)S(1)} %copy-done.12), channel_id=1, source_target_pairs={{0,17},{1,18},{2,19},{3,20},{4,21},{5,22},{6,23},{7,24},{8,25},{9,... | collective-permute-start | bytes 221192 | tf_op jit(solution)/shard_map/ppermute | solution.py:430
  188.5 8.0 %copy-start.2 = (f32[24,24,384]{2,1,0:T(8,128)S(1)}, f32[24,24,384]{2,1,0:T(8,128)}, u32[]{:S(2)}) copy-start(f32[24,24,384]{2,1,0:T(8,128)} %get-tuple-element.73) | copy-start | bytes 2654212
  188.5 8.2 %copy-start.7 = (f32[108,128]{1,0:T(8,128)S(1)}, f32[108,128]{1,0:T(8,128)}, u32[]{:S(2)}) copy-start(f32[108,128]{1,0:T(8,128)} %get-tuple-element.68) | copy-start | bytes 165892
  188.5 8.2 %copy-start.8 = (f32[108,128]{1,0:T(8,128)S(1)}, f32[108,128]{1,0:T(8,128)}, u32[]{:S(2)}) copy-start(f32[108,128]{1,0:T(8,128)} %get-tuple-element.69) | copy-start | bytes 165892
  188.5 55.8 %all-to-all-start.1 = ((f32[64,1,13952]{2,1,0:T(1,128)}), f32[64,1,13952]{2,1,0:T(1,128)}, u32[]{:S(2)}, u32[]{:S(2)}) async-start(f32[64,1,13952]{2,1,0:T(1,128)} %bitcast.41), calls=%async_computation.1 | async-start | bytes 7143424 | tf_op jit(solution)/shard_map/all_to_all | solution.py:420
  196.7 47.6 %collective-permute-start.9 = (f32[2,108,128]{2,1,0:T(8,128)S(1)}, f32[2,108,128]{2,1,0:T(8,128)S(1)}, u32[]{:S(2)}, u32[]{:S(2)}) collective-permute-start(f32[2,108,128]{2,1,0:T(8,128)S(1)} %pad_maximum_fusion.1), channel_id=1, source_target_pairs={{0,0},{2,1},{4,2},{6,3},{8,4},{10,5},{12,6},{14,7},{16,8},{18,9},{... | collective-permute-start | bytes 331784 | tf_op jit(solution)/shard_map/ppermute | solution.py:596
  244.3 9.1 %collective-permute-start.10 = (f32[6976,128]{1,0:T(8,128)}, f32[6976,128]{1,0:T(8,128)}, u32[]{:S(2)}, u32[]{:S(2)}) collective-permute-start(f32[6976,128]{1,0:T(8,128)} %bitcast.14.blocks), channel_id=1, source_target_pairs={{0,1},{1,0},{2,3},{3,2},{4,5},{5,4},{6,7},{7,6},{8,9},{9,8},{10,11... | collective-permute-start | bytes 10715144 | tf_op jit(solution)/shard_map/ppermute | solution.py:603
  (2 other events, 1.3 us)

commit v5 on v4

--- a/solution.py
+++ b/solution.py
@@ -55,6 +55,18 @@
 
 def dot3(a, b, dims):
     return dot(a[0], b[0], dims) + dot(a[0], b[1], dims) + dot(a[1], b[0], dims)
+
+
+def dot3_deep(a, b, dims):
+    (x,), (y,) = dims[0]
+    left = jnp.concatenate([a[0], a[0], a[1]], axis=x)
+    right = jnp.concatenate([b[0], b[1], b[0]], axis=y)
+    return dot(left, right, dims)
+
+
+def dot3_wide(a, b, dims):
+    wide = dot(a[0], jnp.concatenate([b[0], b[1]], axis=1), dims)
+    return wide[:, :128] + wide[:, 128:] + dot(a[1], b[0], dims)
 
 
 def unit(value):
@@ -213,16 +225,53 @@
 
 
 def block_pass(
-    x_l, c_l, east, south, corner, wq_h, wq_l, wp_h, wp_l, wu_h, wu_l, wd_h, wd_l,
-    bias, region, place,
-    keep, send, dscore, o_l, o_e, o_s, o_c,
-    x, cot, qkv, ctx, prob, n2h, n2l, ch, cl, grad, dqkv, dctx, grads, label_row, label_col, sems,
+    x_l, c_l, east, south, corner, region, place, *rest
 ):
+    stored, rest = rest[:9], rest[9:]
+    (
+    keep, send, dscore, x_out, grad_out, dqkv_out,
+    x, cot, qkv, ctx, prob, n2h, n2l, ch, cl, grad, dqkv, dctx, grads, label_row, label_col, norm2, scale2, sems,
+    ) = rest[:-9]
+    held = rest[-9:]
+    wq_h, wq_l, wp_h, wp_l, wu_h, wu_l, wd_h, wd_l, bias = held
+    loads = [pltpu.make_async_copy(a, b, sems.at[i]) for i, (a, b) in enumerate(zip(stored, held))]
+    for i in (0, 1, 8, 2, 3, 4, 5, 6, 7):
+        loads[i].start()
+    core = place[0]
+
+    def piece(i, half, start, rows):
+        source = grads.at[pl.ds(start, rows)]
+        spot = pl.ds(start - half * HALF, rows)
+        for target, here in ((keep, core == half), (send, core != half)):
+            yield here, pltpu.make_async_copy(source, target.at[spot], sems.at[9 + i])
+
+    def start(*what):
+        for here, copy in piece(*what):
+            pl.when(here)(copy.start)
+
+    def finish(*what):
+        for here, copy in piece(*what):
+            pl.when(here)(copy.wait)
+
+    pieces = (
+        (0, 1, HALF, HALF),
+        (1, 0, UP_AT, HALF - UP_AT),
+        (2, 0, 0, UP_AT),
+    )
     find_labels(region, place[1], label_row, label_col)
     gather_windows(x, x_l, east.at[0], south.at[0], corner.at[0])
+    kept = [
+        pltpu.make_async_copy(a, b, sems.at[12 + i])
+        for i, (a, b) in enumerate(((x, x_out), (grad, grad_out), (dqkv, dqkv_out)))
+    ]
+    kept[0].start()
     gather_windows(cot, c_l, east.at[1], south.at[1], corner.at[1])
     n1 = split(unit(x[...])[0])
-    qkv[...] = dot3(n1, (wq_h[...], wq_l[...]), NN)
+    loads[0].wait()
+    loads[1].wait()
+    qkv[...] = dot3_deep(n1, (wq_h[...], wq_l[...]), NN)
+
+    loads[8].wait()
 
     def attend(step, carry):
         w, g = step // GROUPS, step % GROUPS
@@ -232,19 +281,21 @@
         k = split(qkv[rows, pl.ds(pl.multiple_of(D + g * 128, 128), 128)])
         v = split(qkv[rows, pl.ds(pl.multiple_of(2 * D + g * 128, 128), 128)])
         allowed = label_col[w] == label_row[w]
-        score = dot3(q, k, NT) + bias[g]
+        score = dot3_deep(q, k, NT) + bias[g]
         score = jnp.where(jnp.concatenate([allowed] * PER, axis=0), score, -jnp.inf)
         raised = jnp.exp(score - jnp.max(score, axis=-1, keepdims=True))
         p = raised * (1.0 / jnp.sum(raised, axis=-1, keepdims=True))
         prob[step] = p
-        ctx[rows, lanes] = unstacked(dot3(split(p), v, NN))
+        ctx[rows, lanes] = unstacked(dot3_wide(split(p), v, NN))
         return carry
 
-    lax.fori_loop(0, WINS * GROUPS, attend, 0)
-
-    mixed = x[...] + dot3(split(ctx[...]), (wp_h[...], wp_l[...]), NN)
-    n2, scale2 = unit(mixed)
-    n2h[...], n2l[...] = split(n2)
+    lax.fori_loop(0, WINS * GROUPS, attend, 0, unroll=12)
+
+    for i in range(2, 8):
+        loads[i].wait()
+    mixed = x[...] + dot3_deep(split(ctx[...]), (wp_h[...], wp_l[...]), NN)
+    norm2[...], scale2[...] = unit(mixed)
+    n2h[...], n2l[...] = split(norm2[...])
     ch[...], cl[...] = split(cot[...])
     grad[...] = jnp.zeros_like(grad)
 
@@ -252,8 +303,8 @@
         n = (n2h[...], n2l[...])
         c = (ch[...], cl[...])
         up = (wu_h[f], wu_l[f])
-        u = dot3(n, up, NN)
-        back = dot3(c, (wd_h[f], wd_l[f]), NT)
+        u = dot3_deep(n, up, NN)
+        back = dot3_deep(c, (wd_h[f], wd_l[f]), NT)
         inner = 0.7978845608028654 * (u + 0.044715 * u * u * u)
         t = jnp.tanh(inner)
         hidden = split(0.5 * u * (1.0 + t))
@@ -261,23 +312,24 @@
             0.7978845608028654 * (1.0 + 3.0 * 0.044715 * u * u)
         )
         du = split(back * slope)
-        gdown = dot3(hidden, c, TN)
+        gdown = dot3_deep(hidden, c, TN)
         for b in range(3):
             grads[pl.ds(DOWN_AT + 3 * CHUNK * f + b, CHUNK, stride=3), :] = gdown[:, 128 * b : 128 * b + 128]
-        gup = dot3(n, du, TN)
+        gup = dot3_deep(n, du, TN)
         for b in range(2):
             grads[pl.ds(UP_AT + 2 * f + b, D, stride=12), :] = gup[:, 128 * b : 128 * b + 128]
-        grad[...] += dot3(du, up, NT)
+        grad[...] += dot3_deep(du, up, NT)
         return carry
 
     lax.fori_loop(0, CHUNKS, feed, 0)
 
-    mixed = x[...] + dot3(split(ctx[...]), (wp_h[...], wp_l[...]), NN)
-    n2, scale2 = unit(mixed)
-    grad[...] = cot[...] + unit_back(grad[...], n2, scale2)
+    start(*pieces[0])
+    start(*pieces[1])
+    grad[...] = cot[...] + unit_back(grad[...], norm2[...], scale2[...])
+    kept[1].start()
     gm = split(grad[...])
-    dctx[...] = dot3(gm, (wp_h[...], wp_l[...]), NT)
-    gproj = dot3(split(ctx[...]), gm, TN)
+    dctx[...] = dot3_deep(gm, (wp_h[...], wp_l[...]), NT)
+    gproj = dot3_deep(split(ctx[...]), gm, TN)
     for b in range(3):
         grads[pl.ds(PROJ_AT + b, D, stride=3), :] = gproj[:, 128 * b : 128 * b + 128]
     dscore[...] = jnp.zeros_like(dscore)
@@ -293,41 +345,51 @@
         v = split(qkv[rows, v_at])
         d = split(stacked(dctx[rows, q_at]))
         p = prob[step]
-        dp = dot3(d, v, NT)
+        dp = dot3_deep(d, v, NT)
         ds = p * (dp - jnp.sum(dp * p, axis=-1, keepdims=True))
         dscore[g] += ds
         ps, dss = split(p), split(ds)
-        dqkv[rows, v_at] = dot3(ps, d, TN)
-        dqkv[rows, q_at] = unstacked(dot3(dss, k, NN)) * SCALE
-        dqkv[rows, k_at] = dot3(dss, q, TN)
+        dqkv[rows, v_at] = dot3_wide(ps, d, TN)
+        dqkv[rows, q_at] = unstacked(dot3_wide(dss, k, NN)) * SCALE
+        dqkv[rows, k_at] = dot3_wide(dss, q, TN)
         return carry
 
-    lax.fori_loop(0, WINS * GROUPS, attend_back, 0)
-
-    n1, scale1 = unit(x[...])
+    lax.fori_loop(0, WINS * GROUPS, attend_back, 0, unroll=4)
+
+    kept[2].start()
     dq = split(dqkv[...])
-    gqkv = dot3(split(n1), dq, TN)
+    gqkv = dot3_deep(split(unit(x[...])[0]), dq, TN)
     for b in range(9):
         grads[pl.ds(b, D, stride=9), :] = gqkv[:, 128 * b : 128 * b + 128]
-    back = dot3(dq, (wq_h[...], wq_l[...]), NT)
-    grad[...] += unit_back(back, n1, scale1)
-    core = place[0]
-    out = pltpu.make_async_copy(
-        grads.at[pl.ds(pl.multiple_of((1 - core) * HALF, 8), HALF)], send, sems.at[0]
-    )
-    stay = pltpu.make_async_copy(
-        grads.at[pl.ds(pl.multiple_of(core * HALF, 8), HALF)], keep, sems.at[1]
-    )
-    out.start()
-    stay.start()
-    scatter_windows(grad, o_l, o_e, o_s, o_c)
-    out.wait()
-    stay.wait()
+    start(*pieces[2])
+    for copy in kept:
+        copy.wait()
+    for what in pieces:
+        finish(*what)
+
+
+def input_grad(x, grad, dqkv, wq_h, wq_l, o_l, o_e, o_s, o_c, total):
+    n1, scale1 = unit(x[...])
+    back = dot3_deep(split(dqkv[...]), (wq_h[...], wq_l[...]), NT)
+    total[...] = grad[...] + unit_back(back, n1, scale1)
+    scatter_windows(total, o_l, o_e, o_s, o_c)
+
+
+def run_input_grad(x, grad, dqkv, wq_h, wq_l):
+    halo = [(TILE, TILE, D), (TILE, 8, D), (SHIFT, TILE, D), (SHIFT, 8, D)]
+    return pl.pallas_call(
+        input_grad,
+        out_shape=[jax.ShapeDtypeStruct(s, F32) for s in halo],
+        in_specs=[VMEM] * 5,
+        out_specs=[VMEM] * 4,
+        scratch_shapes=[pltpu.VMEM((TOK, D), F32)],
+        compiler_params=PARAMS,
+        name="input_grad",
+    )(x, grad, dqkv, wq_h, wq_l)
 
 
 def run_block(tiles, edges, weights, bias, region, place):
-    halo = [(TILE, TILE, D), (TILE, 8, D), (SHIFT, TILE, D), (SHIFT, 8, D)]
-    outs = [(HALF, 128), (HALF, 128), (GROUPS, PER * WT, WT)] + halo
+    outs = [(HALF, 128), (HALF, 128), (GROUPS, PER * WT, WT), (TOK, D), (TOK, D), (TOK, 3 * D)]
     whole = pl.BlockSpec(memory_space=pl.ANY)
     scratch = [
         pltpu.VMEM((TOK, D), F32),
@@ -345,14 +407,17 @@
         pltpu.VMEM((ROWS, 128), F32),
         pltpu.VMEM((WINS, 1, WT), F32),
         pltpu.VMEM((WINS, WT, 1), F32),
-        pltpu.SemaphoreType.DMA((2,)),
+        pltpu.VMEM((TOK, D), F32),
+        pltpu.VMEM((TOK, 1), F32),
+        pltpu.SemaphoreType.DMA((15,)),
+        *[pltpu.VMEM(a.shape, a.dtype) for a in (*weights, bias)],
     ]
-    args = (*tiles, *edges, *weights, bias, region, place)
+    args = (*tiles, *edges, region, place, *weights, bias)
     return pl.pallas_call(
         block_pass,
         out_shape=[jax.ShapeDtypeStruct(s, F32) for s in outs],
-        in_specs=[VMEM] * (len(args) - 1) + [pl.BlockSpec(memory_space=pltpu.SMEM)],
-        out_specs=[whole] * 2 + [VMEM] * (len(outs) - 2),
+        in_specs=[VMEM] * 6 + [pl.BlockSpec(memory_space=pltpu.SMEM)] + [whole] * 9,
+        out_specs=[whole] * 2 + [VMEM] + [whole] * 3,
         scratch_shapes=scratch,
         compiler_params=PARAMS,
         name="block_pass",
@@ -376,10 +441,12 @@
         return dot(jnp.concatenate(pieces, axis=0), hot, NT)
 
     def step(k, carry):
-        sums[...] += (one(4 * k) + one(4 * k + 1)) + (one(4 * k + 2) + one(4 * k + 3))
+        at = 8 * k
+        quads = [(one(at + i) + one(at + i + 1)) + (one(at + i + 2) + one(at + i + 3)) for i in (0, 4)]
+        sums[...] += quads[0] + quads[1]
         return carry
 
-    lax.fori_loop(0, WT // 4, step, 0)
+    lax.fori_loop(0, WT // 8, step, 0)
     out[...] = jnp.zeros_like(out)
     for p in range(5):
         both = sums[32 * p : 32 * p + 16, :] + sums[32 * p + 16 : 32 * p + 32, :]
@@ -559,7 +626,7 @@
     edges = edges_of(block_input, cotangent)
     core = lon_at % 2
     place = jnp.stack([core, (lat_at == 7).astype(jnp.int32)]).astype(jnp.int32)
-    keep, send, dscore, o_l, o_e, o_s, o_c = run_block(
+    keep, send, dscore, x, grad, dqkv = run_block(
         (block_input, cotangent), edges, pairs, bias, region_ids, place
     )
     came = lax.ppermute(send, BOTH, core_swap())
@@ -568,9 +635,10 @@
     summed = merged(keep, came, line, line_came)
     parts = exchanged(summed.reshape(64, 1, BLOCK * 128), chip_groups())
 
-    _, o_e, o_s, o_c, first_moment, second_moment = lax.optimization_barrier(
-        (summed, o_e, o_s, o_c, first_moment, second_moment)
+    _, dqkv, first_moment, second_moment = lax.optimization_barrier(
+        (summed, dqkv, first_moment, second_moment)
     )
+    o_l, o_e, o_s, o_c = run_input_grad(x, grad, dqkv, pairs[0], pairs[1])
     from_west = around(o_e, "lon", 1)
     from_north = around(o_s, "lat", 1)
     from_corner = diagonal(o_c, 1)

time: 259 us -> 234 us (0.903)
  Pallas kernels: 111 us -> 92.7 us
  waiting for transfers between devices: 82.2 us -> 75.5 us
    pallas_call x1, Pallas kernels: 67.3 us -> 45.7 us  [run_block(): pl.pallas_call(block_pass, out_shape=[jax.ShapeDtypeStruct(s, F32) for s...]
    pallas_call x0 -> x1, Pallas kernels: none -> 6.52 us  [run_input_grad(): pl.pallas_call(input_grad, out_shape=[jax.ShapeDtypeStruct(s, F32) for s...]
    ppermute x2, waiting for transfers between devices: 39.9 us -> 33.5 us  [diagonal(): lax.ppermute(value, BOTH, [(a * lon + o, (a + by) % lat * lon + (o + by)...]
    pallas_call x1, Pallas kernels: 12 us -> 8.67 us  [table_gradient(): pl.pallas_call(table_sum, out_shape=jax.ShapeDtypeStruct((64, 128), F32),...]
  transfers between devices with their start and end apart: 13 -> 13, of which waited for: 3 -> 3; matrix products, arithmetic and copies ran while one was open for 4% -> 4% of each run, Pallas kernels for 10% -> 13%
where the time goes in v5:
time: 234 us; the launch traced here: 233 us
  Pallas kernels  92.7 us (40%)
  waiting for transfers between devices  75.5 us (32%)
  starting transfers between devices  51.4 us (22%)
  local copies, waits for them, and re-layouts  11.3 us (5%)
    pallas_call x1, Pallas kernels, run_block(): pl.pallas_call(block_pass, out_shape=[jax.ShapeDtypeStruct(s, F32) for s...  45.7 us
    ppermute x1, waiting for transfers between devices, per_device(): moments = lax.ppermute(jnp.stack([first_new, second_new]), BOTH, back)  40.9 us
    ppermute x2, waiting for transfers between devices, diagonal(): lax.ppermute(value, BOTH, [(a * lon + o, (a + by) % lat * lon + (o + by)...  33.5 us
    all_to_all x2, starting transfers between devices, exchanged(): lax.all_to_all(value, BOTH, 0, 0, axis_index_groups=groups, tiled=True)  22.5 us
    pallas_call x1, Pallas kernels, prepared(): pl.pallas_call(prepare, out_shape=[jax.ShapeDtypeStruct(s, BF16) for s in...  9.9 us
    ppermute x4, starting transfers between devices, around(): lax.ppermute(value, axis, [(i, (i + by) % size) for i in range(size)])  9.42 us
    ppermute x2, starting transfers between devices, diagonal(): lax.ppermute(value, BOTH, [(a * lon + o, (a + by) % lat * lon + (o + by)...  9.01 us
    pallas_call x1, Pallas kernels, table_gradient(): pl.pallas_call(table_sum, out_shape=jax.ShapeDtypeStruct((64, 128), F32),...  8.67 us
  transfers between devices with their start and end apart: 13, of which 3 were waited for; matrix products, arithmetic and copies ran while one was open for 4% of the time, Pallas kernels for 13%

profile of v5, /device:TPU:1, one launch (start us, length us, event | category | flops | bytes accessed | tf_op | source)
XLA Modules:
  0.0 233.4 jit_solution(1874009776390058927)
XLA Ops:
  0.6 2.3 pack.1
  2.9 1.4 collective-permute-start
  4.3 3.6 %collective-permute-start.1 = (f32[2,6,24,384]{3,2,1,0:T(8,128)}, f32[2,6,24,384]{3,2,1,0:T(8,128)S(1)}, u32[]{:S(2)}, u32[]{:S(2)}) collective-permute-start(f32[2,6,24,384]{3,2,1,0:T(8,128)} %get-tuple-element.44), channel_id=1, source_target_pairs={{0,112},{16,0},{32,16},{48,32},{64,48},{80,64},{96,80},{112,96},{1... | collective-permute-start | bytes 1327112 | tf_op jit(solution)/shard_map/ppermute | solution.py:492
  7.9 5.9 %collective-permute-start.2 = (f32[2,6,8,384]{3,2,1,0:T(8,128)}, f32[2,6,8,384]{3,2,1,0:T(8,128)S(1)}, u32[]{:S(2)}, u32[]{:S(2)}) collective-permute-start(f32[2,6,8,384]{3,2,1,0:T(8,128)} %get-tuple-element.45), channel_id=1, source_target_pairs={{0,127},{1,112},{2,113},{3,114},{4,115},{5,116},{6,117},{7,118},{8... | collective-permute-start | bytes 442376 | tf_op jit(solution)/shard_map/ppermute | solution.py:497
  13.8 9.9 %prepare.1 = (bf16[384,1152]{1,0:T(8,128)(2,1)}, bf16[384,1152]{1,0:T(8,128)(2,1)}, bf16[384,384]{1,0:T(8,128)(2,1)}, bf16[384,384]{1,0:T(8,128)(2,1)}, bf16[6,3...) custom-call(f32[13824,128]{1,0:T(8,128)} %bitcast.33, ...), custom_call_target="tpu_custom_call" | custom-call | tf_op jit(solution)/shard_map/prepare/pallas_call | solution.py:138
  25.4 45.7 %block_pass.1 = (f32[6912,128]{1,0:T(8,128)}, f32[6912,128]{1,0:T(8,128)}, f32[3,576,144]{2,1,0:T(8,128)}, f32[576,384]{1,0:T(8,128)}, f32[576,384]{1,0:T(8,128)}, /*index=5*/f32[576,1152]{1,0:T(8,128)}) custom-call(f32[24,24,384]{2,1,0:T(8,128)} %x_l.1, f32[24,24,384]{2,1,0:T(8,128)} %c_l.1, f32[2,24,8,384]{3,2,1,0:T(8,128)} %copy-done.1, ...), custom_call_target="tpu_custom_call" | custom-call | tf_op jit(solution)/shard_map/block_pass/pallas_call | solution.py:416
  71.2 2.5 %copy.24 = f32[12,144,144]{2,0,1:T(8,128)S(1)} copy(f32[12,144,144]{2,1,0:T(8,128)} %bitcast.42) | data formatting | bytes 1990656 | tf_op jit(solution)/shard_map/reshape | solution.py:457
  73.8 1.7 pad.4.scores
  75.4 8.7 %table_sum.1.line = f32[64,128]{1,0:T(8,128)} custom-call(f32[144,16,144]{2,1,0:T(8,128)} %pad.4.scores, s32[144,144]{1,0:T(8,128)} %index.3), custom_call_target="tpu_custom_call" | custom-call | tf_op jit(solution)/shard_map/table_sum/pallas_call | solution.py:459
  87.5 5.3 %merge.1 = f32[6976,128]{1,0:T(8,128)} custom-call(f32[6912,128]{1,0:T(8,128)} %get-tuple-element.55.keep, f32[6912,128]{1,0:T(8,128)} %copy-done, f32[64,128]{1,0:T(8,128)} %table_sum.1.line, f32[64,128]{1,0:T(8,128)} %copy-done.9), custom_call_target="tpu_custom_call" | custom-call | tf_op jit(solution)/shard_map/merge/pallas_call | solution.py:541
  92.8 14.5 %all-to-all-start = ((f32[64,1,13952]{2,1,0:T(1,128)}), f32[64,1,13952]{2,1,0:T(1,128)}, u32[]{:S(2)}, u32[]{:S(2)}) async-start(f32[64,1,13952]{2,1,0:T(1,128)} %bitcast.38), calls=%async_computation | async-start | bytes 7143424 | tf_op jit(solution)/shard_map/all_to_all | solution.py:487
  107.3 6.5 %input_grad.1 = (f32[24,24,384]{2,1,0:T(8,128)}, f32[24,8,384]{2,1,0:T(8,128)}, f32[6,24,384]{2,1,0:T(8,128)}, f32[6,8,384]{2,1,0:T(8,128)}) custom-call(f32[576,384]{1,0:T(8,128)} %get-tuple-element.58.x, f32[576,384]{1,0:T(8,128)} %get-tuple-element.59.grad, f32[576,1152]{1,0:T(8,128)} %get-tuple-element.61.dqkv, ...), custom_call_target="tpu_custom_call" | custom-call | tf_op jit(solution)/shard_map/input_grad/pallas_call | solution.py:380
  113.8 3.2 %collective-permute-start.5 = (f32[24,8,384]{2,1,0:T(8,128)}, f32[24,8,384]{2,1,0:T(8,128)S(1)}, u32[]{:S(2)}, u32[]{:S(2)}) collective-permute-start(f32[24,8,384]{2,1,0:T(8,128)} %get-tuple-element.62), channel_id=1, source_target_pairs={{0,1},{1,2},{2,3},{3,4},{4,5},{5,6},{6,7},{7,8},{8,9},{9,10},{10,1... | collective-permute-start | bytes 884744 | tf_op jit(solution)/shard_map/ppermute | solution.py:492
  118.3 2.2 collective-permute-start.8
  120.5 3.1 %collective-permute-start.7 = (f32[6,8,384]{2,1,0:T(8,128)}, f32[6,8,384]{2,1,0:T(8,128)S(1)}, u32[]{:S(2)}, u32[]{:S(2)}) collective-permute-start(f32[6,8,384]{2,1,0:T(8,128)} %get-tuple-element.64), channel_id=1, source_target_pairs={{0,17},{1,18},{2,19},{3,20},{4,21},{5,22},{6,23},{7,24},{8,25},{9,... | collective-permute-start | bytes 221192 | tf_op jit(solution)/shard_map/ppermute | solution.py:497
  123.6 1.5 constant_dynamic-slice_fusion.weights
  125.1 33.5 %collective-permute-done.7 = f32[6,8,384]{2,1,0:T(8,128)S(1)} collective-permute-done((f32[6,8,384]{2,1,0:T(8,128)}, f32[6,8,384]{2,1,0:T(8,128)S(1)}, u32[]{:S(2)}, u32[]{:S(2)}) %collective-permute-start.7) | collective-permute-done | bytes 73760 | tf_op jit(solution)/shard_map/ppermute | solution.py:497
  159.3 4.2 %adam.1 = (f32[6976,128]{1,0:T(8,128)}, f32[108,128]{1,0:T(8,128)}, f32[108,128]{1,0:T(8,128)}) custom-call(f32[6976,128]{1,0:T(8,128)} %bitcast.8.parts, f32[108,128]{1,0:T(8,128)} %constant_dynamic-slice_fusion.weights, f32[108,128]{1,0:T(8,128)} %get-tuple-element.84.first, f32[108,128]{1,0:T(8,128)} %get-tuple-element.83.second), custom_call_target="tpu_custom_call" | custom-call | tf_op jit(solution)/shard_map/adam/pallas_call | solution.py:654
  163.5 8.0 %all-to-all-start.1 = ((f32[64,1,13952]{2,1,0:T(1,128)}), f32[64,1,13952]{2,1,0:T(1,128)}, u32[]{:S(2)}, u32[]{:S(2)}) async-start(f32[64,1,13952]{2,1,0:T(1,128)} %bitcast.41), calls=%async_computation.1 | async-start | bytes 7143424 | tf_op jit(solution)/shard_map/all_to_all | solution.py:487
  171.7 5.4 %collective-permute-start.9 = (f32[2,108,128]{2,1,0:T(8,128)S(1)}, f32[2,108,128]{2,1,0:T(8,128)S(1)}, u32[]{:S(2)}, u32[]{:S(2)}) collective-permute-start(f32[2,108,128]{2,1,0:T(8,128)S(1)} %pad_maximum_fusion.1), channel_id=1, source_target_pairs={{0,0},{2,1},{4,2},{6,3},{8,4},{10,5},{12,6},{14,7},{16,8},{18,9},{... | collective-permute-start | bytes 331784 | tf_op jit(solution)/shard_map/ppermute | solution.py:664
  178.1 40.9 %collective-permute-done.9 = f32[2,108,128]{2,1,0:T(8,128)S(1)} collective-permute-done((f32[2,108,128]{2,1,0:T(8,128)S(1)}, f32[2,108,128]{2,1,0:T(8,128)S(1)}, u32[]{:S(2)}, u32[]{:S(2)}) %collective-permute-start.9) | collective-permute-done | bytes 110624 | tf_op jit(solution)/shard_map/ppermute | solution.py:664
  219.0 2.2 collective-permute-start.10
  221.2 5.1 %lay_out_own.1 = (f32[13824,128]{1,0:T(8,128)}, f32[64,128]{1,0:T(8,128)}) custom-call(s32[2]{0:T(128)} %pad_add_fusion.place, f32[6976,128]{1,0:T(8,128)} %bitcast.14.blocks), custom_call_target="tpu_custom_call" | custom-call | tf_op jit(solution)/shard_map/lay_out_own/pallas_call | solution.py:582
  228.4 5.0 %lay_out_other.1 = f32[13824,128]{1,0:T(8,128)} custom-call(s32[2]{0:T(128)} %pad_add_fusion.place, f32[6976,128]{1,0:T(8,128)} %collective-permute-done.10.blocks, f32[13824,128]{1,0:T(8,128)} %get-tuple-element.78.refs_0_), custom_call_target="tpu_custom_call", output_to_operand_aliasing={{}: (2, {})} | custom-call | tf_op jit(solution)/shard_map/lay_out_other/pallas_call | solution.py:601
  (47 shorter events, 10.1 us)
Async XLA Ops:
  2.9 21.4 %collective-permute-start = (f32[2,24,8,384]{3,2,1,0:T(8,128)}, f32[2,24,8,384]{3,2,1,0:T(8,128)S(1)}, u32[]{:S(2)}, u32[]{:S(2)}) collective-permute-start(f32[2,24,8,384]{3,2,1,0:T(8,128)} %get-tuple-element.43), channel_id=1, source_target_pairs={{0,15},{1,0},{2,1},{3,2},{4,3},{5,4},{6,5},{7,6},{8,7},{9,8},{10,9... | collective-permute-start | bytes 1769480 | tf_op jit(solution)/shard_map/ppermute | solution.py:492
  4.3 20.0 %collective-permute-start.1 = (f32[2,6,24,384]{3,2,1,0:T(8,128)}, f32[2,6,24,384]{3,2,1,0:T(8,128)S(1)}, u32[]{:S(2)}, u32[]{:S(2)}) collective-permute-start(f32[2,6,24,384]{3,2,1,0:T(8,128)} %get-tuple-element.44), channel_id=1, source_target_pairs={{0,112},{16,0},{32,16},{48,32},{64,48},{80,64},{96,80},{112,96},{1... | collective-permute-start | bytes 1327112 | tf_op jit(solution)/shard_map/ppermute | solution.py:492
  7.9 16.4 %collective-permute-start.2 = (f32[2,6,8,384]{3,2,1,0:T(8,128)}, f32[2,6,8,384]{3,2,1,0:T(8,128)S(1)}, u32[]{:S(2)}, u32[]{:S(2)}) collective-permute-start(f32[2,6,8,384]{3,2,1,0:T(8,128)} %get-tuple-element.45), channel_id=1, source_target_pairs={{0,127},{1,112},{2,113},{3,114},{4,115},{5,116},{6,117},{7,118},{8... | collective-permute-start | bytes 442376 | tf_op jit(solution)/shard_map/ppermute | solution.py:497
  24.3 0.7 copy-start.4
  24.4 0.8 copy-start.3
  24.4 1.0 copy-start.1
  71.1 14.6 %collective-permute-start.3 = (f32[6912,128]{1,0:T(8,128)}, f32[6912,128]{1,0:T(8,128)S(1)}, u32[]{:S(2)}, u32[]{:S(2)}) collective-permute-start(f32[6912,128]{1,0:T(8,128)} %get-tuple-element.56), channel_id=1, source_target_pairs={{0,1},{1,0},{2,3},{3,2},{4,5},{5,4},{6,7},{7,6},{8,9},{9,8},{10,11... | collective-permute-start | bytes 10616840 | tf_op jit(solution)/shard_map/ppermute | solution.py:632
  84.1 1.6 collective-permute-start.4
  85.7 0.6 copy-start.9
  85.7 1.8 copy-start
  92.8 65.8 %all-to-all-start = ((f32[64,1,13952]{2,1,0:T(1,128)}), f32[64,1,13952]{2,1,0:T(1,128)}, u32[]{:S(2)}, u32[]{:S(2)}) async-start(f32[64,1,13952]{2,1,0:T(1,128)} %bitcast.38), calls=%async_computation | async-start | bytes 7143424 | tf_op jit(solution)/shard_map/all_to_all | solution.py:487
  107.3 11.0 %copy-start.5 = (f32[13824]{0:T(1024)S(1)}, f32[13824]{0:T(1024)}, u32[]{:S(2)}) copy-start(f32[13824]{0:T(1024)} %param.12) | copy-start | bytes 165892
  107.3 11.0 %copy-start.6 = (f32[13824]{0:T(1024)S(1)}, f32[13824]{0:T(1024)}, u32[]{:S(2)}) copy-start(f32[13824]{0:T(1024)} %param.11) | copy-start | bytes 165892
  113.8 44.8 %collective-permute-start.5 = (f32[24,8,384]{2,1,0:T(8,128)}, f32[24,8,384]{2,1,0:T(8,128)S(1)}, u32[]{:S(2)}, u32[]{:S(2)}) collective-permute-start(f32[24,8,384]{2,1,0:T(8,128)} %get-tuple-element.62), channel_id=1, source_target_pairs={{0,1},{1,2},{2,3},{3,4},{4,5},{5,6},{6,7},{7,8},{8,9},{9,10},{10,1... | collective-permute-start | bytes 884744 | tf_op jit(solution)/shard_map/ppermute | solution.py:492
  117.1 41.5 %collective-permute-start.6 = (f32[6,24,384]{2,1,0:T(8,128)}, f32[6,24,384]{2,1,0:T(8,128)S(1)}, u32[]{:S(2)}, u32[]{:S(2)}) collective-permute-start(f32[6,24,384]{2,1,0:T(8,128)} %get-tuple-element.63), channel_id=1, source_target_pairs={{0,16},{16,32},{32,48},{48,64},{64,80},{80,96},{96,112},{112,0},{1... | collective-permute-start | bytes 663560 | tf_op jit(solution)/shard_map/ppermute | solution.py:492
  118.3 40.3 %collective-permute-start.8 = (f32[2,108,128]{2,1,0:T(8,128)S(1)}, f32[2,108,128]{2,1,0:T(8,128)S(1)}, u32[]{:S(2)}, u32[]{:S(2)}) collective-permute-start(f32[2,108,128]{2,1,0:T(8,128)S(1)} %pad_maximum_fusion), channel_id=1, source_target_pairs={{0,0},{1,2},{2,4},{3,6},{4,8},{5,10},{6,12},{7,14},{8,16},{9,18},{... | collective-permute-start | bytes 331784 | tf_op jit(solution)/shard_map/ppermute | solution.py:647
  120.5 38.1 %collective-permute-start.7 = (f32[6,8,384]{2,1,0:T(8,128)}, f32[6,8,384]{2,1,0:T(8,128)S(1)}, u32[]{:S(2)}, u32[]{:S(2)}) collective-permute-start(f32[6,8,384]{2,1,0:T(8,128)} %get-tuple-element.64), channel_id=1, source_target_pairs={{0,17},{1,18},{2,19},{3,20},{4,21},{5,22},{6,23},{7,24},{8,25},{9,... | collective-permute-start | bytes 221192 | tf_op jit(solution)/shard_map/ppermute | solution.py:497
  163.5 8.0 %copy-start.2 = (f32[24,24,384]{2,1,0:T(8,128)S(1)}, f32[24,24,384]{2,1,0:T(8,128)}, u32[]{:S(2)}) copy-start(f32[24,24,384]{2,1,0:T(8,128)} %get-tuple-element.75) | copy-start | bytes 2654212
  163.5 8.2 %copy-start.7 = (f32[108,128]{1,0:T(8,128)S(1)}, f32[108,128]{1,0:T(8,128)}, u32[]{:S(2)}) copy-start(f32[108,128]{1,0:T(8,128)} %get-tuple-element.70) | copy-start | bytes 165892
  163.5 8.2 %copy-start.8 = (f32[108,128]{1,0:T(8,128)S(1)}, f32[108,128]{1,0:T(8,128)}, u32[]{:S(2)}) copy-start(f32[108,128]{1,0:T(8,128)} %get-tuple-element.71) | copy-start | bytes 165892
  163.5 55.5 %all-to-all-start.1 = ((f32[64,1,13952]{2,1,0:T(1,128)}), f32[64,1,13952]{2,1,0:T(1,128)}, u32[]{:S(2)}, u32[]{:S(2)}) async-start(f32[64,1,13952]{2,1,0:T(1,128)} %bitcast.41), calls=%async_computation.1 | async-start | bytes 7143424 | tf_op jit(solution)/shard_map/all_to_all | solution.py:487
  171.7 47.3 %collective-permute-start.9 = (f32[2,108,128]{2,1,0:T(8,128)S(1)}, f32[2,108,128]{2,1,0:T(8,128)S(1)}, u32[]{:S(2)}, u32[]{:S(2)}) collective-permute-start(f32[2,108,128]{2,1,0:T(8,128)S(1)} %pad_maximum_fusion.1), channel_id=1, source_target_pairs={{0,0},{2,1},{4,2},{6,3},{8,4},{10,5},{12,6},{14,7},{16,8},{18,9},{... | collective-permute-start | bytes 331784 | tf_op jit(solution)/shard_map/ppermute | solution.py:664
  219.0 9.4 %collective-permute-start.10 = (f32[6976,128]{1,0:T(8,128)}, f32[6976,128]{1,0:T(8,128)}, u32[]{:S(2)}, u32[]{:S(2)}) collective-permute-start(f32[6976,128]{1,0:T(8,128)} %bitcast.14.blocks), channel_id=1, source_target_pairs={{0,1},{1,0},{2,3},{3,2},{4,5},{5,4},{6,7},{7,6},{8,9},{9,8},{10,11... | collective-permute-start | bytes 10715144 | tf_op jit(solution)/shard_map/ppermute | solution.py:671

commit v6 on v5

--- a/solution.py
+++ b/solution.py
@@ -28,8 +28,12 @@
 ROWS = DOWN_AT + MLP_ROWS
 CHUNK = 256
 CHUNKS = FF // CHUNK
-HALF = ROWS // 2
-OWN = ROWS // 128
+MLP_HALF = MLP_ROWS
+ATT_HALF = UP_AT // 2
+OWN_MLP = MLP_HALF // 64
+OWN_ATT = ATT_HALF // 64
+OWN = OWN_MLP + OWN_ATT
+SUM_BLOCK = OWN_ATT + 1
 BLOCK = OWN + 1
 BATCH = 16
 BIAS = 529
@@ -224,13 +228,21 @@
 SCALE = 1.0 / math.sqrt(32.0)
 
 
-def block_pass(
+def ship(grads, outs, core, rows, sems):
+    for h in range(2):
+        source = grads.at[pl.ds(h * rows, rows)]
+        for target, here in ((outs[0], core == h), (outs[1], core != h)):
+            yield here, pltpu.make_async_copy(source, target, sems.at[h])
+
+
+def forward_and_feed(
     x_l, c_l, east, south, corner, region, place, *rest
 ):
     stored, rest = rest[:9], rest[9:]
     (
-    keep, send, dscore, x_out, grad_out, dqkv_out,
-    x, cot, qkv, ctx, prob, n2h, n2l, ch, cl, grad, dqkv, dctx, grads, label_row, label_col, norm2, scale2, sems,
+        keep, send, x_out, grad_out, qkv_out, prob_out, ctx_out,
+        x, cot, qkv, ctx, prob, n2h, n2l, ch, cl, grad, grads, label_row, label_col, norm2, scale2,
+        sems, prob_sems,
     ) = rest[:-9]
     held = rest[-9:]
     wq_h, wq_l, wp_h, wp_l, wu_h, wu_l, wd_h, wd_l, bias = held
@@ -238,31 +250,11 @@
     for i in (0, 1, 8, 2, 3, 4, 5, 6, 7):
         loads[i].start()
     core = place[0]
-
-    def piece(i, half, start, rows):
-        source = grads.at[pl.ds(start, rows)]
-        spot = pl.ds(start - half * HALF, rows)
-        for target, here in ((keep, core == half), (send, core != half)):
-            yield here, pltpu.make_async_copy(source, target.at[spot], sems.at[9 + i])
-
-    def start(*what):
-        for here, copy in piece(*what):
-            pl.when(here)(copy.start)
-
-    def finish(*what):
-        for here, copy in piece(*what):
-            pl.when(here)(copy.wait)
-
-    pieces = (
-        (0, 1, HALF, HALF),
-        (1, 0, UP_AT, HALF - UP_AT),
-        (2, 0, 0, UP_AT),
-    )
     find_labels(region, place[1], label_row, label_col)
     gather_windows(x, x_l, east.at[0], south.at[0], corner.at[0])
     kept = [
-        pltpu.make_async_copy(a, b, sems.at[12 + i])
-        for i, (a, b) in enumerate(((x, x_out), (grad, grad_out), (dqkv, dqkv_out)))
+        pltpu.make_async_copy(a, b, sems.at[9 + i])
+        for i, (a, b) in enumerate(((x, x_out), (grad, grad_out), (qkv, qkv_out), (ctx, ctx_out)))
     ]
     kept[0].start()
     gather_windows(cot, c_l, east.at[1], south.at[1], corner.at[1])
@@ -270,7 +262,7 @@
     loads[0].wait()
     loads[1].wait()
     qkv[...] = dot3_deep(n1, (wq_h[...], wq_l[...]), NN)
-
+    kept[2].start()
     loads[8].wait()
 
     def attend(step, carry):
@@ -286,11 +278,12 @@
         raised = jnp.exp(score - jnp.max(score, axis=-1, keepdims=True))
         p = raised * (1.0 / jnp.sum(raised, axis=-1, keepdims=True))
         prob[step] = p
+        pltpu.make_async_copy(prob.at[step], prob_out.at[step], prob_sems.at[step]).start()
         ctx[rows, lanes] = unstacked(dot3_wide(split(p), v, NN))
         return carry
 
     lax.fori_loop(0, WINS * GROUPS, attend, 0, unroll=12)
-
+    kept[3].start()
     for i in range(2, 8):
         loads[i].wait()
     mixed = x[...] + dot3_deep(split(ctx[...]), (wp_h[...], wp_l[...]), NN)
@@ -314,25 +307,80 @@
         du = split(back * slope)
         gdown = dot3_deep(hidden, c, TN)
         for b in range(3):
-            grads[pl.ds(DOWN_AT + 3 * CHUNK * f + b, CHUNK, stride=3), :] = gdown[:, 128 * b : 128 * b + 128]
+            grads[pl.ds(MLP_ROWS + 3 * CHUNK * f + b, CHUNK, stride=3), :] = gdown[:, 128 * b : 128 * b + 128]
         gup = dot3_deep(n, du, TN)
         for b in range(2):
-            grads[pl.ds(UP_AT + 2 * f + b, D, stride=12), :] = gup[:, 128 * b : 128 * b + 128]
+            grads[pl.ds(2 * f + b, D, stride=12), :] = gup[:, 128 * b : 128 * b + 128]
         grad[...] += dot3_deep(du, up, NT)
         return carry
 
     lax.fori_loop(0, CHUNKS, feed, 0)
-
-    start(*pieces[0])
-    start(*pieces[1])
+    for here, copy in ship(grads, (keep, send), core, MLP_HALF, sems.at[pl.ds(13, 2)]):
+        pl.when(here)(copy.start)
     grad[...] = cot[...] + unit_back(grad[...], norm2[...], scale2[...])
     kept[1].start()
+    for copy in kept:
+        copy.wait()
+    for step in range(WINS * GROUPS):
+        pltpu.make_async_copy(prob.at[step], prob_out.at[step], prob_sems.at[step]).wait()
+    for here, copy in ship(grads, (keep, send), core, MLP_HALF, sems.at[pl.ds(13, 2)]):
+        pl.when(here)(copy.wait)
+
+
+def run_forward(tiles, edges, weights, bias, region, place):
+    whole = pl.BlockSpec(memory_space=pl.ANY)
+    probs = (WINS * GROUPS, PER * WT, WT)
+    outs = [(MLP_HALF, 128), (MLP_HALF, 128), (TOK, D), (TOK, D), (TOK, 3 * D), probs, (TOK, D)]
+    scratch = [
+        pltpu.VMEM((TOK, D), F32),
+        pltpu.VMEM((TOK, D), F32),
+        pltpu.VMEM((TOK, 3 * D), F32),
+        pltpu.VMEM((TOK, D), F32),
+        pltpu.VMEM(probs, F32),
+        pltpu.VMEM((TOK, D), BF16),
+        pltpu.VMEM((TOK, D), BF16),
+        pltpu.VMEM((TOK, D), BF16),
+        pltpu.VMEM((TOK, D), BF16),
+        pltpu.VMEM((TOK, D), F32),
+        pltpu.VMEM((2 * MLP_ROWS, 128), F32),
+        pltpu.VMEM((WINS, 1, WT), F32),
+        pltpu.VMEM((WINS, WT, 1), F32),
+        pltpu.VMEM((TOK, D), F32),
+        pltpu.VMEM((TOK, 1), F32),
+        pltpu.SemaphoreType.DMA((15,)),
+        pltpu.SemaphoreType.DMA((WINS * GROUPS,)),
+        *[pltpu.VMEM(a.shape, a.dtype) for a in (*weights, bias)],
+    ]
+    args = (*tiles, *edges, region, place, *weights, bias)
+    return pl.pallas_call(
+        forward_and_feed,
+        out_shape=[jax.ShapeDtypeStruct(s, F32) for s in outs],
+        in_specs=[VMEM] * 6 + [pl.BlockSpec(memory_space=pltpu.SMEM)] + [whole] * 9,
+        out_specs=[whole] * len(outs),
+        scratch_shapes=scratch,
+        compiler_params=PARAMS,
+        name="forward_and_feed",
+    )(*args)
+
+
+def attention_back(
+    grad, ctx, wp_h, wp_l, place, qkv_in, x_in, prob_in,
+    keep, send, dscore, dqkv_out,
+    qkv, x, prob, dctx, dqkv, grads, sems, prob_sems,
+):
+    loads = [pltpu.make_async_copy(a, b, sems.at[i]) for i, (a, b) in enumerate(((qkv_in, qkv), (x_in, x)))]
+    loads[0].start()
+    for step in range(WINS * GROUPS):
+        pltpu.make_async_copy(prob_in.at[step], prob.at[step], prob_sems.at[step]).start()
+    loads[1].start()
+    core = place[0]
     gm = split(grad[...])
     dctx[...] = dot3_deep(gm, (wp_h[...], wp_l[...]), NT)
     gproj = dot3_deep(split(ctx[...]), gm, TN)
     for b in range(3):
         grads[pl.ds(PROJ_AT + b, D, stride=3), :] = gproj[:, 128 * b : 128 * b + 128]
     dscore[...] = jnp.zeros_like(dscore)
+    loads[0].wait()
 
     def attend_back(step, carry):
         w, g = step // GROUPS, step % GROUPS
@@ -344,6 +392,7 @@
         k = split(qkv[rows, k_at])
         v = split(qkv[rows, v_at])
         d = split(stacked(dctx[rows, q_at]))
+        pltpu.make_async_copy(prob_in.at[step], prob.at[step], prob_sems.at[step]).wait()
         p = prob[step]
         dp = dot3_deep(d, v, NT)
         ds = p * (dp - jnp.sum(dp * p, axis=-1, keepdims=True))
@@ -355,17 +404,40 @@
         return carry
 
     lax.fori_loop(0, WINS * GROUPS, attend_back, 0, unroll=4)
-
-    kept[2].start()
-    dq = split(dqkv[...])
-    gqkv = dot3_deep(split(unit(x[...])[0]), dq, TN)
+    out = pltpu.make_async_copy(dqkv, dqkv_out, sems.at[2])
+    out.start()
+    loads[1].wait()
+    gqkv = dot3_deep(split(unit(x[...])[0]), split(dqkv[...]), TN)
     for b in range(9):
         grads[pl.ds(b, D, stride=9), :] = gqkv[:, 128 * b : 128 * b + 128]
-    start(*pieces[2])
-    for copy in kept:
-        copy.wait()
-    for what in pieces:
-        finish(*what)
+    for here, copy in ship(grads, (keep, send), core, ATT_HALF, sems.at[pl.ds(3, 2)]):
+        pl.when(here)(copy.start)
+    out.wait()
+    for here, copy in ship(grads, (keep, send), core, ATT_HALF, sems.at[pl.ds(3, 2)]):
+        pl.when(here)(copy.wait)
+
+
+def run_attention_back(grad, ctx, wp_h, wp_l, place, qkv, x, prob):
+    whole = pl.BlockSpec(memory_space=pl.ANY)
+    outs = [(ATT_HALF, 128), (ATT_HALF, 128), (GROUPS, PER * WT, WT), (TOK, 3 * D)]
+    return pl.pallas_call(
+        attention_back,
+        out_shape=[jax.ShapeDtypeStruct(s, F32) for s in outs],
+        in_specs=[VMEM] * 4 + [pl.BlockSpec(memory_space=pltpu.SMEM)] + [whole] * 3,
+        out_specs=[whole] * 2 + [VMEM, whole],
+        scratch_shapes=[
+            pltpu.VMEM((TOK, 3 * D), F32),
+            pltpu.VMEM((TOK, D), F32),
+            pltpu.VMEM(prob.shape, F32),
+            pltpu.VMEM((TOK, D), F32),
+            pltpu.VMEM((TOK, 3 * D), F32),
+            pltpu.VMEM((UP_AT, 128), F32),
+            pltpu.SemaphoreType.DMA((5,)),
+            pltpu.SemaphoreType.DMA((WINS * GROUPS,)),
+        ],
+        compiler_params=PARAMS,
+        name="attention_back",
+    )(grad, ctx, wp_h, wp_l, place, qkv, x, prob)
 
 
 def input_grad(x, grad, dqkv, wq_h, wq_l, o_l, o_e, o_s, o_c, total):
@@ -479,8 +551,83 @@
     return [(d, d ^ 1) for d in range(128)]
 
 
-def worker_pairs():
-    return [(core * 64 + q, d + core) for core in range(2) for q, d in enumerate(chip_order())]
+def worker_of(d):
+    return (d % 2) * 64 + d // 2
+
+
+def piece_rounds():
+    device = {worker_of(d): d for d in range(128)}
+    edges = []
+    for p in range(384):
+        worker, slot = (p, 0) if p < 128 else ((p - 128) // 2, 1 + p % 2)
+        edges.append((p // 3, p % 3, device[worker], slot))
+    rounds = []
+    while edges:
+        by_owner = {}
+        for e in edges:
+            by_owner.setdefault(e[0], []).append(e)
+        taken = {}
+
+        def place_owner(owner, seen):
+            for e in by_owner[owner]:
+                if e[2] not in seen:
+                    seen.add(e[2])
+                    if e[2] not in taken or place_owner(taken[e[2]][0], seen):
+                        taken[e[2]] = e
+                        return True
+            return False
+
+        for owner in range(128):
+            place_owner(owner, set())
+        chosen = sorted(taken.values())
+        rounds.append(chosen)
+        edges = [e for e in edges if e not in chosen]
+    return rounds
+
+
+def looked_up(values, me):
+    return lax.dynamic_slice_in_dim(jnp.asarray(values, jnp.int32), me, 1, 0)[0]
+
+
+def in_order(came, order, me):
+    stacked_parts = jnp.stack(came, axis=1)
+    picked = [
+        lax.dynamic_slice_in_dim(stacked_parts, looked_up([o[i] for o in order], me), 1, 1) for i in range(3)
+    ]
+    return jnp.concatenate(picked, axis=1)
+
+
+def send_moments(moments, me):
+    came = []
+    for chosen in piece_rounds():
+        piece = looked_up([e[1] for e in chosen], me)
+        value = lax.dynamic_slice_in_dim(moments, piece, 1, 1)[:, 0]
+        came.append(lax.ppermute(value, BOTH, [(e[0], e[2]) for e in chosen]))
+    return came
+
+
+def sorted_moments(came, me):
+    order = [[0] * 3 for _ in range(128)]
+    for r, chosen in enumerate(piece_rounds()):
+        for e in chosen:
+            order[e[2]][e[3]] = r
+    return in_order(came, order, me)
+
+
+def return_moments(moments, me):
+    rounds = piece_rounds()
+    came = []
+    for chosen in rounds:
+        slots = [0] * 128
+        for e in chosen:
+            slots[e[2]] = e[3]
+        value = lax.dynamic_slice_in_dim(moments, looked_up(slots, me), 1, 1)[:, 0]
+        came.append(lax.ppermute(value, BOTH, [(e[2], e[0]) for e in chosen]))
+    order = [[0] * 3 for _ in range(128)]
+    for r, chosen in enumerate(rounds):
+        for e in chosen:
+            order[e[0]][e[1]] = r
+    return in_order(came, order, me)
 
 
 def exchanged(value, groups):
@@ -530,85 +677,132 @@
 
 def merge(keep, came, line, line_came, out):
     for q in range(BATCH):
-        rows = slice(q * OWN, q * OWN + OWN)
-        out[q * BLOCK : q * BLOCK + OWN, :] = keep[rows, :] + came[rows, :]
-        out[q * BLOCK + OWN : (q + 1) * BLOCK, :] = line[q : q + 1, :] + line_came[q : q + 1, :]
+        rows = slice(q * OWN_ATT, q * OWN_ATT + OWN_ATT)
+        out[q * SUM_BLOCK : q * SUM_BLOCK + OWN_ATT, :] = keep[rows, :] + came[rows, :]
+        out[q * SUM_BLOCK + OWN_ATT : (q + 1) * SUM_BLOCK, :] = line[q : q + 1, :] + line_came[q : q + 1, :]
 
 
 def merged(keep, came, line, line_came):
-    halves = pl.BlockSpec((BATCH * OWN, 128), lambda i: (i, 0))
+    halves = pl.BlockSpec((BATCH * OWN_ATT, 128), lambda i: (i, 0))
     lines = pl.BlockSpec((BATCH, 128), lambda i: (i, 0))
     return pl.pallas_call(
         merge,
-        out_shape=jax.ShapeDtypeStruct((64 * BLOCK, 128), F32),
+        out_shape=jax.ShapeDtypeStruct((64 * SUM_BLOCK, 128), F32),
         grid=(64 // BATCH,),
         in_specs=[halves, halves, lines, lines],
-        out_specs=pl.BlockSpec((BATCH * BLOCK, 128), lambda i: (i, 0)),
+        out_specs=pl.BlockSpec((BATCH * SUM_BLOCK, 128), lambda i: (i, 0)),
         compiler_params=PARAMS,
         name="merge",
     )(keep, came, line, line_came)
 
 
-def adam(parts, weights, first, second, new, first_new, second_new, factor):
-    total = parts[0:BLOCK, :]
+def add(keep, came, out):
+    out[...] = keep[...] + came[...]
+
+
+def added(keep, came):
+    rows = pl.BlockSpec((MLP_HALF // 4, 128), lambda i: (i, 0))
+    return pl.pallas_call(
+        add,
+        out_shape=jax.ShapeDtypeStruct((MLP_HALF, 128), F32),
+        grid=(4,),
+        in_specs=[rows] * 2,
+        out_specs=rows,
+        compiler_params=PARAMS,
+        name="add",
+    )(keep, came)
+
+
+def adam(mlp, parts, weights, first, second, new, first_new, second_new, factor):
+    total = parts[0:SUM_BLOCK, :]
     for q in range(1, 64):
-        total = total + parts[q * BLOCK : q * BLOCK + BLOCK, :]
+        total = total + parts[q * SUM_BLOCK : q * SUM_BLOCK + SUM_BLOCK, :]
     total = total * factor
-    grad, line = total[:OWN], total[OWN:]
+    deep = mlp[0:OWN_MLP, :]
+    for q in range(1, 64):
+        deep = deep + mlp[q * OWN_MLP : q * OWN_MLP + OWN_MLP, :]
+    grad = jnp.concatenate([total[:OWN_ATT], deep * factor], axis=0)
     m = 0.9 * first[...] + 0.1 * grad
     s = 0.95 * second[...] + 0.05 * grad * grad
     first_new[...] = m
     second_new[...] = s
     fresh = weights[...] - 0.01 * m / (jnp.sqrt(s) + 1e-08)
-    fresh = jnp.concatenate([fresh, line], axis=0)
+    fresh = jnp.concatenate([fresh, total[OWN_ATT:]], axis=0)
     for q in range(64):
         new[q * BLOCK : q * BLOCK + BLOCK, :] = fresh
 
 
-def lay_out(place, blocks, *refs):
-    out = refs[-1]
+def lay_out(other, place, blocks, *refs):
+    out, att, mlp, sems = refs[-4:]
+    i = pl.program_id(0)
+    half = (1 - place[0]) if other else place[0]
     for q in range(BATCH):
-        out[q * OWN : q * OWN + OWN, :] = blocks[q * BLOCK : q * BLOCK + OWN, :]
-
-
-def lay_out_own(place, blocks, out, lines):
-    lay_out(place, blocks, out)
+        at = q * BLOCK
+        att[i, q * OWN_ATT : (q + 1) * OWN_ATT, :] = blocks[at : at + OWN_ATT, :]
+        mlp[i, q * OWN_MLP : (q + 1) * OWN_MLP, :] = blocks[at + OWN_ATT : at + OWN, :]
+
+    def copies(step):
+        rows, more = BATCH * OWN_ATT, BATCH * OWN_MLP
+        yield pltpu.make_async_copy(
+            att.at[step],
+            out.at[pl.ds(pl.multiple_of(half * ATT_HALF + step * rows, 8), rows)],
+            sems.at[0, step],
+        )
+        yield pltpu.make_async_copy(
+            mlp.at[step],
+            out.at[pl.ds(pl.multiple_of(UP_AT + half * MLP_HALF + step * more, 8), more)],
+            sems.at[1, step],
+        )
+
+    for copy in copies(i):
+        copy.start()
+
+    @pl.when(i == 64 // BATCH - 1)
+    def _():
+        for step in range(64 // BATCH):
+            for copy in copies(step):
+                copy.wait()
+
+
+def lay_out_own(place, blocks, lines, out, *scratch):
     for q in range(BATCH):
         lines[q : q + 1, :] = blocks[q * BLOCK + OWN : q * BLOCK + BLOCK, :]
-
-
-def own_half(place, blocks):
+    lay_out(False, place, blocks, out, *scratch)
+
+
+def half_weights(place, blocks, so_far):
     steps = 64 // BATCH
+    whole = pl.BlockSpec(memory_space=pl.ANY)
+    blocks_in = pl.BlockSpec((BATCH * BLOCK, 128), lambda i, spot: (i, 0))
+    weights_out = jax.ShapeDtypeStruct((ROWS, 128), F32)
+    scratch = [
+        pltpu.VMEM((steps, BATCH * OWN_ATT, 128), F32),
+        pltpu.VMEM((steps, BATCH * OWN_MLP, 128), F32),
+        pltpu.SemaphoreType.DMA((2, steps)),
+    ]
+    if so_far is None:
+        return pl.pallas_call(
+            lay_out_own,
+            out_shape=[jax.ShapeDtypeStruct((64, 128), F32), weights_out],
+            grid_spec=pltpu.PrefetchScalarGridSpec(
+                num_scalar_prefetch=1,
+                grid=(steps,),
+                in_specs=[blocks_in],
+                out_specs=[pl.BlockSpec((BATCH, 128), lambda i, spot: (i, 0)), whole],
+                scratch_shapes=scratch,
+            ),
+            compiler_params=PARAMS,
+            name="lay_out_own",
+        )(place, blocks)
     return pl.pallas_call(
-        lay_out_own,
-        out_shape=[jax.ShapeDtypeStruct((ROWS, 128), F32), jax.ShapeDtypeStruct((64, 128), F32)],
+        functools.partial(lay_out, True),
+        out_shape=weights_out,
         grid_spec=pltpu.PrefetchScalarGridSpec(
             num_scalar_prefetch=1,
             grid=(steps,),
-            in_specs=[pl.BlockSpec((BATCH * BLOCK, 128), lambda i, spot: (i, 0))],
-            out_specs=[
-                pl.BlockSpec((BATCH * OWN, 128), lambda i, spot: (spot[0] * steps + i, 0)),
-                pl.BlockSpec((BATCH, 128), lambda i, spot: (i, 0)),
-            ],
-        ),
-        compiler_params=PARAMS,
-        name="lay_out_own",
-    )(place, blocks)
-
-
-def other_half(place, blocks, so_far):
-    steps = 64 // BATCH
-    return pl.pallas_call(
-        lay_out,
-        out_shape=jax.ShapeDtypeStruct((ROWS, 128), F32),
-        grid_spec=pltpu.PrefetchScalarGridSpec(
-            num_scalar_prefetch=1,
-            grid=(steps,),
-            in_specs=[
-                pl.BlockSpec((BATCH * BLOCK, 128), lambda i, spot: (i, 0)),
-                pl.BlockSpec(memory_space=pl.ANY),
-            ],
-            out_specs=pl.BlockSpec((BATCH * OWN, 128), lambda i, spot: ((1 - spot[0]) * steps + i, 0)),
+            in_specs=[blocks_in, whole],
+            out_specs=whole,
+            scratch_shapes=scratch,
         ),
         input_output_aliases={2: 0},
         compiler_params=PARAMS,
@@ -626,42 +820,52 @@
     edges = edges_of(block_input, cotangent)
     core = lon_at % 2
     place = jnp.stack([core, (lat_at == 7).astype(jnp.int32)]).astype(jnp.int32)
-    keep, send, dscore, x, grad, dqkv = run_block(
+    me = lat_at * 16 + lon_at
+    keep, send, x, grad, qkv, prob, ctx = run_forward(
         (block_input, cotangent), edges, pairs, bias, region_ids, place
     )
     came = lax.ppermute(send, BOTH, core_swap())
+    _, first_moment, second_moment = lax.optimization_barrier((send, first_moment, second_moment))
+    moments = jnp.stack([first_moment, second_moment]).reshape(2, 3, OWN_ATT * 128)
+    moments = send_moments(moments, me)
+    worker = core * 64 + lat_at * 8 + lon_at // 2
+    own = jnp.concatenate(
+        [
+            lax.dynamic_slice_in_dim(flat, worker * OWN_ATT, OWN_ATT, 0),
+            lax.dynamic_slice_in_dim(flat, UP_AT + worker * OWN_MLP, OWN_MLP, 0),
+        ]
+    )
+    came, moments = lax.optimization_barrier((came, moments))
+    mlp_sum = added(keep, came)
+    mlp_parts = exchanged(mlp_sum.reshape(64, 1, OWN_MLP * 128), chip_groups())
+
+    _, qkv, ctx, grad = lax.optimization_barrier((mlp_sum, qkv, ctx, grad))
+    keep, send, dscore, dqkv = run_attention_back(grad, ctx, pairs[2], pairs[3], place, qkv, x, prob)
+    came = lax.ppermute(send, BOTH, core_swap())
     line = table_gradient(dscore, bias_index)
     line_came = lax.ppermute(line, BOTH, core_swap())
-    summed = merged(keep, came, line, line_came)
-    parts = exchanged(summed.reshape(64, 1, BLOCK * 128), chip_groups())
-
-    _, dqkv, first_moment, second_moment = lax.optimization_barrier(
-        (summed, dqkv, first_moment, second_moment)
-    )
+    att_sum = merged(keep, came, line, line_came)
+    att_sum, mlp_parts = lax.optimization_barrier((att_sum, mlp_parts))
+    att_parts = exchanged(att_sum.reshape(64, 1, SUM_BLOCK * 128), chip_groups())
+    _, own, moments = lax.optimization_barrier((att_sum, own, moments))
+    moments = sorted_moments(moments, me).reshape(2, OWN, 128)
+    new, first_new, second_new = pl.pallas_call(
+        functools.partial(adam, factor=factor),
+        out_shape=[jax.ShapeDtypeStruct((n, 128), F32) for n in (64 * BLOCK, OWN, OWN)],
+        in_specs=[VMEM] * 5,
+        out_specs=[VMEM] * 3,
+        compiler_params=PARAMS,
+        name="adam",
+    )(mlp_parts.reshape(MLP_HALF, 128), att_parts.reshape(64 * SUM_BLOCK, 128), own, moments[0], moments[1])
+    mine = exchanged(new.reshape(64, 1, BLOCK * 128), chip_groups())
+
+    _, dqkv, first_new, second_new = lax.optimization_barrier((new, dqkv, first_new, second_new))
     o_l, o_e, o_s, o_c = run_input_grad(x, grad, dqkv, pairs[0], pairs[1])
     from_west = around(o_e, "lon", 1)
     from_north = around(o_s, "lat", 1)
     from_corner = diagonal(o_c, 1)
-    pairs_of = worker_pairs()
-    moments = jnp.stack([first_moment.reshape(OWN, 128), second_moment.reshape(OWN, 128)])
-    moments = lax.ppermute(moments, BOTH, pairs_of)
-    parts, from_west, from_north, from_corner, moments = lax.optimization_barrier(
-        (parts, from_west, from_north, from_corner, moments)
-    )
-
-    shard = core * 64 + lat_at * 8 + lon_at // 2
-    own = lax.dynamic_slice_in_dim(flat, shard * OWN, OWN, 0)
-    new, first_new, second_new = pl.pallas_call(
-        functools.partial(adam, factor=factor),
-        out_shape=[jax.ShapeDtypeStruct((n, 128), F32) for n in (64 * BLOCK, OWN, OWN)],
-        in_specs=[VMEM] * 4,
-        out_specs=[VMEM] * 3,
-        compiler_params=PARAMS,
-        name="adam",
-    )(parts.reshape(64 * BLOCK, 128), own, moments[0], moments[1])
-    mine = exchanged(new.reshape(64, 1, BLOCK * 128), chip_groups())
-    back = [(b, a) for a, b in pairs_of]
-    moments = lax.ppermute(jnp.stack([first_new, second_new]), BOTH, back)
+    moments = jnp.stack([first_new, second_new]).reshape(2, 3, OWN_ATT * 128)
+    moments = return_moments(moments, me).reshape(2, -1)
     top = jnp.concatenate([from_corner[:, :SHIFT], from_north[:, SHIFT:]], axis=1)
     rest = jnp.concatenate([from_west[SHIFT:, :SHIFT], o_l[SHIFT:, SHIFT:]], axis=1)
     grad_input = jnp.concatenate([top, rest], axis=0)
@@ -669,17 +873,11 @@
 
     mine = mine.reshape(64 * BLOCK, 128)
     theirs = lax.ppermute(mine, BOTH, core_swap())
-    weights_new, table = own_half(place, mine)
+    table, weights_new = half_weights(place, mine, None)
     table_new = table[: HEADS * 5].reshape(5, HEADS, 128).transpose(1, 0, 2)
     table_new = table_new.reshape(HEADS, 640)[:, :BIAS]
-    weights_new = other_half(place, theirs, weights_new)
-    return (
-        grad_input,
-        weights_new.reshape(-1),
-        moments[0].reshape(-1),
-        moments[1].reshape(-1),
-        table_new,
-    )
+    weights_new = half_weights(place, theirs, weights_new)
+    return (grad_input, weights_new.reshape(-1), moments[0], moments[1], table_new)
 
 
 def solution(mesh):

time: 234 us -> 281 us (1.20)
  starting transfers between devices: 51.4 us -> 95.7 us
  waiting for transfers between devices: 75.5 us -> 34.8 us
  between operations: 0.84 us -> 16.3 us
  local copies, waits for them, and re-layouts: 11.3 us -> 24.5 us
  Pallas kernels: 92.7 us -> 105 us
    ppermute x2, waiting for transfers between devices: 33.5 us -> 0.01 us  [diagonal(): lax.ppermute(value, BOTH, [(a * lon + o, (a + by) % lat * lon + (o + by)...]
    ppermute x2 -> x6, starting transfers between devices: 7.62 us -> 33.1 us  [the longest x3 18.3 us: send_moments(): came.append(lax.ppermute(value, BOTH, [(e[0], e[2]) for e in chosen]))]
    ppermute x2 -> x6, waiting for transfers between devices: 40.9 us -> 17.5 us  [the longest x3 16.5 us: return_moments(): came.append(lax.ppermute(value, BOTH, [(e[2], e[0]) for e in chosen]))]
    all_to_all x2 -> x3, waiting for transfers between devices: 0.01 us -> 17.3 us  [exchanged(): lax.all_to_all(value, BOTH, 0, 0, axis_index_groups=groups, tiled=True)]
    pallas_call x4 -> x6, Pallas kernels: 61.1 us -> 72.8 us  [the longest x1 32 us: run_forward(): pl.pallas_call(forward_and_feed, out_shape=[jax.ShapeDtypeStruct(s, F32)...]
    ppermute x1, starting transfers between devices: 2.25 us -> 9.64 us  [per_device(): theirs = lax.ppermute(mine, BOTH, core_swap())]
    ppermute x2, starting transfers between devices: 9.01 us -> 15.8 us  [diagonal(): lax.ppermute(value, BOTH, [(a * lon + o, (a + by) % lat * lon + (o + by)...]
    dynamic_slice x1 -> x13, local copies, waits for them, and re-layouts: 1.46 us -> 7.13 us  [the longest x8 5.4 us: looked_up(): return lax.dynamic_slice_in_dim(jnp.asarray(values, jnp.int32), me, 1, 0)[0]]
  transfers between devices with their start and end apart: 13 -> 19, of which waited for: 3 -> 4; matrix products, arithmetic and copies ran while one was open for 4% -> 7% of each run, Pallas kernels for 13% -> 20%
where the time goes in v6:
time: 281 us; the launch traced here: 279 us
  Pallas kernels  105 us (37%)
  starting transfers between devices  95.7 us (34%)
  waiting for transfers between devices  34.8 us (12%)
  local copies, waits for them, and re-layouts  24.5 us (9%)
  between operations  16.3 us (6%)
    pallas_call x1, Pallas kernels, run_forward(): pl.pallas_call(forward_and_feed, out_shape=[jax.ShapeDtypeStruct(s, F32)...  32 us
    all_to_all x3, starting transfers between devices, exchanged(): lax.all_to_all(value, BOTH, 0, 0, axis_index_groups=groups, tiled=True)  25.4 us
    pallas_call x1, Pallas kernels, run_attention_back(): pl.pallas_call(attention_back, out_shape=[jax.ShapeDtypeStruct(s, F32) fo...  22 us
    ppermute x3, starting transfers between devices, send_moments(): came.append(lax.ppermute(value, BOTH, [(e[0], e[2]) for e in chosen]))  18.3 us
    all_to_all x3, waiting for transfers between devices, exchanged(): lax.all_to_all(value, BOTH, 0, 0, axis_index_groups=groups, tiled=True)  17.3 us
    ppermute x3, waiting for transfers between devices, return_moments(): came.append(lax.ppermute(value, BOTH, [(e[2], e[0]) for e in chosen]))  16.5 us
    ppermute x2, starting transfers between devices, diagonal(): lax.ppermute(value, BOTH, [(a * lon + o, (a + by) % lat * lon + (o + by)...  15.8 us
    ppermute x3, starting transfers between devices, return_moments(): came.append(lax.ppermute(value, BOTH, [(e[2], e[0]) for e in chosen]))  14.7 us
  transfers between devices with their start and end apart: 19, of which 4 were waited for; matrix products, arithmetic and copies ran while one was open for 7% of the time, Pallas kernels for 20%

profile of v6, /device:TPU:1, one launch (start us, length us, event | category | flops | bytes accessed | tf_op | source)
XLA Modules:
  0.0 278.5 jit_solution(18122403024208770590)
XLA Ops:
  7.9 5.9 %collective-permute-start.2 = (f32[2,6,8,384]{3,2,1,0:T(8,128)}, f32[2,6,8,384]{3,2,1,0:T(8,128)S(1)}, u32[]{:S(2)}, u32[]{:S(2)}) collective-permute-start(f32[2,6,8,384]{3,2,1,0:T(8,128)} %get-tuple-element.60), channel_id=1, source_target_pairs={{0,127},{1,112},{2,113},{3,114},{4,115},{5,116},{6,117},{7,118},{8... | collective-permute-start | bytes 442376 | tf_op jit(solution)/shard_map/ppermute | solution.py:644
  13.8 10.0 %prepare.1 = (bf16[384,1152]{1,0:T(8,128)(2,1)}, bf16[384,1152]{1,0:T(8,128)(2,1)}, bf16[384,384]{1,0:T(8,128)(2,1)}, bf16[384,384]{1,0:T(8,128)(2,1)}, bf16[6,3...) custom-call(f32[13824,128]{1,0:T(8,128)} %bitcast.50, ...), custom_call_target="tpu_custom_call" | custom-call | tf_op jit(solution)/shard_map/prepare/pallas_call | solution.py:142
  25.4 32.0 %forward_and_feed.1 = (f32[4608,128]{1,0:T(8,128)}, f32[4608,128]{1,0:T(8,128)}, f32[576,384]{1,0:T(8,128)}, f32[576,384]{1,0:T(8,128)}, f32[576,1152]{1,0:T(8,1...) custom-call(f32[24,24,384]{2,1,0:T(8,128)} %x_l.1, f32[24,24,384]{2,1,0:T(8,128)} %c_l.1, f32[2,24,8,384]{3,2,1,0:T(8,128)} %copy-done.3, ...), custom_call_target="tpu_custom_call" | custom-call | tf_op jit(solution)/shard_map/forward_and_feed/pallas_call | solution.py:355
  62.9 3.8 %collective-permute-start.4 = (f32[2,4608]{1,0:T(2,128)S(1)}, f32[2,4608]{1,0:T(2,128)S(1)}, u32[]{:S(2)}, u32[]{:S(2)}) collective-permute-start(f32[2,4608]{1,0:T(2,128)S(1)} %get-tuple-element.124), channel_id=1, source_target_pairs={{0,2},{1,8},{2,14},{3,20},{4,26},{5,32},{6,38},{7,44},{8,50},{9,56... | collective-permute-start | bytes 110600 | tf_op jit(solution)/shard_map/ppermute | solution.py:605
  66.7 4.1 %collective-permute-start.5 = (f32[2,4608]{1,0:T(2,128)S(1)}, f32[2,4608]{1,0:T(2,128)S(1)}, u32[]{:S(2)}, u32[]{:S(2)}) collective-permute-start(f32[2,4608]{1,0:T(2,128)S(1)} %get-tuple-element.125), channel_id=1, source_target_pairs={{0,0},{1,6},{2,12},{3,18},{4,24},{5,30},{6,36},{7,42},{8,48},{9,54... | collective-permute-start | bytes 110600 | tf_op jit(solution)/shard_map/ppermute | solution.py:605
  70.8 10.5 %collective-permute-start.6 = (f32[2,4608]{1,0:T(2,128)S(1)}, f32[2,4608]{1,0:T(2,128)S(1)}, u32[]{:S(2)}, u32[]{:S(2)}) collective-permute-start(f32[2,4608]{1,0:T(2,128)S(1)} %get-tuple-element.123), channel_id=1, source_target_pairs={{0,4},{1,10},{2,16},{3,22},{4,28},{5,34},{6,40},{7,46},{8,52},{9,5... | collective-permute-start | bytes 110600 | tf_op jit(solution)/shard_map/ppermute | solution.py:605
  84.3 4.4 %add.98 = f32[4608,128]{1,0:T(8,128)} custom-call(f32[4608,128]{1,0:T(8,128)} %get-tuple-element.70.keep, f32[4608,128]{1,0:T(8,128)} %copy-done.1), custom_call_target="tpu_custom_call" | custom-call | tf_op jit(solution)/shard_map/add/pallas_call | solution.py:705
  88.7 9.4 %all-to-all-start = ((f32[64,1,9216]{2,1,0:T(1,128)}), f32[64,1,9216]{2,1,0:T(1,128)S(1)}, u32[]{:S(2)}, u32[]{:S(2)}) async-start(f32[64,1,9216]{2,1,0:T(1,128)} %bitcast.56), calls=%async_computation | async-start | bytes 4718592 | tf_op jit(solution)/shard_map/all_to_all | solution.py:634
  98.1 22.0 %attention_back.1 = (f32[2304,128]{1,0:T(8,128)}, f32[2304,128]{1,0:T(8,128)}, f32[3,576,144]{2,1,0:T(8,128)}, f32[576,1152]{1,0:T(8,128)}) custom-call(f32[576,384]{1,0:T(8,128)} %get-tuple-element.78.grad, f32[576,384]{1,0:T(8,128)} %get-tuple-element.79.ctx, bf16[384,384]{1,0:T(8,128)(2,1)} %get-tuple-element.63.rest_2_.wp_h, ...), custom_call_target="tpu_custom_call" | custom-call | tf_op jit(solution)/shard_map/attention_back/pallas_call | solution.py:423
  128.5 8.9 %table_sum.1.line = f32[64,128]{1,0:T(8,128)} custom-call(f32[144,16,144]{2,1,0:T(8,128)} %pad.4.scores, s32[144,144]{1,0:T(8,128)} %index.3), custom_call_target="tpu_custom_call" | custom-call | tf_op jit(solution)/shard_map/table_sum/pallas_call | solution.py:531
  160.5 10.3 %all-to-all-start.1 = ((f32[64,1,4736]{2,1,0:T(1,128)}), f32[64,1,4736]{2,1,0:T(1,128)}, u32[]{:S(2)}, u32[]{:S(2)}) async-start(f32[64,1,4736]{2,1,0:T(1,128)} %bitcast.60), calls=%async_computation.1 | async-start | bytes 2424832 | tf_op jit(solution)/shard_map/all_to_all | solution.py:634
  172.4 17.3 %all-to-all-done.1 = f32[64,1,4736]{2,1,0:T(1,128)} async-done(((f32[64,1,4736]{2,1,0:T(1,128)}), f32[64,1,4736]{2,1,0:T(1,128)}, u32[]{:S(2)}, u32[]{:S(2)}) %all-to-all-start.1) | async-done | bytes 1212448 | tf_op jit(solution)/shard_map/all_to_all | solution.py:634
  189.7 4.2 %adam.1 = (f32[6976,128]{1,0:T(8,128)}, f32[108,128]{1,0:T(8,128)}, f32[108,128]{1,0:T(8,128)}) custom-call(f32[4608,128]{1,0:T(8,128)} %bitcast.57, f32[2368,128]{1,0:T(8,128)} %bitcast.13.parts, f32[108,128]{1,0:T(8,128)} %pad_maximum_fusion.4.weights, f32[108,128]{1,0:T(8,128)} %squeeze.75.first, f32[108,128]{1,0:T(8,128)} %squeeze.76.second), custom_call_target="tpu_custom_call" | custom-call | tf_op jit(solution)/shard_map/adam/pallas_call | solution.py:852
  195.6 5.7 %all-to-all-start.2 = ((f32[64,1,13952]{2,1,0:T(1,128)}), f32[64,1,13952]{2,1,0:T(1,128)}, u32[]{:S(2)}, u32[]{:S(2)}) async-start(f32[64,1,13952]{2,1,0:T(1,128)} %bitcast.61), calls=%async_computation.2 | async-start | bytes 7143424 | tf_op jit(solution)/shard_map/all_to_all | solution.py:634
  205.3 4.9 %collective-permute-start.10 = (f32[2,4608]{1,0:T(2,128)S(1)}, f32[2,4608]{1,0:T(2,128)S(1)}, u32[]{:S(2)}, u32[]{:S(2)}) collective-permute-start(f32[2,4608]{1,0:T(2,128)S(1)} %bitcast.72), channel_id=1, source_target_pairs={{0,0},{6,1},{12,2},{18,3},{24,4},{30,5},{36,6},{42,7},{48,8},{54,9... | collective-permute-start | bytes 110600 | tf_op jit(solution)/shard_map/ppermute | solution.py:625
  210.2 6.1 %collective-permute-start.11 = (f32[2,4608]{1,0:T(2,128)S(1)}, f32[2,4608]{1,0:T(2,128)S(1)}, u32[]{:S(2)}, u32[]{:S(2)}) collective-permute-start(f32[2,4608]{1,0:T(2,128)S(1)} %bitcast.74), channel_id=1, source_target_pairs={{4,0},{10,1},{16,2},{22,3},{28,4},{34,5},{40,6},{46,7},{52,8},{58,... | collective-permute-start | bytes 110600 | tf_op jit(solution)/shard_map/ppermute | solution.py:625
  216.3 6.5 %input_grad.1 = (f32[24,24,384]{2,1,0:T(8,128)}, f32[24,8,384]{2,1,0:T(8,128)}, f32[6,24,384]{2,1,0:T(8,128)}, f32[6,8,384]{2,1,0:T(8,128)}) custom-call(f32[576,384]{1,0:T(8,128)} %get-tuple-element.81.x_in.x, f32[576,384]{1,0:T(8,128)} %get-tuple-element.78.grad, f32[576,1152]{1,0:T(8,128)} %get-tuple-element.101.dqkv, ...), custom_call_target="tpu_custom_call" | custom-call | tf_op jit(solution)/shard_map/input_grad/pallas_call | solution.py:452
  223.9 4.1 %collective-permute-start.14 = (f32[24,8,384]{2,1,0:T(8,128)}, f32[24,8,384]{2,1,0:T(8,128)S(1)}, u32[]{:S(2)}, u32[]{:S(2)}) collective-permute-start(f32[24,8,384]{2,1,0:T(8,128)} %get-tuple-element.104), channel_id=1, source_target_pairs={{0,1},{1,2},{2,3},{3,4},{4,5},{5,6},{6,7},{7,8},{8,9},{9,10},{10,1... | collective-permute-start | bytes 884744 | tf_op jit(solution)/shard_map/ppermute | solution.py:639
  228.0 10.3 %collective-permute-done.9 = f32[2,4608]{1,0:T(2,128)S(1)} collective-permute-done((f32[2,4608]{1,0:T(2,128)S(1)}, f32[2,4608]{1,0:T(2,128)S(1)}, u32[]{:S(2)}, u32[]{:S(2)}) %collective-permute-start.9) | collective-permute-done | bytes 36896 | tf_op jit(solution)/shard_map/ppermute | solution.py:625
  238.3 9.9 %collective-permute-start.12 = (f32[6,8,384]{2,1,0:T(8,128)}, f32[6,8,384]{2,1,0:T(8,128)S(1)}, u32[]{:S(2)}, u32[]{:S(2)}) collective-permute-start(f32[6,8,384]{2,1,0:T(8,128)} %get-tuple-element.102), channel_id=1, source_target_pairs={{0,17},{1,18},{2,19},{3,20},{4,21},{5,22},{6,23},{7,24},{8,25},{9,... | collective-permute-start | bytes 221192 | tf_op jit(solution)/shard_map/ppermute | solution.py:644
  248.2 6.3 %collective-permute-done.10 = f32[2,4608]{1,0:T(2,128)S(1)} collective-permute-done((f32[2,4608]{1,0:T(2,128)S(1)}, f32[2,4608]{1,0:T(2,128)S(1)}, u32[]{:S(2)}, u32[]{:S(2)}) %collective-permute-start.10) | collective-permute-done | bytes 36896 | tf_op jit(solution)/shard_map/ppermute | solution.py:625
  255.7 9.6 %collective-permute-start.15 = (f32[6976,128]{1,0:T(8,128)}, f32[6976,128]{1,0:T(8,128)}, u32[]{:S(2)}, u32[]{:S(2)}) collective-permute-start(f32[6976,128]{1,0:T(8,128)} %bitcast.25.blocks), channel_id=1, source_target_pairs={{0,1},{1,0},{2,3},{3,2},{4,5},{5,4},{6,7},{7,6},{8,9},{9,8},{10,11... | collective-permute-start | bytes 10715144 | tf_op jit(solution)/shard_map/ppermute | solution.py:875
  265.3 5.6 %lay_out_own.1 = (f32[64,128]{1,0:T(8,128)}, f32[13824,128]{1,0:T(8,128)}) custom-call(s32[2]{0:T(128)} %pad_add_fusion.place, f32[6976,128]{1,0:T(8,128)} %bitcast.25.blocks), custom_call_target="tpu_custom_call" | custom-call | tf_op jit(solution)/shard_map/lay_out_own/pallas_call | solution.py:784
  273.3 5.0 %lay_out_other.1 = f32[13824,128]{1,0:T(8,128)} custom-call(s32[2]{0:T(128)} %pad_add_fusion.place, f32[6976,128]{1,0:T(8,128)} %collective-permute-done.15.blocks, f32[13824,128]{1,0:T(8,128)} %get-tuple-element.108.refs_0_), custom_call_target="tpu_custom_call", output_to_operand_aliasing={{}: (2, {})} | custom-call | tf_op jit(solution)/shard_map/lay_out_other/pallas_call | solution.py:797
  (107 shorter events, 45.6 us)
Async XLA Ops:
  2.9 21.5 %collective-permute-start = (f32[2,24,8,384]{3,2,1,0:T(8,128)}, f32[2,24,8,384]{3,2,1,0:T(8,128)S(1)}, u32[]{:S(2)}, u32[]{:S(2)}) collective-permute-start(f32[2,24,8,384]{3,2,1,0:T(8,128)} %get-tuple-element.58), channel_id=1, source_target_pairs={{0,15},{1,0},{2,1},{3,2},{4,3},{5,4},{6,5},{7,6},{8,7},{9,8},{10,9... | collective-permute-start | bytes 1769480 | tf_op jit(solution)/shard_map/ppermute | solution.py:639
  4.3 20.1 %collective-permute-start.1 = (f32[2,6,24,384]{3,2,1,0:T(8,128)}, f32[2,6,24,384]{3,2,1,0:T(8,128)S(1)}, u32[]{:S(2)}, u32[]{:S(2)}) collective-permute-start(f32[2,6,24,384]{3,2,1,0:T(8,128)} %get-tuple-element.59), channel_id=1, source_target_pairs={{0,112},{16,0},{32,16},{48,32},{64,48},{80,64},{96,80},{112,96},{1... | collective-permute-start | bytes 1327112 | tf_op jit(solution)/shard_map/ppermute | solution.py:639
  7.9 16.5 %collective-permute-start.2 = (f32[2,6,8,384]{3,2,1,0:T(8,128)}, f32[2,6,8,384]{3,2,1,0:T(8,128)S(1)}, u32[]{:S(2)}, u32[]{:S(2)}) collective-permute-start(f32[2,6,8,384]{3,2,1,0:T(8,128)} %get-tuple-element.60), channel_id=1, source_target_pairs={{0,127},{1,112},{2,113},{3,114},{4,115},{5,116},{6,117},{7,118},{8... | collective-permute-start | bytes 442376 | tf_op jit(solution)/shard_map/ppermute | solution.py:644
  25.4 32.1 %copy-start.17 = (s32[128]{0:T(128)S(1)}, s32[128]{0:T(128)}, u32[]{:S(2)}) copy-start(s32[128]{0:T(128)} %constant.76.clone) | copy-start | bytes 1540
  25.4 34.0 %copy-start.16 = (s32[128]{0:T(128)S(1)}, s32[128]{0:T(128)}, u32[]{:S(2)}) copy-start(s32[128]{0:T(128)} %constant.77.clone) | copy-start | bytes 1540
  25.4 37.2 %copy-start.6 = (f32[13824]{0:T(1024)S(1)}, f32[13824]{0:T(1024)}, u32[]{:S(2)}) copy-start(f32[13824]{0:T(1024)} %param.23) | copy-start | bytes 165892
  25.4 37.3 %copy-start.7 = (f32[13824]{0:T(1024)S(1)}, f32[13824]{0:T(1024)}, u32[]{:S(2)}) copy-start(f32[13824]{0:T(1024)} %param.24) | copy-start | bytes 165892
  57.5 24.9 %collective-permute-start.3 = (f32[4608,128]{1,0:T(8,128)}, f32[4608,128]{1,0:T(8,128)S(1)}, u32[]{:S(2)}, u32[]{:S(2)}) collective-permute-start(f32[4608,128]{1,0:T(8,128)} %get-tuple-element.71), channel_id=1, source_target_pairs={{0,1},{1,0},{2,3},{3,2},{4,5},{5,4},{6,7},{7,6},{8,9},{9,8},{10,11... | collective-permute-start | bytes 7077896 | tf_op jit(solution)/shard_map/ppermute | solution.py:827
  62.9 18.4 %collective-permute-start.4 = (f32[2,4608]{1,0:T(2,128)S(1)}, f32[2,4608]{1,0:T(2,128)S(1)}, u32[]{:S(2)}, u32[]{:S(2)}) collective-permute-start(f32[2,4608]{1,0:T(2,128)S(1)} %get-tuple-element.124), channel_id=1, source_target_pairs={{0,2},{1,8},{2,14},{3,20},{4,26},{5,32},{6,38},{7,44},{8,50},{9,56... | collective-permute-start | bytes 110600 | tf_op jit(solution)/shard_map/ppermute | solution.py:605
  66.7 14.6 %collective-permute-start.5 = (f32[2,4608]{1,0:T(2,128)S(1)}, f32[2,4608]{1,0:T(2,128)S(1)}, u32[]{:S(2)}, u32[]{:S(2)}) collective-permute-start(f32[2,4608]{1,0:T(2,128)S(1)} %get-tuple-element.125), channel_id=1, source_target_pairs={{0,0},{1,6},{2,12},{3,18},{4,24},{5,30},{6,36},{7,42},{8,48},{9,54... | collective-permute-start | bytes 110600 | tf_op jit(solution)/shard_map/ppermute | solution.py:605
  70.8 11.5 %collective-permute-start.6 = (f32[2,4608]{1,0:T(2,128)S(1)}, f32[2,4608]{1,0:T(2,128)S(1)}, u32[]{:S(2)}, u32[]{:S(2)}) collective-permute-start(f32[2,4608]{1,0:T(2,128)S(1)} %get-tuple-element.123), channel_id=1, source_target_pairs={{0,4},{1,10},{2,16},{3,22},{4,28},{5,34},{6,40},{7,46},{8,52},{9,5... | collective-permute-start | bytes 110600 | tf_op jit(solution)/shard_map/ppermute | solution.py:605
  88.7 69.3 %all-to-all-start = ((f32[64,1,9216]{2,1,0:T(1,128)}), f32[64,1,9216]{2,1,0:T(1,128)S(1)}, u32[]{:S(2)}, u32[]{:S(2)}) async-start(f32[64,1,9216]{2,1,0:T(1,128)} %bitcast.56), calls=%async_computation | async-start | bytes 4718592 | tf_op jit(solution)/shard_map/all_to_all | solution.py:634
  120.2 33.2 %collective-permute-start.7 = (f32[2304,128]{1,0:T(8,128)}, f32[2304,128]{1,0:T(8,128)S(1)}, u32[]{:S(2)}, u32[]{:S(2)}) collective-permute-start(f32[2304,128]{1,0:T(8,128)} %get-tuple-element.84), channel_id=1, source_target_pairs={{0,1},{1,0},{2,3},{3,2},{4,5},{5,4},{6,7},{7,6},{8,9},{9,8},{10,11... | collective-permute-start | bytes 3538952 | tf_op jit(solution)/shard_map/ppermute | solution.py:844
  137.4 16.0 %collective-permute-start.8 = (f32[64,128]{1,0:T(8,128)}, f32[64,128]{1,0:T(8,128)}, u32[]{:S(2)}, u32[]{:S(2)}) collective-permute-start(f32[64,128]{1,0:T(8,128)} %table_sum.1.line), channel_id=1, source_target_pairs={{0,1},{1,0},{2,3},{3,2},{4,5},{5,4},{6,7},{7,6},{8,9},{9,8},{10,11... | collective-permute-start | bytes 98312 | tf_op jit(solution)/shard_map/ppermute | solution.py:846
  158.0 31.7 %copy-start = (f32[64,1,9216]{2,1,0:T(1,128)}, f32[64,1,9216]{2,1,0:T(1,128)S(1)}, u32[]{:S(2)}) copy-start(f32[64,1,9216]{2,1,0:T(1,128)S(1)} %all-to-all-done) | copy-start | bytes 7077892
  160.5 29.2 %all-to-all-start.1 = ((f32[64,1,4736]{2,1,0:T(1,128)}), f32[64,1,4736]{2,1,0:T(1,128)}, u32[]{:S(2)}, u32[]{:S(2)}) async-start(f32[64,1,4736]{2,1,0:T(1,128)} %bitcast.60), calls=%async_computation.1 | async-start | bytes 2424832 | tf_op jit(solution)/shard_map/all_to_all | solution.py:634
  195.6 60.1 %all-to-all-start.2 = ((f32[64,1,13952]{2,1,0:T(1,128)}), f32[64,1,13952]{2,1,0:T(1,128)}, u32[]{:S(2)}, u32[]{:S(2)}) async-start(f32[64,1,13952]{2,1,0:T(1,128)} %bitcast.61), calls=%async_computation.2 | async-start | bytes 7143424 | tf_op jit(solution)/shard_map/all_to_all | solution.py:634
  201.5 36.8 %collective-permute-start.9 = (f32[2,4608]{1,0:T(2,128)S(1)}, f32[2,4608]{1,0:T(2,128)S(1)}, u32[]{:S(2)}, u32[]{:S(2)}) collective-permute-start(f32[2,4608]{1,0:T(2,128)S(1)} %bitcast.73), channel_id=1, source_target_pairs={{2,0},{8,1},{14,2},{20,3},{26,4},{32,5},{38,6},{44,7},{50,8},{56,9... | collective-permute-start | bytes 110600 | tf_op jit(solution)/shard_map/ppermute | solution.py:625
  205.3 49.2 %collective-permute-start.10 = (f32[2,4608]{1,0:T(2,128)S(1)}, f32[2,4608]{1,0:T(2,128)S(1)}, u32[]{:S(2)}, u32[]{:S(2)}) collective-permute-start(f32[2,4608]{1,0:T(2,128)S(1)} %bitcast.72), channel_id=1, source_target_pairs={{0,0},{6,1},{12,2},{18,3},{24,4},{30,5},{36,6},{42,7},{48,8},{54,9... | collective-permute-start | bytes 110600 | tf_op jit(solution)/shard_map/ppermute | solution.py:625
  210.2 44.3 %collective-permute-start.11 = (f32[2,4608]{1,0:T(2,128)S(1)}, f32[2,4608]{1,0:T(2,128)S(1)}, u32[]{:S(2)}, u32[]{:S(2)}) collective-permute-start(f32[2,4608]{1,0:T(2,128)S(1)} %bitcast.74), channel_id=1, source_target_pairs={{4,0},{10,1},{16,2},{22,3},{28,4},{34,5},{40,6},{46,7},{52,8},{58,... | collective-permute-start | bytes 110600 | tf_op jit(solution)/shard_map/ppermute | solution.py:625
  223.9 30.7 %collective-permute-start.14 = (f32[24,8,384]{2,1,0:T(8,128)}, f32[24,8,384]{2,1,0:T(8,128)S(1)}, u32[]{:S(2)}, u32[]{:S(2)}) collective-permute-start(f32[24,8,384]{2,1,0:T(8,128)} %get-tuple-element.104), channel_id=1, source_target_pairs={{0,1},{1,2},{2,3},{3,4},{4,5},{5,6},{6,7},{7,8},{8,9},{9,10},{10,1... | collective-permute-start | bytes 884744 | tf_op jit(solution)/shard_map/ppermute | solution.py:639
  228.0 26.6 %collective-permute-start.13 = (f32[6,24,384]{2,1,0:T(8,128)}, f32[6,24,384]{2,1,0:T(8,128)S(1)}, u32[]{:S(2)}, u32[]{:S(2)}) collective-permute-start(f32[6,24,384]{2,1,0:T(8,128)} %get-tuple-element.103), channel_id=1, source_target_pairs={{0,16},{16,32},{32,48},{48,64},{64,80},{80,96},{96,112},{112,0},{1... | collective-permute-start | bytes 663560 | tf_op jit(solution)/shard_map/ppermute | solution.py:639
  238.3 16.4 %collective-permute-start.12 = (f32[6,8,384]{2,1,0:T(8,128)}, f32[6,8,384]{2,1,0:T(8,128)S(1)}, u32[]{:S(2)}, u32[]{:S(2)}) collective-permute-start(f32[6,8,384]{2,1,0:T(8,128)} %get-tuple-element.102), channel_id=1, source_target_pairs={{0,17},{1,18},{2,19},{3,20},{4,21},{5,22},{6,23},{7,24},{8,25},{9,... | collective-permute-start | bytes 221192 | tf_op jit(solution)/shard_map/ppermute | solution.py:644
  255.7 17.6 %collective-permute-start.15 = (f32[6976,128]{1,0:T(8,128)}, f32[6976,128]{1,0:T(8,128)}, u32[]{:S(2)}, u32[]{:S(2)}) collective-permute-start(f32[6976,128]{1,0:T(8,128)} %bitcast.25.blocks), channel_id=1, source_target_pairs={{0,1},{1,0},{2,3},{3,2},{4,5},{5,4},{6,7},{7,6},{8,9},{9,8},{10,11... | collective-permute-start | bytes 10715144 | tf_op jit(solution)/shard_map/ppermute | solution.py:875
  (13 other events, 83.9 us)

commit v7 on v5

--- a/solution.py
+++ b/solution.py
@@ -31,7 +31,7 @@
 HALF = ROWS // 2
 OWN = ROWS // 128
 BLOCK = OWN + 1
-BATCH = 16
+BATCH = 32
 BIAS = 529
 BOTH = ("lat", "lon")
 F32 = jnp.float32
@@ -154,38 +154,50 @@
     )(flat, flat, flat, flat, table, index)
 
 
-def gather_windows(target, local, east, south, corner):
+INNER = TILE - SHIFT
+EDGE = 112
+CORNER = 40
+
+
+def window_rows():
     for wr in range(2):
         for wc in range(2):
             for r in range(WIN):
-                row = wr * WIN + r
-                at = (wr * 2 + wc) * WT + r * WIN
-                if row < TILE - SHIFT:
-                    near, far, k = local, east, row + SHIFT
-                else:
-                    near, far, k = south, corner, row - (TILE - SHIFT)
-                if wc == 0:
-                    target[at : at + WIN, :] = near[k, SHIFT : SHIFT + WIN, :]
-                else:
-                    target[at : at + SHIFT, :] = near[k, SHIFT + WIN : TILE, :]
-                    target[at + SHIFT : at + WIN, :] = far[k, 0:SHIFT, :]
+                yield (wr * 2 + wc) * WT + r * WIN, wc, wr * WIN + r
+
+
+def gather_windows(target, local, east, south, corner):
+    for at, wc, row in window_rows():
+        k, n = row + SHIFT, row - INNER
+        if wc == 0:
+            target[at : at + WIN, :] = (
+                local[k, SHIFT : SHIFT + WIN, :] if n < 0 else south[INNER * n : INNER * n + WIN, :]
+            )
+        else:
+            target[at : at + SHIFT, :] = (
+                local[k, SHIFT + WIN : TILE, :] if n < 0 else south[INNER * n + WIN : INNER * n + INNER, :]
+            )
+            target[at + SHIFT : at + WIN, :] = (
+                east[SHIFT * row : SHIFT * row + SHIFT, :] if n < 0 else corner[SHIFT * n : SHIFT * n + SHIFT, :]
+            )
 
 
 def scatter_windows(source, local, east, south, corner):
-    for wr in range(2):
-        for wc in range(2):
-            for r in range(WIN):
-                row = wr * WIN + r
-                at = (wr * 2 + wc) * WT + r * WIN
-                if row < TILE - SHIFT:
-                    near, far, k = local, east, row + SHIFT
-                else:
-                    near, far, k = south, corner, row - (TILE - SHIFT)
-                if wc == 0:
-                    near[k, SHIFT : SHIFT + WIN, :] = source[at : at + WIN, :]
-                else:
-                    near[k, SHIFT + WIN : TILE, :] = source[at : at + SHIFT, :]
-                    far[k, 0:SHIFT, :] = source[at + SHIFT : at + WIN, :]
+    for at, wc, row in window_rows():
+        k, n = row + SHIFT, row - INNER
+        near = source[at : at + (WIN if wc == 0 else SHIFT), :]
+        if n < 0:
+            first = SHIFT if wc == 0 else SHIFT + WIN
+            local[k, first : first + near.shape[0], :] = near
+        else:
+            first = INNER * n + (0 if wc == 0 else WIN)
+            south[first : first + near.shape[0], :] = near
+        if wc == 1:
+            far = source[at + SHIFT : at + WIN, :]
+            if n < 0:
+                east[SHIFT * row : SHIFT * row + SHIFT, :] = far
+            else:
+                corner[SHIFT * n : SHIFT * n + SHIFT, :] = far
 
 
 def head_lane():
@@ -376,7 +388,7 @@
 
 
 def run_input_grad(x, grad, dqkv, wq_h, wq_l):
-    halo = [(TILE, TILE, D), (TILE, 8, D), (SHIFT, TILE, D), (SHIFT, 8, D)]
+    halo = [(TILE, TILE, D), (EDGE, D), (EDGE, D), (CORNER, D)]
     return pl.pallas_call(
         input_grad,
         out_shape=[jax.ShapeDtypeStruct(s, F32) for s in halo],
@@ -424,8 +436,13 @@
     )(*args)
 
 
-def table_sum(scores, index, out, sums):
+def table_sum(by_head, index, out, sums, scores):
     sums[...] = jnp.zeros_like(sums)
+    for h in range(16):
+        if h < HEADS:
+            scores[:, h, :] = by_head[h // PER, (h % PER) * WT : (h % PER) * WT + WT, :]
+        else:
+            scores[:, h, :] = jnp.zeros((WT, WT), F32)
     column = lax.broadcasted_iota(jnp.int32, (128, WT), 0)
 
     def one(i):
@@ -454,17 +471,15 @@
 
 
 def table_gradient(dscore, index):
-    scores = dscore.reshape(HEADS, WT, WT).transpose(1, 0, 2)
-    scores = jnp.pad(scores, ((0, 0), (0, 4), (0, 0)))
     return pl.pallas_call(
         table_sum,
         out_shape=jax.ShapeDtypeStruct((64, 128), F32),
         in_specs=[VMEM] * 2,
         out_specs=VMEM,
-        scratch_shapes=[pltpu.VMEM((160, 128), F32)],
+        scratch_shapes=[pltpu.VMEM((160, 128), F32), pltpu.VMEM((WT, 16, WT), F32)],
         compiler_params=PARAMS,
         name="table_sum",
-    )(scores, index)
+    )(dscore, index)
 
 
 def chip_order():
@@ -505,27 +520,46 @@
     )
 
 
-def pack(x_east, x_south, c_east, c_south, east, south, corner):
-    for i, (e, t) in enumerate(((x_east, x_south), (c_east, c_south))):
-        east[i] = e[...]
-        south[i] = t[...]
-        corner[i] = t[:, 0:8, :]
+def pack(x, c, east, south, corner):
+    for i, tile in enumerate((x, c)):
+        for k in range(SHIFT, TILE):
+            east[i, SHIFT * (k - SHIFT) : SHIFT * (k - SHIFT) + SHIFT, :] = tile[k, 0:SHIFT, :]
+        for n in range(SHIFT):
+            south[i, INNER * n : INNER * n + INNER, :] = tile[n, SHIFT:TILE, :]
+            corner[i, SHIFT * n : SHIFT * n + SHIFT, :] = tile[n, 0:SHIFT, :]
 
 
 def edges_of(x, c):
-    east_in = pl.BlockSpec((TILE, 8, D), lambda i: (0, 0, 0))
-    south_in = pl.BlockSpec((SHIFT, TILE, D), lambda i: (0, 0, 0))
-    shapes = [(2, TILE, 8, D), (2, SHIFT, TILE, D), (2, SHIFT, 8, D)]
+    shapes = [(2, EDGE, D), (2, EDGE, D), (2, CORNER, D)]
     east, south, corner = pl.pallas_call(
         pack,
         out_shape=[jax.ShapeDtypeStruct(s, F32) for s in shapes],
-        grid=(1,),
-        in_specs=[east_in, south_in] * 2,
-        out_specs=[pl.BlockSpec(s, lambda i: (0, 0, 0, 0)) for s in shapes],
+        in_specs=[VMEM] * 2,
+        out_specs=[VMEM] * 3,
         compiler_params=PARAMS,
         name="pack",
-    )(x, x, c, c)
+    )(x, c)
     return around(east, "lon", -1), around(south, "lat", -1), diagonal(corner, -1)
+
+
+def unpack_edges(local, west, north, corner, out):
+    out[SHIFT:TILE, SHIFT:TILE, :] = local[SHIFT:TILE, SHIFT:TILE, :]
+    for k in range(SHIFT, TILE):
+        out[k, 0:SHIFT, :] = west[SHIFT * (k - SHIFT) : SHIFT * (k - SHIFT) + SHIFT, :]
+    for n in range(SHIFT):
+        out[n, SHIFT:TILE, :] = north[INNER * n : INNER * n + INNER, :]
+        out[n, 0:SHIFT, :] = corner[SHIFT * n : SHIFT * n + SHIFT, :]
+
+
+def with_edges(local, west, north, corner):
+    return pl.pallas_call(
+        unpack_edges,
+        out_shape=jax.ShapeDtypeStruct((TILE, TILE, D), F32),
+        in_specs=[VMEM] * 4,
+        out_specs=VMEM,
+        compiler_params=PARAMS,
+        name="unpack_edges",
+    )(local, west, north, corner)
 
 
 def merge(keep, came, line, line_came, out):
@@ -662,9 +696,7 @@
     mine = exchanged(new.reshape(64, 1, BLOCK * 128), chip_groups())
     back = [(b, a) for a, b in pairs_of]
     moments = lax.ppermute(jnp.stack([first_new, second_new]), BOTH, back)
-    top = jnp.concatenate([from_corner[:, :SHIFT], from_north[:, SHIFT:]], axis=1)
-    rest = jnp.concatenate([from_west[SHIFT:, :SHIFT], o_l[SHIFT:, SHIFT:]], axis=1)
-    grad_input = jnp.concatenate([top, rest], axis=0)
+    grad_input = with_edges(o_l, from_west, from_north, from_corner)
     mine, moments, grad_input = lax.optimization_barrier((mine, moments, grad_input))
 
     mine = mine.reshape(64 * BLOCK, 128)

time: 234 us -> 220 us (0.940)
  starting transfers between devices: 51.4 us -> 44.3 us
  local copies, waits for them, and re-layouts: 11.3 us -> 7 us
  waiting for transfers between devices: 75.5 us -> 72.7 us
    all_to_all x2, starting transfers between devices: 22.5 us -> 16.9 us  [exchanged(): lax.all_to_all(value, BOTH, 0, 0, axis_index_groups=groups, tiled=True)]
    reshape x1 -> x0, local copies, waits for them, and re-layouts: 2.54 us -> none  [table_gradient(): scores = dscore.reshape(HEADS, WT, WT).transpose(1, 0, 2)]
  transfers between devices with their start and end apart: 13 -> 13, of which waited for: 3 -> 4; matrix products, arithmetic and copies ran while one was open for 4% -> 2% of each run, Pallas kernels for 13% -> 15%
where the time goes in v7:
time: 220 us; the launch traced here: 219 us
  Pallas kernels  93.4 us (42%)
  waiting for transfers between devices  72.7 us (33%)
  starting transfers between devices  44.3 us (20%)
  local copies, waits for them, and re-layouts  7 us (3%)
    pallas_call x1, Pallas kernels, run_block(): pl.pallas_call(block_pass, out_shape=[jax.ShapeDtypeStruct(s, F32) for s...  45.7 us
    ppermute x1, waiting for transfers between devices, per_device(): moments = lax.ppermute(jnp.stack([first_new, second_new]), BOTH, back)  39.4 us
    ppermute x2, waiting for transfers between devices, diagonal(): lax.ppermute(value, BOTH, [(a * lon + o, (a + by) % lat * lon + (o + by)...  32.2 us
    all_to_all x2, starting transfers between devices, exchanged(): lax.all_to_all(value, BOTH, 0, 0, axis_index_groups=groups, tiled=True)  16.9 us
    pallas_call x1, Pallas kernels, prepared(): pl.pallas_call(prepare, out_shape=[jax.ShapeDtypeStruct(s, BF16) for s in...  9.89 us
    pallas_call x1, Pallas kernels, table_gradient(): pl.pallas_call(table_sum, out_shape=jax.ShapeDtypeStruct((64, 128), F32),...  9.77 us
    ppermute x4, starting transfers between devices, around(): lax.ppermute(value, axis, [(i, (i + by) % size) for i in range(size)])  9.43 us
    ppermute x2, starting transfers between devices, diagonal(): lax.ppermute(value, BOTH, [(a * lon + o, (a + by) % lat * lon + (o + by)...  9.01 us
  transfers between devices with their start and end apart: 13, of which 4 were waited for; matrix products, arithmetic and copies ran while one was open for 2% of the time, Pallas kernels for 15%

profile of v7, /device:TPU:1, one launch (start us, length us, event | category | flops | bytes accessed | tf_op | source)
XLA Modules:
  0.0 218.9 jit_solution(12528263624253279846)
XLA Ops:
  0.6 2.4 %pack.1 = (f32[2,112,384]{2,1,0:T(8,128)}, f32[2,112,384]{2,1,0:T(8,128)}, f32[2,40,384]{2,1,0:T(8,128)}) custom-call(f32[24,24,384]{2,1,0:T(8,128)} %x_l.1, f32[24,24,384]{2,1,0:T(8,128)} %c_l.1), custom_call_target="tpu_custom_call" | custom-call | tf_op jit(solution)/shard_map/pack/pallas_call | solution.py:534
  3.0 1.4 collective-permute-start
  4.5 3.6 %collective-permute-start.1 = (f32[2,112,384]{2,1,0:T(8,128)}, f32[2,112,384]{2,1,0:T(8,128)S(1)}, u32[]{:S(2)}, u32[]{:S(2)}) collective-permute-start(f32[2,112,384]{2,1,0:T(8,128)} %get-tuple-element.44), channel_id=1, source_target_pairs={{0,112},{16,0},{32,16},{48,32},{64,48},{80,64},{96,80},{112,96},{1... | collective-permute-start | bytes 1032200 | tf_op jit(solution)/shard_map/ppermute | solution.py:507
  8.0 5.9 %collective-permute-start.2 = (f32[2,40,384]{2,1,0:T(8,128)}, f32[2,40,384]{2,1,0:T(8,128)S(1)}, u32[]{:S(2)}, u32[]{:S(2)}) collective-permute-start(f32[2,40,384]{2,1,0:T(8,128)} %get-tuple-element.45), channel_id=1, source_target_pairs={{0,127},{1,112},{2,113},{3,114},{4,115},{5,116},{6,117},{7,118},{8... | collective-permute-start | bytes 368648 | tf_op jit(solution)/shard_map/ppermute | solution.py:512
  13.9 9.9 %prepare.1 = (bf16[384,1152]{1,0:T(8,128)(2,1)}, bf16[384,1152]{1,0:T(8,128)(2,1)}, bf16[384,384]{1,0:T(8,128)(2,1)}, bf16[384,384]{1,0:T(8,128)(2,1)}, bf16[6,3...) custom-call(f32[13824,128]{1,0:T(8,128)} %bitcast.28, ...), custom_call_target="tpu_custom_call" | custom-call | tf_op jit(solution)/shard_map/prepare/pallas_call | solution.py:138
  25.4 45.7 %block_pass.1 = (f32[6912,128]{1,0:T(8,128)}, f32[6912,128]{1,0:T(8,128)}, f32[3,576,144]{2,1,0:T(8,128)}, f32[576,384]{1,0:T(8,128)}, f32[576,384]{1,0:T(8,128)}, /*index=5*/f32[576,1152]{1,0:T(8,128)}) custom-call(f32[24,24,384]{2,1,0:T(8,128)} %x_l.1, f32[24,24,384]{2,1,0:T(8,128)} %c_l.1, f32[2,112,384]{2,1,0:T(8,128)} %copy-done.1, ...), custom_call_target="tpu_custom_call" | custom-call | tf_op jit(solution)/shard_map/block_pass/pallas_call | solution.py:428
  71.3 9.8 %table_sum.1.line = f32[64,128]{1,0:T(8,128)} custom-call(f32[3,576,144]{2,1,0:T(8,128)} %get-tuple-element.57.by_head, s32[144,144]{1,0:T(8,128)} %index.3), custom_call_target="tpu_custom_call" | custom-call | tf_op jit(solution)/shard_map/table_sum/pallas_call | solution.py:474
  83.2 1.2 copy-done
  84.4 4.5 %merge.1 = f32[6976,128]{1,0:T(8,128)} custom-call(f32[6912,128]{1,0:T(8,128)} %get-tuple-element.55.keep, f32[6912,128]{1,0:T(8,128)} %copy-done, f32[64,128]{1,0:T(8,128)} %table_sum.1.line, f32[64,128]{1,0:T(8,128)} %copy-done.11), custom_call_target="tpu_custom_call" | custom-call | tf_op jit(solution)/shard_map/merge/pallas_call | solution.py:575
  88.9 9.4 %all-to-all-start = ((f32[64,1,13952]{2,1,0:T(1,128)}), f32[64,1,13952]{2,1,0:T(1,128)}, u32[]{:S(2)}, u32[]{:S(2)}) async-start(f32[64,1,13952]{2,1,0:T(1,128)} %bitcast.33), calls=%async_computation | async-start | bytes 7143424 | tf_op jit(solution)/shard_map/all_to_all | solution.py:502
  98.4 6.4 %input_grad.1 = (f32[24,24,384]{2,1,0:T(8,128)}, f32[112,384]{1,0:T(8,128)}, f32[112,384]{1,0:T(8,128)}, f32[40,384]{1,0:T(8,128)}) custom-call(f32[576,384]{1,0:T(8,128)} %get-tuple-element.58.x, f32[576,384]{1,0:T(8,128)} %get-tuple-element.59.grad, f32[576,1152]{1,0:T(8,128)} %get-tuple-element.61.dqkv, bf16[384,1152]{1,0:T(8,128)(2,1)} %get-tuple-element.46.rest_0_.wq_h, ...), custom_call_target="tpu_custom_call" | custom-call | tf_op jit(solution)/shard_map/input_grad/pallas_call | solution.py:392
  104.8 3.2 %collective-permute-start.5 = (f32[112,384]{1,0:T(8,128)}, f32[112,384]{1,0:T(8,128)S(1)}, u32[]{:S(2)}, u32[]{:S(2)}) collective-permute-start(f32[112,384]{1,0:T(8,128)} %get-tuple-element.62), channel_id=1, source_target_pairs={{0,1},{1,2},{2,3},{3,4},{4,5},{5,6},{6,7},{7,8},{8,9},{9,10},{10,1... | collective-permute-start | bytes 516104 | tf_op jit(solution)/shard_map/ppermute | solution.py:507
  109.2 2.4 %collective-permute-start.8 = (f32[2,108,128]{2,1,0:T(8,128)S(1)}, f32[2,108,128]{2,1,0:T(8,128)S(1)}, u32[]{:S(2)}, u32[]{:S(2)}) collective-permute-start(f32[2,108,128]{2,1,0:T(8,128)S(1)} %pad_maximum_fusion), channel_id=1, source_target_pairs={{0,0},{1,2},{2,4},{3,6},{4,8},{5,10},{6,12},{7,14},{8,16},{9,18},{... | collective-permute-start | bytes 331784 | tf_op jit(solution)/shard_map/ppermute | solution.py:681
  111.7 3.1 %collective-permute-start.7 = (f32[40,384]{1,0:T(8,128)}, f32[40,384]{1,0:T(8,128)S(1)}, u32[]{:S(2)}, u32[]{:S(2)}) collective-permute-start(f32[40,384]{1,0:T(8,128)} %get-tuple-element.64), channel_id=1, source_target_pairs={{0,17},{1,18},{2,19},{3,20},{4,21},{5,22},{6,23},{7,24},{8,25},{9,... | collective-permute-start | bytes 184328 | tf_op jit(solution)/shard_map/ppermute | solution.py:512
  114.8 1.5 constant_dynamic-slice_fusion.weights
  116.2 32.1 %collective-permute-done.7.corner = f32[40,384]{1,0:T(8,128)S(1)} collective-permute-done((f32[40,384]{1,0:T(8,128)}, f32[40,384]{1,0:T(8,128)S(1)}, u32[]{:S(2)}, u32[]{:S(2)}) %collective-permute-start.7) | collective-permute-done | bytes 61472 | tf_op jit(solution)/shard_map/ppermute | solution.py:512
  149.2 4.2 %adam.1 = (f32[6976,128]{1,0:T(8,128)}, f32[108,128]{1,0:T(8,128)}, f32[108,128]{1,0:T(8,128)}) custom-call(f32[6976,128]{1,0:T(8,128)} %bitcast.6.parts, f32[108,128]{1,0:T(8,128)} %constant_dynamic-slice_fusion.weights, f32[108,128]{1,0:T(8,128)} %get-tuple-element.84.first, f32[108,128]{1,0:T(8,128)} %get-tuple-element.83.second), custom_call_target="tpu_custom_call" | custom-call | tf_op jit(solution)/shard_map/adam/pallas_call | solution.py:688
  153.4 7.6 %all-to-all-start.1 = ((f32[64,1,13952]{2,1,0:T(1,128)}), f32[64,1,13952]{2,1,0:T(1,128)}, u32[]{:S(2)}, u32[]{:S(2)}) async-start(f32[64,1,13952]{2,1,0:T(1,128)} %bitcast.35), calls=%async_computation.1 | async-start | bytes 7143424 | tf_op jit(solution)/shard_map/all_to_all | solution.py:502
  161.0 4.5 %collective-permute-start.9 = (f32[2,108,128]{2,1,0:T(8,128)S(1)}, f32[2,108,128]{2,1,0:T(8,128)S(1)}, u32[]{:S(2)}, u32[]{:S(2)}) collective-permute-start(f32[2,108,128]{2,1,0:T(8,128)S(1)} %pad_maximum_fusion.1), channel_id=1, source_target_pairs={{0,0},{2,1},{4,2},{6,3},{8,4},{10,5},{12,6},{14,7},{16,8},{18,9},{... | collective-permute-start | bytes 331784 | tf_op jit(solution)/shard_map/ppermute | solution.py:698
  165.5 2.3 %unpack_edges.1 = f32[24,24,384]{2,1,0:T(8,128)} custom-call(f32[24,24,384]{2,1,0:T(8,128)} %get-tuple-element.72.local, f32[112,384]{1,0:T(8,128)} %copy-done.3, f32[112,384]{1,0:T(8,128)} %copy-done.4, f32[40,384]{1,0:T(8,128)} %copy-done.6), custom_call_target="tpu_custom_call" | custom-call | tf_op jit(solution)/shard_map/unpack_edges/pallas_call | solution.py:555
  167.8 39.4 %collective-permute-done.9 = f32[2,108,128]{2,1,0:T(8,128)S(1)} collective-permute-done((f32[2,108,128]{2,1,0:T(8,128)S(1)}, f32[2,108,128]{2,1,0:T(8,128)S(1)}, u32[]{:S(2)}, u32[]{:S(2)}) %collective-permute-start.9) | collective-permute-done | bytes 110624 | tf_op jit(solution)/shard_map/ppermute | solution.py:698
  207.2 1.4 collective-permute-start.10
  208.6 4.1 %lay_out_own.1 = (f32[13824,128]{1,0:T(8,128)}, f32[64,128]{1,0:T(8,128)}) custom-call(s32[2]{0:T(128)} %pad_add_fusion.place, f32[6976,128]{1,0:T(8,128)} %bitcast.12.blocks), custom_call_target="tpu_custom_call" | custom-call | tf_op jit(solution)/shard_map/lay_out_own/pallas_call | solution.py:616
  214.9 4.1 %lay_out_other.1 = f32[13824,128]{1,0:T(8,128)} custom-call(s32[2]{0:T(128)} %pad_add_fusion.place, f32[6976,128]{1,0:T(8,128)} %collective-permute-done.10.blocks, f32[13824,128]{1,0:T(8,128)} %get-tuple-element.78.refs_0_), custom_call_target="tpu_custom_call", output_to_operand_aliasing={{}: (2, {})} | custom-call | tf_op jit(solution)/shard_map/lay_out_other/pallas_call | solution.py:635
  (46 shorter events, 8.0 us)
Async XLA Ops:
  3.0 21.5 %collective-permute-start = (f32[2,112,384]{2,1,0:T(8,128)}, f32[2,112,384]{2,1,0:T(8,128)S(1)}, u32[]{:S(2)}, u32[]{:S(2)}) collective-permute-start(f32[2,112,384]{2,1,0:T(8,128)} %get-tuple-element.43), channel_id=1, source_target_pairs={{0,15},{1,0},{2,1},{3,2},{4,3},{5,4},{6,5},{7,6},{8,7},{9,8},{10,9... | collective-permute-start | bytes 1032200 | tf_op jit(solution)/shard_map/ppermute | solution.py:507
  4.5 20.1 %collective-permute-start.1 = (f32[2,112,384]{2,1,0:T(8,128)}, f32[2,112,384]{2,1,0:T(8,128)S(1)}, u32[]{:S(2)}, u32[]{:S(2)}) collective-permute-start(f32[2,112,384]{2,1,0:T(8,128)} %get-tuple-element.44), channel_id=1, source_target_pairs={{0,112},{16,0},{32,16},{48,32},{64,48},{80,64},{96,80},{112,96},{1... | collective-permute-start | bytes 1032200 | tf_op jit(solution)/shard_map/ppermute | solution.py:507
  8.0 16.5 %collective-permute-start.2 = (f32[2,40,384]{2,1,0:T(8,128)}, f32[2,40,384]{2,1,0:T(8,128)S(1)}, u32[]{:S(2)}, u32[]{:S(2)}) collective-permute-start(f32[2,40,384]{2,1,0:T(8,128)} %get-tuple-element.45), channel_id=1, source_target_pairs={{0,127},{1,112},{2,113},{3,114},{4,115},{5,116},{6,117},{7,118},{8... | collective-permute-start | bytes 368648 | tf_op jit(solution)/shard_map/ppermute | solution.py:512
  24.5 0.6 copy-start.5
  24.5 0.8 copy-start.1
  24.5 0.9 copy-start.2
  71.2 11.4 %collective-permute-start.3 = (f32[6912,128]{1,0:T(8,128)}, f32[6912,128]{1,0:T(8,128)S(1)}, u32[]{:S(2)}, u32[]{:S(2)}) collective-permute-start(f32[6912,128]{1,0:T(8,128)} %get-tuple-element.56), channel_id=1, source_target_pairs={{0,1},{1,0},{2,3},{3,2},{4,5},{5,4},{6,7},{7,6},{8,9},{9,8},{10,11... | collective-permute-start | bytes 10616840 | tf_op jit(solution)/shard_map/ppermute | solution.py:666
  81.0 1.6 collective-permute-start.4
  82.6 1.8 copy-start
  88.9 59.5 %all-to-all-start = ((f32[64,1,13952]{2,1,0:T(1,128)}), f32[64,1,13952]{2,1,0:T(1,128)}, u32[]{:S(2)}, u32[]{:S(2)}) async-start(f32[64,1,13952]{2,1,0:T(1,128)} %bitcast.33), calls=%async_computation | async-start | bytes 7143424 | tf_op jit(solution)/shard_map/all_to_all | solution.py:502
  98.3 10.9 %copy-start.7 = (f32[13824]{0:T(1024)S(1)}, f32[13824]{0:T(1024)}, u32[]{:S(2)}) copy-start(f32[13824]{0:T(1024)} %param.12) | copy-start | bytes 165892
  98.3 10.9 %copy-start.8 = (f32[13824]{0:T(1024)S(1)}, f32[13824]{0:T(1024)}, u32[]{:S(2)}) copy-start(f32[13824]{0:T(1024)} %param.11) | copy-start | bytes 165892
  104.8 43.6 %collective-permute-start.5 = (f32[112,384]{1,0:T(8,128)}, f32[112,384]{1,0:T(8,128)S(1)}, u32[]{:S(2)}, u32[]{:S(2)}) collective-permute-start(f32[112,384]{1,0:T(8,128)} %get-tuple-element.62), channel_id=1, source_target_pairs={{0,1},{1,2},{2,3},{3,4},{4,5},{5,6},{6,7},{7,8},{8,9},{9,10},{10,1... | collective-permute-start | bytes 516104 | tf_op jit(solution)/shard_map/ppermute | solution.py:507
  108.0 40.4 %collective-permute-start.6 = (f32[112,384]{1,0:T(8,128)}, f32[112,384]{1,0:T(8,128)S(1)}, u32[]{:S(2)}, u32[]{:S(2)}) collective-permute-start(f32[112,384]{1,0:T(8,128)} %get-tuple-element.63), channel_id=1, source_target_pairs={{0,16},{16,32},{32,48},{48,64},{64,80},{80,96},{96,112},{112,0},{1... | collective-permute-start | bytes 516104 | tf_op jit(solution)/shard_map/ppermute | solution.py:507
  109.2 39.1 %collective-permute-start.8 = (f32[2,108,128]{2,1,0:T(8,128)S(1)}, f32[2,108,128]{2,1,0:T(8,128)S(1)}, u32[]{:S(2)}, u32[]{:S(2)}) collective-permute-start(f32[2,108,128]{2,1,0:T(8,128)S(1)} %pad_maximum_fusion), channel_id=1, source_target_pairs={{0,0},{1,2},{2,4},{3,6},{4,8},{5,10},{6,12},{7,14},{8,16},{9,18},{... | collective-permute-start | bytes 331784 | tf_op jit(solution)/shard_map/ppermute | solution.py:681
  111.7 36.7 %collective-permute-start.7 = (f32[40,384]{1,0:T(8,128)}, f32[40,384]{1,0:T(8,128)S(1)}, u32[]{:S(2)}, u32[]{:S(2)}) collective-permute-start(f32[40,384]{1,0:T(8,128)} %get-tuple-element.64), channel_id=1, source_target_pairs={{0,17},{1,18},{2,19},{3,20},{4,21},{5,22},{6,23},{7,24},{8,25},{9,... | collective-permute-start | bytes 184328 | tf_op jit(solution)/shard_map/ppermute | solution.py:512
  148.4 5.0 %copy-start.6 = (f32[40,384]{1,0:T(8,128)}, f32[40,384]{1,0:T(8,128)S(1)}, u32[]{:S(2)}) copy-start(f32[40,384]{1,0:T(8,128)S(1)} %collective-permute-done.7.corner) | copy-start | bytes 184324
  148.4 5.0 %copy-start.3 = (f32[112,384]{1,0:T(8,128)}, f32[112,384]{1,0:T(8,128)S(1)}, u32[]{:S(2)}) copy-start(f32[112,384]{1,0:T(8,128)S(1)} %collective-permute-done.5.west) | copy-start | bytes 516100
  148.4 5.0 %copy-start.4 = (f32[112,384]{1,0:T(8,128)}, f32[112,384]{1,0:T(8,128)S(1)}, u32[]{:S(2)}) copy-start(f32[112,384]{1,0:T(8,128)S(1)} %collective-permute-done.6.north) | copy-start | bytes 516100
  153.4 7.6 %copy-start.9 = (f32[108,128]{1,0:T(8,128)S(1)}, f32[108,128]{1,0:T(8,128)}, u32[]{:S(2)}) copy-start(f32[108,128]{1,0:T(8,128)} %get-tuple-element.70) | copy-start | bytes 165892
  153.4 7.6 %copy-start.10 = (f32[108,128]{1,0:T(8,128)S(1)}, f32[108,128]{1,0:T(8,128)}, u32[]{:S(2)}) copy-start(f32[108,128]{1,0:T(8,128)} %get-tuple-element.71) | copy-start | bytes 165892
  153.4 53.8 %all-to-all-start.1 = ((f32[64,1,13952]{2,1,0:T(1,128)}), f32[64,1,13952]{2,1,0:T(1,128)}, u32[]{:S(2)}, u32[]{:S(2)}) async-start(f32[64,1,13952]{2,1,0:T(1,128)} %bitcast.35), calls=%async_computation.1 | async-start | bytes 7143424 | tf_op jit(solution)/shard_map/all_to_all | solution.py:502
  161.0 46.2 %collective-permute-start.9 = (f32[2,108,128]{2,1,0:T(8,128)S(1)}, f32[2,108,128]{2,1,0:T(8,128)S(1)}, u32[]{:S(2)}, u32[]{:S(2)}) collective-permute-start(f32[2,108,128]{2,1,0:T(8,128)S(1)} %pad_maximum_fusion.1), channel_id=1, source_target_pairs={{0,0},{2,1},{4,2},{6,3},{8,4},{10,5},{12,6},{14,7},{16,8},{18,9},{... | collective-permute-start | bytes 331784 | tf_op jit(solution)/shard_map/ppermute | solution.py:698
  207.2 7.7 %collective-permute-start.10 = (f32[6976,128]{1,0:T(8,128)}, f32[6976,128]{1,0:T(8,128)}, u32[]{:S(2)}, u32[]{:S(2)}) collective-permute-start(f32[6976,128]{1,0:T(8,128)} %bitcast.12.blocks), channel_id=1, source_target_pairs={{0,1},{1,0},{2,3},{3,2},{4,5},{5,4},{6,7},{7,6},{8,9},{9,8},{10,11... | collective-permute-start | bytes 10715144 | tf_op jit(solution)/shard_map/ppermute | solution.py:703
  (1 other events, 0.6 us)

commit v8 on v7

--- a/solution.py
+++ b/solution.py
@@ -81,27 +81,11 @@
     return scale * (grad - mean - normed * along)
 
 
-STEPS = 6
-
-
-def prepare(qkv, proj, up, down, table, index, wq_h, wq_l, wp_h, wp_l, wu_h, wu_l, wd_h, wd_l, bias):
-    for flat, rows, blocks, high, low in (
-        (qkv, D // STEPS, 9, wq_h, wq_l),
-        (proj, D // STEPS, 3, wp_h, wp_l),
-        (down, FF // STEPS, 3, wd_h.at[0], wd_l.at[0]),
-    ):
-        for b in range(blocks):
-            h, l = split(flat[pl.ds(b, rows, stride=blocks), :])
-            high[:, 128 * b : 128 * b + 128] = h
-            low[:, 128 * b : 128 * b + 128] = l
-    for f in range(CHUNKS):
-        for b in range(2):
-            h, l = split(up[pl.ds(2 * f + b, D // STEPS, stride=12), :])
-            wu_h[f, :, 128 * b : 128 * b + 128] = h
-            wu_l[f, :, 128 * b : 128 * b + 128] = l
+def lookup(table, index, bias):
     lines = jnp.concatenate([table[...], jnp.zeros((HEADS, 640 - BIAS), F32)], axis=1)
-    for k in range(WT // 8 // STEPS):
-        at = pl.multiple_of((pl.program_id(0) * (WT // 8 // STEPS) + k) * 8, 8)
+
+    def rows_of(step, carry):
+        at = pl.multiple_of(step * 8, 8)
         columns = index[pl.ds(at, 8), :]
         columns = jnp.concatenate([columns, jnp.zeros((8, 256 - WT), jnp.int32)], axis=1)
         low = columns & 127
@@ -119,39 +103,27 @@
                 )
                 found = jnp.where(part == p, taken, found)
             bias[h // PER, pl.ds(pl.multiple_of((h % PER) * WT + at, 8), 8), :] = found[:, :WT]
-
-
-def prepared(flat, table, index):
-    shapes = [(D, 3 * D)] * 2 + [(D, D)] * 2 + [(CHUNKS, D, CHUNK)] * 2 + [(CHUNKS, CHUNK, D)] * 2
-    piece = D // STEPS
-    outs = [
-        *[pl.BlockSpec((piece, 3 * D), lambda i: (i, 0))] * 2,
-        *[pl.BlockSpec((piece, D), lambda i: (i, 0))] * 2,
-        *[pl.BlockSpec((CHUNKS, piece, CHUNK), lambda i: (0, i, 0))] * 2,
-        *[pl.BlockSpec((1, CHUNK, D), lambda i: (i, 0, 0))] * 2,
-        pl.BlockSpec((GROUPS, PER * WT, WT), lambda i: (0, 0, 0)),
-    ]
-
-    def part(at, rows):
-        return pl.BlockSpec((rows // STEPS, 128), lambda i: (at * STEPS // rows + i, 0))
-
+        return carry
+
+    lax.fori_loop(0, WT // 8, rows_of, 0, unroll=3)
+
+
+def bias_of_pairs(table, index):
     return pl.pallas_call(
-        prepare,
-        out_shape=[jax.ShapeDtypeStruct(s, BF16) for s in shapes]
-        + [jax.ShapeDtypeStruct((GROUPS, PER * WT, WT), F32)],
-        grid=(STEPS,),
-        in_specs=[
-            part(0, QKV_ROWS),
-            part(PROJ_AT, PROJ_ROWS),
-            part(UP_AT, MLP_ROWS),
-            part(DOWN_AT, MLP_ROWS),
-            pl.BlockSpec((HEADS, BIAS), lambda i: (0, 0)),
-            pl.BlockSpec((WT, WT), lambda i: (0, 0)),
-        ],
-        out_specs=outs,
-        compiler_params=PARAMS,
-        name="prepare",
-    )(flat, flat, flat, flat, table, index)
+        lookup,
+        out_shape=jax.ShapeDtypeStruct((GROUPS, PER * WT, WT), F32),
+        in_specs=[VMEM] * 2,
+        out_specs=VMEM,
+        compiler_params=PARAMS,
+        name="lookup",
+    )(table, index)
+
+
+def pair_of(flat, at, rows, blocks, high, low):
+    for b in range(blocks):
+        h, l = split(flat[pl.ds(at + b, rows, stride=blocks), :])
+        high[:, 128 * b : 128 * b + 128] = h
+        low[:, 128 * b : 128 * b + 128] = l
 
 
 INNER = TILE - SHIFT
@@ -239,15 +211,18 @@
 def block_pass(
     x_l, c_l, east, south, corner, region, place, *rest
 ):
-    stored, rest = rest[:9], rest[9:]
+    flat_in, bias = rest[:2]
+    rest = rest[2:]
     (
     keep, send, dscore, x_out, grad_out, dqkv_out,
     x, cot, qkv, ctx, prob, n2h, n2l, ch, cl, grad, dqkv, dctx, grads, label_row, label_col, norm2, scale2, sems,
     ) = rest[:-9]
     held = rest[-9:]
-    wq_h, wq_l, wp_h, wp_l, wu_h, wu_l, wd_h, wd_l, bias = held
-    loads = [pltpu.make_async_copy(a, b, sems.at[i]) for i, (a, b) in enumerate(zip(stored, held))]
-    for i in (0, 1, 8, 2, 3, 4, 5, 6, 7):
+    flat, wq_h, wq_l, wp_h, wp_l, wu_h, wu_l, wd_h, wd_l = held
+    loads = []
+    for i, (at, n) in enumerate(((0, QKV_ROWS), (QKV_ROWS, ROWS - QKV_ROWS))):
+        rows = pl.ds(at, n)
+        loads.append(pltpu.make_async_copy(flat_in.at[rows], flat.at[rows], sems.at[i]))
         loads[i].start()
     core = place[0]
 
@@ -280,10 +255,8 @@
     gather_windows(cot, c_l, east.at[1], south.at[1], corner.at[1])
     n1 = split(unit(x[...])[0])
     loads[0].wait()
-    loads[1].wait()
+    pair_of(flat, 0, D, 9, wq_h, wq_l)
     qkv[...] = dot3_deep(n1, (wq_h[...], wq_l[...]), NN)
-
-    loads[8].wait()
 
     def attend(step, carry):
         w, g = step // GROUPS, step % GROUPS
@@ -303,8 +276,8 @@
 
     lax.fori_loop(0, WINS * GROUPS, attend, 0, unroll=12)
 
-    for i in range(2, 8):
-        loads[i].wait()
+    loads[1].wait()
+    pair_of(flat, PROJ_AT, D, 3, wp_h, wp_l)
     mixed = x[...] + dot3_deep(split(ctx[...]), (wp_h[...], wp_l[...]), NN)
     norm2[...], scale2[...] = unit(mixed)
     n2h[...], n2l[...] = split(norm2[...])
@@ -312,6 +285,11 @@
     grad[...] = jnp.zeros_like(grad)
 
     def feed(f, carry):
+        pair_of(flat, DOWN_AT + 3 * CHUNK * f, CHUNK, 3, wd_h.at[f], wd_l.at[f])
+        for b in range(2):
+            h, l = split(flat[pl.ds(UP_AT + 2 * f + b, D, stride=12), :])
+            wu_h[f, :, 128 * b : 128 * b + 128] = h
+            wu_l[f, :, 128 * b : 128 * b + 128] = l
         n = (n2h[...], n2l[...])
         c = (ch[...], cl[...])
         up = (wu_h[f], wu_l[f])
@@ -380,27 +358,37 @@
         finish(*what)
 
 
-def input_grad(x, grad, dqkv, wq_h, wq_l, o_l, o_e, o_s, o_c, total):
+def input_grad(x, grad, dqkv, flat, o_l, o_e, o_s, o_c, total, wq_h, wq_l):
+    pair_of(flat, 0, D, 9, wq_h, wq_l)
     n1, scale1 = unit(x[...])
     back = dot3_deep(split(dqkv[...]), (wq_h[...], wq_l[...]), NT)
     total[...] = grad[...] + unit_back(back, n1, scale1)
     scatter_windows(total, o_l, o_e, o_s, o_c)
 
 
-def run_input_grad(x, grad, dqkv, wq_h, wq_l):
+def run_input_grad(x, grad, dqkv, flat):
     halo = [(TILE, TILE, D), (EDGE, D), (EDGE, D), (CORNER, D)]
+
+    def first(*shape):
+        return pl.BlockSpec(shape, lambda i: (0,) * len(shape))
+
     return pl.pallas_call(
         input_grad,
         out_shape=[jax.ShapeDtypeStruct(s, F32) for s in halo],
-        in_specs=[VMEM] * 5,
-        out_specs=[VMEM] * 4,
-        scratch_shapes=[pltpu.VMEM((TOK, D), F32)],
+        grid=(1,),
+        in_specs=[first(TOK, D), first(TOK, D), first(TOK, 3 * D), first(QKV_ROWS, 128)],
+        out_specs=[first(*s) for s in halo],
+        scratch_shapes=[
+            pltpu.VMEM((TOK, D), F32),
+            pltpu.VMEM((D, 3 * D), BF16),
+            pltpu.VMEM((D, 3 * D), BF16),
+        ],
         compiler_params=PARAMS,
         name="input_grad",
-    )(x, grad, dqkv, wq_h, wq_l)
-
-
-def run_block(tiles, edges, weights, bias, region, place):
+    )(x, grad, dqkv, flat)
+
+
+def run_block(tiles, edges, flat, bias, region, place):
     outs = [(HALF, 128), (HALF, 128), (GROUPS, PER * WT, WT), (TOK, D), (TOK, D), (TOK, 3 * D)]
     whole = pl.BlockSpec(memory_space=pl.ANY)
     scratch = [
@@ -422,13 +410,17 @@
         pltpu.VMEM((TOK, D), F32),
         pltpu.VMEM((TOK, 1), F32),
         pltpu.SemaphoreType.DMA((15,)),
-        *[pltpu.VMEM(a.shape, a.dtype) for a in (*weights, bias)],
+        pltpu.VMEM((ROWS, 128), F32),
+        *[pltpu.VMEM((D, 3 * D), BF16)] * 2,
+        *[pltpu.VMEM((D, D), BF16)] * 2,
+        *[pltpu.VMEM((CHUNKS, D, CHUNK), BF16)] * 2,
+        *[pltpu.VMEM((CHUNKS, CHUNK, D), BF16)] * 2,
     ]
-    args = (*tiles, *edges, region, place, *weights, bias)
+    args = (*tiles, *edges, region, place, flat, bias)
     return pl.pallas_call(
         block_pass,
         out_shape=[jax.ShapeDtypeStruct(s, F32) for s in outs],
-        in_specs=[VMEM] * 6 + [pl.BlockSpec(memory_space=pltpu.SMEM)] + [whole] * 9,
+        in_specs=[VMEM] * 6 + [pl.BlockSpec(memory_space=pltpu.SMEM)] + [whole, VMEM],
         out_specs=[whole] * 2 + [VMEM] + [whole] * 3,
         scratch_shapes=scratch,
         compiler_params=PARAMS,
@@ -656,12 +648,12 @@
     lat_at, lon_at = lax.axis_index("lat"), lax.axis_index("lon")
     factor = 1.0 / math.sqrt(TOK * 128)
     flat = weights.reshape(ROWS, 128)
-    *pairs, bias = prepared(flat, bias_table, bias_index)
+    bias = bias_of_pairs(bias_table, bias_index)
     edges = edges_of(block_input, cotangent)
     core = lon_at % 2
     place = jnp.stack([core, (lat_at == 7).astype(jnp.int32)]).astype(jnp.int32)
     keep, send, dscore, x, grad, dqkv = run_block(
-        (block_input, cotangent), edges, pairs, bias, region_ids, place
+        (block_input, cotangent), edges, flat, bias, region_ids, place
     )
     came = lax.ppermute(send, BOTH, core_swap())
     line = table_gradient(dscore, bias_index)
@@ -672,7 +664,7 @@
     _, dqkv, first_moment, second_moment = lax.optimization_barrier(
         (summed, dqkv, first_moment, second_moment)
     )
-    o_l, o_e, o_s, o_c = run_input_grad(x, grad, dqkv, pairs[0], pairs[1])
+    o_l, o_e, o_s, o_c = run_input_grad(x, grad, dqkv, flat)
     from_west = around(o_e, "lon", 1)
     from_north = around(o_s, "lat", 1)
     from_corner = diagonal(o_c, 1)

time: 220 us -> 221 us (level)
  starting transfers between devices: 44.3 us -> 50.5 us
  waiting for transfers between devices: 72.7 us -> 70.1 us
  Pallas kernels: 93.4 us -> 91 us
    ppermute x1, waiting for transfers between devices: 0.01 us -> 5 us  [per_device(): moments = lax.ppermute(moments, BOTH, pairs_of)]
    ppermute x2, waiting for transfers between devices: 32.2 us -> 27.6 us  [diagonal(): lax.ppermute(value, BOTH, [(a * lon + o, (a + by) % lat * lon + (o + by)...]
    all_to_all x2, starting transfers between devices: 16.9 us -> 21 us  [exchanged(): lax.all_to_all(value, BOTH, 0, 0, axis_index_groups=groups, tiled=True)]
    pallas_call x1, Pallas kernels: 9.89 us -> 6.44 us  [bias_of_pairs(): pl.pallas_call(lookup, out_shape=jax.ShapeDtypeStruct((GROUPS, PER * WT,...]
    ppermute x1, starting transfers between devices: 1.44 us -> 4.79 us  [per_device(): theirs = lax.ppermute(mine, BOTH, core_swap())]
    ppermute x4, starting transfers between devices: 9.43 us -> 6.19 us  [around(): lax.ppermute(value, axis, [(i, (i + by) % size) for i in range(size)])]
    ppermute x1, waiting for transfers between devices: 39.4 us -> 36.2 us  [per_device(): moments = lax.ppermute(jnp.stack([first_new, second_new]), BOTH, back)]
  transfers between devices with their start and end apart: 13 -> 13, of which waited for: 4 -> 5; matrix products, arithmetic and copies ran while one was open for 2% -> 2% of each run, Pallas kernels for 15% -> 13%
where the time goes in v8:
time: 221 us; the launch traced here: 220 us
  Pallas kernels  91 us (41%)
  waiting for transfers between devices  70.1 us (32%)
  starting transfers between devices  50.5 us (23%)
  local copies, waits for them, and re-layouts  6.96 us (3%)
    pallas_call x1, Pallas kernels, run_block(): pl.pallas_call(block_pass, out_shape=[jax.ShapeDtypeStruct(s, F32) for s...  46.6 us
    ppermute x1, waiting for transfers between devices, per_device(): moments = lax.ppermute(jnp.stack([first_new, second_new]), BOTH, back)  36.2 us
    ppermute x2, waiting for transfers between devices, diagonal(): lax.ppermute(value, BOTH, [(a * lon + o, (a + by) % lat * lon + (o + by)...  27.6 us
    all_to_all x2, starting transfers between devices, exchanged(): lax.all_to_all(value, BOTH, 0, 0, axis_index_groups=groups, tiled=True)  21 us
    ppermute x2, starting transfers between devices, diagonal(): lax.ppermute(value, BOTH, [(a * lon + o, (a + by) % lat * lon + (o + by)...  9.86 us
    pallas_call x1, Pallas kernels, table_gradient(): pl.pallas_call(table_sum, out_shape=jax.ShapeDtypeStruct((64, 128), F32),...  9.78 us
    pallas_call x1, Pallas kernels, run_input_grad(): pl.pallas_call(input_grad, out_shape=[jax.ShapeDtypeStruct(s, F32) for s...  6.65 us
    pallas_call x1, Pallas kernels, bias_of_pairs(): pl.pallas_call(lookup, out_shape=jax.ShapeDtypeStruct((GROUPS, PER * WT,...  6.44 us
  transfers between devices with their start and end apart: 13, of which 5 were waited for; matrix products, arithmetic and copies ran while one was open for 2% of the time, Pallas kernels for 13%

profile of v8, /device:TPU:1, one launch (start us, length us, event | category | flops | bytes accessed | tf_op | source)
XLA Modules:
  0.0 220.0 jit_solution(5369451560419550166)
XLA Ops:
  0.6 2.4 %pack.1 = (f32[2,112,384]{2,1,0:T(8,128)}, f32[2,112,384]{2,1,0:T(8,128)}, f32[2,40,384]{2,1,0:T(8,128)}) custom-call(f32[24,24,384]{2,1,0:T(8,128)} %x_l.1, f32[24,24,384]{2,1,0:T(8,128)} %c_l.1), custom_call_target="tpu_custom_call" | custom-call | tf_op jit(solution)/shard_map/pack/pallas_call | solution.py:526
  3.0 1.4 collective-permute-start
  4.5 3.6 %collective-permute-start.1 = (f32[2,112,384]{2,1,0:T(8,128)}, f32[2,112,384]{2,1,0:T(8,128)S(1)}, u32[]{:S(2)}, u32[]{:S(2)}) collective-permute-start(f32[2,112,384]{2,1,0:T(8,128)} %get-tuple-element.35), channel_id=1, source_target_pairs={{0,112},{16,0},{32,16},{48,32},{64,48},{80,64},{96,80},{112,96},{1... | collective-permute-start | bytes 1032200 | tf_op jit(solution)/shard_map/ppermute | solution.py:499
  8.0 5.9 %collective-permute-start.2 = (f32[2,40,384]{2,1,0:T(8,128)}, f32[2,40,384]{2,1,0:T(8,128)S(1)}, u32[]{:S(2)}, u32[]{:S(2)}) collective-permute-start(f32[2,40,384]{2,1,0:T(8,128)} %get-tuple-element.36), channel_id=1, source_target_pairs={{0,127},{1,112},{2,113},{3,114},{4,115},{5,116},{6,117},{7,118},{8... | collective-permute-start | bytes 368648 | tf_op jit(solution)/shard_map/ppermute | solution.py:504
  14.0 6.4 %lookup.1.rest_1_ = f32[3,576,144]{2,1,0:T(8,128)} custom-call(f32[12,529]{1,0:T(8,128)} %table.1, s32[144,144]{1,0:T(8,128)} %index.3), custom_call_target="tpu_custom_call" | custom-call | tf_op jit(solution)/shard_map/lookup/pallas_call | solution.py:112
  21.9 46.6 %block_pass.1 = (f32[6912,128]{1,0:T(8,128)}, f32[6912,128]{1,0:T(8,128)}, f32[3,576,144]{2,1,0:T(8,128)}, f32[576,384]{1,0:T(8,128)}, f32[576,384]{1,0:T(8,128)}, /*index=5*/f32[576,1152]{1,0:T(8,128)}) custom-call(f32[24,24,384]{2,1,0:T(8,128)} %x_l.1, f32[24,24,384]{2,1,0:T(8,128)} %c_l.1, f32[2,112,384]{2,1,0:T(8,128)} %copy-done.1, ...), custom_call_target="tpu_custom_call" | custom-call | tf_op jit(solution)/shard_map/block_pass/pallas_call | solution.py:420
  68.9 9.8 %table_sum.1.line = f32[64,128]{1,0:T(8,128)} custom-call(f32[3,576,144]{2,1,0:T(8,128)} %get-tuple-element.39.by_head, s32[144,144]{1,0:T(8,128)} %index.3), custom_call_target="tpu_custom_call" | custom-call | tf_op jit(solution)/shard_map/table_sum/pallas_call | solution.py:466
  78.8 1.2 collective-permute-done.4.line_came
  81.9 4.5 %merge.1 = f32[6976,128]{1,0:T(8,128)} custom-call(f32[6912,128]{1,0:T(8,128)} %get-tuple-element.37.keep, f32[6912,128]{1,0:T(8,128)} %copy-done, f32[64,128]{1,0:T(8,128)} %table_sum.1.line, f32[64,128]{1,0:T(8,128)} %copy-done.11), custom_call_target="tpu_custom_call" | custom-call | tf_op jit(solution)/shard_map/merge/pallas_call | solution.py:567
  86.4 13.0 %all-to-all-start = ((f32[64,1,13952]{2,1,0:T(1,128)}), f32[64,1,13952]{2,1,0:T(1,128)}, u32[]{:S(2)}, u32[]{:S(2)}) async-start(f32[64,1,13952]{2,1,0:T(1,128)} %bitcast.31), calls=%async_computation | async-start | bytes 7143424 | tf_op jit(solution)/shard_map/all_to_all | solution.py:494
  99.4 6.7 %input_grad.1 = (f32[24,24,384]{2,1,0:T(8,128)}, f32[112,384]{1,0:T(8,128)}, f32[112,384]{1,0:T(8,128)}, f32[40,384]{1,0:T(8,128)}) custom-call(f32[576,384]{1,0:T(8,128)} %get-tuple-element.40.x, f32[576,384]{1,0:T(8,128)} %get-tuple-element.41.grad, f32[576,1152]{1,0:T(8,128)} %get-tuple-element.43.dqkv, f32[13824,128]{1,0:T(8,128)} %bitcast.29), custom_call_target="tpu_custom_call" | custom-call | tf_op jit(solution)/shard_map/input_grad/pallas_call | solution.py:375
  106.1 3.9 %collective-permute-start.7 = (f32[40,384]{1,0:T(8,128)}, f32[40,384]{1,0:T(8,128)S(1)}, u32[]{:S(2)}, u32[]{:S(2)}) collective-permute-start(f32[40,384]{1,0:T(8,128)} %get-tuple-element.46), channel_id=1, source_target_pairs={{0,17},{1,18},{2,19},{3,20},{4,21},{5,22},{6,23},{7,24},{8,25},{9,... | collective-permute-start | bytes 184328 | tf_op jit(solution)/shard_map/ppermute | solution.py:504
  111.2 3.8 %collective-permute-start.8 = (f32[2,108,128]{2,1,0:T(8,128)S(1)}, f32[2,108,128]{2,1,0:T(8,128)S(1)}, u32[]{:S(2)}, u32[]{:S(2)}) collective-permute-start(f32[2,108,128]{2,1,0:T(8,128)S(1)} %pad_maximum_fusion), channel_id=1, source_target_pairs={{0,0},{1,2},{2,4},{3,6},{4,8},{5,10},{6,12},{7,14},{8,16},{9,18},{... | collective-permute-start | bytes 331784 | tf_op jit(solution)/shard_map/ppermute | solution.py:673
  115.0 1.5 constant_dynamic-slice_fusion.weights
  116.5 27.6 %collective-permute-done.7.corner = f32[40,384]{1,0:T(8,128)S(1)} collective-permute-done((f32[40,384]{1,0:T(8,128)}, f32[40,384]{1,0:T(8,128)S(1)}, u32[]{:S(2)}, u32[]{:S(2)}) %collective-permute-start.7) | collective-permute-done | bytes 61472 | tf_op jit(solution)/shard_map/ppermute | solution.py:504
  144.0 5.0 %collective-permute-done.8 = f32[2,108,128]{2,1,0:T(8,128)S(1)} collective-permute-done((f32[2,108,128]{2,1,0:T(8,128)S(1)}, f32[2,108,128]{2,1,0:T(8,128)S(1)}, u32[]{:S(2)}, u32[]{:S(2)}) %collective-permute-start.8) | collective-permute-done | bytes 110624 | tf_op jit(solution)/shard_map/ppermute | solution.py:673
  149.8 4.2 %adam.1 = (f32[6976,128]{1,0:T(8,128)}, f32[108,128]{1,0:T(8,128)}, f32[108,128]{1,0:T(8,128)}) custom-call(f32[6976,128]{1,0:T(8,128)} %bitcast.6.parts, f32[108,128]{1,0:T(8,128)} %constant_dynamic-slice_fusion.weights, f32[108,128]{1,0:T(8,128)} %get-tuple-element.66.first, f32[108,128]{1,0:T(8,128)} %get-tuple-element.65.second), custom_call_target="tpu_custom_call" | custom-call | tf_op jit(solution)/shard_map/adam/pallas_call | solution.py:680
  154.0 8.0 %all-to-all-start.1 = ((f32[64,1,13952]{2,1,0:T(1,128)}), f32[64,1,13952]{2,1,0:T(1,128)}, u32[]{:S(2)}, u32[]{:S(2)}) async-start(f32[64,1,13952]{2,1,0:T(1,128)} %bitcast.33), calls=%async_computation.1 | async-start | bytes 7143424 | tf_op jit(solution)/shard_map/all_to_all | solution.py:494
  162.1 4.3 %collective-permute-start.9 = (f32[2,108,128]{2,1,0:T(8,128)S(1)}, f32[2,108,128]{2,1,0:T(8,128)S(1)}, u32[]{:S(2)}, u32[]{:S(2)}) collective-permute-start(f32[2,108,128]{2,1,0:T(8,128)S(1)} %pad_maximum_fusion.1), channel_id=1, source_target_pairs={{0,0},{2,1},{4,2},{6,3},{8,4},{10,5},{12,6},{14,7},{16,8},{18,9},{... | collective-permute-start | bytes 331784 | tf_op jit(solution)/shard_map/ppermute | solution.py:690
  166.4 2.3 %unpack_edges.1 = f32[24,24,384]{2,1,0:T(8,128)} custom-call(f32[24,24,384]{2,1,0:T(8,128)} %get-tuple-element.54.local, f32[112,384]{1,0:T(8,128)} %copy-done.3, f32[112,384]{1,0:T(8,128)} %copy-done.4, f32[40,384]{1,0:T(8,128)} %copy-done.6), custom_call_target="tpu_custom_call" | custom-call | tf_op jit(solution)/shard_map/unpack_edges/pallas_call | solution.py:547
  168.7 36.2 %collective-permute-done.9 = f32[2,108,128]{2,1,0:T(8,128)S(1)} collective-permute-done((f32[2,108,128]{2,1,0:T(8,128)S(1)}, f32[2,108,128]{2,1,0:T(8,128)S(1)}, u32[]{:S(2)}, u32[]{:S(2)}) %collective-permute-start.9) | collective-permute-done | bytes 110624 | tf_op jit(solution)/shard_map/ppermute | solution.py:690
  204.9 4.8 %collective-permute-start.10 = (f32[6976,128]{1,0:T(8,128)}, f32[6976,128]{1,0:T(8,128)}, u32[]{:S(2)}, u32[]{:S(2)}) collective-permute-start(f32[6976,128]{1,0:T(8,128)} %bitcast.12.blocks), channel_id=1, source_target_pairs={{0,1},{1,0},{2,3},{3,2},{4,5},{5,4},{6,7},{7,6},{8,9},{9,8},{10,11... | collective-permute-start | bytes 10715144 | tf_op jit(solution)/shard_map/ppermute | solution.py:695
  209.7 4.1 %lay_out_own.1 = (f32[13824,128]{1,0:T(8,128)}, f32[64,128]{1,0:T(8,128)}) custom-call(s32[2]{0:T(128)} %pad_add_fusion.place, f32[6976,128]{1,0:T(8,128)} %bitcast.12.blocks), custom_call_target="tpu_custom_call" | custom-call | tf_op jit(solution)/shard_map/lay_out_own/pallas_call | solution.py:608
  215.9 4.1 %lay_out_other.1 = f32[13824,128]{1,0:T(8,128)} custom-call(s32[2]{0:T(128)} %pad_add_fusion.place, f32[6976,128]{1,0:T(8,128)} %collective-permute-done.10.blocks, f32[13824,128]{1,0:T(8,128)} %get-tuple-element.60.refs_0_), custom_call_target="tpu_custom_call", output_to_operand_aliasing={{}: (2, {})} | custom-call | tf_op jit(solution)/shard_map/lay_out_other/pallas_call | solution.py:627
  (46 shorter events, 8.0 us)
Async XLA Ops:
  3.0 17.9 %collective-permute-start = (f32[2,112,384]{2,1,0:T(8,128)}, f32[2,112,384]{2,1,0:T(8,128)S(1)}, u32[]{:S(2)}, u32[]{:S(2)}) collective-permute-start(f32[2,112,384]{2,1,0:T(8,128)} %get-tuple-element.34), channel_id=1, source_target_pairs={{0,15},{1,0},{2,1},{3,2},{4,3},{5,4},{6,5},{7,6},{8,7},{9,8},{10,9... | collective-permute-start | bytes 1032200 | tf_op jit(solution)/shard_map/ppermute | solution.py:499
  4.5 16.5 %collective-permute-start.1 = (f32[2,112,384]{2,1,0:T(8,128)}, f32[2,112,384]{2,1,0:T(8,128)S(1)}, u32[]{:S(2)}, u32[]{:S(2)}) collective-permute-start(f32[2,112,384]{2,1,0:T(8,128)} %get-tuple-element.35), channel_id=1, source_target_pairs={{0,112},{16,0},{32,16},{48,32},{64,48},{80,64},{96,80},{112,96},{1... | collective-permute-start | bytes 1032200 | tf_op jit(solution)/shard_map/ppermute | solution.py:499
  8.0 12.9 %collective-permute-start.2 = (f32[2,40,384]{2,1,0:T(8,128)}, f32[2,40,384]{2,1,0:T(8,128)S(1)}, u32[]{:S(2)}, u32[]{:S(2)}) collective-permute-start(f32[2,40,384]{2,1,0:T(8,128)} %get-tuple-element.36), channel_id=1, source_target_pairs={{0,127},{1,112},{2,113},{3,114},{4,115},{5,116},{6,117},{7,118},{8... | collective-permute-start | bytes 368648 | tf_op jit(solution)/shard_map/ppermute | solution.py:504
  21.0 0.7 copy-start.5
  21.0 0.8 copy-start.1
  21.0 0.9 copy-start.2
  68.5 11.6 %collective-permute-start.3 = (f32[6912,128]{1,0:T(8,128)}, f32[6912,128]{1,0:T(8,128)S(1)}, u32[]{:S(2)}, u32[]{:S(2)}) collective-permute-start(f32[6912,128]{1,0:T(8,128)} %get-tuple-element.38), channel_id=1, source_target_pairs={{0,1},{1,0},{2,3},{3,2},{4,5},{5,4},{6,7},{7,6},{8,9},{9,8},{10,11... | collective-permute-start | bytes 10616840 | tf_op jit(solution)/shard_map/ppermute | solution.py:658
  78.6 1.4 collective-permute-start.4
  80.1 1.8 copy-start
  86.4 62.7 %all-to-all-start = ((f32[64,1,13952]{2,1,0:T(1,128)}), f32[64,1,13952]{2,1,0:T(1,128)}, u32[]{:S(2)}, u32[]{:S(2)}) async-start(f32[64,1,13952]{2,1,0:T(1,128)} %bitcast.31), calls=%async_computation | async-start | bytes 7143424 | tf_op jit(solution)/shard_map/all_to_all | solution.py:494
  99.4 11.8 %copy-start.7 = (f32[13824]{0:T(1024)S(1)}, f32[13824]{0:T(1024)}, u32[]{:S(2)}) copy-start(f32[13824]{0:T(1024)} %param.12) | copy-start | bytes 165892
  99.4 11.8 %copy-start.8 = (f32[13824]{0:T(1024)S(1)}, f32[13824]{0:T(1024)}, u32[]{:S(2)}) copy-start(f32[13824]{0:T(1024)} %param.11) | copy-start | bytes 165892
  106.1 37.9 %collective-permute-start.7 = (f32[40,384]{1,0:T(8,128)}, f32[40,384]{1,0:T(8,128)S(1)}, u32[]{:S(2)}, u32[]{:S(2)}) collective-permute-start(f32[40,384]{1,0:T(8,128)} %get-tuple-element.46), channel_id=1, source_target_pairs={{0,17},{1,18},{2,19},{3,20},{4,21},{5,22},{6,23},{7,24},{8,25},{9,... | collective-permute-start | bytes 184328 | tf_op jit(solution)/shard_map/ppermute | solution.py:504
  110.0 39.0 %collective-permute-start.5 = (f32[112,384]{1,0:T(8,128)}, f32[112,384]{1,0:T(8,128)S(1)}, u32[]{:S(2)}, u32[]{:S(2)}) collective-permute-start(f32[112,384]{1,0:T(8,128)} %get-tuple-element.44), channel_id=1, source_target_pairs={{0,1},{1,2},{2,3},{3,4},{4,5},{5,6},{6,7},{7,8},{8,9},{9,10},{10,1... | collective-permute-start | bytes 516104 | tf_op jit(solution)/shard_map/ppermute | solution.py:499
  110.0 39.0 %collective-permute-start.6 = (f32[112,384]{1,0:T(8,128)}, f32[112,384]{1,0:T(8,128)S(1)}, u32[]{:S(2)}, u32[]{:S(2)}) collective-permute-start(f32[112,384]{1,0:T(8,128)} %get-tuple-element.45), channel_id=1, source_target_pairs={{0,16},{16,32},{32,48},{48,64},{64,80},{80,96},{96,112},{112,0},{1... | collective-permute-start | bytes 516104 | tf_op jit(solution)/shard_map/ppermute | solution.py:499
  111.2 37.8 %collective-permute-start.8 = (f32[2,108,128]{2,1,0:T(8,128)S(1)}, f32[2,108,128]{2,1,0:T(8,128)S(1)}, u32[]{:S(2)}, u32[]{:S(2)}) collective-permute-start(f32[2,108,128]{2,1,0:T(8,128)S(1)} %pad_maximum_fusion), channel_id=1, source_target_pairs={{0,0},{1,2},{2,4},{3,6},{4,8},{5,10},{6,12},{7,14},{8,16},{9,18},{... | collective-permute-start | bytes 331784 | tf_op jit(solution)/shard_map/ppermute | solution.py:673
  144.0 10.0 %copy-start.6 = (f32[40,384]{1,0:T(8,128)}, f32[40,384]{1,0:T(8,128)S(1)}, u32[]{:S(2)}) copy-start(f32[40,384]{1,0:T(8,128)S(1)} %collective-permute-done.7.corner) | copy-start | bytes 184324
  149.1 5.0 %copy-start.3 = (f32[112,384]{1,0:T(8,128)}, f32[112,384]{1,0:T(8,128)S(1)}, u32[]{:S(2)}) copy-start(f32[112,384]{1,0:T(8,128)S(1)} %collective-permute-done.5.west) | copy-start | bytes 516100
  149.1 5.0 %copy-start.4 = (f32[112,384]{1,0:T(8,128)}, f32[112,384]{1,0:T(8,128)S(1)}, u32[]{:S(2)}) copy-start(f32[112,384]{1,0:T(8,128)S(1)} %collective-permute-done.6.north) | copy-start | bytes 516100
  154.0 8.1 %copy-start.9 = (f32[108,128]{1,0:T(8,128)S(1)}, f32[108,128]{1,0:T(8,128)}, u32[]{:S(2)}) copy-start(f32[108,128]{1,0:T(8,128)} %get-tuple-element.52) | copy-start | bytes 165892
  154.0 8.1 %copy-start.10 = (f32[108,128]{1,0:T(8,128)S(1)}, f32[108,128]{1,0:T(8,128)}, u32[]{:S(2)}) copy-start(f32[108,128]{1,0:T(8,128)} %get-tuple-element.53) | copy-start | bytes 165892
  154.0 50.9 %all-to-all-start.1 = ((f32[64,1,13952]{2,1,0:T(1,128)}), f32[64,1,13952]{2,1,0:T(1,128)}, u32[]{:S(2)}, u32[]{:S(2)}) async-start(f32[64,1,13952]{2,1,0:T(1,128)} %bitcast.33), calls=%async_computation.1 | async-start | bytes 7143424 | tf_op jit(solution)/shard_map/all_to_all | solution.py:494
  162.1 42.8 %collective-permute-start.9 = (f32[2,108,128]{2,1,0:T(8,128)S(1)}, f32[2,108,128]{2,1,0:T(8,128)S(1)}, u32[]{:S(2)}, u32[]{:S(2)}) collective-permute-start(f32[2,108,128]{2,1,0:T(8,128)S(1)} %pad_maximum_fusion.1), channel_id=1, source_target_pairs={{0,0},{2,1},{4,2},{6,3},{8,4},{10,5},{12,6},{14,7},{16,8},{18,9},{... | collective-permute-start | bytes 331784 | tf_op jit(solution)/shard_map/ppermute | solution.py:690
  204.9 11.0 %collective-permute-start.10 = (f32[6976,128]{1,0:T(8,128)}, f32[6976,128]{1,0:T(8,128)}, u32[]{:S(2)}, u32[]{:S(2)}) collective-permute-start(f32[6976,128]{1,0:T(8,128)} %bitcast.12.blocks), channel_id=1, source_target_pairs={{0,1},{1,0},{2,3},{3,2},{4,5},{5,4},{6,7},{7,6},{8,9},{9,8},{10,11... | collective-permute-start | bytes 10715144 | tf_op jit(solution)/shard_map/ppermute | solution.py:695
  (1 other events, 0.6 us)

commit v9 on v8

--- a/solution.py
+++ b/solution.py
@@ -650,6 +650,10 @@
     flat = weights.reshape(ROWS, 128)
     bias = bias_of_pairs(bias_table, bias_index)
     edges = edges_of(block_input, cotangent)
+    pairs_of = worker_pairs()
+    moments = jnp.stack([first_moment.reshape(OWN, 128), second_moment.reshape(OWN, 128)])
+    moments = lax.ppermute(moments, BOTH, pairs_of)
+    *edges, moments = lax.optimization_barrier((*edges, moments))
     core = lon_at % 2
     place = jnp.stack([core, (lat_at == 7).astype(jnp.int32)]).astype(jnp.int32)
     keep, send, dscore, x, grad, dqkv = run_block(
@@ -661,18 +665,13 @@
     summed = merged(keep, came, line, line_came)
     parts = exchanged(summed.reshape(64, 1, BLOCK * 128), chip_groups())
 
-    _, dqkv, first_moment, second_moment = lax.optimization_barrier(
-        (summed, dqkv, first_moment, second_moment)
-    )
+    _, dqkv = lax.optimization_barrier((summed, dqkv))
     o_l, o_e, o_s, o_c = run_input_grad(x, grad, dqkv, flat)
     from_west = around(o_e, "lon", 1)
     from_north = around(o_s, "lat", 1)
     from_corner = diagonal(o_c, 1)
-    pairs_of = worker_pairs()
-    moments = jnp.stack([first_moment.reshape(OWN, 128), second_moment.reshape(OWN, 128)])
-    moments = lax.ppermute(moments, BOTH, pairs_of)
-    parts, from_west, from_north, from_corner, moments = lax.optimization_barrier(
-        (parts, from_west, from_north, from_corner, moments)
+    parts, from_west, from_north, from_corner = lax.optimization_barrier(
+        (parts, from_west, from_north, from_corner)
     )
 
     shard = core * 64 + lat_at * 8 + lon_at // 2
@@ -689,13 +688,14 @@
     back = [(b, a) for a, b in pairs_of]
     moments = lax.ppermute(jnp.stack([first_new, second_new]), BOTH, back)
     grad_input = with_edges(o_l, from_west, from_north, from_corner)
-    mine, moments, grad_input = lax.optimization_barrier((mine, moments, grad_input))
+    mine, grad_input = lax.optimization_barrier((mine, grad_input))
 
     mine = mine.reshape(64 * BLOCK, 128)
     theirs = lax.ppermute(mine, BOTH, core_swap())
     weights_new, table = own_half(place, mine)
     table_new = table[: HEADS * 5].reshape(5, HEADS, 128).transpose(1, 0, 2)
     table_new = table_new.reshape(HEADS, 640)[:, :BIAS]
+    theirs, moments = lax.optimization_barrier((theirs, moments))
     weights_new = other_half(place, theirs, weights_new)
     return (
         grad_input,

time: 221 us -> 222 us (level)
  starting transfers between devices: 50.5 us -> 48.1 us
    all_to_all x2, waiting for transfers between devices: 0.01 us -> 37.5 us  [exchanged(): lax.all_to_all(value, BOTH, 0, 0, axis_index_groups=groups, tiled=True)]
    ppermute x1, waiting for transfers between devices: 36.2 us -> 0.09 us  [per_device(): moments = lax.ppermute(jnp.stack([first_new, second_new]), BOTH, back)]
    ppermute x1, waiting for transfers between devices: 5 us -> 0.01 us  [per_device(): moments = lax.ppermute(moments, BOTH, pairs_of)]
    ppermute x2, waiting for transfers between devices: 27.6 us -> 30.8 us  [diagonal(): lax.ppermute(value, BOTH, [(a * lon + o, (a + by) % lat * lon + (o + by)...]
    ppermute x1, starting transfers between devices: 4.27 us -> 2.01 us  [per_device(): moments = lax.ppermute(jnp.stack([first_new, second_new]), BOTH, back)]
  transfers between devices with their start and end apart: 13 -> 13, of which waited for: 5 -> 6; matrix products, arithmetic and copies ran while one was open for 2% -> 2% of each run, Pallas kernels for 13% -> 13%
where the time goes in v9:
time: 222 us; the launch traced here: 220 us
  Pallas kernels  91.1 us (41%)
  waiting for transfers between devices  71.2 us (32%)
  starting transfers between devices  48.1 us (22%)
  local copies, waits for them, and re-layouts  6.87 us (3%)
    pallas_call x1, Pallas kernels, run_block(): pl.pallas_call(block_pass, out_shape=[jax.ShapeDtypeStruct(s, F32) for s...  46.6 us
    all_to_all x2, waiting for transfers between devices, exchanged(): lax.all_to_all(value, BOTH, 0, 0, axis_index_groups=groups, tiled=True)  37.5 us
    ppermute x2, waiting for transfers between devices, diagonal(): lax.ppermute(value, BOTH, [(a * lon + o, (a + by) % lat * lon + (o + by)...  30.8 us
    all_to_all x2, starting transfers between devices, exchanged(): lax.all_to_all(value, BOTH, 0, 0, axis_index_groups=groups, tiled=True)  21 us
    ppermute x2, starting transfers between devices, diagonal(): lax.ppermute(value, BOTH, [(a * lon + o, (a + by) % lat * lon + (o + by)...  9.86 us
    pallas_call x1, Pallas kernels, table_gradient(): pl.pallas_call(table_sum, out_shape=jax.ShapeDtypeStruct((64, 128), F32),...  9.79 us
    pallas_call x1, Pallas kernels, run_input_grad(): pl.pallas_call(input_grad, out_shape=[jax.ShapeDtypeStruct(s, F32) for s...  6.62 us
    ppermute x1, starting transfers between devices, per_device(): theirs = lax.ppermute(mine, BOTH, core_swap())  6.57 us
  transfers between devices with their start and end apart: 13, of which 6 were waited for; matrix products, arithmetic and copies ran while one was open for 2% of the time, Pallas kernels for 13%

profile of v9, /device:TPU:1, one launch (start us, length us, event | category | flops | bytes accessed | tf_op | source)
XLA Modules:
  0.0 219.5 jit_solution(10384982822314604175)
XLA Ops:
  0.6 2.4 %pack.1 = (f32[2,112,384]{2,1,0:T(8,128)}, f32[2,112,384]{2,1,0:T(8,128)}, f32[2,40,384]{2,1,0:T(8,128)}) custom-call(f32[24,24,384]{2,1,0:T(8,128)} %x_l.1, f32[24,24,384]{2,1,0:T(8,128)} %c_l.1), custom_call_target="tpu_custom_call" | custom-call | tf_op jit(solution)/shard_map/pack/pallas_call | solution.py:526
  3.0 1.4 collective-permute-start
  4.5 3.6 %collective-permute-start.1 = (f32[2,112,384]{2,1,0:T(8,128)}, f32[2,112,384]{2,1,0:T(8,128)S(1)}, u32[]{:S(2)}, u32[]{:S(2)}) collective-permute-start(f32[2,112,384]{2,1,0:T(8,128)} %get-tuple-element.37), channel_id=1, source_target_pairs={{0,112},{16,0},{32,16},{48,32},{64,48},{80,64},{96,80},{112,96},{1... | collective-permute-start | bytes 1032200 | tf_op jit(solution)/shard_map/ppermute | solution.py:499
  8.0 5.9 %collective-permute-start.2 = (f32[2,40,384]{2,1,0:T(8,128)}, f32[2,40,384]{2,1,0:T(8,128)S(1)}, u32[]{:S(2)}, u32[]{:S(2)}) collective-permute-start(f32[2,40,384]{2,1,0:T(8,128)} %get-tuple-element.38), channel_id=1, source_target_pairs={{0,127},{1,112},{2,113},{3,114},{4,115},{5,116},{6,117},{7,118},{8... | collective-permute-start | bytes 368648 | tf_op jit(solution)/shard_map/ppermute | solution.py:504
  14.8 1.9 collective-permute-start.3
  16.8 6.5 %lookup.1.rest_1_ = f32[3,576,144]{2,1,0:T(8,128)} custom-call(f32[12,529]{1,0:T(8,128)} %table.1, s32[144,144]{1,0:T(8,128)} %index.3), custom_call_target="tpu_custom_call" | custom-call | tf_op jit(solution)/shard_map/lookup/pallas_call | solution.py:112
  24.8 46.6 %block_pass.1 = (f32[6912,128]{1,0:T(8,128)}, f32[6912,128]{1,0:T(8,128)}, f32[3,576,144]{2,1,0:T(8,128)}, f32[576,384]{1,0:T(8,128)}, f32[576,384]{1,0:T(8,128)}, /*index=5*/f32[576,1152]{1,0:T(8,128)}) custom-call(f32[24,24,384]{2,1,0:T(8,128)} %x_l.1, f32[24,24,384]{2,1,0:T(8,128)} %c_l.1, f32[2,112,384]{2,1,0:T(8,128)} %copy-done.1, ...), custom_call_target="tpu_custom_call" | custom-call | tf_op jit(solution)/shard_map/block_pass/pallas_call | solution.py:420
  71.4 9.8 %table_sum.1.line = f32[64,128]{1,0:T(8,128)} custom-call(f32[3,576,144]{2,1,0:T(8,128)} %get-tuple-element.44.by_head, s32[144,144]{1,0:T(8,128)} %index.3), custom_call_target="tpu_custom_call" | custom-call | tf_op jit(solution)/shard_map/table_sum/pallas_call | solution.py:466
  83.4 1.2 copy-done
  84.6 4.5 %merge.1 = f32[6976,128]{1,0:T(8,128)} custom-call(f32[6912,128]{1,0:T(8,128)} %get-tuple-element.42.keep, f32[6912,128]{1,0:T(8,128)} %copy-done, f32[64,128]{1,0:T(8,128)} %table_sum.1.line, f32[64,128]{1,0:T(8,128)} %copy-done.9), custom_call_target="tpu_custom_call" | custom-call | tf_op jit(solution)/shard_map/merge/pallas_call | solution.py:567
  89.1 12.6 %all-to-all-start = ((f32[64,1,13952]{2,1,0:T(1,128)}), f32[64,1,13952]{2,1,0:T(1,128)}, u32[]{:S(2)}, u32[]{:S(2)}) async-start(f32[64,1,13952]{2,1,0:T(1,128)} %bitcast.31), calls=%async_computation | async-start | bytes 7143424 | tf_op jit(solution)/shard_map/all_to_all | solution.py:494
  101.7 1.5 constant_dynamic-slice_fusion.weights
  103.2 6.6 %input_grad.1 = (f32[24,24,384]{2,1,0:T(8,128)}, f32[112,384]{1,0:T(8,128)}, f32[112,384]{1,0:T(8,128)}, f32[40,384]{1,0:T(8,128)}) custom-call(f32[576,384]{1,0:T(8,128)} %get-tuple-element.45.x, f32[576,384]{1,0:T(8,128)} %get-tuple-element.46.grad, f32[576,1152]{1,0:T(8,128)} %get-tuple-element.48.dqkv, f32[13824,128]{1,0:T(8,128)} %bitcast.30), custom_call_target="tpu_custom_call" | custom-call | tf_op jit(solution)/shard_map/input_grad/pallas_call | solution.py:375
  109.8 3.9 %collective-permute-start.8 = (f32[40,384]{1,0:T(8,128)}, f32[40,384]{1,0:T(8,128)S(1)}, u32[]{:S(2)}, u32[]{:S(2)}) collective-permute-start(f32[40,384]{1,0:T(8,128)} %get-tuple-element.51), channel_id=1, source_target_pairs={{0,17},{1,18},{2,19},{3,20},{4,21},{5,22},{6,23},{7,24},{8,25},{9,... | collective-permute-start | bytes 184328 | tf_op jit(solution)/shard_map/ppermute | solution.py:504
  113.8 1.2 collective-permute-start.7
  115.6 30.8 %collective-permute-done.8.corner = f32[40,384]{1,0:T(8,128)S(1)} collective-permute-done((f32[40,384]{1,0:T(8,128)}, f32[40,384]{1,0:T(8,128)S(1)}, u32[]{:S(2)}, u32[]{:S(2)}) %collective-permute-start.8) | collective-permute-done | bytes 61472 | tf_op jit(solution)/shard_map/ppermute | solution.py:504
  148.2 4.3 %adam.1 = (f32[6976,128]{1,0:T(8,128)}, f32[108,128]{1,0:T(8,128)}, f32[108,128]{1,0:T(8,128)}) custom-call(f32[6976,128]{1,0:T(8,128)} %bitcast.6.parts, f32[108,128]{1,0:T(8,128)} %constant_dynamic-slice_fusion.weights, f32[108,128]{1,0:T(8,128)} %get-tuple-element.70.first, f32[108,128]{1,0:T(8,128)} %get-tuple-element.69.second), custom_call_target="tpu_custom_call" | custom-call | tf_op jit(solution)/shard_map/adam/pallas_call | solution.py:679
  152.4 8.4 %all-to-all-start.1 = ((f32[64,1,13952]{2,1,0:T(1,128)}), f32[64,1,13952]{2,1,0:T(1,128)}, u32[]{:S(2)}, u32[]{:S(2)}) async-start(f32[64,1,13952]{2,1,0:T(1,128)} %bitcast.33), calls=%async_computation.1 | async-start | bytes 7143424 | tf_op jit(solution)/shard_map/all_to_all | solution.py:494
  160.9 2.3 %unpack_edges.1 = f32[24,24,384]{2,1,0:T(8,128)} custom-call(f32[24,24,384]{2,1,0:T(8,128)} %get-tuple-element.55.local, f32[112,384]{1,0:T(8,128)} %copy-done.3, f32[112,384]{1,0:T(8,128)} %copy-done.4, f32[40,384]{1,0:T(8,128)} %copy-done.6), custom_call_target="tpu_custom_call" | custom-call | tf_op jit(solution)/shard_map/unpack_edges/pallas_call | solution.py:547
  163.1 37.5 %all-to-all-done.1 = f32[64,1,13952]{2,1,0:T(1,128)} async-done(((f32[64,1,13952]{2,1,0:T(1,128)}), f32[64,1,13952]{2,1,0:T(1,128)}, u32[]{:S(2)}, u32[]{:S(2)}) %all-to-all-start.1) | async-done | bytes 3571744 | tf_op jit(solution)/shard_map/all_to_all | solution.py:494
  200.6 6.6 %collective-permute-start.9 = (f32[6976,128]{1,0:T(8,128)}, f32[6976,128]{1,0:T(8,128)}, u32[]{:S(2)}, u32[]{:S(2)}) collective-permute-start(f32[6976,128]{1,0:T(8,128)} %bitcast.10.blocks), channel_id=1, source_target_pairs={{0,1},{1,0},{2,3},{3,2},{4,5},{5,4},{6,7},{7,6},{8,9},{9,8},{10,11... | collective-permute-start | bytes 10715144 | tf_op jit(solution)/shard_map/ppermute | solution.py:694
  207.2 2.0 collective-permute-start.10
  209.2 4.1 %lay_out_own.1 = (f32[13824,128]{1,0:T(8,128)}, f32[64,128]{1,0:T(8,128)}) custom-call(s32[2]{0:T(128)} %pad_add_fusion.place, f32[6976,128]{1,0:T(8,128)} %bitcast.10.blocks), custom_call_target="tpu_custom_call" | custom-call | tf_op jit(solution)/shard_map/lay_out_own/pallas_call | solution.py:608
  215.5 4.1 %lay_out_other.1 = f32[13824,128]{1,0:T(8,128)} custom-call(s32[2]{0:T(128)} %pad_add_fusion.place, f32[6976,128]{1,0:T(8,128)} %collective-permute-done.9.blocks, f32[13824,128]{1,0:T(8,128)} %get-tuple-element.64.refs_0_), custom_call_target="tpu_custom_call", output_to_operand_aliasing={{}: (2, {})} | custom-call | tf_op jit(solution)/shard_map/lay_out_other/pallas_call | solution.py:627
  (42 shorter events, 9.2 us)
Async XLA Ops:
  3.0 20.8 %collective-permute-start = (f32[2,112,384]{2,1,0:T(8,128)}, f32[2,112,384]{2,1,0:T(8,128)S(1)}, u32[]{:S(2)}, u32[]{:S(2)}) collective-permute-start(f32[2,112,384]{2,1,0:T(8,128)} %get-tuple-element.36), channel_id=1, source_target_pairs={{0,15},{1,0},{2,1},{3,2},{4,3},{5,4},{6,5},{7,6},{8,7},{9,8},{10,9... | collective-permute-start | bytes 1032200 | tf_op jit(solution)/shard_map/ppermute | solution.py:499
  4.5 19.4 %collective-permute-start.1 = (f32[2,112,384]{2,1,0:T(8,128)}, f32[2,112,384]{2,1,0:T(8,128)S(1)}, u32[]{:S(2)}, u32[]{:S(2)}) collective-permute-start(f32[2,112,384]{2,1,0:T(8,128)} %get-tuple-element.37), channel_id=1, source_target_pairs={{0,112},{16,0},{32,16},{48,32},{64,48},{80,64},{96,80},{112,96},{1... | collective-permute-start | bytes 1032200 | tf_op jit(solution)/shard_map/ppermute | solution.py:499
  8.0 15.8 %collective-permute-start.2 = (f32[2,40,384]{2,1,0:T(8,128)}, f32[2,40,384]{2,1,0:T(8,128)S(1)}, u32[]{:S(2)}, u32[]{:S(2)}) collective-permute-start(f32[2,40,384]{2,1,0:T(8,128)} %get-tuple-element.38), channel_id=1, source_target_pairs={{0,127},{1,112},{2,113},{3,114},{4,115},{5,116},{6,117},{7,118},{8... | collective-permute-start | bytes 368648 | tf_op jit(solution)/shard_map/ppermute | solution.py:504
  14.8 9.0 %collective-permute-start.3 = (f32[2,108,128]{2,1,0:T(8,128)S(1)}, f32[2,108,128]{2,1,0:T(8,128)S(1)}, u32[]{:S(2)}, u32[]{:S(2)}) collective-permute-start(f32[2,108,128]{2,1,0:T(8,128)S(1)} %pad_maximum_fusion), channel_id=1, source_target_pairs={{0,0},{1,2},{2,4},{3,6},{4,8},{5,10},{6,12},{7,14},{8,16},{9,18},{... | collective-permute-start | bytes 331784 | tf_op jit(solution)/shard_map/ppermute | solution.py:655
  23.8 0.7 copy-start.5
  23.9 0.8 copy-start.1
  23.9 0.9 copy-start.2
  71.3 11.4 %collective-permute-start.4 = (f32[6912,128]{1,0:T(8,128)}, f32[6912,128]{1,0:T(8,128)S(1)}, u32[]{:S(2)}, u32[]{:S(2)}) collective-permute-start(f32[6912,128]{1,0:T(8,128)} %get-tuple-element.43), channel_id=1, source_target_pairs={{0,1},{1,0},{2,3},{3,2},{4,5},{5,4},{6,7},{7,6},{8,9},{9,8},{10,11... | collective-permute-start | bytes 10616840 | tf_op jit(solution)/shard_map/ppermute | solution.py:662
  81.2 1.6 collective-permute-start.5
  82.8 0.6 copy-start.9
  82.8 1.8 copy-start
  89.1 59.0 %all-to-all-start = ((f32[64,1,13952]{2,1,0:T(1,128)}), f32[64,1,13952]{2,1,0:T(1,128)}, u32[]{:S(2)}, u32[]{:S(2)}) async-start(f32[64,1,13952]{2,1,0:T(1,128)} %bitcast.31), calls=%async_computation | async-start | bytes 7143424 | tf_op jit(solution)/shard_map/all_to_all | solution.py:494
  109.8 36.5 %collective-permute-start.8 = (f32[40,384]{1,0:T(8,128)}, f32[40,384]{1,0:T(8,128)S(1)}, u32[]{:S(2)}, u32[]{:S(2)}) collective-permute-start(f32[40,384]{1,0:T(8,128)} %get-tuple-element.51), channel_id=1, source_target_pairs={{0,17},{1,18},{2,19},{3,20},{4,21},{5,22},{6,23},{7,24},{8,25},{9,... | collective-permute-start | bytes 184328 | tf_op jit(solution)/shard_map/ppermute | solution.py:504
  113.8 33.5 %collective-permute-start.6 = (f32[112,384]{1,0:T(8,128)}, f32[112,384]{1,0:T(8,128)S(1)}, u32[]{:S(2)}, u32[]{:S(2)}) collective-permute-start(f32[112,384]{1,0:T(8,128)} %get-tuple-element.49), channel_id=1, source_target_pairs={{0,1},{1,2},{2,3},{3,4},{4,5},{5,6},{6,7},{7,8},{8,9},{9,10},{10,1... | collective-permute-start | bytes 516104 | tf_op jit(solution)/shard_map/ppermute | solution.py:499
  113.8 34.4 %collective-permute-start.7 = (f32[112,384]{1,0:T(8,128)}, f32[112,384]{1,0:T(8,128)S(1)}, u32[]{:S(2)}, u32[]{:S(2)}) collective-permute-start(f32[112,384]{1,0:T(8,128)} %get-tuple-element.50), channel_id=1, source_target_pairs={{0,16},{16,32},{32,48},{48,64},{64,80},{80,96},{96,112},{112,0},{1... | collective-permute-start | bytes 516104 | tf_op jit(solution)/shard_map/ppermute | solution.py:499
  146.4 6.1 %copy-start.6 = (f32[40,384]{1,0:T(8,128)}, f32[40,384]{1,0:T(8,128)S(1)}, u32[]{:S(2)}) copy-start(f32[40,384]{1,0:T(8,128)S(1)} %collective-permute-done.8.corner) | copy-start | bytes 184324
  147.3 5.1 %copy-start.3 = (f32[112,384]{1,0:T(8,128)}, f32[112,384]{1,0:T(8,128)S(1)}, u32[]{:S(2)}) copy-start(f32[112,384]{1,0:T(8,128)S(1)} %collective-permute-done.6.west) | copy-start | bytes 516100
  148.1 4.3 %copy-start.4 = (f32[112,384]{1,0:T(8,128)}, f32[112,384]{1,0:T(8,128)S(1)}, u32[]{:S(2)}) copy-start(f32[112,384]{1,0:T(8,128)S(1)} %collective-permute-done.7.north) | copy-start | bytes 516100
  152.4 54.8 %copy-start.7 = (f32[108,128]{1,0:T(8,128)S(1)}, f32[108,128]{1,0:T(8,128)}, u32[]{:S(2)}) copy-start(f32[108,128]{1,0:T(8,128)} %get-tuple-element.61) | copy-start | bytes 165892
  152.4 54.8 %copy-start.8 = (f32[108,128]{1,0:T(8,128)S(1)}, f32[108,128]{1,0:T(8,128)}, u32[]{:S(2)}) copy-start(f32[108,128]{1,0:T(8,128)} %get-tuple-element.62) | copy-start | bytes 165892
  152.4 48.2 %all-to-all-start.1 = ((f32[64,1,13952]{2,1,0:T(1,128)}), f32[64,1,13952]{2,1,0:T(1,128)}, u32[]{:S(2)}, u32[]{:S(2)}) async-start(f32[64,1,13952]{2,1,0:T(1,128)} %bitcast.33), calls=%async_computation.1 | async-start | bytes 7143424 | tf_op jit(solution)/shard_map/all_to_all | solution.py:494
  200.6 14.2 %collective-permute-start.9 = (f32[6976,128]{1,0:T(8,128)}, f32[6976,128]{1,0:T(8,128)}, u32[]{:S(2)}, u32[]{:S(2)}) collective-permute-start(f32[6976,128]{1,0:T(8,128)} %bitcast.10.blocks), channel_id=1, source_target_pairs={{0,1},{1,0},{2,3},{3,2},{4,5},{5,4},{6,7},{7,6},{8,9},{9,8},{10,11... | collective-permute-start | bytes 10715144 | tf_op jit(solution)/shard_map/ppermute | solution.py:694
  207.2 7.6 %collective-permute-start.10 = (f32[2,108,128]{2,1,0:T(8,128)S(1)}, f32[2,108,128]{2,1,0:T(8,128)S(1)}, u32[]{:S(2)}, u32[]{:S(2)}) collective-permute-start(f32[2,108,128]{2,1,0:T(8,128)S(1)} %pad_maximum_fusion.1), channel_id=1, source_target_pairs={{0,0},{2,1},{4,2},{6,3},{8,4},{10,5},{12,6},{14,7},{16,8},{18,9},{... | collective-permute-start | bytes 331784 | tf_op jit(solution)/shard_map/ppermute | solution.py:689

commit v10 on v7

--- a/solution.py
+++ b/solution.py
@@ -366,7 +366,7 @@
         dqkv[rows, k_at] = dot3_wide(dss, q, TN)
         return carry
 
-    lax.fori_loop(0, WINS * GROUPS, attend_back, 0, unroll=4)
+    lax.fori_loop(0, WINS * GROUPS, attend_back, 0, unroll=12)
 
     kept[2].start()
     dq = split(dqkv[...])

time: 220 us -> 218 us (level)
  Pallas kernels: 93.4 us -> 91.2 us
    pallas_call x1, Pallas kernels: 45.7 us -> 43.5 us  [run_block(): pl.pallas_call(block_pass, out_shape=[jax.ShapeDtypeStruct(s, F32) for s...]
where the time goes in v10:
time: 218 us; the launch traced here: 217 us
  Pallas kernels  91.2 us (42%)
  waiting for transfers between devices  72.9 us (33%)
  starting transfers between devices  44.3 us (20%)
  local copies, waits for them, and re-layouts  7 us (3%)
    pallas_call x1, Pallas kernels, run_block(): pl.pallas_call(block_pass, out_shape=[jax.ShapeDtypeStruct(s, F32) for s...  43.5 us
    ppermute x1, waiting for transfers between devices, per_device(): moments = lax.ppermute(jnp.stack([first_new, second_new]), BOTH, back)  39.4 us
    ppermute x2, waiting for transfers between devices, diagonal(): lax.ppermute(value, BOTH, [(a * lon + o, (a + by) % lat * lon + (o + by)...  32.4 us
    all_to_all x2, starting transfers between devices, exchanged(): lax.all_to_all(value, BOTH, 0, 0, axis_index_groups=groups, tiled=True)  16.9 us
    pallas_call x1, Pallas kernels, prepared(): pl.pallas_call(prepare, out_shape=[jax.ShapeDtypeStruct(s, BF16) for s in...  9.89 us
    pallas_call x1, Pallas kernels, table_gradient(): pl.pallas_call(table_sum, out_shape=jax.ShapeDtypeStruct((64, 128), F32),...  9.77 us
    ppermute x4, starting transfers between devices, around(): lax.ppermute(value, axis, [(i, (i + by) % size) for i in range(size)])  9.43 us
    ppermute x2, starting transfers between devices, diagonal(): lax.ppermute(value, BOTH, [(a * lon + o, (a + by) % lat * lon + (o + by)...  9.01 us
  transfers between devices with their start and end apart: 13, of which 4 were waited for; matrix products, arithmetic and copies ran while one was open for 2% of the time, Pallas kernels for 15%

profile of v10, /device:TPU:1, one launch (start us, length us, event | category | flops | bytes accessed | tf_op | source)
XLA Modules:
  0.0 216.9 jit_solution(14484955232439542958)
XLA Ops:
  0.6 2.4 %pack.1 = (f32[2,112,384]{2,1,0:T(8,128)}, f32[2,112,384]{2,1,0:T(8,128)}, f32[2,40,384]{2,1,0:T(8,128)}) custom-call(f32[24,24,384]{2,1,0:T(8,128)} %x_l.1, f32[24,24,384]{2,1,0:T(8,128)} %c_l.1), custom_call_target="tpu_custom_call" | custom-call | tf_op jit(solution)/shard_map/pack/pallas_call | solution.py:534
  3.0 1.4 collective-permute-start
  4.5 3.6 %collective-permute-start.1 = (f32[2,112,384]{2,1,0:T(8,128)}, f32[2,112,384]{2,1,0:T(8,128)S(1)}, u32[]{:S(2)}, u32[]{:S(2)}) collective-permute-start(f32[2,112,384]{2,1,0:T(8,128)} %get-tuple-element.44), channel_id=1, source_target_pairs={{0,112},{16,0},{32,16},{48,32},{64,48},{80,64},{96,80},{112,96},{1... | collective-permute-start | bytes 1032200 | tf_op jit(solution)/shard_map/ppermute | solution.py:507
  8.0 5.9 %collective-permute-start.2 = (f32[2,40,384]{2,1,0:T(8,128)}, f32[2,40,384]{2,1,0:T(8,128)S(1)}, u32[]{:S(2)}, u32[]{:S(2)}) collective-permute-start(f32[2,40,384]{2,1,0:T(8,128)} %get-tuple-element.45), channel_id=1, source_target_pairs={{0,127},{1,112},{2,113},{3,114},{4,115},{5,116},{6,117},{7,118},{8... | collective-permute-start | bytes 368648 | tf_op jit(solution)/shard_map/ppermute | solution.py:512
  13.9 9.9 %prepare.1 = (bf16[384,1152]{1,0:T(8,128)(2,1)}, bf16[384,1152]{1,0:T(8,128)(2,1)}, bf16[384,384]{1,0:T(8,128)(2,1)}, bf16[384,384]{1,0:T(8,128)(2,1)}, bf16[6,3...) custom-call(f32[13824,128]{1,0:T(8,128)} %bitcast.28, ...), custom_call_target="tpu_custom_call" | custom-call | tf_op jit(solution)/shard_map/prepare/pallas_call | solution.py:138
  25.4 43.5 %block_pass.1 = (f32[6912,128]{1,0:T(8,128)}, f32[6912,128]{1,0:T(8,128)}, f32[3,576,144]{2,1,0:T(8,128)}, f32[576,384]{1,0:T(8,128)}, f32[576,384]{1,0:T(8,128)}, /*index=5*/f32[576,1152]{1,0:T(8,128)}) custom-call(f32[24,24,384]{2,1,0:T(8,128)} %x_l.1, f32[24,24,384]{2,1,0:T(8,128)} %c_l.1, f32[2,112,384]{2,1,0:T(8,128)} %copy-done.1, ...), custom_call_target="tpu_custom_call" | custom-call | tf_op jit(solution)/shard_map/block_pass/pallas_call | solution.py:428
  69.3 9.8 %table_sum.1.line = f32[64,128]{1,0:T(8,128)} custom-call(f32[3,576,144]{2,1,0:T(8,128)} %get-tuple-element.57.by_head, s32[144,144]{1,0:T(8,128)} %index.3), custom_call_target="tpu_custom_call" | custom-call | tf_op jit(solution)/shard_map/table_sum/pallas_call | solution.py:474
  81.2 1.2 copy-done
  82.4 4.5 %merge.1 = f32[6976,128]{1,0:T(8,128)} custom-call(f32[6912,128]{1,0:T(8,128)} %get-tuple-element.55.keep, f32[6912,128]{1,0:T(8,128)} %copy-done, f32[64,128]{1,0:T(8,128)} %table_sum.1.line, f32[64,128]{1,0:T(8,128)} %copy-done.11), custom_call_target="tpu_custom_call" | custom-call | tf_op jit(solution)/shard_map/merge/pallas_call | solution.py:575
  86.9 9.4 %all-to-all-start = ((f32[64,1,13952]{2,1,0:T(1,128)}), f32[64,1,13952]{2,1,0:T(1,128)}, u32[]{:S(2)}, u32[]{:S(2)}) async-start(f32[64,1,13952]{2,1,0:T(1,128)} %bitcast.33), calls=%async_computation | async-start | bytes 7143424 | tf_op jit(solution)/shard_map/all_to_all | solution.py:502
  96.4 6.4 %input_grad.1 = (f32[24,24,384]{2,1,0:T(8,128)}, f32[112,384]{1,0:T(8,128)}, f32[112,384]{1,0:T(8,128)}, f32[40,384]{1,0:T(8,128)}) custom-call(f32[576,384]{1,0:T(8,128)} %get-tuple-element.58.x, f32[576,384]{1,0:T(8,128)} %get-tuple-element.59.grad, f32[576,1152]{1,0:T(8,128)} %get-tuple-element.61.dqkv, bf16[384,1152]{1,0:T(8,128)(2,1)} %get-tuple-element.46.rest_0_.wq_h, ...), custom_call_target="tpu_custom_call" | custom-call | tf_op jit(solution)/shard_map/input_grad/pallas_call | solution.py:392
  102.8 3.2 %collective-permute-start.5 = (f32[112,384]{1,0:T(8,128)}, f32[112,384]{1,0:T(8,128)S(1)}, u32[]{:S(2)}, u32[]{:S(2)}) collective-permute-start(f32[112,384]{1,0:T(8,128)} %get-tuple-element.62), channel_id=1, source_target_pairs={{0,1},{1,2},{2,3},{3,4},{4,5},{5,6},{6,7},{7,8},{8,9},{9,10},{10,1... | collective-permute-start | bytes 516104 | tf_op jit(solution)/shard_map/ppermute | solution.py:507
  107.2 2.2 %collective-permute-start.8 = (f32[2,108,128]{2,1,0:T(8,128)S(1)}, f32[2,108,128]{2,1,0:T(8,128)S(1)}, u32[]{:S(2)}, u32[]{:S(2)}) collective-permute-start(f32[2,108,128]{2,1,0:T(8,128)S(1)} %pad_maximum_fusion), channel_id=1, source_target_pairs={{0,0},{1,2},{2,4},{3,6},{4,8},{5,10},{6,12},{7,14},{8,16},{9,18},{... | collective-permute-start | bytes 331784 | tf_op jit(solution)/shard_map/ppermute | solution.py:681
  109.5 3.1 %collective-permute-start.7 = (f32[40,384]{1,0:T(8,128)}, f32[40,384]{1,0:T(8,128)S(1)}, u32[]{:S(2)}, u32[]{:S(2)}) collective-permute-start(f32[40,384]{1,0:T(8,128)} %get-tuple-element.64), channel_id=1, source_target_pairs={{0,17},{1,18},{2,19},{3,20},{4,21},{5,22},{6,23},{7,24},{8,25},{9,... | collective-permute-start | bytes 184328 | tf_op jit(solution)/shard_map/ppermute | solution.py:512
  112.5 1.5 constant_dynamic-slice_fusion.weights
  114.0 32.4 %collective-permute-done.7.corner = f32[40,384]{1,0:T(8,128)S(1)} collective-permute-done((f32[40,384]{1,0:T(8,128)}, f32[40,384]{1,0:T(8,128)S(1)}, u32[]{:S(2)}, u32[]{:S(2)}) %collective-permute-start.7) | collective-permute-done | bytes 61472 | tf_op jit(solution)/shard_map/ppermute | solution.py:512
  147.2 4.2 %adam.1 = (f32[6976,128]{1,0:T(8,128)}, f32[108,128]{1,0:T(8,128)}, f32[108,128]{1,0:T(8,128)}) custom-call(f32[6976,128]{1,0:T(8,128)} %bitcast.6.parts, f32[108,128]{1,0:T(8,128)} %constant_dynamic-slice_fusion.weights, f32[108,128]{1,0:T(8,128)} %get-tuple-element.84.first, f32[108,128]{1,0:T(8,128)} %get-tuple-element.83.second), custom_call_target="tpu_custom_call" | custom-call | tf_op jit(solution)/shard_map/adam/pallas_call | solution.py:688
  151.4 7.6 %all-to-all-start.1 = ((f32[64,1,13952]{2,1,0:T(1,128)}), f32[64,1,13952]{2,1,0:T(1,128)}, u32[]{:S(2)}, u32[]{:S(2)}) async-start(f32[64,1,13952]{2,1,0:T(1,128)} %bitcast.35), calls=%async_computation.1 | async-start | bytes 7143424 | tf_op jit(solution)/shard_map/all_to_all | solution.py:502
  159.0 4.5 %collective-permute-start.9 = (f32[2,108,128]{2,1,0:T(8,128)S(1)}, f32[2,108,128]{2,1,0:T(8,128)S(1)}, u32[]{:S(2)}, u32[]{:S(2)}) collective-permute-start(f32[2,108,128]{2,1,0:T(8,128)S(1)} %pad_maximum_fusion.1), channel_id=1, source_target_pairs={{0,0},{2,1},{4,2},{6,3},{8,4},{10,5},{12,6},{14,7},{16,8},{18,9},{... | collective-permute-start | bytes 331784 | tf_op jit(solution)/shard_map/ppermute | solution.py:698
  163.5 2.3 %unpack_edges.1 = f32[24,24,384]{2,1,0:T(8,128)} custom-call(f32[24,24,384]{2,1,0:T(8,128)} %get-tuple-element.72.local, f32[112,384]{1,0:T(8,128)} %copy-done.3, f32[112,384]{1,0:T(8,128)} %copy-done.4, f32[40,384]{1,0:T(8,128)} %copy-done.6), custom_call_target="tpu_custom_call" | custom-call | tf_op jit(solution)/shard_map/unpack_edges/pallas_call | solution.py:555
  165.8 39.4 %collective-permute-done.9 = f32[2,108,128]{2,1,0:T(8,128)S(1)} collective-permute-done((f32[2,108,128]{2,1,0:T(8,128)S(1)}, f32[2,108,128]{2,1,0:T(8,128)S(1)}, u32[]{:S(2)}, u32[]{:S(2)}) %collective-permute-start.9) | collective-permute-done | bytes 110624 | tf_op jit(solution)/shard_map/ppermute | solution.py:698
  205.2 1.4 collective-permute-start.10
  206.6 4.1 %lay_out_own.1 = (f32[13824,128]{1,0:T(8,128)}, f32[64,128]{1,0:T(8,128)}) custom-call(s32[2]{0:T(128)} %pad_add_fusion.place, f32[6976,128]{1,0:T(8,128)} %bitcast.12.blocks), custom_call_target="tpu_custom_call" | custom-call | tf_op jit(solution)/shard_map/lay_out_own/pallas_call | solution.py:616
  212.9 4.1 %lay_out_other.1 = f32[13824,128]{1,0:T(8,128)} custom-call(s32[2]{0:T(128)} %pad_add_fusion.place, f32[6976,128]{1,0:T(8,128)} %collective-permute-done.10.blocks, f32[13824,128]{1,0:T(8,128)} %get-tuple-element.78.refs_0_), custom_call_target="tpu_custom_call", output_to_operand_aliasing={{}: (2, {})} | custom-call | tf_op jit(solution)/shard_map/lay_out_other/pallas_call | solution.py:635
  (46 shorter events, 8.2 us)
Async XLA Ops:
  3.0 21.5 %collective-permute-start = (f32[2,112,384]{2,1,0:T(8,128)}, f32[2,112,384]{2,1,0:T(8,128)S(1)}, u32[]{:S(2)}, u32[]{:S(2)}) collective-permute-start(f32[2,112,384]{2,1,0:T(8,128)} %get-tuple-element.43), channel_id=1, source_target_pairs={{0,15},{1,0},{2,1},{3,2},{4,3},{5,4},{6,5},{7,6},{8,7},{9,8},{10,9... | collective-permute-start | bytes 1032200 | tf_op jit(solution)/shard_map/ppermute | solution.py:507
  4.5 20.1 %collective-permute-start.1 = (f32[2,112,384]{2,1,0:T(8,128)}, f32[2,112,384]{2,1,0:T(8,128)S(1)}, u32[]{:S(2)}, u32[]{:S(2)}) collective-permute-start(f32[2,112,384]{2,1,0:T(8,128)} %get-tuple-element.44), channel_id=1, source_target_pairs={{0,112},{16,0},{32,16},{48,32},{64,48},{80,64},{96,80},{112,96},{1... | collective-permute-start | bytes 1032200 | tf_op jit(solution)/shard_map/ppermute | solution.py:507
  8.0 16.5 %collective-permute-start.2 = (f32[2,40,384]{2,1,0:T(8,128)}, f32[2,40,384]{2,1,0:T(8,128)S(1)}, u32[]{:S(2)}, u32[]{:S(2)}) collective-permute-start(f32[2,40,384]{2,1,0:T(8,128)} %get-tuple-element.45), channel_id=1, source_target_pairs={{0,127},{1,112},{2,113},{3,114},{4,115},{5,116},{6,117},{7,118},{8... | collective-permute-start | bytes 368648 | tf_op jit(solution)/shard_map/ppermute | solution.py:512
  24.5 0.6 copy-start.5
  24.5 0.8 copy-start.1
  24.5 0.9 copy-start.2
  69.0 11.6 %collective-permute-start.3 = (f32[6912,128]{1,0:T(8,128)}, f32[6912,128]{1,0:T(8,128)S(1)}, u32[]{:S(2)}, u32[]{:S(2)}) collective-permute-start(f32[6912,128]{1,0:T(8,128)} %get-tuple-element.56), channel_id=1, source_target_pairs={{0,1},{1,0},{2,3},{3,2},{4,5},{5,4},{6,7},{7,6},{8,9},{9,8},{10,11... | collective-permute-start | bytes 10616840 | tf_op jit(solution)/shard_map/ppermute | solution.py:666
  79.0 1.6 collective-permute-start.4
  80.6 1.8 copy-start
  86.9 59.5 %all-to-all-start = ((f32[64,1,13952]{2,1,0:T(1,128)}), f32[64,1,13952]{2,1,0:T(1,128)}, u32[]{:S(2)}, u32[]{:S(2)}) async-start(f32[64,1,13952]{2,1,0:T(1,128)} %bitcast.33), calls=%async_computation | async-start | bytes 7143424 | tf_op jit(solution)/shard_map/all_to_all | solution.py:502
  96.3 10.9 %copy-start.7 = (f32[13824]{0:T(1024)S(1)}, f32[13824]{0:T(1024)}, u32[]{:S(2)}) copy-start(f32[13824]{0:T(1024)} %param.12) | copy-start | bytes 165892
  96.3 10.9 %copy-start.8 = (f32[13824]{0:T(1024)S(1)}, f32[13824]{0:T(1024)}, u32[]{:S(2)}) copy-start(f32[13824]{0:T(1024)} %param.11) | copy-start | bytes 165892
  102.8 43.6 %collective-permute-start.5 = (f32[112,384]{1,0:T(8,128)}, f32[112,384]{1,0:T(8,128)S(1)}, u32[]{:S(2)}, u32[]{:S(2)}) collective-permute-start(f32[112,384]{1,0:T(8,128)} %get-tuple-element.62), channel_id=1, source_target_pairs={{0,1},{1,2},{2,3},{3,4},{4,5},{5,6},{6,7},{7,8},{8,9},{9,10},{10,1... | collective-permute-start | bytes 516104 | tf_op jit(solution)/shard_map/ppermute | solution.py:507
  106.0 40.4 %collective-permute-start.6 = (f32[112,384]{1,0:T(8,128)}, f32[112,384]{1,0:T(8,128)S(1)}, u32[]{:S(2)}, u32[]{:S(2)}) collective-permute-start(f32[112,384]{1,0:T(8,128)} %get-tuple-element.63), channel_id=1, source_target_pairs={{0,16},{16,32},{32,48},{48,64},{64,80},{80,96},{96,112},{112,0},{1... | collective-permute-start | bytes 516104 | tf_op jit(solution)/shard_map/ppermute | solution.py:507
  107.2 39.1 %collective-permute-start.8 = (f32[2,108,128]{2,1,0:T(8,128)S(1)}, f32[2,108,128]{2,1,0:T(8,128)S(1)}, u32[]{:S(2)}, u32[]{:S(2)}) collective-permute-start(f32[2,108,128]{2,1,0:T(8,128)S(1)} %pad_maximum_fusion), channel_id=1, source_target_pairs={{0,0},{1,2},{2,4},{3,6},{4,8},{5,10},{6,12},{7,14},{8,16},{9,18},{... | collective-permute-start | bytes 331784 | tf_op jit(solution)/shard_map/ppermute | solution.py:681
  109.5 36.9 %collective-permute-start.7 = (f32[40,384]{1,0:T(8,128)}, f32[40,384]{1,0:T(8,128)S(1)}, u32[]{:S(2)}, u32[]{:S(2)}) collective-permute-start(f32[40,384]{1,0:T(8,128)} %get-tuple-element.64), channel_id=1, source_target_pairs={{0,17},{1,18},{2,19},{3,20},{4,21},{5,22},{6,23},{7,24},{8,25},{9,... | collective-permute-start | bytes 184328 | tf_op jit(solution)/shard_map/ppermute | solution.py:512
  146.4 5.0 %copy-start.6 = (f32[40,384]{1,0:T(8,128)}, f32[40,384]{1,0:T(8,128)S(1)}, u32[]{:S(2)}) copy-start(f32[40,384]{1,0:T(8,128)S(1)} %collective-permute-done.7.corner) | copy-start | bytes 184324
  146.4 5.0 %copy-start.3 = (f32[112,384]{1,0:T(8,128)}, f32[112,384]{1,0:T(8,128)S(1)}, u32[]{:S(2)}) copy-start(f32[112,384]{1,0:T(8,128)S(1)} %collective-permute-done.5.west) | copy-start | bytes 516100
  146.4 5.0 %copy-start.4 = (f32[112,384]{1,0:T(8,128)}, f32[112,384]{1,0:T(8,128)S(1)}, u32[]{:S(2)}) copy-start(f32[112,384]{1,0:T(8,128)S(1)} %collective-permute-done.6.north) | copy-start | bytes 516100
  151.4 7.6 %copy-start.9 = (f32[108,128]{1,0:T(8,128)S(1)}, f32[108,128]{1,0:T(8,128)}, u32[]{:S(2)}) copy-start(f32[108,128]{1,0:T(8,128)} %get-tuple-element.70) | copy-start | bytes 165892
  151.4 7.6 %copy-start.10 = (f32[108,128]{1,0:T(8,128)S(1)}, f32[108,128]{1,0:T(8,128)}, u32[]{:S(2)}) copy-start(f32[108,128]{1,0:T(8,128)} %get-tuple-element.71) | copy-start | bytes 165892
  151.4 53.8 %all-to-all-start.1 = ((f32[64,1,13952]{2,1,0:T(1,128)}), f32[64,1,13952]{2,1,0:T(1,128)}, u32[]{:S(2)}, u32[]{:S(2)}) async-start(f32[64,1,13952]{2,1,0:T(1,128)} %bitcast.35), calls=%async_computation.1 | async-start | bytes 7143424 | tf_op jit(solution)/shard_map/all_to_all | solution.py:502
  159.0 46.2 %collective-permute-start.9 = (f32[2,108,128]{2,1,0:T(8,128)S(1)}, f32[2,108,128]{2,1,0:T(8,128)S(1)}, u32[]{:S(2)}, u32[]{:S(2)}) collective-permute-start(f32[2,108,128]{2,1,0:T(8,128)S(1)} %pad_maximum_fusion.1), channel_id=1, source_target_pairs={{0,0},{2,1},{4,2},{6,3},{8,4},{10,5},{12,6},{14,7},{16,8},{18,9},{... | collective-permute-start | bytes 331784 | tf_op jit(solution)/shard_map/ppermute | solution.py:698
  205.2 7.7 %collective-permute-start.10 = (f32[6976,128]{1,0:T(8,128)}, f32[6976,128]{1,0:T(8,128)}, u32[]{:S(2)}, u32[]{:S(2)}) collective-permute-start(f32[6976,128]{1,0:T(8,128)} %bitcast.12.blocks), channel_id=1, source_target_pairs={{0,1},{1,0},{2,3},{3,2},{4,5},{5,4},{6,7},{7,6},{8,9},{9,8},{10,11... | collective-permute-start | bytes 10715144 | tf_op jit(solution)/shard_map/ppermute | solution.py:703
  (1 other events, 0.6 us)
